TPU v7x, 256 devices: a whole 4x4x8 slice. The times are simulated.
256 devices in a mesh: gx: 8 (over z), gy: 16 (over y, x), gz: 2 (over core).
Axes of the slice: x: 4, y: 4, z: 8, core: 2. Of those that a mesh axis runs over, the one named last changes fastest.
Arguments:
- tensor: float32 [1024, 1024, 256], P('gx', 'gy', 'gz'), may hold values from -60 to 60
- factor_a: float32 [1024, 64], P(('gx', 'gy', 'gz')), may hold values from -6 to 6
- factor_b: float32 [1024, 64], P(('gy', 'gx', 'gz')), may hold values from -6 to 6
- factor_c: float32 [256, 64], P(('gz', 'gx', 'gy')), may hold values from -6 to 6
Outputs:
- slope_a: float32 [1024, 64], P(('gx', 'gy', 'gz'))
- slope_b: float32 [1024, 64], P(('gy', 'gx', 'gz'))
- slope_c: float32 [256, 64], P(('gz', 'gx', 'gy'))
All inputs are finite; a program needn't handle non-finite values.
Results may differ from a plain program's by a relative error of at most 0.0003.
Values sent between devices are 32-bit elements; how exact they have to be, the bound alone decides.
No kernel may reach another device: no remote copies, remote signals or barrier semaphores. Data moves between devices by JAX's collectives and lax.ppermute only.
A program may use at most 64 MiB of HBM per device.

v0:
```python
import jax
import jax.numpy as jnp
from jax import lax
from jax.sharding import PartitionSpec as P

STEPS = 2


step_size = 0.1


def gram_local(matrix):
    return jnp.dot(
        matrix.T, matrix, precision=lax.Precision.HIGHEST, preferred_element_type=jnp.float32
    )


def gather_blocks(own_a, own_b, own_c):
    block_a = lax.all_gather(own_a, ("gy", "gz"), axis=0, tiled=True)
    block_b = lax.all_gather(own_b, ("gx", "gz"), axis=0, tiled=True)
    block_c = lax.all_gather(own_c, ("gx", "gy"), axis=0, tiled=True)
    return (block_a, block_b, block_c)


def gram_sums(own_a, own_b, own_c):
    gram_a, gram_b, gram_c = lax.psum(
        (gram_local(own_a), gram_local(own_b), gram_local(own_c)), ("gx", "gy", "gz")
    )
    return (gram_a, gram_b, gram_c)


def partials(tensor, block_a, block_b, block_c):
    highest = lax.Precision.HIGHEST
    along_k = jnp.einsum("ijk,kr->jri", tensor, block_c, precision=highest)
    moment_a = jnp.einsum("jri,jr->ir", along_k, block_b, precision=highest)
    moment_b = jnp.einsum("jri,ir->jr", along_k, block_a, precision=highest)
    along_i = jnp.einsum("ijk,ir->rjk", tensor, block_a, precision=highest)
    moment_c = jnp.einsum("rjk,jr->kr", along_i, block_b, precision=highest)
    return (moment_a, moment_b, moment_c)


def slopes(first, second, third, moment_a, moment_b, moment_c, grams, counts):
    highest = lax.Precision.HIGHEST
    gram_a, gram_b, gram_c = grams
    count_i, count_j, count_k = counts
    slope_a = (jnp.dot(first, gram_b * gram_c, precision=highest) - moment_a) / (count_j * count_k)
    slope_b = (jnp.dot(second, gram_a * gram_c, precision=highest) - moment_b) / (count_i * count_k)
    slope_c = (jnp.dot(third, gram_a * gram_b, precision=highest) - moment_c) / (count_i * count_j)
    return (slope_a, slope_b, slope_c)


def shards(tensor, factor_a, factor_b, factor_c):
    counts = (
        float(tensor.shape[0] * lax.axis_size("gx")),
        float(tensor.shape[1] * lax.axis_size("gy")),
        float(tensor.shape[2] * lax.axis_size("gz")),
    )
    own_a, own_b, own_c = (factor_a, factor_b, factor_c)
    for round_index in range(STEPS):
        block_a, block_b, block_c = gather_blocks(own_a, own_b, own_c)
        grams = gram_sums(own_a, own_b, own_c)
        moment_a, moment_b, moment_c = partials(tensor, block_a, block_b, block_c)
        moment_a = lax.psum_scatter(moment_a, ("gy", "gz"), scatter_dimension=0, tiled=True)
        moment_b = lax.psum_scatter(moment_b, ("gx", "gz"), scatter_dimension=0, tiled=True)
        moment_c = lax.psum_scatter(moment_c, ("gx", "gy"), scatter_dimension=0, tiled=True)
        slope_a, slope_b, slope_c = slopes(
            own_a, own_b, own_c, moment_a, moment_b, moment_c, grams, counts
        )
        if round_index + 1 < STEPS:
            own_a = own_a - step_size * slope_a
            own_b = own_b - step_size * slope_b
            own_c = own_c - step_size * slope_c
    return (slope_a, slope_b, slope_c)


def solution(mesh):
    placed = (
        P("gx", "gy", "gz"),
        P(("gx", "gy", "gz"), None),
        P(("gy", "gx", "gz"), None),
        P(("gz", "gx", "gy"), None),
    )
    return jax.shard_map(
        shards,
        mesh=mesh,
        in_specs=placed,
        out_specs=(
            P(("gx", "gy", "gz"), None),
            P(("gy", "gx", "gz"), None),
            P(("gz", "gx", "gy"), None),
        ),
        check_vma=False,
    )
```

profile of v0, /device:TPU:1, one launch (start us, length us, event | category | flops | bytes accessed | tf_op | source)
XLA Modules:
  0.0 1523.7 jit_solution(15160832706329019883)
XLA Ops:
  7.2 1.0 fusion.29
  8.2 21.6 %all-gather.1 = f32[16,4,64]{2,1,0:T(4,128)S(1)} all-gather(f32[1,4,64]{2,1,0:T(4,128)} %bitcast.117), channel_id=1, replica_groups=mesh['gx'=8,'gy'=16,'gz'=2] {'gx','gz'}, dimensions={0}, use_global_device_ids=true | all-gather | bytes 17408 | tf_op jit(solution)/shard_map/all_gather | solution.py:20
  29.8 284.8 %all-gather = f32[128,1,64]{2,1,0:T(1,128)S(1)} all-gather(f32[1,1,64]{2,1,0:T(1,128)} %bitcast.121), channel_id=1, replica_groups=mesh['gx'=8,'gy'=16,'gz'=2] {'gx','gy'}, dimensions={0}, use_global_device_ids=true | all-gather | bytes 33024 | tf_op jit(solution)/shard_map/all_gather | solution.py:21
  314.7 1.0 fusion.30
  315.7 77.7 %all-gather.2 = f32[32,4,64]{2,1,0:T(4,128)S(1)} all-gather(f32[1,4,64]{2,1,0:T(4,128)} %bitcast.118), channel_id=1, replica_groups=mesh['gx'=8,'gy'=16,'gz'=2] {'gy','gz'}, dimensions={0}, use_global_device_ids=true | all-gather | bytes 33792 | tf_op jit(solution)/shard_map/all_gather | solution.py:19
  393.5 9.2 fusion.9
  403.4 42.5 %all-reduce.1 = f32[64,64]{1,0:T(8,128)S(1)} all-reduce(f32[64,64]{1,0:T(8,128)S(1)} %bitcast.113), channel_id=3, replica_groups=mesh['gx'=8,'gy'=16,'gz'=2] {'gx','gz'}, use_global_device_ids=true, to_apply=%region_4.0.clone | all-reduce | flops 4096 | bytes 32768
  447.3 76.9 %all-reduce.7 = (f32[64,64]{1,0:T(8,128)S(1)}, f32[64,64]{1,0:T(8,128)S(1)}, f32[64,64]{1,0:T(8,128)S(1)}) all-reduce(f32[64,64]{1,0:T(8,128)S(1)} %fusion.29, f32[64,64]{1,0:T(8,128)S(1)} %broadcast_multiply_fusion.1, f32[64,64]{1,0:T(8,128)S(1)} %fusion.30), channel_id=1, replica_groups=mesh['gx'=8,'gy'=16,'gz'=2] {'gx','gy','gz'}, use_global_device_ids=true, to_apply=%region_0.0 | all-reduce | flops 12288 | bytes 98304 | tf_op jit(solution)/shard_map/psum | solution.py:26
  524.4 17.3 %all-gather.3 = f32[16,4,64]{2,1,0:T(4,128)S(1)} all-gather(f32[1,4,64]{2,1,0:T(4,128)S(1)} %bitcast.115), channel_id=1, replica_groups=mesh['gx'=8,'gy'=16,'gz'=2] {'gx','gz'}, dimensions={0}, use_global_device_ids=true | all-gather | bytes 17408 | tf_op jit(solution)/shard_map/all_gather | solution.py:20
  543.2 119.2 %all-reduce = f32[128,64]{1,0:T(8,128)S(1)} all-reduce(f32[128,64]{1,0:T(8,128)S(1)} %bitcast.111), channel_id=2, replica_groups=mesh['gx'=8,'gy'=16,'gz'=2] {'gy','gz'}, use_global_device_ids=true, to_apply=%region_2.0.clone | all-reduce | flops 8192 | bytes 65536
  662.5 26.8 %all-gather.5 = f32[32,4,64]{2,1,0:T(4,128)S(1)} all-gather(f32[1,4,64]{2,1,0:T(4,128)S(1)} %bitcast.116), channel_id=1, replica_groups=mesh['gx'=8,'gy'=16,'gz'=2] {'gy','gz'}, dimensions={0}, use_global_device_ids=true | all-gather | bytes 33792 | tf_op jit(solution)/shard_map/all_gather | solution.py:19
  689.3 7.2 fusion
  696.5 2.4 multiply_reduce_fusion
  699.6 7.2 fusion.2
  706.8 2.4 multiply_reduce_fusion.2
  711.2 203.8 %all-reduce.11.cloned.1.call-done = (f32[128,64]{1,0:T(8,128)}, f32[128,64]{1,0:T(8,128)}) async-done(((f32[128,64]{1,0:T(8,128)}, f32[128,64]{1,0:T(8,128)}), (f32[128,64]{1,0:T(8,128)}, f32[128,64]{1,0:T(8,128)})) %all-reduce.11.cloned.1.call-update) | async-done | bytes 65552
  914.9 1.5 fusion.19
  916.5 285.2 %all-gather.4 = f32[128,1,64]{2,1,0:T(1,128)S(1)} all-gather(f32[1,1,64]{2,1,0:T(1,128)S(1)} %bitcast.120), channel_id=1, replica_groups=mesh['gx'=8,'gy'=16,'gz'=2] {'gx','gy'}, dimensions={0}, use_global_device_ids=true | all-gather | bytes 33024 | tf_op jit(solution)/shard_map/all_gather | solution.py:21
  1201.6 9.3 fusion.8
  1211.5 103.3 %all-reduce.4 = f32[64,64]{1,0:T(8,128)S(1)} all-reduce(f32[64,64]{1,0:T(8,128)S(1)} %bitcast.114), channel_id=6, replica_groups=mesh['gx'=8,'gy'=16,'gz'=2] {'gx','gz'}, use_global_device_ids=true, to_apply=%region_10.0.clone | all-reduce | flops 4096 | bytes 32768
  1314.9 121.7 %all-reduce.3 = f32[128,64]{1,0:T(8,128)S(1)} all-reduce(f32[128,64]{1,0:T(8,128)S(1)} %bitcast.112), channel_id=5, replica_groups=mesh['gx'=8,'gy'=16,'gz'=2] {'gy','gz'}, use_global_device_ids=true, to_apply=%region_8.0.clone | all-reduce | flops 8192 | bytes 65536
  1436.6 76.7 %all-reduce.6 = (f32[64,64]{1,0:T(8,128)S(1)}, f32[64,64]{1,0:T(8,128)S(1)}, f32[64,64]{1,0:T(8,128)S(1)}) all-reduce(f32[64,64]{1,0:T(8,128)S(1)} %fusion.31, f32[64,64]{1,0:T(8,128)S(1)} %broadcast_multiply_fusion, f32[64,64]{1,0:T(8,128)S(1)} %fusion.32), channel_id=1, replica_groups=mesh['gx'=8,'gy'=16,'gz'=2] {'gx','gy','gz'}, use_global_device_ids=true, to_apply=%region_5.0 | all-reduce | flops 12288 | bytes 98304 | tf_op jit(solution)/shard_map/psum | solution.py:26
  1513.4 2.0 fusion.20
  1515.4 0.7 fusion.10
  (34 shorter events, 6.6 us)
Async XLA Ops:
  7.2 907.8 %all-reduce.11.cloned.1.call-start = ((), (), s32[]{:S(2)}) async-start(), calls=%async_computation | async-start | bytes 262144
  402.8 43.2 %copy-start.2 = (f32[1,64]{1,0:T(1,128)S(1)}, f32[1,64]{1,0:T(1,128)}, u32[]{:S(2)}) copy-start(f32[1,64]{1,0:T(1,128)} %param.7) | copy-start | bytes 772
  402.8 43.3 %copy-start.5 = (u32[256]{0:T(256)S(1)}, u32[256]{0:T(256)}, u32[]{:S(2)}) copy-start(u32[256]{0:T(256)} %constant.32) | copy-start | bytes 3076
  402.8 121.5 %copy-start = (f32[4,64]{1,0:T(4,128)S(1)}, f32[4,64]{1,0:T(4,128)}, u32[]{:S(2)}) copy-start(f32[4,64]{1,0:T(4,128)} %param.6) | copy-start | bytes 3076
  402.8 139.0 %copy-start.4 = (u32[256]{0:T(256)S(1)}, u32[256]{0:T(256)}, u32[]{:S(2)}) copy-start(u32[256]{0:T(256)} %constant.28) | copy-start | bytes 3076
  402.8 259.5 %copy-start.1 = (f32[4,64]{1,0:T(4,128)S(1)}, f32[4,64]{1,0:T(4,128)}, u32[]{:S(2)}) copy-start(f32[4,64]{1,0:T(4,128)} %param.5) | copy-start | bytes 3076
  706.8 3.7 copy-start.3
Sparse Core Ops, SparseCore 0:
  710.1 204.7 all-reduce.10
where the time goes:
time: 1520 us
  blocking collectives  1250 us (82%)
  waiting for transfers between devices  204 us (13%)
  matrix products  40.5 us (3%)
  between operations  15.5 us (1%)
    all_gather x2, blocking collectives, gather_blocks(): block_c = lax.all_gather(own_c, ('gx', 'gy'), axis=0, tiled=True)  570 us
    unnamed x4, blocking collectives  387 us
    unnamed x2, waiting for transfers between devices  204 us
    psum x2, blocking collectives, gram_sums(): lax.psum((gram_local(own_a), gram_local(own_b), gram_local(own_c)), ('gx'...  154 us
    all_gather x2, blocking collectives, gather_blocks(): block_a = lax.all_gather(own_a, ('gy', 'gz'), axis=0, tiled=True)  105 us
    all_gather x2, blocking collectives, gather_blocks(): block_b = lax.all_gather(own_b, ('gx', 'gz'), axis=0, tiled=True)  39 us
  transfers between devices with their start and end apart: 1, of which 1 were waited for; matrix products, arithmetic and copies ran while one was open for 0% of the time, Pallas kernels for 0%

commit v1 on v0

v1 whole, which is shorter than its diff:
```python
import functools

import jax
import jax.numpy as jnp
from jax import lax
from jax.experimental import pallas as pl
from jax.experimental.pallas import tpu as pltpu
from jax.sharding import PartitionSpec as P

STEPS = 2
STEP_SIZE = 0.1
F32 = jnp.float32
BF16 = jnp.bfloat16
HIGHEST = lax.Precision.HIGHEST
VMEM = pl.BlockSpec(memory_space=pltpu.VMEM)
CHUNK = 512


def split(x):
    high = x.astype(BF16)
    return high, (x - high.astype(F32)).astype(BF16)


def prep_kernel(count_i, count_j, count_k, t_ref, rows_ref, turned_ref):
    def natural(c, _):
        at = pl.multiple_of(c * CHUNK, CHUNK)
        high, low = split(t_ref[pl.ds(at, CHUNK), :])
        rows_ref[pl.ds(at, CHUNK), :count_k] = high
        rows_ref[pl.ds(at, CHUNK), count_k:] = low
        return 0

    lax.fori_loop(0, count_i * count_j // CHUNK, natural, 0)

    def turned(j, _):
        high, low = split(t_ref[pl.ds(j, count_i, stride=count_j), :].T)
        at = pl.multiple_of(j * count_k, count_k)
        turned_ref[pl.ds(at, count_k), :count_i] = high
        turned_ref[pl.ds(at, count_k), count_i:] = low
        return 0

    lax.fori_loop(0, count_j, turned, 0, unroll=2)


def prep(tensor):
    count_i, count_j, count_k = tensor.shape
    return pl.pallas_call(
        functools.partial(prep_kernel, count_i, count_j, count_k),
        out_shape=(
            jax.ShapeDtypeStruct((count_i * count_j, 2 * count_k), BF16),
            jax.ShapeDtypeStruct((count_j * count_k, 2 * count_i), BF16),
        ),
        in_specs=[VMEM],
        out_specs=(VMEM, VMEM),
        compiler_params=pltpu.CompilerParams(vmem_limit_bytes=24 << 20),
        cost_estimate=pl.CostEstimate(flops=1 << 24, bytes_accessed=12 << 20, transcendentals=0),
        name="prep",
    )(tensor.reshape(count_i * count_j, count_k))


def wide(x, upper):
    lower = lax.broadcasted_iota(jnp.int32, x.shape, 1) < x.shape[1] // 2
    turned = pltpu.roll(x, x.shape[1] // 2, 1)
    return jnp.where(lower, turned, x) if upper else jnp.where(lower, x, turned)


def weights(x):
    high = x.astype(BF16).astype(F32)
    lower = lax.broadcasted_iota(jnp.int32, x.shape, 1) < x.shape[1] // 2
    both = jnp.where(lower, high, x - high).astype(BF16)
    return jnp.concatenate([both, both], axis=0)


def gram(x):
    return lax.dot_general(
        x, x, (((0,), (0,)), ((), ())), precision=HIGHEST, preferred_element_type=F32
    )


def round_kernel(keep, scale, mixed, ac_ref, b_ref, rows_ref, turned_ref, oa_ref, ob_ref, oc_ref, a2_ref, b2_ref, ma_ref, c_ref):
    count_i, count_j, count_k = a2_ref.shape[0], b2_ref.shape[0], c_ref.shape[0]
    if mixed:
        groups, each = ac_ref.shape[0], ac_ref.shape[1]
        ac = ac_ref[...].reshape(count_i, ac_ref.shape[2])
        for g in range(each):
            c_ref[g * groups : (g + 1) * groups, :] = ac_ref[:, g, :]
        c2 = wide(c_ref[...], True)
    else:
        ac = ac_ref[...]
        c2 = wide(ac, True)
    a2 = wide(ac, False)
    b2 = wide(b_ref[...], False)
    a2_ref[...] = a2
    b2_ref[...] = b2
    weights_a, weights_c = weights(a2), weights(c2)
    per_i, per_j = CHUNK // count_j, CHUNK // count_k

    def step(c, carry):
        moment_b, moment_c = carry
        at = pl.multiple_of(c * CHUNK, CHUNK)
        y = jnp.dot(rows_ref[pl.ds(at, CHUNK), :], weights_c, preferred_element_type=F32)
        y = y.reshape(per_i, count_j, y.shape[1])
        at_i = pl.multiple_of(c * per_i, per_i)
        ma_ref[pl.ds(at_i, per_i), :] = jnp.sum(y * b2_ref[...][None], axis=1)
        for n in range(per_i):
            moment_b = moment_b + y[n] * a2_ref[pl.ds(c * per_i + n, 1), :]
        z = jnp.dot(turned_ref[pl.ds(at, CHUNK), :], weights_a, preferred_element_type=F32)
        z = z.reshape(per_j, count_k, z.shape[1])
        for n in range(per_j):
            moment_c = moment_c + z[n] * b2_ref[pl.ds(c * per_j + n, 1), :]
        return moment_b, moment_c

    moment_b, moment_c = lax.fori_loop(
        0,
        count_i * count_j // CHUNK,
        step,
        (jnp.zeros(b2.shape, F32), jnp.zeros(c2.shape, F32)),
    )
    gram_a, gram_b, gram_c = gram(a2), gram(b2), gram(c2)

    def result(factor, gram_one, gram_two, moment, weight, factor_scale):
        model = jnp.dot(factor, gram_one * gram_two, precision=HIGHEST, preferred_element_type=F32)
        partial = 0.5 * model - (moment + pltpu.roll(moment, moment.shape[1] // 2, 1))
        out = partial * factor_scale
        return out + factor * weight if weight else out

    oa_ref[...] = result(a2, gram_b, gram_c, ma_ref[...], keep[0], scale[0])
    ob_ref[...] = result(b2, gram_a, gram_c, moment_b, keep[1], scale[1])
    oc_ref[...] = result(c2, gram_a, gram_b, moment_c, keep[2], scale[2])


def partials(keep, scale, ac, b, rows, turned, sizes):
    count_i, count_j, count_k = sizes
    width = b.shape[1]
    return pl.pallas_call(
        functools.partial(round_kernel, keep, scale, ac.ndim == 3),
        out_shape=tuple(jax.ShapeDtypeStruct((n, width), F32) for n in sizes),
        in_specs=[VMEM] * 4,
        out_specs=(VMEM,) * 3,
        scratch_shapes=[
            pltpu.VMEM((count_i, width), F32),
            pltpu.VMEM((count_j, width), F32),
            pltpu.VMEM((count_i, width), F32),
            pltpu.VMEM((count_k, width), F32),
        ],
        compiler_params=pltpu.CompilerParams(vmem_limit_bytes=24 << 20),
        cost_estimate=pl.CostEstimate(flops=1 << 30, bytes_accessed=8 << 20, transcendentals=0),
        name="partials",
    )(ac, b, rows, turned)


def send_all(x, axis):
    count = lax.axis_size(axis)
    return lax.all_to_all(jnp.broadcast_to(x[None], (count, *x.shape)), axis, 0, 0, tiled=True)


def shift(x, axis, stride, count, by):
    total = lax.axis_size(axis)
    pairs = []
    for n in range(total):
        place = n // stride % count
        pairs.append((n, n + ((place + by) % count - place) * stride))
    return lax.ppermute(x, axis, pairs)


def ring8(x):
    below, above = shift(x, "gx", 1, 8, 1), shift(x, "gx", 1, 8, -1)
    two = x + above
    three = two + below
    return three + (shift(three, "gx", 1, 8, -3) + shift(two, "gx", 1, 8, 3))


def ring4(x, stride):
    ones = shift(x, "gy", stride, 4, 1) + shift(x, "gy", stride, 4, -1)
    return (x + ones) + shift(x, "gy", stride, 4, 2)


def swap(x):
    return lax.ppermute(x, "gz", [(0, 1), (1, 0)])


def shards(tensor, factor_a, factor_b, factor_c):
    count_x, count_y, count_z = (lax.axis_size(n) for n in ("gx", "gy", "gz"))
    sizes = count_i, count_j, count_k = tensor.shape
    whole = (
        float(count_j * count_y * count_k * count_z),
        float(count_i * count_x * count_k * count_z),
        float(count_i * count_x * count_j * count_y),
    )
    copies = (count_y * count_z, count_x * count_z, count_x * count_y)
    rank = factor_a.shape[1]
    rows, turned = prep(tensor)

    own = lax.all_gather(jnp.concatenate([factor_a, factor_b], axis=1), "gz", axis=0, tiled=True)
    each = own.shape[0]
    padded_c = jnp.pad(factor_c, ((0, each - 1), (0, 0)))
    along_x = send_all(jnp.concatenate([own[:, rank:], padded_c], axis=1), "gx")
    block_b = along_x.reshape(count_j, 2 * rank)
    block_ac = send_all(jnp.concatenate([own[:, :rank], along_x[:, 0, rank:]], axis=1), "gy")

    keep = tuple(1.0 / n for n in copies)
    scale = tuple(-STEP_SIZE / n for n in whole)
    part_a, part_b, part_c = partials(keep, scale, block_ac, block_b, rows, turned, sizes)
    lower = lax.broadcasted_iota(jnp.int32, (count_k, 2 * rank), 1) < rank
    tall_b = jnp.pad(part_b, ((0, count_k - count_j), (0, 0)))
    bc = ring8(jnp.where(lower, tall_b, part_c))
    ac = ring4(ring4(jnp.where(lower, part_a, bc), 1), 4)
    ab = jnp.concatenate([ac[:, :rank], bc[:, :rank]], axis=1)
    ab = ab + swap(ab)
    ac = jnp.concatenate([ab[:, :rank], ac[:, rank:]], axis=1)
    block_b = ab[:count_j, rank:]
    block_b = jnp.concatenate([block_b, block_b], axis=1)

    scale = tuple(1.0 / n for n in whole)
    part_a, part_b, part_c = partials((0.0,) * 3, scale, ac, block_b, rows, turned, sizes)
    slots_b = jnp.pad(
        part_b.reshape(count_x, each, 2 * rank), ((0, 0), (0, count_y - each), (0, 0))
    )
    slots_c = part_c.reshape(count_x, count_y, 2 * rank)
    lower = lax.broadcasted_iota(jnp.int32, slots_c.shape, 2) < rank
    bc = jnp.sum(
        lax.all_to_all(jnp.where(lower, slots_b, slots_c), "gx", 0, 0, tiled=True), axis=0
    )
    slots_c = jnp.pad(bc[:, None, rank:], ((0, 0), (0, each - 1), (0, 0)))
    slots_a = part_a.reshape(count_y, each, 2 * rank)[:, :, :rank]
    ac = jnp.sum(
        lax.all_to_all(jnp.concatenate([slots_a, slots_c], axis=2), "gy", 0, 0, tiled=True), axis=0
    )
    ab = jnp.concatenate([ac[:, :rank], bc[:each, :rank]], axis=1)
    ab = ab + swap(ab)
    mine = lax.dynamic_slice_in_dim(ab, lax.axis_index("gz") * (each // 2), each // 2, axis=0)
    return mine[:, :rank], mine[:, rank:], ac[:1, rank:]


def solution(mesh):
    factors = (
        P(("gx", "gy", "gz"), None),
        P(("gy", "gx", "gz"), None),
        P(("gz", "gx", "gy"), None),
    )
    return jax.shard_map(
        shards,
        mesh=mesh,
        in_specs=(P("gx", "gy", "gz"), *factors),
        out_specs=factors,
        check_vma=False,
    )
```

time: 1520 us -> 122 us (0.08)
  blocking collectives: 1250 us -> 14.6 us
  waiting for transfers between devices: 204 us -> 32.4 us
  matrix products: 40.5 us -> 0 us
  starting transfers between devices: 0.04 us -> 39.9 us
  Pallas kernels: 0 us -> 17.1 us
    all_gather x6 -> x1, blocking collectives: 714 us -> 4.7 us  [shards(): lax.all_gather(jnp.concatenate([factor_a, factor_b], axis=1), 'gz', axis=...]
    unnamed x4 -> x0, blocking collectives: 387 us -> none
    unnamed x2 -> x0, waiting for transfers between devices: 204 us -> none
    psum x2 -> x0, blocking collectives: 154 us -> none  [gram_sums(): lax.psum((gram_local(own_a), gram_local(own_b), gram_local(own_c)), ('gx'...]
    dot_general x14 -> x0, matrix products: 40.5 us -> none  [the longest x2 18.5 us: partials(): along_k = jnp.einsum('ijk,kr->jri', tensor, block_c, precision=highest)]
    ppermute x0 -> x12, starting transfers between devices: none -> 23.2 us  [the longest x2 11.6 us: swap(): return lax.ppermute(x, 'gz', [(0, 1), (1, 0)])]
    ppermute x0 -> x12, waiting for transfers between devices: none -> 19.4 us  [the longest x10 18.3 us: shift(): return lax.ppermute(x, axis, pairs)]
    pallas_call x0 -> x3, Pallas kernels: none -> 17.1 us  [the longest x2 11.4 us: partials(): pl.pallas_call(functools.partial(round_kernel, keep, scale, ac.ndim == 3)...]
  transfers between devices with their start and end apart: 1 -> 15, of which waited for: 1 -> 13; matrix products, arithmetic and copies ran while one was open for 0% -> 0% of each run, Pallas kernels for 0% -> 5%
where the time goes in v1:
time: 122 us; the launch traced here: 121 us
  starting transfers between devices  39.9 us (33%)
  waiting for transfers between devices  32.4 us (27%)
  Pallas kernels  17.1 us (14%)
  blocking collectives  14.6 us (12%)
  local copies, waits for them, and re-layouts  13.4 us (11%)
  other arithmetic  2.9 us (2%)
    ppermute x10, waiting for transfers between devices, shift(): return lax.ppermute(x, axis, pairs)  18.3 us
    all_to_all x2, starting transfers between devices, send_all(): lax.all_to_all(jnp.broadcast_to(x[None], (count, *x.shape)), axis, 0, 0,...  13.2 us
    ppermute x2, starting transfers between devices, swap(): return lax.ppermute(x, 'gz', [(0, 1), (1, 0)])  11.6 us
    ppermute x10, starting transfers between devices, shift(): return lax.ppermute(x, axis, pairs)  11.6 us
    pallas_call x2, Pallas kernels, partials(): pl.pallas_call(functools.partial(round_kernel, keep, scale, ac.ndim == 3)...  11.4 us
    unnamed x10, local copies, waits for them, and re-layouts  10.5 us
    all_to_all x1, blocking collectives, shards(): lax.all_to_all(jnp.where(lower, slots_b, slots_c), 'gx', 0, 0, tiled=True)  9.9 us
    all_to_all x2, waiting for transfers between devices, send_all(): lax.all_to_all(jnp.broadcast_to(x[None], (count, *x.shape)), axis, 0, 0,...  6.55 us
  transfers between devices with their start and end apart: 15, of which 13 were waited for; matrix products, arithmetic and copies ran while one was open for 0% of the time, Pallas kernels for 5%

profile of v1, /device:TPU:1, one launch (start us, length us, event | category | flops | bytes accessed | tf_op | source)
XLA Modules:
  0.0 121.0 jit_solution(15514385111501282782)
XLA Ops:
  1.4 4.7 %all-gather = f32[2,4,128]{2,1,0:T(4,128)S(1)} all-gather(f32[1,4,128]{2,1,0:T(4,128)S(1)} %maximum_bitcast_fusion), channel_id=1, replica_groups=mesh['gx'=8,'gy'=16,'gz'=2] {'gz'}, dimensions={0}, use_global_device_ids=true | all-gather | bytes 6144 | tf_op jit(solution)/shard_map/all_gather | solution.py:193
  7.5 6.4 %all-to-all-start = ((f32[8,8,128]{2,1,0:T(8,128)}), f32[8,8,128]{2,1,0:T(8,128)S(1)}, u32[]{:S(2)}, u32[]{:S(2)}) async-start(f32[8,8,128]{2,1,0:T(8,128)} %broadcast_in_dim.6), calls=%async_computation | async-start | bytes 65536 | tf_op jit(solution)/shard_map/all_to_all | solution.py:153
  14.0 2.2 %copy-done.4 = f32[128,64,128]{2,1,0:T(8,128)S(1)} copy-done((f32[128,64,128]{2,1,0:T(8,128)S(1)}, f32[128,64,128]{2,1,0:T(8,128)}, u32[]{:S(2)}) %copy-start.4) | copy-done | bytes 4194328
  16.2 5.7 %prep.1 = (bf16[8192,256]{1,0:T(8,128)(2,1)S(1)}, bf16[8192,256]{1,0:T(8,128)(2,1)S(1)}) custom-call(f32[8192,128]{1,0:T(8,128)S(1)} %bitcast.14), custom_call_target="tpu_custom_call" | custom-call | flops 16777216 | bytes 12582912 | tf_op jit(solution)/shard_map/prep/pallas_call | solution.py:46
  23.8 2.0 %copy-done.2 = bf16[8192,256]{1,0:T(8,128)(2,1)} copy-done((bf16[8192,256]{1,0:T(8,128)(2,1)}, bf16[8192,256]{1,0:T(8,128)(2,1)S(1)}, u32[]{:S(2)}) %copy-start.2) | copy-done | bytes 4194328
  26.6 6.8 %all-to-all-start.1 = ((f32[16,8,128]{2,1,0:T(8,128)}), f32[16,8,128]{2,1,0:T(8,128)S(1)}, u32[]{:S(2)}, u32[]{:S(2)}) async-start(f32[16,8,128]{2,1,0:T(8,128)} %broadcast_in_dim.7), calls=%async_computation.1 | async-start | bytes 131072 | tf_op jit(solution)/shard_map/all_to_all | solution.py:153
  33.3 6.5 %all-to-all-done.1.ac_ref = f32[16,8,128]{2,1,0:T(8,128)S(1)} async-done(((f32[16,8,128]{2,1,0:T(8,128)}), f32[16,8,128]{2,1,0:T(8,128)S(1)}, u32[]{:S(2)}, u32[]{:S(2)}) %all-to-all-start.1) | async-done | bytes 65568 | tf_op jit(solution)/shard_map/all_to_all | solution.py:153
  39.9 2.2 %copy-done.1 = bf16[8192,256]{1,0:T(8,128)(2,1)S(1)} copy-done((bf16[8192,256]{1,0:T(8,128)(2,1)S(1)}, bf16[8192,256]{1,0:T(8,128)(2,1)}, u32[]{:S(2)}) %copy-start.1) | copy-done | bytes 4194328
  42.1 2.2 %copy-done.3 = bf16[8192,256]{1,0:T(8,128)(2,1)S(1)} copy-done((bf16[8192,256]{1,0:T(8,128)(2,1)S(1)}, bf16[8192,256]{1,0:T(8,128)(2,1)}, u32[]{:S(2)}) %copy-start.3) | copy-done | bytes 4194328
  44.3 5.7 %partials.2 = (f32[128,128]{1,0:T(8,128)S(1)}, f32[64,128]{1,0:T(8,128)S(1)}, f32[128,128]{1,0:T(8,128)S(1)}) custom-call(f32[16,8,128]{2,1,0:T(8,128)S(1)} %all-to-all-done.1.ac_ref, f32[64,128]{1,0:T(8,128)S(1)} %bitcast.15, bf16[8192,256]{1,0:T(8,128)(2,1)S(1)} %copy-done.1, bf16[8192,256]{1,0:T(8,128)(2,1)S(1)} %copy-done.3), custom_call_target="tpu_custom_call" | custom-call | flops 1073741824 | bytes 8388608 | tf_op jit(solution)/shard_map/partials/pallas_call | solution.py:134
  50.0 2.7 %collective-permute-start = (f32[128,128]{1,0:T(8,128)S(1)}, f32[128,128]{1,0:T(8,128)S(1)}, u32[]{:S(2)}, u32[]{:S(2)}) collective-permute-start(f32[128,128]{1,0:T(8,128)S(1)} %pad_select_fusion.1), channel_id=1, source_target_pairs={{0,224},{32,0},{64,32},{96,64},{128,96},{160,128},{192,160},{224,1... | collective-permute-start | bytes 196616 | tf_op jit(solution)/shard_map/ppermute | solution.py:162
  54.1 3.0 %collective-permute-done.1 = f32[128,128]{1,0:T(8,128)S(1)} collective-permute-done((f32[128,128]{1,0:T(8,128)S(1)}, f32[128,128]{1,0:T(8,128)S(1)}, u32[]{:S(2)}, u32[]{:S(2)}) %collective-permute-start.1) | collective-permute-done | bytes 65568 | tf_op jit(solution)/shard_map/ppermute | solution.py:162
  60.4 2.7 %collective-permute-done.2 = f32[128,128]{1,0:T(8,128)S(1)} collective-permute-done((f32[128,128]{1,0:T(8,128)S(1)}, f32[128,128]{1,0:T(8,128)S(1)}, u32[]{:S(2)}, u32[]{:S(2)}) %collective-permute-start.2) | collective-permute-done | bytes 65568 | tf_op jit(solution)/shard_map/ppermute | solution.py:162
  63.2 2.0 %collective-permute-done.3 = f32[128,128]{1,0:T(8,128)S(1)} collective-permute-done((f32[128,128]{1,0:T(8,128)S(1)}, f32[128,128]{1,0:T(8,128)S(1)}, u32[]{:S(2)}, u32[]{:S(2)}) %collective-permute-start.3) | collective-permute-done | bytes 65568 | tf_op jit(solution)/shard_map/ppermute | solution.py:162
  65.5 2.4 %collective-permute-start.5 = (f32[128,128]{1,0:T(8,128)S(1)}, f32[128,128]{1,0:T(8,128)S(1)}, u32[]{:S(2)}, u32[]{:S(2)}) collective-permute-start(f32[128,128]{1,0:T(8,128)S(1)} %get-tuple-element.19), channel_id=1, source_target_pairs={{0,6},{2,0},{4,2},{6,4},{8,14},{10,8},{12,10},{14,12},{16,22},{18,... | collective-permute-start | bytes 196616 | tf_op jit(solution)/shard_map/ppermute | solution.py:162
  69.8 2.7 %collective-permute-done.6 = f32[128,128]{1,0:T(8,128)S(1)} collective-permute-done((f32[128,128]{1,0:T(8,128)S(1)}, f32[128,128]{1,0:T(8,128)S(1)}, u32[]{:S(2)}, u32[]{:S(2)}) %collective-permute-start.6) | collective-permute-done | bytes 65568 | tf_op jit(solution)/shard_map/ppermute | solution.py:162
  72.9 2.4 %collective-permute-start.8 = (f32[128,128]{1,0:T(8,128)S(1)}, f32[128,128]{1,0:T(8,128)S(1)}, u32[]{:S(2)}, u32[]{:S(2)}) collective-permute-start(f32[128,128]{1,0:T(8,128)S(1)} %add_add_fusion.1), channel_id=1, source_target_pairs={{0,24},{2,26},{4,28},{6,30},{8,0},{10,2},{12,4},{14,6},{16,8},{18,... | collective-permute-start | bytes 196616 | tf_op jit(solution)/shard_map/ppermute | solution.py:162
  77.2 2.7 %collective-permute-done.9 = f32[128,128]{1,0:T(8,128)S(1)} collective-permute-done((f32[128,128]{1,0:T(8,128)S(1)}, f32[128,128]{1,0:T(8,128)S(1)}, u32[]{:S(2)}, u32[]{:S(2)}) %collective-permute-start.9) | collective-permute-done | bytes 65568 | tf_op jit(solution)/shard_map/ppermute | solution.py:162
  80.1 8.7 %collective-permute-start.10 = (f32[128,128]{1,0:T(8,128)S(1)}, f32[128,128]{1,0:T(8,128)S(1)}, u32[]{:S(2)}, u32[]{:S(2)}) collective-permute-start(f32[128,128]{1,0:T(8,128)S(1)} %pad_maximum_fusion), channel_id=1, source_target_pairs={{0,1},{1,0},{2,3},{3,2},{4,5},{5,4},{6,7},{7,6},{8,9},{9,8},{10,11... | collective-permute-start | bytes 196616 | tf_op jit(solution)/shard_map/ppermute | solution.py:178
  90.1 5.7 %partials.3 = (f32[128,128]{1,0:T(8,128)S(1)}, f32[64,128]{1,0:T(8,128)S(1)}, f32[128,128]{1,0:T(8,128)S(1)}) custom-call(f32[128,128]{1,0:T(8,128)S(1)} %pad_maximum_fusion.1.ac_ref, f32[64,128]{1,0:T(8,128)S(1)} %pad_maximum_fusion.2.b_ref, bf16[8192,256]{1,0:T(8,128)(2,1)S(1)} %copy-done.1, bf16[8192,256]{1,0:T(8,128)(2,1)S(1)} %copy-done.3), custom_call_target="tpu_custom_call" | custom-call | flops 1073741824 | bytes 8388608 | tf_op jit(solution)/shard_map/partials/pallas_call | solution.py:134
  95.8 9.9 %all_to_all.20 = f32[8,16,128]{2,1,0:T(8,128)S(1)} all-to-all(f32[8,16,128]{2,1,0:T(8,128)S(1)} %pad_select_fusion), channel_id=1, replica_groups=mesh['gx'=8,'gy'=16,'gz'=2] {'gx'}, dimensions={0} | all-to-all | bytes 131072 | tf_op jit(solution)/shard_map/all_to_all | solution.py:221
  106.5 3.5 %all-to-all-start.3 = ((f32[16,8,128]{2,1,0:T(8,128)}), f32[16,8,128]{2,1,0:T(8,128)S(1)}, u32[]{:S(2)}, u32[]{:S(2)}) async-start(f32[16,8,128]{2,1,0:T(8,128)} %select_maximum_fusion), calls=%async_computation.3 | async-start | bytes 131072 | tf_op jit(solution)/shard_map/all_to_all | solution.py:226
  110.0 6.4 %all-to-all-done.3 = f32[16,8,128]{2,1,0:T(8,128)S(1)} async-done(((f32[16,8,128]{2,1,0:T(8,128)}), f32[16,8,128]{2,1,0:T(8,128)S(1)}, u32[]{:S(2)}, u32[]{:S(2)}) %all-to-all-start.3) | async-done | bytes 65568 | tf_op jit(solution)/shard_map/all_to_all | solution.py:226
  116.5 2.9 %collective-permute-start.11 = (f32[8,128]{1,0:T(8,128)S(1)}, f32[8,128]{1,0:T(8,128)S(1)}, u32[]{:S(2)}, u32[]{:S(2)}) collective-permute-start(f32[8,128]{1,0:T(8,128)S(1)} %pad_maximum_fusion.4), channel_id=1, source_target_pairs={{0,1},{1,0},{2,3},{3,2},{4,5},{5,4},{6,7},{7,6},{8,9},{9,8},{10,11... | collective-permute-start | bytes 12296 | tf_op jit(solution)/shard_map/ppermute | solution.py:178
  (51 shorter events, 18.1 us)
Async XLA Ops:
  7.5 18.3 %all-to-all-start = ((f32[8,8,128]{2,1,0:T(8,128)}), f32[8,8,128]{2,1,0:T(8,128)S(1)}, u32[]{:S(2)}, u32[]{:S(2)}) async-start(f32[8,8,128]{2,1,0:T(8,128)} %broadcast_in_dim.6), calls=%async_computation | async-start | bytes 65536 | tf_op jit(solution)/shard_map/all_to_all | solution.py:153
  14.0 2.2 %copy-start.4 = (f32[128,64,128]{2,1,0:T(8,128)S(1)}, f32[128,64,128]{2,1,0:T(8,128)}, u32[]{:S(2)}) copy-start(f32[128,64,128]{2,1,0:T(8,128)} %param.4) | copy-start | bytes 12582916
  21.8 1.9 %copy-start = (bf16[8192,256]{1,0:T(8,128)(2,1)}, bf16[8192,256]{1,0:T(8,128)(2,1)S(1)}, u32[]{:S(2)}) copy-start(bf16[8192,256]{1,0:T(8,128)(2,1)S(1)} %get-tuple-element.11.rows_ref) | copy-start | bytes 12582916
  23.8 2.0 %copy-start.2 = (bf16[8192,256]{1,0:T(8,128)(2,1)}, bf16[8192,256]{1,0:T(8,128)(2,1)S(1)}, u32[]{:S(2)}) copy-start(bf16[8192,256]{1,0:T(8,128)(2,1)S(1)} %get-tuple-element.12.turned_ref) | copy-start | bytes 12582916
  26.6 13.3 %all-to-all-start.1 = ((f32[16,8,128]{2,1,0:T(8,128)}), f32[16,8,128]{2,1,0:T(8,128)S(1)}, u32[]{:S(2)}, u32[]{:S(2)}) async-start(f32[16,8,128]{2,1,0:T(8,128)} %broadcast_in_dim.7), calls=%async_computation.1 | async-start | bytes 131072 | tf_op jit(solution)/shard_map/all_to_all | solution.py:153
  39.9 2.2 %copy-start.1 = (bf16[8192,256]{1,0:T(8,128)(2,1)S(1)}, bf16[8192,256]{1,0:T(8,128)(2,1)}, u32[]{:S(2)}) copy-start(bf16[8192,256]{1,0:T(8,128)(2,1)} %copy-done) | copy-start | bytes 12582916
  42.1 2.2 %copy-start.3 = (bf16[8192,256]{1,0:T(8,128)(2,1)S(1)}, bf16[8192,256]{1,0:T(8,128)(2,1)}, u32[]{:S(2)}) copy-start(bf16[8192,256]{1,0:T(8,128)(2,1)} %copy-done.2) | copy-start | bytes 12582916
  50.0 4.0 %collective-permute-start = (f32[128,128]{1,0:T(8,128)S(1)}, f32[128,128]{1,0:T(8,128)S(1)}, u32[]{:S(2)}, u32[]{:S(2)}) collective-permute-start(f32[128,128]{1,0:T(8,128)S(1)} %pad_select_fusion.1), channel_id=1, source_target_pairs={{0,224},{32,0},{64,32},{96,64},{128,96},{160,128},{192,160},{224,1... | collective-permute-start | bytes 196616 | tf_op jit(solution)/shard_map/ppermute | solution.py:162
  52.7 4.3 %collective-permute-start.1 = (f32[128,128]{1,0:T(8,128)S(1)}, f32[128,128]{1,0:T(8,128)S(1)}, u32[]{:S(2)}, u32[]{:S(2)}) collective-permute-start(f32[128,128]{1,0:T(8,128)S(1)} %pad_select_fusion.1), channel_id=1, source_target_pairs={{0,32},{32,64},{64,96},{96,128},{128,160},{160,192},{192,224},{224... | collective-permute-start | bytes 196616 | tf_op jit(solution)/shard_map/ppermute | solution.py:162
  57.1 6.1 %collective-permute-start.2 = (f32[128,128]{1,0:T(8,128)S(1)}, f32[128,128]{1,0:T(8,128)S(1)}, u32[]{:S(2)}, u32[]{:S(2)}) collective-permute-start(f32[128,128]{1,0:T(8,128)S(1)} %get-tuple-element.21), channel_id=1, source_target_pairs={{0,160},{32,192},{64,224},{96,0},{128,32},{160,64},{192,96},{224,1... | collective-permute-start | bytes 196616 | tf_op jit(solution)/shard_map/ppermute | solution.py:162
  58.9 6.2 %collective-permute-start.3 = (f32[128,128]{1,0:T(8,128)S(1)}, f32[128,128]{1,0:T(8,128)S(1)}, u32[]{:S(2)}, u32[]{:S(2)}) collective-permute-start(f32[128,128]{1,0:T(8,128)S(1)} %get-tuple-element.22), channel_id=1, source_target_pairs={{0,96},{32,128},{64,160},{96,192},{128,224},{160,0},{192,32},{224,... | collective-permute-start | bytes 196616 | tf_op jit(solution)/shard_map/ppermute | solution.py:162
  65.1 4.7 %collective-permute-start.4 = (f32[128,128]{1,0:T(8,128)S(1)}, f32[128,128]{1,0:T(8,128)S(1)}, u32[]{:S(2)}, u32[]{:S(2)}) collective-permute-start(f32[128,128]{1,0:T(8,128)S(1)} %get-tuple-element.19), channel_id=1, source_target_pairs={{0,2},{2,4},{4,6},{6,0},{8,10},{10,12},{12,14},{14,8},{16,18},{18,... | collective-permute-start | bytes 196616 | tf_op jit(solution)/shard_map/ppermute | solution.py:162
  65.5 4.3 %collective-permute-start.5 = (f32[128,128]{1,0:T(8,128)S(1)}, f32[128,128]{1,0:T(8,128)S(1)}, u32[]{:S(2)}, u32[]{:S(2)}) collective-permute-start(f32[128,128]{1,0:T(8,128)S(1)} %get-tuple-element.19), channel_id=1, source_target_pairs={{0,6},{2,0},{4,2},{6,4},{8,14},{10,8},{12,10},{14,12},{16,22},{18,... | collective-permute-start | bytes 196616 | tf_op jit(solution)/shard_map/ppermute | solution.py:162
  67.9 4.6 %collective-permute-start.6 = (f32[128,128]{1,0:T(8,128)S(1)}, f32[128,128]{1,0:T(8,128)S(1)}, u32[]{:S(2)}, u32[]{:S(2)}) collective-permute-start(f32[128,128]{1,0:T(8,128)S(1)} %get-tuple-element.19), channel_id=1, source_target_pairs={{0,4},{2,6},{4,0},{6,2},{8,12},{10,14},{12,8},{14,10},{16,20},{18,... | collective-permute-start | bytes 196616 | tf_op jit(solution)/shard_map/ppermute | solution.py:162
  72.5 4.4 %collective-permute-start.7 = (f32[128,128]{1,0:T(8,128)S(1)}, f32[128,128]{1,0:T(8,128)S(1)}, u32[]{:S(2)}, u32[]{:S(2)}) collective-permute-start(f32[128,128]{1,0:T(8,128)S(1)} %add_add_fusion.1), channel_id=1, source_target_pairs={{0,8},{2,10},{4,12},{6,14},{8,16},{10,18},{12,20},{14,22},{16,24},... | collective-permute-start | bytes 196616 | tf_op jit(solution)/shard_map/ppermute | solution.py:162
  72.9 4.3 %collective-permute-start.8 = (f32[128,128]{1,0:T(8,128)S(1)}, f32[128,128]{1,0:T(8,128)S(1)}, u32[]{:S(2)}, u32[]{:S(2)}) collective-permute-start(f32[128,128]{1,0:T(8,128)S(1)} %add_add_fusion.1), channel_id=1, source_target_pairs={{0,24},{2,26},{4,28},{6,30},{8,0},{10,2},{12,4},{14,6},{16,8},{18,... | collective-permute-start | bytes 196616 | tf_op jit(solution)/shard_map/ppermute | solution.py:162
  75.3 4.6 %collective-permute-start.9 = (f32[128,128]{1,0:T(8,128)S(1)}, f32[128,128]{1,0:T(8,128)S(1)}, u32[]{:S(2)}, u32[]{:S(2)}) collective-permute-start(f32[128,128]{1,0:T(8,128)S(1)} %add_add_fusion.1), channel_id=1, source_target_pairs={{0,16},{2,18},{4,20},{6,22},{8,24},{10,26},{12,28},{14,30},{16,0},... | collective-permute-start | bytes 196616 | tf_op jit(solution)/shard_map/ppermute | solution.py:162
  80.1 9.6 %collective-permute-start.10 = (f32[128,128]{1,0:T(8,128)S(1)}, f32[128,128]{1,0:T(8,128)S(1)}, u32[]{:S(2)}, u32[]{:S(2)}) collective-permute-start(f32[128,128]{1,0:T(8,128)S(1)} %pad_maximum_fusion), channel_id=1, source_target_pairs={{0,1},{1,0},{2,3},{3,2},{4,5},{5,4},{6,7},{7,6},{8,9},{9,8},{10,11... | collective-permute-start | bytes 196616 | tf_op jit(solution)/shard_map/ppermute | solution.py:178
  106.5 10.0 %all-to-all-start.3 = ((f32[16,8,128]{2,1,0:T(8,128)}), f32[16,8,128]{2,1,0:T(8,128)S(1)}, u32[]{:S(2)}, u32[]{:S(2)}) async-start(f32[16,8,128]{2,1,0:T(8,128)} %select_maximum_fusion), calls=%async_computation.3 | async-start | bytes 131072 | tf_op jit(solution)/shard_map/all_to_all | solution.py:226
  116.5 3.8 %collective-permute-start.11 = (f32[8,128]{1,0:T(8,128)S(1)}, f32[8,128]{1,0:T(8,128)S(1)}, u32[]{:S(2)}, u32[]{:S(2)}) collective-permute-start(f32[8,128]{1,0:T(8,128)S(1)} %pad_maximum_fusion.4), channel_id=1, source_target_pairs={{0,1},{1,0},{2,3},{3,2},{4,5},{5,4},{6,7},{7,6},{8,9},{9,8},{10,11... | collective-permute-start | bytes 12296 | tf_op jit(solution)/shard_map/ppermute | solution.py:178

commit v2 on v0

v2 whole, which is shorter than its diff:
```python
import functools

import jax
import jax.numpy as jnp
from jax import lax
from jax.experimental import pallas as pl
from jax.experimental.pallas import tpu as pltpu
from jax.sharding import PartitionSpec as P

STEPS = 2
STEP_SIZE = 0.1
F32 = jnp.float32
BF16 = jnp.bfloat16
HIGHEST = lax.Precision.HIGHEST
VMEM_BYTES = 60 << 20
GRID = 8
CHUNK = 512


def split(x):
    high = x.astype(BF16)
    return high, (x - high.astype(F32)).astype(BF16)


def rows_kernel(t_ref, out_ref):
    width = t_ref.shape[1]

    def step(c, _):
        at = pl.multiple_of(c * 128, 128)
        high, low = split(t_ref[pl.ds(at, 128), :])
        out_ref[pl.ds(at, 128), :width] = high
        out_ref[pl.ds(at, 128), width:] = low
        return 0

    lax.fori_loop(0, t_ref.shape[0] // 128, step, 0, unroll=2)


def split_rows(tensor):
    count_i, count_j, count_k = tensor.shape
    block = count_i * count_j // GRID
    return pl.pallas_call(
        rows_kernel,
        grid=(GRID,),
        out_shape=jax.ShapeDtypeStruct((count_i * count_j, 2 * count_k), BF16),
        in_specs=[pl.BlockSpec((block, count_k), lambda n: (n, 0))],
        out_specs=pl.BlockSpec((block, 2 * count_k), lambda n: (n, 0)),
        compiler_params=pltpu.CompilerParams(vmem_limit_bytes=VMEM_BYTES),
        cost_estimate=pl.CostEstimate(flops=1 << 24, bytes_accessed=8 << 20, transcendentals=0),
        name="split_rows",
    )(tensor.reshape(count_i * count_j, count_k))


def turned_kernel(t_ref, out_ref):
    count_i, per, count_k = t_ref.shape
    for j in range(per):
        high, low = split(t_ref[:, j, :].T)
        out_ref[j * count_k : (j + 1) * count_k, :count_i] = high
        out_ref[j * count_k : (j + 1) * count_k, count_i:] = low


def split_turned(tensor):
    count_i, count_j, count_k = tensor.shape
    per = count_j // GRID
    return pl.pallas_call(
        turned_kernel,
        grid=(GRID,),
        out_shape=jax.ShapeDtypeStruct((count_j * count_k, 2 * count_i), BF16),
        in_specs=[pl.BlockSpec((count_i, per, count_k), lambda n: (0, n, 0))],
        out_specs=pl.BlockSpec((per * count_k, 2 * count_i), lambda n: (n, 0)),
        compiler_params=pltpu.CompilerParams(vmem_limit_bytes=VMEM_BYTES),
        cost_estimate=pl.CostEstimate(flops=1 << 24, bytes_accessed=8 << 20, transcendentals=0),
        name="split_turned",
    )(tensor)


def lower_half(shape):
    return lax.broadcasted_iota(jnp.int32, shape, len(shape) - 1) < shape[-1] // 2


def turn(x):
    return pltpu.roll(x, x.shape[1] // 2, 1)


def weights(x):
    high = x.astype(BF16).astype(F32)
    both = jnp.where(lower_half(x.shape), high, x - high).astype(BF16)
    return jnp.concatenate([both, both], axis=0)


def gram(x):
    return lax.dot_general(
        x, x, (((0,), (0,)), ((), ())), precision=HIGHEST, preferred_element_type=F32
    )


def unpack_first(ac_ref, b_ref, a2_ref, b2_ref, c2_ref):
    slots, each = ac_ref.shape[0], ac_ref.shape[1]
    own = a2_ref.shape[0] // slots
    core = lax.axis_index("gz")
    flat = ac_ref.reshape(slots * each, ac_ref.shape[2])
    for n in range(slots):
        a2_ref[n * own : (n + 1) * own, :] = ac_ref[n, :own, :]
    count = c2_ref.shape[0] // each
    for g in range(each):
        c2_ref[g * count : (g + 1) * count, :] = flat[pl.ds(core * each + g, count, stride=2 * each), :]
    a, b, c = a2_ref[...], b_ref[...], c2_ref[...]
    a2_ref[...] = jnp.where(lower_half(a.shape), a, turn(a))
    b2_ref[...] = jnp.where(lower_half(b.shape), b, turn(b))
    c2_ref[...] = jnp.where(lower_half(c.shape), turn(c), c)


def unpack_second(all_ref, a2_ref, b2_ref, c2_ref):
    half, count_c = a2_ref.shape[0] // 2, c2_ref.shape[0]
    a = all_ref[:half, :]
    c = all_ref[half : half + count_c, :]
    b2_ref[...] = all_ref[half + count_c :, :]
    lower = lower_half(a.shape)
    a2_ref[:half, :] = jnp.where(lower, a, turn(a))
    a2_ref[half:, :] = jnp.where(lower, turn(a), a)
    core = lax.axis_index("gz")
    keep = lower_half(c.shape).astype(jnp.int32) != core
    c2_ref[...] = jnp.where(keep, c, turn(c))


def pack_first(a, b, c, out_ref):
    half, count_c = a.shape[0] // 2, c.shape[0]
    out_ref[:half, :] = jnp.where(lower_half((half, a.shape[1])), a[:half], a[half:])
    out_ref[half : half + count_c, :] = c
    out_ref[half + count_c :, :] = b


def pack_second(a, b, c, bc_ref, ac_ref):
    core = lax.axis_index("gz")
    slots, tall, width = bc_ref.shape
    own = b.shape[0] // slots
    lower = lower_half((own, width))
    for n in range(slots):
        g, z = n // 2, n % 2
        block = jnp.where(core == z, c[g * tall : (g + 1) * tall], 0.0)
        bc_ref[n, :, :] = block
        bc_ref[n, :own, :] = jnp.where(lower, b[n * own : (n + 1) * own], block[:own])
    slots, each, width = ac_ref.shape
    own = a.shape[0] // slots
    for n in range(slots):
        ac_ref[n, :, :] = jnp.zeros((each, width), F32)
        ac_ref[n, :own, :] = a[n * own : (n + 1) * own]


def round_kernel(first, keep, scale, *refs):
    n_in, n_out = (2, 1) if first else (1, 2)
    small, (rows_ref, turned_ref) = refs[:n_in], refs[n_in : n_in + 2]
    outs = refs[n_in + 2 : n_in + 2 + n_out]
    a2_ref, b2_ref, c2_ref, wa_ref, wc_ref, ma_ref, mb_ref, mc_ref = refs[n_in + 2 + n_out :]
    count_i, count_j, count_k = a2_ref.shape[0], b2_ref.shape[0], c2_ref.shape[0]
    at_step = pl.program_id(0)

    @pl.when(at_step == 0)
    def _():
        (unpack_first if first else unpack_second)(*small, a2_ref, b2_ref, c2_ref)
        wa_ref[...] = weights(a2_ref[...])
        wc_ref[...] = weights(c2_ref[...])
        mb_ref[...] = jnp.zeros(mb_ref.shape, F32)
        mc_ref[...] = jnp.zeros(mc_ref.shape, F32)

    per_i, per_j = CHUNK // count_j, CHUNK // count_k
    chunks = rows_ref.shape[0] // CHUNK
    moment_b, moment_c = mb_ref[...], mc_ref[...]
    for n in range(chunks):
        c = at_step * chunks + n
        y = jnp.dot(rows_ref[n * CHUNK : (n + 1) * CHUNK, :], wc_ref[...], preferred_element_type=F32)
        y = y.reshape(per_i, count_j, y.shape[1])
        at_i = pl.multiple_of(c * per_i, per_i)
        ma_ref[pl.ds(at_i, per_i), :] = jnp.sum(y * b2_ref[...][None], axis=1)
        for m in range(per_i):
            moment_b = moment_b + y[m] * a2_ref[pl.ds(at_i + m, 1), :]
        z = jnp.dot(turned_ref[n * CHUNK : (n + 1) * CHUNK, :], wa_ref[...], preferred_element_type=F32)
        z = z.reshape(per_j, count_k, z.shape[1])
        for m in range(per_j):
            moment_c = moment_c + z[m] * b2_ref[pl.ds(c * per_j + m, 1), :]
    mb_ref[...] = moment_b
    mc_ref[...] = moment_c

    @pl.when(at_step == pl.num_programs(0) - 1)
    def _():
        a2, b2, c2 = a2_ref[...], b2_ref[...], c2_ref[...]
        gram_a, gram_b, gram_c = gram(a2), gram(b2), gram(c2)

        def result(factor, gram_one, gram_two, moment, weight, factor_scale):
            model = jnp.dot(
                factor, gram_one * gram_two, precision=HIGHEST, preferred_element_type=F32
            )
            out = (0.5 * model - (moment + turn(moment))) * factor_scale
            return out + factor * weight if weight else out

        a = result(a2, gram_b, gram_c, ma_ref[...], keep[0], scale[0])
        b = result(b2, gram_a, gram_c, mb_ref[...], keep[1], scale[1])
        c = result(c2, gram_a, gram_b, mc_ref[...], keep[2], scale[2])
        (pack_first if first else pack_second)(a, b, c, *outs)


def partials(first, keep, scale, small, rows, turned, sizes, out_shapes):
    count_i, count_j, count_k = sizes
    width = small[0].shape[-1]
    tall = rows.shape[0] // GRID

    def whole(shape):
        return pl.BlockSpec(shape, lambda n: (0,) * len(shape))

    return pl.pallas_call(
        functools.partial(round_kernel, first, keep, scale),
        grid=(GRID,),
        out_shape=tuple(jax.ShapeDtypeStruct(s, F32) for s in out_shapes),
        in_specs=[whole(x.shape) for x in small]
        + [pl.BlockSpec((tall, x.shape[1]), lambda n: (n, 0)) for x in (rows, turned)],
        out_specs=tuple(whole(s) for s in out_shapes),
        scratch_shapes=[
            pltpu.VMEM((count_i, width), F32),
            pltpu.VMEM((count_j, width), F32),
            pltpu.VMEM((count_k, width), F32),
            pltpu.VMEM((2 * count_i, width), BF16),
            pltpu.VMEM((2 * count_k, width), BF16),
            pltpu.VMEM((count_i, width), F32),
            pltpu.VMEM((count_j, width), F32),
            pltpu.VMEM((count_k, width), F32),
        ],
        compiler_params=pltpu.CompilerParams(vmem_limit_bytes=VMEM_BYTES),
        cost_estimate=pl.CostEstimate(flops=1 << 30, bytes_accessed=8 << 20, transcendentals=0),
        name="partials",
    )(*small, rows, turned)


def send_all(x, axes):
    count = 1
    for name in axes:
        count *= lax.axis_size(name)
    return lax.all_to_all(jnp.broadcast_to(x[None], (count, *x.shape)), axes, 0, 0, tiled=True)


def shift(x, axis, stride, count, by):
    pairs = []
    for n in range(lax.axis_size(axis)):
        place = n // stride % count
        to = n + ((place + by) % count - place) * stride
        pairs.append((2 * n + 1, 2 * to + 1))
    return lax.ppermute(x, (axis, "gz"), pairs)


def ring8(x):
    below, above = shift(x, "gx", 1, 8, 1), shift(x, "gx", 1, 8, -1)
    two = x + above
    three = two + below
    return three + (shift(three, "gx", 1, 8, -3) + shift(two, "gx", 1, 8, 3))


def ring4(x, stride):
    ones = shift(x, "gy", stride, 4, 1) + shift(x, "gy", stride, 4, -1)
    return (x + ones) + shift(x, "gy", stride, 4, 2)


def shards(tensor, factor_a, factor_b, factor_c):
    count_x, count_y, count_z = (lax.axis_size(n) for n in ("gx", "gy", "gz"))
    core = lax.axis_index("gz")
    sizes = count_i, count_j, count_k = tensor.shape
    whole = (
        float(count_j * count_y * count_k * count_z),
        float(count_i * count_x * count_k * count_z),
        float(count_i * count_x * count_j * count_y),
    )
    copies = (count_y * count_z, count_x * count_z, count_x * count_y)
    own, rank = factor_a.shape
    wide = 2 * rank

    rows = split_rows(tensor)
    padded_c = jnp.pad(factor_c, ((0, own - 1), (0, 0)))
    along_x = send_all(jnp.concatenate([factor_b, padded_c], axis=1), ("gx", "gz"))
    tensor, along_x = lax.optimization_barrier((tensor, along_x))
    turned = split_turned(tensor)
    rows_c = along_x.reshape(count_x, count_z, own, wide)[:, :, 0, rank:]
    rows_c = jnp.where(core == 0, rows_c[:, 0], rows_c[:, 1])
    rows, factor_a = lax.optimization_barrier((rows, factor_a))
    padded_a = jnp.pad(factor_a, ((0, count_x - own), (0, 0)))
    along_y = send_all(jnp.concatenate([padded_a, rows_c], axis=1), ("gy", "gz"))

    keep = tuple(1.0 / n for n in copies)
    scale = tuple(-STEP_SIZE / n for n in whole)
    half = count_i // 2
    packed_shape = (half + count_k + count_j, wide)
    (packed,) = partials(
        True, keep, scale, (along_y, along_x.reshape(count_j, wide)), rows, turned, sizes, (packed_shape,)
    )
    other = lax.ppermute(packed, "gz", [(0, 1)])
    middle = slice(half, half + count_k)
    sums = packed + other
    both_c = jnp.where(lower_half((count_k, wide)), other[middle], packed[middle])
    cb = ring8(jnp.concatenate([both_c, sums[half + count_k :]], axis=0))
    ac = ring4(ring4(jnp.concatenate([sums[:half], cb[:count_k]], axis=0), 1), 4)
    packed = jnp.concatenate([ac, cb[count_k:]], axis=0)
    packed = jnp.where(core == 1, packed, lax.ppermute(packed, "gz", [(1, 0)]))

    scale = tuple(1.0 / n for n in whole)
    slots_bc, slots_a = partials(
        False,
        (0.0,) * 3,
        scale,
        (packed,),
        rows,
        turned,
        sizes,
        ((count_x * count_z, count_y, wide), (count_y * count_z, 2 * own, wide)),
    )
    bc = jnp.sum(lax.all_to_all(slots_bc, ("gx", "gz"), 0, 0, tiled=True), axis=0)
    mine = jnp.arange(count_z)[None, :, None, None] == core
    slots_c = jnp.where(mine, bc[:, None, None, rank:], 0.0).reshape(count_y * count_z, 1, rank)
    slots_c = jnp.pad(slots_c, ((0, 0), (0, 2 * own - 1), (0, 0)))
    slots_ac = jnp.concatenate([slots_a[:, :, :rank], slots_c], axis=2)
    ac = jnp.sum(lax.all_to_all(slots_ac, ("gy", "gz"), 0, 0, tiled=True), axis=0)
    return ac[:own, :rank], bc[:own, :rank], ac[:1, rank:]


def solution(mesh):
    factors = (
        P(("gx", "gy", "gz"), None),
        P(("gy", "gx", "gz"), None),
        P(("gz", "gx", "gy"), None),
    )
    return jax.shard_map(
        shards,
        mesh=mesh,
        in_specs=(P("gx", "gy", "gz"), *factors),
        out_specs=factors,
        check_vma=False,
    )
```

time: 1520 us -> 146 us (0.10)
  blocking collectives: 1250 us -> 0 us
  waiting for transfers between devices: 204 us -> 30.1 us
  starting transfers between devices: 0.04 us -> 71.7 us
  matrix products: 40.5 us -> 0 us
  Pallas kernels: 0 us -> 32.4 us
    all_gather x6 -> x0, blocking collectives: 714 us -> none  [the longest x2 570 us: gather_blocks(): block_c = lax.all_gather(own_c, ('gx', 'gy'), axis=0, tiled=True)]
    unnamed x4 -> x0, blocking collectives: 387 us -> none
    unnamed x2 -> x0, waiting for transfers between devices: 204 us -> none
    psum x2 -> x0, blocking collectives: 154 us -> none  [gram_sums(): lax.psum((gram_local(own_a), gram_local(own_b), gram_local(own_c)), ('gx'...]
    ppermute x0 -> x12, starting transfers between devices: none -> 40.6 us  [the longest x10 38.1 us: shift(): return lax.ppermute(x, (axis, 'gz'), pairs)]
    dot_general x14 -> x0, matrix products: 40.5 us -> none  [the longest x2 18.5 us: partials(): along_k = jnp.einsum('ijk,kr->jri', tensor, block_c, precision=highest)]
    pallas_call x0 -> x4, Pallas kernels: none -> 32.4 us  [the longest x2 17.8 us: partials(): pl.pallas_call(functools.partial(round_kernel, first, keep, scale), grid=...]
    all_to_all x0 -> x4, starting transfers between devices: none -> 31.1 us  [the longest x2 17.5 us: send_all(): lax.all_to_all(jnp.broadcast_to(x[None], (count, *x.shape)), axes, 0, 0,...]
  transfers between devices with their start and end apart: 1 -> 16, of which waited for: 1 -> 12; matrix products, arithmetic and copies ran while one was open for 0% -> 0% of each run, Pallas kernels for 0% -> 10%
where the time goes in v2:
time: 146 us; the launch traced here: 144 us
  starting transfers between devices  71.7 us (49%)
  Pallas kernels  32.4 us (22%)
  waiting for transfers between devices  30.1 us (21%)
  other arithmetic  5.24 us (4%)
  local copies, waits for them, and re-layouts  3.96 us (3%)
    ppermute x10, starting transfers between devices, shift(): return lax.ppermute(x, (axis, 'gz'), pairs)  38.1 us
    pallas_call x2, Pallas kernels, partials(): pl.pallas_call(functools.partial(round_kernel, first, keep, scale), grid=...  17.8 us
    all_to_all x2, starting transfers between devices, send_all(): lax.all_to_all(jnp.broadcast_to(x[None], (count, *x.shape)), axes, 0, 0,...  17.5 us
    ppermute x10, waiting for transfers between devices, shift(): return lax.ppermute(x, (axis, 'gz'), pairs)  10.3 us
    all_to_all x1, waiting for transfers between devices, shards(): lax.all_to_all(slots_bc, ('gx', 'gz'), 0, 0, tiled=True)  9.05 us
    pallas_call x1, Pallas kernels, split_turned(): pl.pallas_call(turned_kernel, grid=(GRID,), out_shape=jax.ShapeDtypeStruc...  7.78 us
    all_to_all x1, starting transfers between devices, shards(): lax.all_to_all(slots_ac, ('gy', 'gz'), 0, 0, tiled=True)  7.62 us
    all_to_all x1, waiting for transfers between devices, shards(): lax.all_to_all(slots_ac, ('gy', 'gz'), 0, 0, tiled=True)  7.05 us
  transfers between devices with their start and end apart: 16, of which 12 were waited for; matrix products, arithmetic and copies ran while one was open for 0% of the time, Pallas kernels for 10%

profile of v2, /device:TPU:1, one launch (start us, length us, event | category | flops | bytes accessed | tf_op | source)
XLA Modules:
  0.0 144.3 jit_solution(15788756382125479976)
XLA Ops:
  2.0 10.0 %all-to-all-start = ((f32[16,4,128]{2,1,0:T(4,128)}), f32[16,4,128]{2,1,0:T(4,128)S(1)}, u32[]{:S(2)}, u32[]{:S(2)}) async-start(f32[16,4,128]{2,1,0:T(4,128)} %broadcast_in_dim.40), calls=%async_computation | async-start | bytes 65536 | tf_op jit(solution)/shard_map/all_to_all | solution.py:236
  12.0 6.8 %split_rows.1.refs_2_.refs_1_ = bf16[8192,256]{1,0:T(8,128)(2,1)} custom-call(f32[8192,128]{1,0:T(8,128)} %bitcast.8), custom_call_target="tpu_custom_call" | custom-call | flops 16777216 | bytes 8388608 | tf_op jit(solution)/shard_map/split_rows/pallas_call | solution.py:41
  20.2 7.5 %all-to-all-start.1 = ((f32[32,8,128]{2,1,0:T(8,128)}), f32[32,8,128]{2,1,0:T(8,128)S(1)}, u32[]{:S(2)}, u32[]{:S(2)}) async-start(f32[32,8,128]{2,1,0:T(8,128)} %broadcast_in_dim.41), calls=%async_computation.1 | async-start | bytes 262144 | tf_op jit(solution)/shard_map/all_to_all | solution.py:236
  27.7 7.8 %split_turned.1.refs_3_.refs_2_ = bf16[8192,256]{1,0:T(8,128)(2,1)} custom-call(f32[128,64,128]{2,1,0:T(8,128)} %t_ref), custom_call_target="tpu_custom_call" | custom-call | flops 16777216 | bytes 8388608 | tf_op jit(solution)/shard_map/split_turned/pallas_call | solution.py:64
  36.2 8.9 %partials.2 = f32[256,128]{1,0:T(8,128)} custom-call(f32[32,8,128]{2,1,0:T(8,128)} %copy-done, f32[64,128]{1,0:T(8,128)} %bitcast.9, bf16[8192,256]{1,0:T(8,128)(2,1)} %split_rows.1.refs_2_.refs_1_, bf16[8192,256]{1,0:T(8,128)(2,1)} %split_turned.1.refs_3_.refs_2_), custom_call_target="tpu_custom_call" | custom-call | flops 1073741824 | bytes 8388608 | tf_op jit(solution)/shard_map/partials/pallas_call | solution.py:209
  46.4 2.1 %collective-permute-done = f32[256,128]{1,0:T(8,128)S(1)} collective-permute-done((f32[256,128]{1,0:T(8,128)}, f32[256,128]{1,0:T(8,128)S(1)}, u32[]{:S(2)}, u32[]{:S(2)}) %collective-permute-start) | collective-permute-done | bytes 131104 | tf_op jit(solution)/shard_map/ppermute | solution.py:291
  50.3 2.7 %collective-permute-start.2 = (f32[192,128]{1,0:T(8,128)S(1)}, f32[192,128]{1,0:T(8,128)S(1)}, u32[]{:S(2)}, u32[]{:S(2)}) collective-permute-start(f32[192,128]{1,0:T(8,128)S(1)} %pad_maximum_fusion.1), channel_id=1, source_target_pairs={{1,33},{33,65},{65,97},{97,129},{129,161},{161,193},{193,225},{225... | collective-permute-start | bytes 294920 | tf_op jit(solution)/shard_map/ppermute | solution.py:245
  53.0 3.8 %collective-permute-start.1 = (f32[192,128]{1,0:T(8,128)S(1)}, f32[192,128]{1,0:T(8,128)S(1)}, u32[]{:S(2)}, u32[]{:S(2)}) collective-permute-start(f32[192,128]{1,0:T(8,128)S(1)} %pad_maximum_fusion.1), channel_id=1, source_target_pairs={{1,225},{33,1},{65,33},{97,65},{129,97},{161,129},{193,161},{225,1... | collective-permute-start | bytes 294920 | tf_op jit(solution)/shard_map/ppermute | solution.py:245
  58.4 5.1 %collective-permute-start.3 = (f32[192,128]{1,0:T(8,128)S(1)}, f32[192,128]{1,0:T(8,128)S(1)}, u32[]{:S(2)}, u32[]{:S(2)}) collective-permute-start(f32[192,128]{1,0:T(8,128)S(1)} %get-tuple-element.15), channel_id=1, source_target_pairs={{1,161},{33,193},{65,225},{97,1},{129,33},{161,65},{193,97},{225,1... | collective-permute-start | bytes 294920 | tf_op jit(solution)/shard_map/ppermute | solution.py:245
  63.6 4.0 %collective-permute-start.4 = (f32[192,128]{1,0:T(8,128)S(1)}, f32[192,128]{1,0:T(8,128)S(1)}, u32[]{:S(2)}, u32[]{:S(2)}) collective-permute-start(f32[192,128]{1,0:T(8,128)S(1)} %get-tuple-element.16), channel_id=1, source_target_pairs={{1,97},{33,129},{65,161},{97,193},{129,225},{161,1},{193,33},{225,... | collective-permute-start | bytes 294920 | tf_op jit(solution)/shard_map/ppermute | solution.py:245
  67.6 1.8 %collective-permute-done.3 = f32[192,128]{1,0:T(8,128)S(1)} collective-permute-done((f32[192,128]{1,0:T(8,128)S(1)}, f32[192,128]{1,0:T(8,128)S(1)}, u32[]{:S(2)}, u32[]{:S(2)}) %collective-permute-start.3) | collective-permute-done | bytes 98336 | tf_op jit(solution)/shard_map/ppermute | solution.py:245
  69.5 3.6 %collective-permute-done.4 = f32[192,128]{1,0:T(8,128)S(1)} collective-permute-done((f32[192,128]{1,0:T(8,128)S(1)}, f32[192,128]{1,0:T(8,128)S(1)}, u32[]{:S(2)}, u32[]{:S(2)}) %collective-permute-start.4) | collective-permute-done | bytes 98336 | tf_op jit(solution)/shard_map/ppermute | solution.py:245
  73.2 4.8 %collective-permute-start.7 = (f32[192,128]{1,0:T(8,128)S(1)}, f32[192,128]{1,0:T(8,128)S(1)}, u32[]{:S(2)}, u32[]{:S(2)}) collective-permute-start(f32[192,128]{1,0:T(8,128)S(1)} %pad_maximum_fusion.2), channel_id=1, source_target_pairs={{1,5},{3,7},{5,1},{7,3},{9,13},{11,15},{13,9},{15,11},{17,21},{19,... | collective-permute-start | bytes 294920 | tf_op jit(solution)/shard_map/ppermute | solution.py:245
  78.0 2.2 %collective-permute-start.5 = (f32[192,128]{1,0:T(8,128)S(1)}, f32[192,128]{1,0:T(8,128)S(1)}, u32[]{:S(2)}, u32[]{:S(2)}) collective-permute-start(f32[192,128]{1,0:T(8,128)S(1)} %pad_maximum_fusion.2), channel_id=1, source_target_pairs={{1,3},{3,5},{5,7},{7,1},{9,11},{11,13},{13,15},{15,9},{17,19},{19,... | collective-permute-start | bytes 294920 | tf_op jit(solution)/shard_map/ppermute | solution.py:245
  80.2 4.3 %collective-permute-start.6 = (f32[192,128]{1,0:T(8,128)S(1)}, f32[192,128]{1,0:T(8,128)S(1)}, u32[]{:S(2)}, u32[]{:S(2)}) collective-permute-start(f32[192,128]{1,0:T(8,128)S(1)} %pad_maximum_fusion.2), channel_id=1, source_target_pairs={{1,7},{3,1},{5,3},{7,5},{9,15},{11,9},{13,11},{15,13},{17,23},{19,... | collective-permute-start | bytes 294920 | tf_op jit(solution)/shard_map/ppermute | solution.py:245
  86.1 4.6 %collective-permute-start.10 = (f32[192,128]{1,0:T(8,128)S(1)}, f32[192,128]{1,0:T(8,128)S(1)}, u32[]{:S(2)}, u32[]{:S(2)}) collective-permute-start(f32[192,128]{1,0:T(8,128)S(1)} %add_add_fusion.1), channel_id=1, source_target_pairs={{1,17},{3,19},{5,21},{7,23},{9,25},{11,27},{13,29},{15,31},{17,1},... | collective-permute-start | bytes 294920 | tf_op jit(solution)/shard_map/ppermute | solution.py:245
  90.7 2.2 %collective-permute-start.8 = (f32[192,128]{1,0:T(8,128)S(1)}, f32[192,128]{1,0:T(8,128)S(1)}, u32[]{:S(2)}, u32[]{:S(2)}) collective-permute-start(f32[192,128]{1,0:T(8,128)S(1)} %add_add_fusion.1), channel_id=1, source_target_pairs={{1,9},{3,11},{5,13},{7,15},{9,17},{11,19},{13,21},{15,23},{17,25},... | collective-permute-start | bytes 294920 | tf_op jit(solution)/shard_map/ppermute | solution.py:245
  93.0 4.2 %collective-permute-start.9 = (f32[192,128]{1,0:T(8,128)S(1)}, f32[192,128]{1,0:T(8,128)S(1)}, u32[]{:S(2)}, u32[]{:S(2)}) collective-permute-start(f32[192,128]{1,0:T(8,128)S(1)} %add_add_fusion.1), channel_id=1, source_target_pairs={{1,25},{3,27},{5,29},{7,31},{9,1},{11,3},{13,5},{15,7},{17,9},{19,... | collective-permute-start | bytes 294920 | tf_op jit(solution)/shard_map/ppermute | solution.py:245
  101.9 8.9 %partials.3 = (f32[16,16,128]{2,1,0:T(8,128)}, f32[32,8,128]{2,1,0:T(8,128)}) custom-call(f32[256,128]{1,0:T(8,128)} %broadcast_select_fusion.refs_0_, bf16[8192,256]{1,0:T(8,128)(2,1)} %split_rows.1.refs_2_.refs_1_, bf16[8192,256]{1,0:T(8,128)(2,1)} %split_turned.1.refs_3_.refs_2_), custom_call_target="tpu_custom_call" | custom-call | flops 1073741824 | bytes 8388608 | tf_op jit(solution)/shard_map/partials/pallas_call | solution.py:209
  110.8 6.0 %all-to-all-start.2 = ((f32[16,16,128]{2,1,0:T(8,128)}), f32[16,16,128]{2,1,0:T(8,128)S(1)}, u32[]{:S(2)}, u32[]{:S(2)}) async-start(f32[16,16,128]{2,1,0:T(8,128)} %get-tuple-element.14), calls=%async_computation.2 | async-start | bytes 262144 | tf_op jit(solution)/shard_map/all_to_all | solution.py:311
  116.9 9.1 %all-to-all-done.2 = f32[16,16,128]{2,1,0:T(8,128)S(1)} async-done(((f32[16,16,128]{2,1,0:T(8,128)}), f32[16,16,128]{2,1,0:T(8,128)S(1)}, u32[]{:S(2)}, u32[]{:S(2)}) %all-to-all-start.2) | async-done | bytes 131104 | tf_op jit(solution)/shard_map/all_to_all | solution.py:311
  126.2 1.7 %select_maximum_fusion = f32[32,8,128]{2,1,0:T(8,128)} fusion(f32[32,1,64]{2,1,0:T(1,128)S(1)} %broadcast_select_fusion.1, f32[32,8,64]{2,1,0:T(8,128)} %bitcast.10), kind=kLoop, calls=%fused_computation | loop fusion | flops 98304 | bytes 204800 | tf_op jit(solution)/shard_map/concatenate | solution.py:315
  127.8 7.6 %all-to-all-start.3 = ((f32[32,8,128]{2,1,0:T(8,128)}), f32[32,8,128]{2,1,0:T(8,128)S(1)}, u32[]{:S(2)}, u32[]{:S(2)}) async-start(f32[32,8,128]{2,1,0:T(8,128)} %select_maximum_fusion), calls=%async_computation.3 | async-start | bytes 262144 | tf_op jit(solution)/shard_map/all_to_all | solution.py:316
  136.0 7.0 %all-to-all-done.3 = f32[32,8,128]{2,1,0:T(8,128)S(1)} async-done(((f32[32,8,128]{2,1,0:T(8,128)}), f32[32,8,128]{2,1,0:T(8,128)S(1)}, u32[]{:S(2)}, u32[]{:S(2)}) %all-to-all-start.3) | async-done | bytes 131104 | tf_op jit(solution)/shard_map/all_to_all | solution.py:316
  (51 shorter events, 16.5 us)
Async XLA Ops:
  2.0 17.4 %all-to-all-start = ((f32[16,4,128]{2,1,0:T(4,128)}), f32[16,4,128]{2,1,0:T(4,128)S(1)}, u32[]{:S(2)}, u32[]{:S(2)}) async-start(f32[16,4,128]{2,1,0:T(4,128)} %broadcast_in_dim.40), calls=%async_computation | async-start | bytes 65536 | tf_op jit(solution)/shard_map/all_to_all | solution.py:236
  12.0 7.5 %copy-start.2 = (f32[4,64]{1,0:T(4,128)S(1)}, f32[4,64]{1,0:T(4,128)}, u32[]{:S(2)}) copy-start(f32[4,64]{1,0:T(4,128)} %param.5) | copy-start | bytes 3076
  19.4 16.1 %copy-start.1 = (f32[16,4,128]{2,1,0:T(4,128)}, f32[16,4,128]{2,1,0:T(4,128)S(1)}, u32[]{:S(2)}) copy-start(f32[16,4,128]{2,1,0:T(4,128)S(1)} %all-to-all-done) | copy-start | bytes 98308
  20.2 15.3 %all-to-all-start.1 = ((f32[32,8,128]{2,1,0:T(8,128)}), f32[32,8,128]{2,1,0:T(8,128)S(1)}, u32[]{:S(2)}, u32[]{:S(2)}) async-start(f32[32,8,128]{2,1,0:T(8,128)} %broadcast_in_dim.41), calls=%async_computation.1 | async-start | bytes 262144 | tf_op jit(solution)/shard_map/all_to_all | solution.py:236
  35.5 0.7 copy-start
  45.1 3.4 %collective-permute-start = (f32[256,128]{1,0:T(8,128)}, f32[256,128]{1,0:T(8,128)S(1)}, u32[]{:S(2)}, u32[]{:S(2)}) collective-permute-start(f32[256,128]{1,0:T(8,128)} %partials.2), channel_id=1, source_target_pairs={{0,1},{2,3},{4,5},{6,7},{8,9},{10,11},{12,13},{14,15},{16,17},{18,... | collective-permute-start | bytes 393224 | tf_op jit(solution)/shard_map/ppermute | solution.py:291
  50.3 6.6 %collective-permute-start.2 = (f32[192,128]{1,0:T(8,128)S(1)}, f32[192,128]{1,0:T(8,128)S(1)}, u32[]{:S(2)}, u32[]{:S(2)}) collective-permute-start(f32[192,128]{1,0:T(8,128)S(1)} %pad_maximum_fusion.1), channel_id=1, source_target_pairs={{1,33},{33,65},{65,97},{97,129},{129,161},{161,193},{193,225},{225... | collective-permute-start | bytes 294920 | tf_op jit(solution)/shard_map/ppermute | solution.py:245
  53.0 5.4 %collective-permute-start.1 = (f32[192,128]{1,0:T(8,128)S(1)}, f32[192,128]{1,0:T(8,128)S(1)}, u32[]{:S(2)}, u32[]{:S(2)}) collective-permute-start(f32[192,128]{1,0:T(8,128)S(1)} %pad_maximum_fusion.1), channel_id=1, source_target_pairs={{1,225},{33,1},{65,33},{97,65},{129,97},{161,129},{193,161},{225,1... | collective-permute-start | bytes 294920 | tf_op jit(solution)/shard_map/ppermute | solution.py:245
  58.4 11.0 %collective-permute-start.3 = (f32[192,128]{1,0:T(8,128)S(1)}, f32[192,128]{1,0:T(8,128)S(1)}, u32[]{:S(2)}, u32[]{:S(2)}) collective-permute-start(f32[192,128]{1,0:T(8,128)S(1)} %get-tuple-element.15), channel_id=1, source_target_pairs={{1,161},{33,193},{65,225},{97,1},{129,33},{161,65},{193,97},{225,1... | collective-permute-start | bytes 294920 | tf_op jit(solution)/shard_map/ppermute | solution.py:245
  63.6 9.5 %collective-permute-start.4 = (f32[192,128]{1,0:T(8,128)S(1)}, f32[192,128]{1,0:T(8,128)S(1)}, u32[]{:S(2)}, u32[]{:S(2)}) collective-permute-start(f32[192,128]{1,0:T(8,128)S(1)} %get-tuple-element.16), channel_id=1, source_target_pairs={{1,97},{33,129},{65,161},{97,193},{129,225},{161,1},{193,33},{225,... | collective-permute-start | bytes 294920 | tf_op jit(solution)/shard_map/ppermute | solution.py:245
  73.2 11.3 %collective-permute-start.7 = (f32[192,128]{1,0:T(8,128)S(1)}, f32[192,128]{1,0:T(8,128)S(1)}, u32[]{:S(2)}, u32[]{:S(2)}) collective-permute-start(f32[192,128]{1,0:T(8,128)S(1)} %pad_maximum_fusion.2), channel_id=1, source_target_pairs={{1,5},{3,7},{5,1},{7,3},{9,13},{11,15},{13,9},{15,11},{17,21},{19,... | collective-permute-start | bytes 294920 | tf_op jit(solution)/shard_map/ppermute | solution.py:245
  78.0 6.6 %collective-permute-start.5 = (f32[192,128]{1,0:T(8,128)S(1)}, f32[192,128]{1,0:T(8,128)S(1)}, u32[]{:S(2)}, u32[]{:S(2)}) collective-permute-start(f32[192,128]{1,0:T(8,128)S(1)} %pad_maximum_fusion.2), channel_id=1, source_target_pairs={{1,3},{3,5},{5,7},{7,1},{9,11},{11,13},{13,15},{15,9},{17,19},{19,... | collective-permute-start | bytes 294920 | tf_op jit(solution)/shard_map/ppermute | solution.py:245
  80.2 5.9 %collective-permute-start.6 = (f32[192,128]{1,0:T(8,128)S(1)}, f32[192,128]{1,0:T(8,128)S(1)}, u32[]{:S(2)}, u32[]{:S(2)}) collective-permute-start(f32[192,128]{1,0:T(8,128)S(1)} %pad_maximum_fusion.2), channel_id=1, source_target_pairs={{1,7},{3,1},{5,3},{7,5},{9,15},{11,9},{13,11},{15,13},{17,23},{19,... | collective-permute-start | bytes 294920 | tf_op jit(solution)/shard_map/ppermute | solution.py:245
  86.1 11.1 %collective-permute-start.10 = (f32[192,128]{1,0:T(8,128)S(1)}, f32[192,128]{1,0:T(8,128)S(1)}, u32[]{:S(2)}, u32[]{:S(2)}) collective-permute-start(f32[192,128]{1,0:T(8,128)S(1)} %add_add_fusion.1), channel_id=1, source_target_pairs={{1,17},{3,19},{5,21},{7,23},{9,25},{11,27},{13,29},{15,31},{17,1},... | collective-permute-start | bytes 294920 | tf_op jit(solution)/shard_map/ppermute | solution.py:245
  90.7 6.6 %collective-permute-start.8 = (f32[192,128]{1,0:T(8,128)S(1)}, f32[192,128]{1,0:T(8,128)S(1)}, u32[]{:S(2)}, u32[]{:S(2)}) collective-permute-start(f32[192,128]{1,0:T(8,128)S(1)} %add_add_fusion.1), channel_id=1, source_target_pairs={{1,9},{3,11},{5,13},{7,15},{9,17},{11,19},{13,21},{15,23},{17,25},... | collective-permute-start | bytes 294920 | tf_op jit(solution)/shard_map/ppermute | solution.py:245
  93.0 5.9 %collective-permute-start.9 = (f32[192,128]{1,0:T(8,128)S(1)}, f32[192,128]{1,0:T(8,128)S(1)}, u32[]{:S(2)}, u32[]{:S(2)}) collective-permute-start(f32[192,128]{1,0:T(8,128)S(1)} %add_add_fusion.1), channel_id=1, source_target_pairs={{1,25},{3,27},{5,29},{7,31},{9,1},{11,3},{13,5},{15,7},{17,9},{19,... | collective-permute-start | bytes 294920 | tf_op jit(solution)/shard_map/ppermute | solution.py:245
  98.9 2.3 %collective-permute-start.11 = (f32[256,128]{1,0:T(8,128)S(1)}, f32[256,128]{1,0:T(8,128)S(1)}, u32[]{:S(2)}, u32[]{:S(2)}) collective-permute-start(f32[256,128]{1,0:T(8,128)S(1)} %pad_maximum_fusion), channel_id=1, source_target_pairs={{1,0},{3,2},{5,4},{7,6},{9,8},{11,10},{13,12},{15,14},{17,16},{19,... | collective-permute-start | bytes 393224 | tf_op jit(solution)/shard_map/ppermute | solution.py:298
  110.8 15.2 %all-to-all-start.2 = ((f32[16,16,128]{2,1,0:T(8,128)}), f32[16,16,128]{2,1,0:T(8,128)S(1)}, u32[]{:S(2)}, u32[]{:S(2)}) async-start(f32[16,16,128]{2,1,0:T(8,128)} %get-tuple-element.14), calls=%async_computation.2 | async-start | bytes 262144 | tf_op jit(solution)/shard_map/all_to_all | solution.py:311
  127.8 15.3 %all-to-all-start.3 = ((f32[32,8,128]{2,1,0:T(8,128)}), f32[32,8,128]{2,1,0:T(8,128)S(1)}, u32[]{:S(2)}, u32[]{:S(2)}) async-start(f32[32,8,128]{2,1,0:T(8,128)} %select_maximum_fusion), calls=%async_computation.3 | async-start | bytes 262144 | tf_op jit(solution)/shard_map/all_to_all | solution.py:316

commit v3 on v0

v3 whole, which is shorter than its diff:
```python
import functools

import jax
import jax.numpy as jnp
from jax import lax
from jax.experimental import pallas as pl
from jax.experimental.pallas import tpu as pltpu
from jax.sharding import PartitionSpec as P

STEPS = 2
STEP_SIZE = 0.1
F32 = jnp.float32
BF16 = jnp.bfloat16
HIGHEST = lax.Precision.HIGHEST
VMEM = pl.BlockSpec(memory_space=pltpu.VMEM)
HBM = pl.BlockSpec(memory_space=pltpu.HBM)
CHUNK = 512
UNROLL = 2


def split(x):
    high = x.astype(BF16)
    return high, (x - high.astype(F32)).astype(BF16)


def lower_half(shape):
    return lax.broadcasted_iota(jnp.int32, shape, len(shape) - 1) < shape[-1] // 2


def turn(x):
    return pltpu.roll(x, x.shape[1] // 2, 1)


def from_lower(x):
    return jnp.where(lower_half(x.shape), x, turn(x))


def from_upper(x):
    return jnp.where(lower_half(x.shape), turn(x), x)


def gram(x):
    return lax.dot_general(
        x, x, (((0,), (0,)), ((), ())), precision=HIGHEST, preferred_element_type=F32
    )


def unpack_first(ac_ref, b_ref, a2_ref, b2_ref, c2_ref):
    slots, each = ac_ref.shape[0], ac_ref.shape[1]
    own = a2_ref.shape[0] // slots
    core = lax.axis_index("gz")
    flat = ac_ref.reshape(slots * each, ac_ref.shape[2])
    for n in range(slots):
        a2_ref[n * own : (n + 1) * own, :] = ac_ref[n, :own, :]
    count = c2_ref.shape[0] // each
    for g in range(each):
        c2_ref[g * count : (g + 1) * count, :] = flat[pl.ds(core * each + g, count, stride=2 * each), :]
    a2_ref[...] = from_lower(a2_ref[...])
    b2_ref[...] = from_lower(b_ref[...])
    c2_ref[...] = from_upper(c2_ref[...])


def unpack_second(ac_ref, cb_ref, a2_ref, b2_ref, c2_ref):
    a2_ref[...] = from_lower(ac_ref[...])
    b2_ref[...] = from_upper(cb_ref[: b2_ref.shape[0], :])
    c2_ref[...] = from_upper(ac_ref[...])


def pack_first(a, b, c_ref, ab_ref, out_c_ref):
    count_b = b.shape[0]
    lower = lower_half(b.shape)
    ab_ref[:count_b, :] = jnp.where(lower, a[:count_b], b)
    ab_ref[count_b:, :] = jnp.where(lower_half(a[count_b:].shape), a[count_b:], 0.0)
    out_c_ref[...] = c_ref[...]


def pack_second(a, b, c_ref, ac_ref, b_ref):
    core = lax.axis_index("gz")
    slots, each, width = ac_ref.shape
    own, apart = a.shape[0] // slots, c_ref.shape[0] // each
    lower = lower_half((own, width))
    for n in range(slots):
        block = c_ref[pl.ds(n // 2, each, stride=apart), :]
        block = jnp.where(core == n % 2, block, 0.0)
        ac_ref[n, :, :] = block
        ac_ref[n, :own, :] = jnp.where(lower, a[n * own : (n + 1) * own], block[:own])
    b_ref[...] = b


def round_kernel(first, keep, scale, *refs):
    small, t_ref, outs = refs[:2], refs[2], refs[3:5]
    a2_ref, b2_ref, c2_ref, wc_ref, at_ref, ma_ref = refs[5:11]
    if first:
        t_hbm, (t_ref, sems) = t_ref, refs[11:]
    count_i, count_j, count_k = a2_ref.shape[0], b2_ref.shape[0], c2_ref.shape[0]
    width = a2_ref.shape[1]
    rank = width // 2
    chunks = t_ref.shape[0] // CHUNK
    per = CHUNK // count_j

    def fetch(c):
        at = pl.ds(pl.multiple_of(c * CHUNK, CHUNK), CHUNK)
        return pltpu.make_async_copy(t_hbm.at[at, :], t_ref.at[at, :], sems.at[c])

    for c in range(chunks if first else 0):
        fetch(c).start()

    (unpack_first if first else unpack_second)(*small, a2_ref, b2_ref, c2_ref)
    a2, b2, c2 = a2_ref[...], b2_ref[...], c2_ref[...]
    high = c2.astype(BF16).astype(F32)
    both = jnp.where(lower_half(c2.shape), high, c2 - high).astype(BF16)
    wc_ref[:count_k, :] = both
    wc_ref[count_k:, :] = both
    at_ref[...] = a2.T[:rank]
    turned_b = b2.T[:rank]
    turned_b = jnp.concatenate([turned_b] * (128 // count_j), axis=1)
    gram_a, gram_b, gram_c = gram(a2), gram(b2), gram(c2)

    def model(factor, one, two):
        return 0.5 * jnp.dot(factor, one * two, precision=HIGHEST, preferred_element_type=F32)

    model_a = model(a2, gram_b, gram_c)
    model_b = model(b2, gram_a, gram_c)
    model_c = model(c2, gram_a, gram_b)
    group = 128 // count_j
    lane = lax.broadcasted_iota(jnp.int32, (rank, 128), 1) // count_j

    def step(c, carry):
        moment_b, moment_c = carry
        if first:
            fetch(c).wait()
        high, low = split(t_ref[pl.ds(pl.multiple_of(c * CHUNK, CHUNK), CHUNK), :])
        terms = jnp.concatenate([high, low], axis=1)
        y = jnp.dot(terms, wc_ref[...], preferred_element_type=F32)
        y = y.reshape(per, count_j, width)
        at_i = pl.multiple_of(c * per, per)
        ma_ref[pl.ds(at_i, per), :] = jnp.sum(y * b2_ref[...][None], axis=1)
        for m in range(per):
            moment_b = moment_b + y[m] * a2_ref[pl.ds(at_i + m, 1), :]
        near = pltpu.roll(at_ref[...], count_i - at_i, 1)
        pieces = []
        for m in range(0, per, group):
            columns = jnp.broadcast_to(near[:, m : m + 1], (rank, 128))
            for g in range(1, group):
                other = jnp.broadcast_to(near[:, m + g : m + g + 1], (rank, 128))
                columns = jnp.where(lane == g, other, columns)
            pieces.append(columns * turned_b)
        rows_high, rows_low = split(jnp.concatenate(pieces, axis=1))
        rows = jnp.concatenate([rows_high, rows_low], axis=0)
        moment_c = moment_c + jnp.dot(rows, terms, preferred_element_type=F32)
        return moment_b, moment_c

    moment_b, moment_c = lax.fori_loop(
        0,
        chunks,
        step,
        (jnp.zeros((count_j, width), F32), jnp.zeros((width, 2 * count_k), F32)),
        unroll=UNROLL,
    )
    moment_c = moment_c[:, :count_k] + moment_c[:, count_k:]
    moment_c = moment_c[:rank] + moment_c[rank:]
    moment_c = jnp.concatenate([moment_c, moment_c], axis=0).T
    moment_a = ma_ref[...]

    def result(factor, whole, moment, weight, factor_scale):
        out = (whole - moment) * factor_scale
        return out + factor * weight if weight else out

    a = result(a2_ref[...], model_a, moment_a + turn(moment_a), keep[0], scale[0])
    b = result(b2_ref[...], model_b, moment_b + turn(moment_b), keep[1], scale[1])
    c2_ref[...] = result(c2_ref[...], model_c, moment_c, keep[2], scale[2])
    (pack_first if first else pack_second)(a, b, c2_ref, *outs)


def partials(first, keep, scale, small, tensor, out_shapes):
    count_i, count_j, count_k = tensor.shape
    width = small[0].shape[-1]
    tall = count_i * count_j
    fetched = [pltpu.VMEM((tall, count_k), F32), pltpu.SemaphoreType.DMA((tall // CHUNK,))]
    fetched = fetched if first else []
    return pl.pallas_call(
        functools.partial(round_kernel, first, keep, scale),
        out_shape=tuple(jax.ShapeDtypeStruct(s, F32) for s in out_shapes),
        in_specs=[VMEM, VMEM, HBM if first else VMEM],
        out_specs=(VMEM, VMEM),
        scratch_shapes=[
            pltpu.VMEM((count_i, width), F32),
            pltpu.VMEM((count_j, width), F32),
            pltpu.VMEM((count_k, width), F32),
            pltpu.VMEM((2 * count_k, width), BF16),
            pltpu.VMEM((width // 2, count_i), F32),
            pltpu.VMEM((count_i, width), F32),
            *fetched,
        ],
        compiler_params=pltpu.CompilerParams(vmem_limit_bytes=(60 if first else 24) << 20),
        cost_estimate=pl.CostEstimate(flops=1 << 30, bytes_accessed=4 << 20, transcendentals=0),
        name="partials",
    )(*small, tensor.reshape(tall, count_k))


def send_all(x, axes):
    count = 1
    for name in axes:
        count *= lax.axis_size(name)
    return lax.all_to_all(jnp.broadcast_to(x[None], (count, *x.shape)), axes, 0, 0, tiled=True)


def shift(x, axis, stride, count, by):
    pairs = []
    for n in range(lax.axis_size(axis)):
        place = n // stride % count
        pairs.append((n, n + ((place + by) % count - place) * stride))
    return lax.ppermute(x, axis, pairs)


def ring8(x):
    below, above = shift(x, "gx", 1, 8, 1), shift(x, "gx", 1, 8, -1)
    two = x + above
    three = two + below
    return three + (shift(three, "gx", 1, 8, -3) + shift(two, "gx", 1, 8, 3))


def ring4(x, stride):
    ones = shift(x, "gy", stride, 4, 1) + shift(x, "gy", stride, 4, -1)
    return (x + ones) + shift(x, "gy", stride, 4, 2)


def swap(x):
    return lax.ppermute(x, "gz", [(0, 1), (1, 0)])


def shards(tensor, factor_a, factor_b, factor_c):
    count_x, count_y, count_z = (lax.axis_size(n) for n in ("gx", "gy", "gz"))
    core = lax.axis_index("gz")
    count_i, count_j, count_k = tensor.shape
    whole = (
        float(count_j * count_y * count_k * count_z),
        float(count_i * count_x * count_k * count_z),
        float(count_i * count_x * count_j * count_y),
    )
    copies = (count_y * count_z, count_x * count_z, count_x * count_y)
    own, rank = factor_a.shape
    wide = 2 * rank

    padded_c = jnp.pad(factor_c, ((0, own - 1), (0, 0)))
    along_x = send_all(jnp.concatenate([factor_b, padded_c], axis=1), ("gx", "gz"))
    rows_c = along_x.reshape(count_x, count_z, own, wide)[:, :, 0, rank:]
    rows_c = jnp.where(core == 0, rows_c[:, 0], rows_c[:, 1])
    padded_a = jnp.pad(factor_a, ((0, count_x - own), (0, 0)))
    along_y = send_all(jnp.concatenate([padded_a, rows_c], axis=1), ("gy", "gz"))

    keep = tuple(1.0 / n for n in copies)
    scale = tuple(-STEP_SIZE / n for n in whole)
    small = (along_y, along_x.reshape(count_j, wide))
    ab, c = partials(True, keep, scale, small, tensor, ((count_i, wide), (count_k, wide)))
    ab = ab + swap(ab)
    cb = ring8(jnp.where(lower_half(c.shape), c, ab))
    ac = ring4(ring4(jnp.concatenate([ab[:, :rank], cb[:, :rank]], axis=1), 1), 4)

    scale = tuple(1.0 / n for n in whole)
    shapes = ((count_y * count_z, 2 * own, wide), (count_j, wide))
    slots_ac, b = partials(False, (0.0,) * 3, scale, (ac, cb), tensor, shapes)
    ac = jnp.sum(lax.all_to_all(slots_ac, ("gy", "gz"), 0, 0, tiled=True), axis=0)
    mine = (jnp.arange(count_z) == core)[None, :, None, None]
    slots_c = jnp.where(mine, ac[:, None, None, rank:], 0.0)
    slots_c = jnp.pad(slots_c, ((0, 0), (0, 0), (0, own - 1), (0, 0)))
    slots_b = b.reshape(count_x, count_z, own, wide)[..., :rank]
    slots_bc = jnp.concatenate([slots_b, slots_c], axis=3).reshape(-1, own, wide)
    bc = jnp.sum(lax.all_to_all(slots_bc, ("gx", "gz"), 0, 0, tiled=True), axis=0)
    return ac[:own, :rank], bc[:, :rank], bc[:1, rank:]


def solution(mesh):
    factors = (
        P(("gx", "gy", "gz"), None),
        P(("gy", "gx", "gz"), None),
        P(("gz", "gx", "gy"), None),
    )
    return jax.shard_map(
        shards,
        mesh=mesh,
        in_specs=(P("gx", "gy", "gz"), *factors),
        out_specs=factors,
        check_vma=False,
    )
```

time: 1520 us -> 115 us (0.08)
  blocking collectives: 1250 us -> 15 us
  waiting for transfers between devices: 204 us -> 37.3 us
  matrix products: 40.5 us -> 0 us
  starting transfers between devices: 0.04 us -> 39.1 us
    all_gather x6 -> x0, blocking collectives: 714 us -> none  [the longest x2 570 us: gather_blocks(): block_c = lax.all_gather(own_c, ('gx', 'gy'), axis=0, tiled=True)]
    unnamed x4 -> x0, blocking collectives: 387 us -> none
    unnamed x2 -> x0, waiting for transfers between devices: 204 us -> none
    psum x2 -> x0, blocking collectives: 154 us -> none  [gram_sums(): lax.psum((gram_local(own_a), gram_local(own_b), gram_local(own_c)), ('gx'...]
    dot_general x14 -> x0, matrix products: 40.5 us -> none  [the longest x2 18.5 us: partials(): along_k = jnp.einsum('ijk,kr->jri', tensor, block_c, precision=highest)]
    all_to_all x0 -> x3, starting transfers between devices: none -> 25.7 us  [the longest x1 9.98 us: send_all(): lax.all_to_all(jnp.broadcast_to(x[None], (count, *x.shape)), axes, 0, 0,...]
    all_to_all x0 -> x3, waiting for transfers between devices: none -> 21.9 us  [the longest x1 7.73 us: shards(): lax.all_to_all(slots_ac, ('gy', 'gz'), 0, 0, tiled=True)]
    ppermute x0 -> x11, waiting for transfers between devices: none -> 15.4 us  [the longest x10 14.2 us: shift(): return lax.ppermute(x, axis, pairs)]
  transfers between devices with their start and end apart: 1 -> 14, of which waited for: 1 -> 11; matrix products, arithmetic and copies ran while one was open for 0% -> 1% of each run, Pallas kernels for 0% -> 0%
where the time goes in v3:
time: 115 us; the launch traced here: 114 us
  starting transfers between devices  39.1 us (34%)
  waiting for transfers between devices  37.3 us (32%)
  blocking collectives  15 us (13%)
  Pallas kernels  14.5 us (13%)
  local copies, waits for them, and re-layouts  4.14 us (4%)
  other arithmetic  3.43 us (3%)
    all_to_all x1, blocking collectives, send_all(): lax.all_to_all(jnp.broadcast_to(x[None], (count, *x.shape)), axes, 0, 0,...  15 us
    pallas_call x2, Pallas kernels, partials(): pl.pallas_call(functools.partial(round_kernel, first, keep, scale), out_s...  14.5 us
    ppermute x10, waiting for transfers between devices, shift(): return lax.ppermute(x, axis, pairs)  14.2 us
    ppermute x10, starting transfers between devices, shift(): return lax.ppermute(x, axis, pairs)  12.9 us
    all_to_all x1, starting transfers between devices, send_all(): lax.all_to_all(jnp.broadcast_to(x[None], (count, *x.shape)), axes, 0, 0,...  9.98 us
    all_to_all x1, starting transfers between devices, shards(): lax.all_to_all(slots_ac, ('gy', 'gz'), 0, 0, tiled=True)  8.11 us
    all_to_all x1, waiting for transfers between devices, shards(): lax.all_to_all(slots_ac, ('gy', 'gz'), 0, 0, tiled=True)  7.73 us
    all_to_all x1, starting transfers between devices, shards(): lax.all_to_all(slots_bc, ('gx', 'gz'), 0, 0, tiled=True)  7.61 us
  transfers between devices with their start and end apart: 14, of which 11 were waited for; matrix products, arithmetic and copies ran while one was open for 1% of the time, Pallas kernels for 0%

profile of v3, /device:TPU:1, one launch (start us, length us, event | category | flops | bytes accessed | tf_op | source)
XLA Modules:
  0.0 114.2 jit_solution(3178319100981706200)
XLA Ops:
  2.0 10.0 %all-to-all-start = ((f32[16,4,128]{2,1,0:T(4,128)}), f32[16,4,128]{2,1,0:T(4,128)S(1)}, u32[]{:S(2)}, u32[]{:S(2)}) async-start(f32[16,4,128]{2,1,0:T(4,128)} %broadcast_in_dim.34), calls=%async_computation | async-start | bytes 65536 | tf_op jit(solution)/shard_map/all_to_all | solution.py:205
  12.0 7.4 %all-to-all-done = f32[16,4,128]{2,1,0:T(4,128)S(1)} async-done(((f32[16,4,128]{2,1,0:T(4,128)}), f32[16,4,128]{2,1,0:T(4,128)S(1)}, u32[]{:S(2)}, u32[]{:S(2)}) %all-to-all-start) | async-done | bytes 32800 | tf_op jit(solution)/shard_map/all_to_all | solution.py:205
  20.3 15.0 %all_to_all.20.refs_0_ = f32[32,8,128]{2,1,0:T(8,128)} all-to-all(f32[32,8,128]{2,1,0:T(8,128)S(1)} %broadcast_in_dim.35), channel_id=1, replica_groups=mesh['gx'=8,'gy'=16,'gz'=2] {'gy','gz'}, dimensions={0} | all-to-all | bytes 262144 | tf_op jit(solution)/shard_map/all_to_all | solution.py:205
  35.3 8.4 %partials.2 = (f32[128,128]{1,0:T(8,128)}, f32[128,128]{1,0:T(8,128)}) custom-call(f32[32,8,128]{2,1,0:T(8,128)} %all_to_all.20.refs_0_, f32[64,128]{1,0:T(8,128)} %bitcast.16, f32[8192,128]{1,0:T(8,128)} %bitcast.12), custom_call_target="tpu_custom_call" | custom-call | flops 1073741824 | bytes 4194304 | tf_op jit(solution)/shard_map/partials/pallas_call | solution.py:181
  44.2 1.1 collective-permute-done
  45.3 0.9 broadcast_select_fusion
  46.5 2.4 %collective-permute-start.1 = (f32[128,128]{1,0:T(8,128)S(1)}, f32[128,128]{1,0:T(8,128)S(1)}, u32[]{:S(2)}, u32[]{:S(2)}) collective-permute-start(f32[128,128]{1,0:T(8,128)S(1)} %get-tuple-element.13), channel_id=1, source_target_pairs={{0,224},{32,0},{64,32},{96,64},{128,96},{160,128},{192,160},{224,1... | collective-permute-start | bytes 196616 | tf_op jit(solution)/shard_map/ppermute | solution.py:213
  48.9 1.6 %collective-permute-done.2 = f32[128,128]{1,0:T(8,128)S(1)} collective-permute-done((f32[128,128]{1,0:T(8,128)S(1)}, f32[128,128]{1,0:T(8,128)S(1)}, u32[]{:S(2)}, u32[]{:S(2)}) %collective-permute-start.2) | collective-permute-done | bytes 65568 | tf_op jit(solution)/shard_map/ppermute | solution.py:213
  51.4 3.7 %collective-permute-start.3 = (f32[128,128]{1,0:T(8,128)S(1)}, f32[128,128]{1,0:T(8,128)S(1)}, u32[]{:S(2)}, u32[]{:S(2)}) collective-permute-start(f32[128,128]{1,0:T(8,128)S(1)} %get-tuple-element.11), channel_id=1, source_target_pairs={{0,160},{32,192},{64,224},{96,0},{128,32},{160,64},{192,96},{224,1... | collective-permute-start | bytes 196616 | tf_op jit(solution)/shard_map/ppermute | solution.py:213
  55.2 1.7 %collective-permute-done.4 = f32[128,128]{1,0:T(8,128)S(1)} collective-permute-done((f32[128,128]{1,0:T(8,128)S(1)}, f32[128,128]{1,0:T(8,128)S(1)}, u32[]{:S(2)}, u32[]{:S(2)}) %collective-permute-start.4) | collective-permute-done | bytes 65568 | tf_op jit(solution)/shard_map/ppermute | solution.py:213
  56.8 1.8 %collective-permute-done.3 = f32[128,128]{1,0:T(8,128)S(1)} collective-permute-done((f32[128,128]{1,0:T(8,128)S(1)}, f32[128,128]{1,0:T(8,128)S(1)}, u32[]{:S(2)}, u32[]{:S(2)}) %collective-permute-start.3) | collective-permute-done | bytes 65568 | tf_op jit(solution)/shard_map/ppermute | solution.py:213
  59.7 1.9 %collective-permute-start.6 = (f32[128,128]{1,0:T(8,128)S(1)}, f32[128,128]{1,0:T(8,128)S(1)}, u32[]{:S(2)}, u32[]{:S(2)}) collective-permute-start(f32[128,128]{1,0:T(8,128)S(1)} %pad_maximum_fusion), channel_id=1, source_target_pairs={{0,6},{2,0},{4,2},{6,4},{8,14},{10,8},{12,10},{14,12},{16,22},{18,... | collective-permute-start | bytes 196616 | tf_op jit(solution)/shard_map/ppermute | solution.py:213
  61.6 1.9 %collective-permute-done.7 = f32[128,128]{1,0:T(8,128)S(1)} collective-permute-done((f32[128,128]{1,0:T(8,128)S(1)}, f32[128,128]{1,0:T(8,128)S(1)}, u32[]{:S(2)}, u32[]{:S(2)}) %collective-permute-start.7) | collective-permute-done | bytes 65568 | tf_op jit(solution)/shard_map/ppermute | solution.py:213
  63.5 2.9 %collective-permute-done.5 = f32[128,128]{1,0:T(8,128)S(1)} collective-permute-done((f32[128,128]{1,0:T(8,128)S(1)}, f32[128,128]{1,0:T(8,128)S(1)}, u32[]{:S(2)}, u32[]{:S(2)}) %collective-permute-start.5) | collective-permute-done | bytes 65568 | tf_op jit(solution)/shard_map/ppermute | solution.py:213
  66.4 1.1 collective-permute-start.10
  67.5 1.7 %collective-permute-start.9 = (f32[128,128]{1,0:T(8,128)S(1)}, f32[128,128]{1,0:T(8,128)S(1)}, u32[]{:S(2)}, u32[]{:S(2)}) collective-permute-start(f32[128,128]{1,0:T(8,128)S(1)} %add_add_fusion.1), channel_id=1, source_target_pairs={{0,24},{2,26},{4,28},{6,30},{8,0},{10,2},{12,4},{14,6},{16,8},{18,... | collective-permute-start | bytes 196616 | tf_op jit(solution)/shard_map/ppermute | solution.py:213
  69.2 1.9 %collective-permute-done.10 = f32[128,128]{1,0:T(8,128)S(1)} collective-permute-done((f32[128,128]{1,0:T(8,128)S(1)}, f32[128,128]{1,0:T(8,128)S(1)}, u32[]{:S(2)}, u32[]{:S(2)}) %collective-permute-start.10) | collective-permute-done | bytes 65568 | tf_op jit(solution)/shard_map/ppermute | solution.py:213
  71.1 2.4 %collective-permute-done.8 = f32[128,128]{1,0:T(8,128)S(1)} collective-permute-done((f32[128,128]{1,0:T(8,128)S(1)}, f32[128,128]{1,0:T(8,128)S(1)}, u32[]{:S(2)}, u32[]{:S(2)}) %collective-permute-start.8) | collective-permute-done | bytes 65568 | tf_op jit(solution)/shard_map/ppermute | solution.py:213
  73.5 2.2 %copy-done = f32[128,64,128]{2,1,0:T(8,128)S(1)} copy-done((f32[128,64,128]{2,1,0:T(8,128)S(1)}, f32[128,64,128]{2,1,0:T(8,128)}, u32[]{:S(2)}) %copy-start) | copy-done | bytes 4194328
  75.7 6.1 %partials.3 = (f32[32,8,128]{2,1,0:T(8,128)}, f32[64,128]{1,0:T(8,128)S(1)}) custom-call(f32[128,128]{1,0:T(8,128)S(1)} %add_add_fusion.refs_0_, f32[128,128]{1,0:T(8,128)S(1)} %add_add_fusion.2.refs_1_, f32[8192,128]{1,0:T(8,128)S(1)} %bitcast.13), custom_call_target="tpu_custom_call" | custom-call | flops 1073741824 | bytes 4194304 | tf_op jit(solution)/shard_map/partials/pallas_call | solution.py:181
  81.8 8.1 %all-to-all-start.2 = ((f32[32,8,128]{2,1,0:T(8,128)}), f32[32,8,128]{2,1,0:T(8,128)S(1)}, u32[]{:S(2)}, u32[]{:S(2)}) async-start(f32[32,8,128]{2,1,0:T(8,128)} %get-tuple-element.9), calls=%async_computation.2 | async-start | bytes 262144 | tf_op jit(solution)/shard_map/all_to_all | solution.py:263
  89.9 7.7 %all-to-all-done.2 = f32[32,8,128]{2,1,0:T(8,128)S(1)} async-done(((f32[32,8,128]{2,1,0:T(8,128)}), f32[32,8,128]{2,1,0:T(8,128)S(1)}, u32[]{:S(2)}, u32[]{:S(2)}) %all-to-all-start.2) | async-done | bytes 131104 | tf_op jit(solution)/shard_map/all_to_all | solution.py:263
  98.6 7.6 %all-to-all-start.3 = ((f32[16,4,128]{2,1,0:T(4,128)}), f32[16,4,128]{2,1,0:T(4,128)S(1)}, u32[]{:S(2)}, u32[]{:S(2)}) async-start(f32[16,4,128]{2,1,0:T(4,128)} %bitcast.6), calls=%async_computation.3 | async-start | bytes 65536 | tf_op jit(solution)/shard_map/all_to_all | solution.py:269
  106.7 6.8 %all-to-all-done.3 = f32[16,4,128]{2,1,0:T(4,128)S(1)} async-done(((f32[16,4,128]{2,1,0:T(4,128)}), f32[16,4,128]{2,1,0:T(4,128)S(1)}, u32[]{:S(2)}, u32[]{:S(2)}) %all-to-all-start.3) | async-done | bytes 32800 | tf_op jit(solution)/shard_map/all_to_all | solution.py:269
  (35 shorter events, 7.0 us)
Async XLA Ops:
  2.0 17.4 %all-to-all-start = ((f32[16,4,128]{2,1,0:T(4,128)}), f32[16,4,128]{2,1,0:T(4,128)S(1)}, u32[]{:S(2)}, u32[]{:S(2)}) async-start(f32[16,4,128]{2,1,0:T(4,128)} %broadcast_in_dim.34), calls=%async_computation | async-start | bytes 65536 | tf_op jit(solution)/shard_map/all_to_all | solution.py:205
  19.4 15.9 %copy-start.1 = (f32[16,4,128]{2,1,0:T(4,128)}, f32[16,4,128]{2,1,0:T(4,128)S(1)}, u32[]{:S(2)}) copy-start(f32[16,4,128]{2,1,0:T(4,128)S(1)} %all-to-all-done) | copy-start | bytes 98308
  43.7 1.6 %collective-permute-start = (f32[128,128]{1,0:T(8,128)}, f32[128,128]{1,0:T(8,128)S(1)}, u32[]{:S(2)}, u32[]{:S(2)}) collective-permute-start(f32[128,128]{1,0:T(8,128)} %get-tuple-element.7), channel_id=1, source_target_pairs={{0,1},{1,0},{2,3},{3,2},{4,5},{5,4},{6,7},{7,6},{8,9},{9,8},{10,11... | collective-permute-start | bytes 196616 | tf_op jit(solution)/shard_map/ppermute | solution.py:229
  46.2 4.4 %collective-permute-start.2 = (f32[128,128]{1,0:T(8,128)S(1)}, f32[128,128]{1,0:T(8,128)S(1)}, u32[]{:S(2)}, u32[]{:S(2)}) collective-permute-start(f32[128,128]{1,0:T(8,128)S(1)} %get-tuple-element.13), channel_id=1, source_target_pairs={{0,32},{32,64},{64,96},{96,128},{128,160},{160,192},{192,224},{224... | collective-permute-start | bytes 196616 | tf_op jit(solution)/shard_map/ppermute | solution.py:213
  46.5 4.1 %collective-permute-start.1 = (f32[128,128]{1,0:T(8,128)S(1)}, f32[128,128]{1,0:T(8,128)S(1)}, u32[]{:S(2)}, u32[]{:S(2)}) collective-permute-start(f32[128,128]{1,0:T(8,128)S(1)} %get-tuple-element.13), channel_id=1, source_target_pairs={{0,224},{32,0},{64,32},{96,64},{128,96},{160,128},{192,160},{224,1... | collective-permute-start | bytes 196616 | tf_op jit(solution)/shard_map/ppermute | solution.py:213
  50.6 6.2 %collective-permute-start.4 = (f32[128,128]{1,0:T(8,128)S(1)}, f32[128,128]{1,0:T(8,128)S(1)}, u32[]{:S(2)}, u32[]{:S(2)}) collective-permute-start(f32[128,128]{1,0:T(8,128)S(1)} %get-tuple-element.12), channel_id=1, source_target_pairs={{0,96},{32,128},{64,160},{96,192},{128,224},{160,0},{192,32},{224,... | collective-permute-start | bytes 196616 | tf_op jit(solution)/shard_map/ppermute | solution.py:213
  51.4 7.2 %collective-permute-start.3 = (f32[128,128]{1,0:T(8,128)S(1)}, f32[128,128]{1,0:T(8,128)S(1)}, u32[]{:S(2)}, u32[]{:S(2)}) collective-permute-start(f32[128,128]{1,0:T(8,128)S(1)} %get-tuple-element.11), channel_id=1, source_target_pairs={{0,160},{32,192},{64,224},{96,0},{128,32},{160,64},{192,96},{224,1... | collective-permute-start | bytes 196616 | tf_op jit(solution)/shard_map/ppermute | solution.py:213
  58.8 4.7 %collective-permute-start.7 = (f32[128,128]{1,0:T(8,128)S(1)}, f32[128,128]{1,0:T(8,128)S(1)}, u32[]{:S(2)}, u32[]{:S(2)}) collective-permute-start(f32[128,128]{1,0:T(8,128)S(1)} %pad_maximum_fusion), channel_id=1, source_target_pairs={{0,4},{2,6},{4,0},{6,2},{8,12},{10,14},{12,8},{14,10},{16,20},{18,... | collective-permute-start | bytes 196616 | tf_op jit(solution)/shard_map/ppermute | solution.py:213
  59.7 3.8 %collective-permute-start.6 = (f32[128,128]{1,0:T(8,128)S(1)}, f32[128,128]{1,0:T(8,128)S(1)}, u32[]{:S(2)}, u32[]{:S(2)}) collective-permute-start(f32[128,128]{1,0:T(8,128)S(1)} %pad_maximum_fusion), channel_id=1, source_target_pairs={{0,6},{2,0},{4,2},{6,4},{8,14},{10,8},{12,10},{14,12},{16,22},{18,... | collective-permute-start | bytes 196616 | tf_op jit(solution)/shard_map/ppermute | solution.py:213
  61.6 4.8 %collective-permute-start.5 = (f32[128,128]{1,0:T(8,128)S(1)}, f32[128,128]{1,0:T(8,128)S(1)}, u32[]{:S(2)}, u32[]{:S(2)}) collective-permute-start(f32[128,128]{1,0:T(8,128)S(1)} %pad_maximum_fusion), channel_id=1, source_target_pairs={{0,2},{2,4},{4,6},{6,0},{8,10},{10,12},{12,14},{14,8},{16,18},{18,... | collective-permute-start | bytes 196616 | tf_op jit(solution)/shard_map/ppermute | solution.py:213
  66.4 4.7 %collective-permute-start.10 = (f32[128,128]{1,0:T(8,128)S(1)}, f32[128,128]{1,0:T(8,128)S(1)}, u32[]{:S(2)}, u32[]{:S(2)}) collective-permute-start(f32[128,128]{1,0:T(8,128)S(1)} %add_add_fusion.1), channel_id=1, source_target_pairs={{0,16},{2,18},{4,20},{6,22},{8,24},{10,26},{12,28},{14,30},{16,0},... | collective-permute-start | bytes 196616 | tf_op jit(solution)/shard_map/ppermute | solution.py:213
  67.5 3.6 %collective-permute-start.9 = (f32[128,128]{1,0:T(8,128)S(1)}, f32[128,128]{1,0:T(8,128)S(1)}, u32[]{:S(2)}, u32[]{:S(2)}) collective-permute-start(f32[128,128]{1,0:T(8,128)S(1)} %add_add_fusion.1), channel_id=1, source_target_pairs={{0,24},{2,26},{4,28},{6,30},{8,0},{10,2},{12,4},{14,6},{16,8},{18,... | collective-permute-start | bytes 196616 | tf_op jit(solution)/shard_map/ppermute | solution.py:213
  69.2 4.3 %collective-permute-start.8 = (f32[128,128]{1,0:T(8,128)S(1)}, f32[128,128]{1,0:T(8,128)S(1)}, u32[]{:S(2)}, u32[]{:S(2)}) collective-permute-start(f32[128,128]{1,0:T(8,128)S(1)} %add_add_fusion.1), channel_id=1, source_target_pairs={{0,8},{2,10},{4,12},{6,14},{8,16},{10,18},{12,20},{14,22},{16,24},... | collective-permute-start | bytes 196616 | tf_op jit(solution)/shard_map/ppermute | solution.py:213
  73.5 2.2 %copy-start = (f32[128,64,128]{2,1,0:T(8,128)S(1)}, f32[128,64,128]{2,1,0:T(8,128)}, u32[]{:S(2)}) copy-start(f32[128,64,128]{2,1,0:T(8,128)} %param.4) | copy-start | bytes 12582916
  81.8 15.9 %all-to-all-start.2 = ((f32[32,8,128]{2,1,0:T(8,128)}), f32[32,8,128]{2,1,0:T(8,128)S(1)}, u32[]{:S(2)}, u32[]{:S(2)}) async-start(f32[32,8,128]{2,1,0:T(8,128)} %get-tuple-element.9), calls=%async_computation.2 | async-start | bytes 262144 | tf_op jit(solution)/shard_map/all_to_all | solution.py:263
  98.6 15.0 %all-to-all-start.3 = ((f32[16,4,128]{2,1,0:T(4,128)}), f32[16,4,128]{2,1,0:T(4,128)S(1)}, u32[]{:S(2)}, u32[]{:S(2)}) async-start(f32[16,4,128]{2,1,0:T(4,128)} %bitcast.6), calls=%async_computation.3 | async-start | bytes 65536 | tf_op jit(solution)/shard_map/all_to_all | solution.py:269
  113.6 0.6 copy-start.2

commit v4 on v3

--- a/solution.py
+++ b/solution.py
@@ -15,7 +15,6 @@
 VMEM = pl.BlockSpec(memory_space=pltpu.VMEM)
 HBM = pl.BlockSpec(memory_space=pltpu.HBM)
 CHUNK = 512
-UNROLL = 2
 
 
 def split(x):
@@ -155,7 +154,7 @@
         chunks,
         step,
         (jnp.zeros((count_j, width), F32), jnp.zeros((width, 2 * count_k), F32)),
-        unroll=UNROLL,
+        unroll=True,
     )
     moment_c = moment_c[:, :count_k] + moment_c[:, count_k:]
     moment_c = moment_c[:rank] + moment_c[rank:]
@@ -178,6 +177,9 @@
     tall = count_i * count_j
     fetched = [pltpu.VMEM((tall, count_k), F32), pltpu.SemaphoreType.DMA((tall // CHUNK,))]
     fetched = fetched if first else []
+    tensor = tensor.reshape(tall, count_k)
+    if first:
+        tensor = pltpu.with_memory_space_constraint(tensor, pltpu.HBM)
     return pl.pallas_call(
         functools.partial(round_kernel, first, keep, scale),
         out_shape=tuple(jax.ShapeDtypeStruct(s, F32) for s in out_shapes),
@@ -192,17 +194,18 @@
             pltpu.VMEM((count_i, width), F32),
             *fetched,
         ],
-        compiler_params=pltpu.CompilerParams(vmem_limit_bytes=(60 if first else 24) << 20),
+        compiler_params=pltpu.CompilerParams(vmem_limit_bytes=24 << 20),
         cost_estimate=pl.CostEstimate(flops=1 << 30, bytes_accessed=4 << 20, transcendentals=0),
         name="partials",
-    )(*small, tensor.reshape(tall, count_k))
-
-
-def send_all(x, axes):
+    )(*small, tensor)
+
+
+def send_all(left, right, axes):
     count = 1
     for name in axes:
         count *= lax.axis_size(name)
-    return lax.all_to_all(jnp.broadcast_to(x[None], (count, *x.shape)), axes, 0, 0, tiled=True)
+    both = jnp.concatenate([left, right], axis=1)
+    return lax.all_to_all(jnp.broadcast_to(both[None], (count, *both.shape)), axes, 0, 0, tiled=True)
 
 
 def shift(x, axis, stride, count, by):
@@ -243,11 +246,11 @@
     wide = 2 * rank
 
     padded_c = jnp.pad(factor_c, ((0, own - 1), (0, 0)))
-    along_x = send_all(jnp.concatenate([factor_b, padded_c], axis=1), ("gx", "gz"))
+    along_x = send_all(factor_b, padded_c, ("gx", "gz"))
     rows_c = along_x.reshape(count_x, count_z, own, wide)[:, :, 0, rank:]
     rows_c = jnp.where(core == 0, rows_c[:, 0], rows_c[:, 1])
-    padded_a = jnp.pad(factor_a, ((0, count_x - own), (0, 0)))
-    along_y = send_all(jnp.concatenate([padded_a, rows_c], axis=1), ("gy", "gz"))
+    padded_a = lax.optimization_barrier(jnp.pad(factor_a, ((0, count_x - own), (0, 0))))
+    along_y = send_all(padded_a, rows_c, ("gy", "gz"))
 
     keep = tuple(1.0 / n for n in copies)
     scale = tuple(-STEP_SIZE / n for n in whole)
@@ -266,8 +269,8 @@
     slots_c = jnp.pad(slots_c, ((0, 0), (0, 0), (0, own - 1), (0, 0)))
     slots_b = b.reshape(count_x, count_z, own, wide)[..., :rank]
     slots_bc = jnp.concatenate([slots_b, slots_c], axis=3).reshape(-1, own, wide)
-    bc = jnp.sum(lax.all_to_all(slots_bc, ("gx", "gz"), 0, 0, tiled=True), axis=0)
-    return ac[:own, :rank], bc[:, :rank], bc[:1, rank:]
+    bc = lax.all_to_all(slots_bc, ("gx", "gz"), 0, 0, tiled=True)
+    return ac[:own, :rank], jnp.sum(bc[:, :, :rank], axis=0), jnp.sum(bc[:, :1, rank:], axis=0)
 
 
 def solution(mesh):

time: 115 us -> 107 us (0.930)
  Pallas kernels: 14.5 us -> 9.85 us
  local copies, waits for them, and re-layouts: 4.14 us -> 2.05 us
    pallas_call x2, Pallas kernels: 14.5 us -> 9.85 us  [partials(): pl.pallas_call(functools.partial(round_kernel, first, keep, scale), out_s...]
    unnamed x6 -> x2, local copies, waits for them, and re-layouts: 2.19 us -> 0.01 us
    reduce_sum x1 -> x2, other arithmetic: 0.03 us -> 1.21 us  [the longest x1 0.61 us: shards(): jnp.sum(bc[:, :1, rank:], axis=0)]
where the time goes in v4:
time: 107 us; the launch traced here: 106 us
  starting transfers between devices  39.2 us (37%)
  waiting for transfers between devices  36.3 us (34%)
  blocking collectives  15.2 us (14%)
  Pallas kernels  9.85 us (9%)
  other arithmetic  3.04 us (3%)
  local copies, waits for them, and re-layouts  2.05 us (2%)
    all_to_all x1, blocking collectives, send_all(): lax.all_to_all(jnp.broadcast_to(both[None], (count, *both.shape)), axes,...  15.2 us
    ppermute x10, waiting for transfers between devices, shift(): return lax.ppermute(x, axis, pairs)  14.2 us
    ppermute x10, starting transfers between devices, shift(): return lax.ppermute(x, axis, pairs)  13 us
    all_to_all x1, starting transfers between devices, send_all(): lax.all_to_all(jnp.broadcast_to(both[None], (count, *both.shape)), axes,...  9.98 us
    pallas_call x2, Pallas kernels, partials(): pl.pallas_call(functools.partial(round_kernel, first, keep, scale), out_s...  9.85 us
    all_to_all x1, starting transfers between devices, shards(): lax.all_to_all(slots_ac, ('gy', 'gz'), 0, 0, tiled=True)  8.1 us
    all_to_all x1, waiting for transfers between devices, shards(): lax.all_to_all(slots_ac, ('gy', 'gz'), 0, 0, tiled=True)  7.73 us
    all_to_all x1, starting transfers between devices, shards(): bc = lax.all_to_all(slots_bc, ('gx', 'gz'), 0, 0, tiled=True)  7.61 us
  transfers between devices with their start and end apart: 14, of which 11 were waited for; matrix products, arithmetic and copies ran while one was open for 1% of the time, Pallas kernels for 0%

profile of v4, /device:TPU:1, one launch (start us, length us, event | category | flops | bytes accessed | tf_op | source)
XLA Modules:
  0.0 106.3 jit_solution(6466727106677744032)
XLA Ops:
  2.0 10.0 %all-to-all-start = ((f32[16,4,128]{2,1,0:T(4,128)}), f32[16,4,128]{2,1,0:T(4,128)S(1)}, u32[]{:S(2)}, u32[]{:S(2)}) async-start(f32[16,4,128]{2,1,0:T(4,128)} %broadcast_in_dim.34), calls=%async_computation | async-start | bytes 65536 | tf_op jit(solution)/shard_map/all_to_all | solution.py:208
  12.7 6.7 %all-to-all-done = f32[16,4,128]{2,1,0:T(4,128)S(1)} async-done(((f32[16,4,128]{2,1,0:T(4,128)}), f32[16,4,128]{2,1,0:T(4,128)S(1)}, u32[]{:S(2)}, u32[]{:S(2)}) %all-to-all-start) | async-done | bytes 32800 | tf_op jit(solution)/shard_map/all_to_all | solution.py:208
  19.6 15.2 %all_to_all.20.refs_0_ = f32[32,8,128]{2,1,0:T(8,128)S(1)} all-to-all(f32[32,8,128]{2,1,0:T(8,128)S(1)} %broadcast_in_dim.35), channel_id=1, replica_groups=mesh['gx'=8,'gy'=16,'gz'=2] {'gy','gz'}, dimensions={0} | all-to-all | bytes 262144 | tf_op jit(solution)/shard_map/all_to_all | solution.py:208
  34.7 6.1 %partials.2 = (f32[128,128]{1,0:T(8,128)S(1)}, f32[128,128]{1,0:T(8,128)S(1)}) custom-call(f32[32,8,128]{2,1,0:T(8,128)S(1)} %all_to_all.20.refs_0_, f32[64,128]{1,0:T(8,128)S(1)} %bitcast.15, f32[8192,128]{1,0:T(8,128)} %bitcast.12), custom_call_target="tpu_custom_call" | custom-call | flops 1073741824 | bytes 4194304 | tf_op jit(solution)/shard_map/partials/pallas_call | solution.py:183
  41.4 0.9 collective-permute-done
  42.6 2.4 %collective-permute-start.1 = (f32[128,128]{1,0:T(8,128)S(1)}, f32[128,128]{1,0:T(8,128)S(1)}, u32[]{:S(2)}, u32[]{:S(2)}) collective-permute-start(f32[128,128]{1,0:T(8,128)S(1)} %get-tuple-element.13), channel_id=1, source_target_pairs={{0,224},{32,0},{64,32},{96,64},{128,96},{160,128},{192,160},{224,1... | collective-permute-start | bytes 196616 | tf_op jit(solution)/shard_map/ppermute | solution.py:216
  45.1 1.6 %collective-permute-done.2 = f32[128,128]{1,0:T(8,128)S(1)} collective-permute-done((f32[128,128]{1,0:T(8,128)S(1)}, f32[128,128]{1,0:T(8,128)S(1)}, u32[]{:S(2)}, u32[]{:S(2)}) %collective-permute-start.2) | collective-permute-done | bytes 65568 | tf_op jit(solution)/shard_map/ppermute | solution.py:216
  46.7 0.8 collective-permute-start.4
  47.6 3.7 %collective-permute-start.3 = (f32[128,128]{1,0:T(8,128)S(1)}, f32[128,128]{1,0:T(8,128)S(1)}, u32[]{:S(2)}, u32[]{:S(2)}) collective-permute-start(f32[128,128]{1,0:T(8,128)S(1)} %get-tuple-element.11), channel_id=1, source_target_pairs={{0,160},{32,192},{64,224},{96,0},{128,32},{160,64},{192,96},{224,1... | collective-permute-start | bytes 196616 | tf_op jit(solution)/shard_map/ppermute | solution.py:216
  51.3 1.7 %collective-permute-done.4 = f32[128,128]{1,0:T(8,128)S(1)} collective-permute-done((f32[128,128]{1,0:T(8,128)S(1)}, f32[128,128]{1,0:T(8,128)S(1)}, u32[]{:S(2)}, u32[]{:S(2)}) %collective-permute-start.4) | collective-permute-done | bytes 65568 | tf_op jit(solution)/shard_map/ppermute | solution.py:216
  53.0 1.8 %collective-permute-done.3 = f32[128,128]{1,0:T(8,128)S(1)} collective-permute-done((f32[128,128]{1,0:T(8,128)S(1)}, f32[128,128]{1,0:T(8,128)S(1)}, u32[]{:S(2)}, u32[]{:S(2)}) %collective-permute-start.3) | collective-permute-done | bytes 65568 | tf_op jit(solution)/shard_map/ppermute | solution.py:216
  54.8 1.0 collective-permute-start.7
  55.8 1.8 %collective-permute-start.6 = (f32[128,128]{1,0:T(8,128)S(1)}, f32[128,128]{1,0:T(8,128)S(1)}, u32[]{:S(2)}, u32[]{:S(2)}) collective-permute-start(f32[128,128]{1,0:T(8,128)S(1)} %pad_maximum_fusion), channel_id=1, source_target_pairs={{0,6},{2,0},{4,2},{6,4},{8,14},{10,8},{12,10},{14,12},{16,22},{18,... | collective-permute-start | bytes 196616 | tf_op jit(solution)/shard_map/ppermute | solution.py:216
  57.6 1.9 %collective-permute-done.7 = f32[128,128]{1,0:T(8,128)S(1)} collective-permute-done((f32[128,128]{1,0:T(8,128)S(1)}, f32[128,128]{1,0:T(8,128)S(1)}, u32[]{:S(2)}, u32[]{:S(2)}) %collective-permute-start.7) | collective-permute-done | bytes 65568 | tf_op jit(solution)/shard_map/ppermute | solution.py:216
  59.5 2.9 %collective-permute-done.5 = f32[128,128]{1,0:T(8,128)S(1)} collective-permute-done((f32[128,128]{1,0:T(8,128)S(1)}, f32[128,128]{1,0:T(8,128)S(1)}, u32[]{:S(2)}, u32[]{:S(2)}) %collective-permute-start.5) | collective-permute-done | bytes 65568 | tf_op jit(solution)/shard_map/ppermute | solution.py:216
  62.4 1.2 %collective-permute-start.10 = (f32[128,128]{1,0:T(8,128)S(1)}, f32[128,128]{1,0:T(8,128)S(1)}, u32[]{:S(2)}, u32[]{:S(2)}) collective-permute-start(f32[128,128]{1,0:T(8,128)S(1)} %add_add_fusion.1), channel_id=1, source_target_pairs={{0,16},{2,18},{4,20},{6,22},{8,24},{10,26},{12,28},{14,30},{16,0},... | collective-permute-start | bytes 196616 | tf_op jit(solution)/shard_map/ppermute | solution.py:216
  63.6 1.7 %collective-permute-start.9 = (f32[128,128]{1,0:T(8,128)S(1)}, f32[128,128]{1,0:T(8,128)S(1)}, u32[]{:S(2)}, u32[]{:S(2)}) collective-permute-start(f32[128,128]{1,0:T(8,128)S(1)} %add_add_fusion.1), channel_id=1, source_target_pairs={{0,24},{2,26},{4,28},{6,30},{8,0},{10,2},{12,4},{14,6},{16,8},{18,... | collective-permute-start | bytes 196616 | tf_op jit(solution)/shard_map/ppermute | solution.py:216
  65.3 1.8 %collective-permute-done.10 = f32[128,128]{1,0:T(8,128)S(1)} collective-permute-done((f32[128,128]{1,0:T(8,128)S(1)}, f32[128,128]{1,0:T(8,128)S(1)}, u32[]{:S(2)}, u32[]{:S(2)}) %collective-permute-start.10) | collective-permute-done | bytes 65568 | tf_op jit(solution)/shard_map/ppermute | solution.py:216
  67.1 2.5 %collective-permute-done.8 = f32[128,128]{1,0:T(8,128)S(1)} collective-permute-done((f32[128,128]{1,0:T(8,128)S(1)}, f32[128,128]{1,0:T(8,128)S(1)}, u32[]{:S(2)}, u32[]{:S(2)}) %collective-permute-start.8) | collective-permute-done | bytes 65568 | tf_op jit(solution)/shard_map/ppermute | solution.py:216
  69.7 3.7 %partials.3 = (f32[32,8,128]{2,1,0:T(8,128)}, f32[64,128]{1,0:T(8,128)S(1)}) custom-call(f32[128,128]{1,0:T(8,128)S(1)} %add_add_fusion.refs_0_, f32[128,128]{1,0:T(8,128)S(1)} %add_add_fusion.2.refs_1_, f32[8192,128]{1,0:T(8,128)S(1)} %bitcast.13), custom_call_target="tpu_custom_call" | custom-call | flops 1073741824 | bytes 4194304 | tf_op jit(solution)/shard_map/partials/pallas_call | solution.py:183
  73.4 8.1 %all-to-all-start.2 = ((f32[32,8,128]{2,1,0:T(8,128)}), f32[32,8,128]{2,1,0:T(8,128)S(1)}, u32[]{:S(2)}, u32[]{:S(2)}) async-start(f32[32,8,128]{2,1,0:T(8,128)} %get-tuple-element.9), calls=%async_computation.2 | async-start | bytes 262144 | tf_op jit(solution)/shard_map/all_to_all | solution.py:266
  81.5 7.7 %all-to-all-done.2 = f32[32,8,128]{2,1,0:T(8,128)S(1)} async-done(((f32[32,8,128]{2,1,0:T(8,128)}), f32[32,8,128]{2,1,0:T(8,128)S(1)}, u32[]{:S(2)}, u32[]{:S(2)}) %all-to-all-start.2) | async-done | bytes 131104 | tf_op jit(solution)/shard_map/all_to_all | solution.py:266
  90.1 7.6 %all-to-all-start.3 = ((f32[16,4,128]{2,1,0:T(4,128)}), f32[16,4,128]{2,1,0:T(4,128)S(1)}, u32[]{:S(2)}, u32[]{:S(2)}) async-start(f32[16,4,128]{2,1,0:T(4,128)} %bitcast.6), calls=%async_computation.3 | async-start | bytes 65536 | tf_op jit(solution)/shard_map/all_to_all | solution.py:272
  98.3 6.8 %all-to-all-done.3 = f32[16,4,128]{2,1,0:T(4,128)S(1)} async-done(((f32[16,4,128]{2,1,0:T(4,128)}), f32[16,4,128]{2,1,0:T(4,128)S(1)}, u32[]{:S(2)}, u32[]{:S(2)}) %all-to-all-start.3) | async-done | bytes 32800 | tf_op jit(solution)/shard_map/all_to_all | solution.py:272
  (32 shorter events, 5.9 us)
Async XLA Ops:
  2.0 17.4 %all-to-all-start = ((f32[16,4,128]{2,1,0:T(4,128)}), f32[16,4,128]{2,1,0:T(4,128)S(1)}, u32[]{:S(2)}, u32[]{:S(2)}) async-start(f32[16,4,128]{2,1,0:T(4,128)} %broadcast_in_dim.34), calls=%async_computation | async-start | bytes 65536 | tf_op jit(solution)/shard_map/all_to_all | solution.py:208
  19.4 50.3 %copy-start = (f32[128,64,128]{2,1,0:T(8,128)S(1)}, f32[128,64,128]{2,1,0:T(8,128)}, u32[]{:S(2)}) copy-start(f32[128,64,128]{2,1,0:T(8,128)} %param.4) | copy-start | bytes 12582916
  40.9 1.4 %collective-permute-start = (f32[128,128]{1,0:T(8,128)S(1)}, f32[128,128]{1,0:T(8,128)S(1)}, u32[]{:S(2)}, u32[]{:S(2)}) collective-permute-start(f32[128,128]{1,0:T(8,128)S(1)} %get-tuple-element.7), channel_id=1, source_target_pairs={{0,1},{1,0},{2,3},{3,2},{4,5},{5,4},{6,7},{7,6},{8,9},{9,8},{10,11... | collective-permute-start | bytes 196616 | tf_op jit(solution)/shard_map/ppermute | solution.py:232
  42.3 4.4 %collective-permute-start.2 = (f32[128,128]{1,0:T(8,128)S(1)}, f32[128,128]{1,0:T(8,128)S(1)}, u32[]{:S(2)}, u32[]{:S(2)}) collective-permute-start(f32[128,128]{1,0:T(8,128)S(1)} %get-tuple-element.13), channel_id=1, source_target_pairs={{0,32},{32,64},{64,96},{96,128},{128,160},{160,192},{192,224},{224... | collective-permute-start | bytes 196616 | tf_op jit(solution)/shard_map/ppermute | solution.py:216
  42.6 4.1 %collective-permute-start.1 = (f32[128,128]{1,0:T(8,128)S(1)}, f32[128,128]{1,0:T(8,128)S(1)}, u32[]{:S(2)}, u32[]{:S(2)}) collective-permute-start(f32[128,128]{1,0:T(8,128)S(1)} %get-tuple-element.13), channel_id=1, source_target_pairs={{0,224},{32,0},{64,32},{96,64},{128,96},{160,128},{192,160},{224,1... | collective-permute-start | bytes 196616 | tf_op jit(solution)/shard_map/ppermute | solution.py:216
  46.7 6.2 %collective-permute-start.4 = (f32[128,128]{1,0:T(8,128)S(1)}, f32[128,128]{1,0:T(8,128)S(1)}, u32[]{:S(2)}, u32[]{:S(2)}) collective-permute-start(f32[128,128]{1,0:T(8,128)S(1)} %get-tuple-element.12), channel_id=1, source_target_pairs={{0,96},{32,128},{64,160},{96,192},{128,224},{160,0},{192,32},{224,... | collective-permute-start | bytes 196616 | tf_op jit(solution)/shard_map/ppermute | solution.py:216
  47.6 7.1 %collective-permute-start.3 = (f32[128,128]{1,0:T(8,128)S(1)}, f32[128,128]{1,0:T(8,128)S(1)}, u32[]{:S(2)}, u32[]{:S(2)}) collective-permute-start(f32[128,128]{1,0:T(8,128)S(1)} %get-tuple-element.11), channel_id=1, source_target_pairs={{0,160},{32,192},{64,224},{96,0},{128,32},{160,64},{192,96},{224,1... | collective-permute-start | bytes 196616 | tf_op jit(solution)/shard_map/ppermute | solution.py:216
  54.8 4.7 %collective-permute-start.7 = (f32[128,128]{1,0:T(8,128)S(1)}, f32[128,128]{1,0:T(8,128)S(1)}, u32[]{:S(2)}, u32[]{:S(2)}) collective-permute-start(f32[128,128]{1,0:T(8,128)S(1)} %pad_maximum_fusion), channel_id=1, source_target_pairs={{0,4},{2,6},{4,0},{6,2},{8,12},{10,14},{12,8},{14,10},{16,20},{18,... | collective-permute-start | bytes 196616 | tf_op jit(solution)/shard_map/ppermute | solution.py:216
  55.8 3.7 %collective-permute-start.6 = (f32[128,128]{1,0:T(8,128)S(1)}, f32[128,128]{1,0:T(8,128)S(1)}, u32[]{:S(2)}, u32[]{:S(2)}) collective-permute-start(f32[128,128]{1,0:T(8,128)S(1)} %pad_maximum_fusion), channel_id=1, source_target_pairs={{0,6},{2,0},{4,2},{6,4},{8,14},{10,8},{12,10},{14,12},{16,22},{18,... | collective-permute-start | bytes 196616 | tf_op jit(solution)/shard_map/ppermute | solution.py:216
  57.6 4.8 %collective-permute-start.5 = (f32[128,128]{1,0:T(8,128)S(1)}, f32[128,128]{1,0:T(8,128)S(1)}, u32[]{:S(2)}, u32[]{:S(2)}) collective-permute-start(f32[128,128]{1,0:T(8,128)S(1)} %pad_maximum_fusion), channel_id=1, source_target_pairs={{0,2},{2,4},{4,6},{6,0},{8,10},{10,12},{12,14},{14,8},{16,18},{18,... | collective-permute-start | bytes 196616 | tf_op jit(solution)/shard_map/ppermute | solution.py:216
  62.4 4.7 %collective-permute-start.10 = (f32[128,128]{1,0:T(8,128)S(1)}, f32[128,128]{1,0:T(8,128)S(1)}, u32[]{:S(2)}, u32[]{:S(2)}) collective-permute-start(f32[128,128]{1,0:T(8,128)S(1)} %add_add_fusion.1), channel_id=1, source_target_pairs={{0,16},{2,18},{4,20},{6,22},{8,24},{10,26},{12,28},{14,30},{16,0},... | collective-permute-start | bytes 196616 | tf_op jit(solution)/shard_map/ppermute | solution.py:216
  63.6 3.5 %collective-permute-start.9 = (f32[128,128]{1,0:T(8,128)S(1)}, f32[128,128]{1,0:T(8,128)S(1)}, u32[]{:S(2)}, u32[]{:S(2)}) collective-permute-start(f32[128,128]{1,0:T(8,128)S(1)} %add_add_fusion.1), channel_id=1, source_target_pairs={{0,24},{2,26},{4,28},{6,30},{8,0},{10,2},{12,4},{14,6},{16,8},{18,... | collective-permute-start | bytes 196616 | tf_op jit(solution)/shard_map/ppermute | solution.py:216
  65.3 4.3 %collective-permute-start.8 = (f32[128,128]{1,0:T(8,128)S(1)}, f32[128,128]{1,0:T(8,128)S(1)}, u32[]{:S(2)}, u32[]{:S(2)}) collective-permute-start(f32[128,128]{1,0:T(8,128)S(1)} %add_add_fusion.1), channel_id=1, source_target_pairs={{0,8},{2,10},{4,12},{6,14},{8,16},{10,18},{12,20},{14,22},{16,24},... | collective-permute-start | bytes 196616 | tf_op jit(solution)/shard_map/ppermute | solution.py:216
  73.4 15.8 %all-to-all-start.2 = ((f32[32,8,128]{2,1,0:T(8,128)}), f32[32,8,128]{2,1,0:T(8,128)S(1)}, u32[]{:S(2)}, u32[]{:S(2)}) async-start(f32[32,8,128]{2,1,0:T(8,128)} %get-tuple-element.9), calls=%async_computation.2 | async-start | bytes 262144 | tf_op jit(solution)/shard_map/all_to_all | solution.py:266
  90.1 15.0 %all-to-all-start.3 = ((f32[16,4,128]{2,1,0:T(4,128)}), f32[16,4,128]{2,1,0:T(4,128)S(1)}, u32[]{:S(2)}, u32[]{:S(2)}) async-start(f32[16,4,128]{2,1,0:T(4,128)} %bitcast.6), calls=%async_computation.3 | async-start | bytes 65536 | tf_op jit(solution)/shard_map/all_to_all | solution.py:272

commit v5 on v4

--- a/solution.py
+++ b/solution.py
@@ -88,9 +88,9 @@
 
 def round_kernel(first, keep, scale, *refs):
     small, t_ref, outs = refs[:2], refs[2], refs[3:5]
-    a2_ref, b2_ref, c2_ref, wc_ref, at_ref, ma_ref = refs[5:11]
     if first:
-        t_hbm, (t_ref, sems) = t_ref, refs[11:]
+        t_hbm, t_ref, sems = t_ref, refs[5], refs[-1]
+    a2_ref, b2_ref, c2_ref, wc_ref, at_ref, ma_ref = refs[6:12] if first else refs[5:]
     count_i, count_j, count_k = a2_ref.shape[0], b2_ref.shape[0], c2_ref.shape[0]
     width = a2_ref.shape[1]
     rank = width // 2
@@ -171,20 +171,18 @@
     (pack_first if first else pack_second)(a, b, c2_ref, *outs)
 
 
-def partials(first, keep, scale, small, tensor, out_shapes):
-    count_i, count_j, count_k = tensor.shape
+def partials(first, keep, scale, small, tensor, sizes, out_shapes):
+    count_i, count_j, count_k = sizes
     width = small[0].shape[-1]
     tall = count_i * count_j
-    fetched = [pltpu.VMEM((tall, count_k), F32), pltpu.SemaphoreType.DMA((tall // CHUNK,))]
-    fetched = fetched if first else []
-    tensor = tensor.reshape(tall, count_k)
     if first:
         tensor = pltpu.with_memory_space_constraint(tensor, pltpu.HBM)
+        out_shapes += ((tall, count_k),)
     return pl.pallas_call(
         functools.partial(round_kernel, first, keep, scale),
         out_shape=tuple(jax.ShapeDtypeStruct(s, F32) for s in out_shapes),
         in_specs=[VMEM, VMEM, HBM if first else VMEM],
-        out_specs=(VMEM, VMEM),
+        out_specs=(VMEM,) * len(out_shapes),
         scratch_shapes=[
             pltpu.VMEM((count_i, width), F32),
             pltpu.VMEM((count_j, width), F32),
@@ -192,20 +190,62 @@
             pltpu.VMEM((2 * count_k, width), BF16),
             pltpu.VMEM((width // 2, count_i), F32),
             pltpu.VMEM((count_i, width), F32),
-            *fetched,
-        ],
+        ]
+        + [pltpu.SemaphoreType.DMA((tall // CHUNK,))] * first,
         compiler_params=pltpu.CompilerParams(vmem_limit_bytes=24 << 20),
         cost_estimate=pl.CostEstimate(flops=1 << 30, bytes_accessed=4 << 20, transcendentals=0),
         name="partials",
     )(*small, tensor)
 
 
-def send_all(left, right, axes):
-    count = 1
-    for name in axes:
-        count *= lax.axis_size(name)
-    both = jnp.concatenate([left, right], axis=1)
-    return lax.all_to_all(jnp.broadcast_to(both[None], (count, *both.shape)), axes, 0, 0, tiled=True)
+def first_kernel(a_hbm, b_hbm, c_hbm, slots_ref, a_out_ref, a_ref, b_ref, c_ref, sems):
+    own, rank = a_ref.shape
+    pairs = ((a_hbm, a_ref), (b_hbm, b_ref), (c_hbm, c_ref))
+    copies = [pltpu.make_async_copy(x, y, sems.at[n]) for n, (x, y) in enumerate(pairs)]
+    for copy in copies:
+        copy.start()
+    a_out_ref[...] = jnp.zeros(a_out_ref.shape, F32)
+    for copy in copies:
+        copy.wait()
+    a_out_ref[:own, :rank] = a_ref[...]
+    slot = jnp.concatenate([b_ref[...], jnp.broadcast_to(c_ref[...], (own, rank))], axis=1)
+    for n in range(slots_ref.shape[0]):
+        slots_ref[n, :, :] = slot
+
+
+def first_slots(a, b, c, count, tall):
+    own, rank = a.shape
+    factors = [pltpu.with_memory_space_constraint(x, pltpu.HBM) for x in (a, b, c)]
+    return pl.pallas_call(
+        first_kernel,
+        out_shape=(
+            jax.ShapeDtypeStruct((count, own, 2 * rank), F32),
+            jax.ShapeDtypeStruct((tall, 2 * rank), F32),
+        ),
+        in_specs=[HBM] * 3,
+        out_specs=(VMEM, VMEM),
+        scratch_shapes=[pltpu.VMEM(x.shape, F32) for x in (a, b, c)]
+        + [pltpu.SemaphoreType.DMA((3,))],
+        compiler_params=pltpu.CompilerParams(vmem_limit_bytes=4 << 20),
+        name="first_slots",
+    )(*factors)
+
+
+def last_kernel(ac_ref, bc_ref, a_ref, b_ref, c_ref):
+    own, rank = a_ref.shape
+    bc = jnp.sum(bc_ref[...], axis=0)
+    a_ref[...] = ac_ref[:own, :rank]
+    b_ref[...] = bc[:, :rank]
+    c_ref[...] = bc[:1, rank:]
+
+
+def last_sums(ac, bc, own, rank):
+    return pl.pallas_call(
+        last_kernel,
+        out_shape=tuple(jax.ShapeDtypeStruct((n, rank), F32) for n in (own, own, 1)),
+        compiler_params=pltpu.CompilerParams(vmem_limit_bytes=4 << 20),
+        name="last_sums",
+    )(ac, bc)
 
 
 def shift(x, axis, stride, count, by):
@@ -245,24 +285,28 @@
     own, rank = factor_a.shape
     wide = 2 * rank
 
-    padded_c = jnp.pad(factor_c, ((0, own - 1), (0, 0)))
-    along_x = send_all(factor_b, padded_c, ("gx", "gz"))
-    rows_c = along_x.reshape(count_x, count_z, own, wide)[:, :, 0, rank:]
+    slots, rows_a = first_slots(factor_a, factor_b, factor_c, count_x * count_z, count_x)
+    along_x = lax.all_to_all(slots, ("gx", "gz"), 0, 0, tiled=True)
+    rows_c = along_x.reshape(count_x, count_z, own, wide)[:, :, 0]
     rows_c = jnp.where(core == 0, rows_c[:, 0], rows_c[:, 1])
-    padded_a = lax.optimization_barrier(jnp.pad(factor_a, ((0, count_x - own), (0, 0))))
-    along_y = send_all(padded_a, rows_c, ("gy", "gz"))
+    slot = jnp.where(lower_half(rows_c.shape), rows_a, rows_c)
+    slots = jnp.broadcast_to(slot[None], (count_y * count_z, count_x, wide))
+    along_y = lax.all_to_all(slots, ("gy", "gz"), 0, 0, tiled=True)
 
     keep = tuple(1.0 / n for n in copies)
     scale = tuple(-STEP_SIZE / n for n in whole)
     small = (along_y, along_x.reshape(count_j, wide))
-    ab, c = partials(True, keep, scale, small, tensor, ((count_i, wide), (count_k, wide)))
+    sizes = tensor.shape
+    tensor = tensor.reshape(count_i * count_j, count_k)
+    shapes = ((count_i, wide), (count_k, wide))
+    ab, c, tensor = partials(True, keep, scale, small, tensor, sizes, shapes)
     ab = ab + swap(ab)
     cb = ring8(jnp.where(lower_half(c.shape), c, ab))
     ac = ring4(ring4(jnp.concatenate([ab[:, :rank], cb[:, :rank]], axis=1), 1), 4)
 
     scale = tuple(1.0 / n for n in whole)
     shapes = ((count_y * count_z, 2 * own, wide), (count_j, wide))
-    slots_ac, b = partials(False, (0.0,) * 3, scale, (ac, cb), tensor, shapes)
+    slots_ac, b = partials(False, (0.0,) * 3, scale, (ac, cb), tensor, sizes, shapes)
     ac = jnp.sum(lax.all_to_all(slots_ac, ("gy", "gz"), 0, 0, tiled=True), axis=0)
     mine = (jnp.arange(count_z) == core)[None, :, None, None]
     slots_c = jnp.where(mine, ac[:, None, None, rank:], 0.0)
@@ -270,7 +314,7 @@
     slots_b = b.reshape(count_x, count_z, own, wide)[..., :rank]
     slots_bc = jnp.concatenate([slots_b, slots_c], axis=3).reshape(-1, own, wide)
     bc = lax.all_to_all(slots_bc, ("gx", "gz"), 0, 0, tiled=True)
-    return ac[:own, :rank], jnp.sum(bc[:, :, :rank], axis=0), jnp.sum(bc[:, :1, rank:], axis=0)
+    return last_sums(ac, bc, own, rank)
 
 
 def solution(mesh):

time: 107 us -> 105 us (0.981)
  blocking collectives: 15.2 us -> 29.7 us
  starting transfers between devices: 39.2 us -> 31.5 us
  waiting for transfers between devices: 36.3 us -> 30.3 us
  other arithmetic: 3.04 us -> 0.37 us
  Pallas kernels: 9.85 us -> 11.8 us
  local copies, waits for them, and re-layouts: 2.05 us -> 0.1 us
    all_to_all x1 -> x2, blocking collectives: 15.2 us -> 29.7 us  [the longest x1 14.9 us: shards(): along_y = lax.all_to_all(slots, ('gy', 'gz'), 0, 0, tiled=True)]
    all_to_all x2 -> x1, starting transfers between devices: 17.6 us -> 9.99 us  [shards(): along_x = lax.all_to_all(slots, ('gx', 'gz'), 0, 0, tiled=True)]
    all_to_all x2 -> x1, waiting for transfers between devices: 13.5 us -> 7.38 us  [shards(): along_x = lax.all_to_all(slots, ('gx', 'gz'), 0, 0, tiled=True)]
    pallas_call x0 -> x2, Pallas kernels: none -> 2 us  [the longest x1 1.4 us: first_slots(): pl.pallas_call(first_kernel, out_shape=(jax.ShapeDtypeStruct((count, own,...]
    reduce_sum x2 -> x0, other arithmetic: 1.21 us -> none  [the longest x1 0.61 us: shards(): jnp.sum(bc[:, :1, rank:], axis=0)]
  transfers between devices with their start and end apart: 14 -> 13, of which waited for: 11 -> 10; matrix products, arithmetic and copies ran while one was open for 1% -> 0% of each run, Pallas kernels for 0% -> 0%
where the time goes in v5:
time: 105 us; the launch traced here: 104 us
  starting transfers between devices  31.5 us (30%)
  waiting for transfers between devices  30.3 us (29%)
  blocking collectives  29.7 us (28%)
  Pallas kernels  11.8 us (11%)
    all_to_all x1, blocking collectives, shards(): along_y = lax.all_to_all(slots, ('gy', 'gz'), 0, 0, tiled=True)  14.9 us
    all_to_all x1, blocking collectives, shards(): bc = lax.all_to_all(slots_bc, ('gx', 'gz'), 0, 0, tiled=True)  14.8 us
    ppermute x10, waiting for transfers between devices, shift(): return lax.ppermute(x, axis, pairs)  14.2 us
    ppermute x10, starting transfers between devices, shift(): return lax.ppermute(x, axis, pairs)  12.9 us
    all_to_all x1, starting transfers between devices, shards(): along_x = lax.all_to_all(slots, ('gx', 'gz'), 0, 0, tiled=True)  9.99 us
    pallas_call x2, Pallas kernels, partials(): pl.pallas_call(functools.partial(round_kernel, first, keep, scale), out_s...  9.76 us
    all_to_all x1, starting transfers between devices, shards(): lax.all_to_all(slots_ac, ('gy', 'gz'), 0, 0, tiled=True)  8.11 us
    all_to_all x1, waiting for transfers between devices, shards(): lax.all_to_all(slots_ac, ('gy', 'gz'), 0, 0, tiled=True)  7.73 us
  transfers between devices with their start and end apart: 13, of which 10 were waited for; matrix products, arithmetic and copies ran while one was open for 0% of the time, Pallas kernels for 0%

profile of v5, /device:TPU:1, one launch (start us, length us, event | category | flops | bytes accessed | tf_op | source)
XLA Modules:
  0.0 104.4 jit_solution(14881896450415516504)
XLA Ops:
  0.6 1.4 %first_slots.1 = (f32[16,4,128]{2,1,0:T(4,128)}, f32[8,128]{1,0:T(8,128)S(1)}) custom-call(f32[4,64]{1,0:T(4,128)} %a_hbm.1, f32[4,64]{1,0:T(4,128)} %b_hbm.1, f32[1,64]{1,0:T(1,128)} %c_hbm.1), custom_call_target="tpu_custom_call" | custom-call | tf_op jit(solution)/shard_map/first_slots/pallas_call | solution.py:219
  2.0 10.0 %all-to-all-start = ((f32[16,4,128]{2,1,0:T(4,128)}), f32[16,4,128]{2,1,0:T(4,128)S(1)}, u32[]{:S(2)}, u32[]{:S(2)}) async-start(f32[16,4,128]{2,1,0:T(4,128)} %get-tuple-element.11), calls=%async_computation | async-start | bytes 65536 | tf_op jit(solution)/shard_map/all_to_all | solution.py:289
  12.0 7.4 %all-to-all-done = f32[16,4,128]{2,1,0:T(4,128)S(1)} async-done(((f32[16,4,128]{2,1,0:T(4,128)}), f32[16,4,128]{2,1,0:T(4,128)S(1)}, u32[]{:S(2)}, u32[]{:S(2)}) %all-to-all-start) | async-done | bytes 32800 | tf_op jit(solution)/shard_map/all_to_all | solution.py:289
  19.5 14.9 %all_to_all.20.refs_0_ = f32[32,8,128]{2,1,0:T(8,128)S(1)} all-to-all(f32[32,8,128]{2,1,0:T(8,128)S(1)} %broadcast_in_dim.28), channel_id=1, replica_groups=mesh['gx'=8,'gy'=16,'gz'=2] {'gy','gz'}, dimensions={0} | all-to-all | bytes 262144 | tf_op jit(solution)/shard_map/all_to_all | solution.py:294
  34.4 6.0 %partials.2 = (f32[128,128]{1,0:T(8,128)S(1)}, f32[128,128]{1,0:T(8,128)S(1)}, f32[8192,128]{1,0:T(8,128)S(1)}) custom-call(f32[32,8,128]{2,1,0:T(8,128)S(1)} %all_to_all.20.refs_0_, f32[64,128]{1,0:T(8,128)S(1)} %bitcast.17, f32[8192,128]{1,0:T(8,128)} %bitcast.19), custom_call_target="tpu_custom_call" | custom-call | flops 1073741824 | bytes 4194304 | tf_op jit(solution)/shard_map/partials/pallas_call | solution.py:181
  40.9 0.9 collective-permute-done
  42.2 2.4 %collective-permute-start.1 = (f32[128,128]{1,0:T(8,128)S(1)}, f32[128,128]{1,0:T(8,128)S(1)}, u32[]{:S(2)}, u32[]{:S(2)}) collective-permute-start(f32[128,128]{1,0:T(8,128)S(1)} %get-tuple-element.19), channel_id=1, source_target_pairs={{0,224},{32,0},{64,32},{96,64},{128,96},{160,128},{192,160},{224,1... | collective-permute-start | bytes 196616 | tf_op jit(solution)/shard_map/ppermute | solution.py:256
  44.6 1.6 %collective-permute-done.2 = f32[128,128]{1,0:T(8,128)S(1)} collective-permute-done((f32[128,128]{1,0:T(8,128)S(1)}, f32[128,128]{1,0:T(8,128)S(1)}, u32[]{:S(2)}, u32[]{:S(2)}) %collective-permute-start.2) | collective-permute-done | bytes 65568 | tf_op jit(solution)/shard_map/ppermute | solution.py:256
  46.3 0.8 collective-permute-start.4
  47.1 3.7 %collective-permute-start.3 = (f32[128,128]{1,0:T(8,128)S(1)}, f32[128,128]{1,0:T(8,128)S(1)}, u32[]{:S(2)}, u32[]{:S(2)}) collective-permute-start(f32[128,128]{1,0:T(8,128)S(1)} %get-tuple-element.17), channel_id=1, source_target_pairs={{0,160},{32,192},{64,224},{96,0},{128,32},{160,64},{192,96},{224,1... | collective-permute-start | bytes 196616 | tf_op jit(solution)/shard_map/ppermute | solution.py:256
  50.8 1.7 %collective-permute-done.4 = f32[128,128]{1,0:T(8,128)S(1)} collective-permute-done((f32[128,128]{1,0:T(8,128)S(1)}, f32[128,128]{1,0:T(8,128)S(1)}, u32[]{:S(2)}, u32[]{:S(2)}) %collective-permute-start.4) | collective-permute-done | bytes 65568 | tf_op jit(solution)/shard_map/ppermute | solution.py:256
  52.5 1.8 %collective-permute-done.3 = f32[128,128]{1,0:T(8,128)S(1)} collective-permute-done((f32[128,128]{1,0:T(8,128)S(1)}, f32[128,128]{1,0:T(8,128)S(1)}, u32[]{:S(2)}, u32[]{:S(2)}) %collective-permute-start.3) | collective-permute-done | bytes 65568 | tf_op jit(solution)/shard_map/ppermute | solution.py:256
  54.4 0.9 collective-permute-start.7
  55.3 1.9 %collective-permute-start.6 = (f32[128,128]{1,0:T(8,128)S(1)}, f32[128,128]{1,0:T(8,128)S(1)}, u32[]{:S(2)}, u32[]{:S(2)}) collective-permute-start(f32[128,128]{1,0:T(8,128)S(1)} %pad_maximum_fusion), channel_id=1, source_target_pairs={{0,6},{2,0},{4,2},{6,4},{8,14},{10,8},{12,10},{14,12},{16,22},{18,... | collective-permute-start | bytes 196616 | tf_op jit(solution)/shard_map/ppermute | solution.py:256
  57.3 1.9 %collective-permute-done.7 = f32[128,128]{1,0:T(8,128)S(1)} collective-permute-done((f32[128,128]{1,0:T(8,128)S(1)}, f32[128,128]{1,0:T(8,128)S(1)}, u32[]{:S(2)}, u32[]{:S(2)}) %collective-permute-start.7) | collective-permute-done | bytes 65568 | tf_op jit(solution)/shard_map/ppermute | solution.py:256
  59.2 2.9 %collective-permute-done.5 = f32[128,128]{1,0:T(8,128)S(1)} collective-permute-done((f32[128,128]{1,0:T(8,128)S(1)}, f32[128,128]{1,0:T(8,128)S(1)}, u32[]{:S(2)}, u32[]{:S(2)}) %collective-permute-start.5) | collective-permute-done | bytes 65568 | tf_op jit(solution)/shard_map/ppermute | solution.py:256
  62.0 1.1 %collective-permute-start.10 = (f32[128,128]{1,0:T(8,128)S(1)}, f32[128,128]{1,0:T(8,128)S(1)}, u32[]{:S(2)}, u32[]{:S(2)}) collective-permute-start(f32[128,128]{1,0:T(8,128)S(1)} %add_add_fusion.1), channel_id=1, source_target_pairs={{0,16},{2,18},{4,20},{6,22},{8,24},{10,26},{12,28},{14,30},{16,0},... | collective-permute-start | bytes 196616 | tf_op jit(solution)/shard_map/ppermute | solution.py:256
  63.1 1.7 %collective-permute-start.9 = (f32[128,128]{1,0:T(8,128)S(1)}, f32[128,128]{1,0:T(8,128)S(1)}, u32[]{:S(2)}, u32[]{:S(2)}) collective-permute-start(f32[128,128]{1,0:T(8,128)S(1)} %add_add_fusion.1), channel_id=1, source_target_pairs={{0,24},{2,26},{4,28},{6,30},{8,0},{10,2},{12,4},{14,6},{16,8},{18,... | collective-permute-start | bytes 196616 | tf_op jit(solution)/shard_map/ppermute | solution.py:256
  64.8 1.9 %collective-permute-done.10 = f32[128,128]{1,0:T(8,128)S(1)} collective-permute-done((f32[128,128]{1,0:T(8,128)S(1)}, f32[128,128]{1,0:T(8,128)S(1)}, u32[]{:S(2)}, u32[]{:S(2)}) %collective-permute-start.10) | collective-permute-done | bytes 65568 | tf_op jit(solution)/shard_map/ppermute | solution.py:256
  66.8 2.4 %collective-permute-done.8 = f32[128,128]{1,0:T(8,128)S(1)} collective-permute-done((f32[128,128]{1,0:T(8,128)S(1)}, f32[128,128]{1,0:T(8,128)S(1)}, u32[]{:S(2)}, u32[]{:S(2)}) %collective-permute-start.8) | collective-permute-done | bytes 65568 | tf_op jit(solution)/shard_map/ppermute | solution.py:256
  69.2 3.7 %partials.3 = (f32[32,8,128]{2,1,0:T(8,128)}, f32[64,128]{1,0:T(8,128)S(1)}) custom-call(f32[128,128]{1,0:T(8,128)S(1)} %add_add_fusion.refs_0_, f32[128,128]{1,0:T(8,128)S(1)} %add_add_fusion.2.refs_1_, f32[8192,128]{1,0:T(8,128)S(1)} %get-tuple-element.14.refs_2_), custom_call_target="tpu_custom_call" | custom-call | flops 1073741824 | bytes 4194304 | tf_op jit(solution)/shard_map/partials/pallas_call | solution.py:181
  72.9 8.1 %all-to-all-start.2 = ((f32[32,8,128]{2,1,0:T(8,128)}), f32[32,8,128]{2,1,0:T(8,128)S(1)}, u32[]{:S(2)}, u32[]{:S(2)}) async-start(f32[32,8,128]{2,1,0:T(8,128)} %get-tuple-element.15), calls=%async_computation.2 | async-start | bytes 262144 | tf_op jit(solution)/shard_map/all_to_all | solution.py:310
  81.0 7.7 %all-to-all-done.2 = f32[32,8,128]{2,1,0:T(8,128)S(1)} async-done(((f32[32,8,128]{2,1,0:T(8,128)}), f32[32,8,128]{2,1,0:T(8,128)S(1)}, u32[]{:S(2)}, u32[]{:S(2)}) %all-to-all-start.2) | async-done | bytes 131104 | tf_op jit(solution)/shard_map/all_to_all | solution.py:310
  89.0 14.8 %all_to_all.21.bc_ref = f32[16,4,128]{2,1,0:T(4,128)S(1)} all-to-all(f32[16,4,128]{2,1,0:T(4,128)S(1)} %bitcast.21), channel_id=1, replica_groups=mesh['gx'=8,'gy'=16,'gz'=2] {'gx','gz'}, dimensions={0} | all-to-all | bytes 65536 | tf_op jit(solution)/shard_map/all_to_all | solution.py:316
  (24 shorter events, 1.9 us)
Async XLA Ops:
  2.0 17.4 %all-to-all-start = ((f32[16,4,128]{2,1,0:T(4,128)}), f32[16,4,128]{2,1,0:T(4,128)S(1)}, u32[]{:S(2)}, u32[]{:S(2)}) async-start(f32[16,4,128]{2,1,0:T(4,128)} %get-tuple-element.11), calls=%async_computation | async-start | bytes 65536 | tf_op jit(solution)/shard_map/all_to_all | solution.py:289
  40.4 1.4 %collective-permute-start = (f32[128,128]{1,0:T(8,128)S(1)}, f32[128,128]{1,0:T(8,128)S(1)}, u32[]{:S(2)}, u32[]{:S(2)}) collective-permute-start(f32[128,128]{1,0:T(8,128)S(1)} %get-tuple-element.12), channel_id=1, source_target_pairs={{0,1},{1,0},{2,3},{3,2},{4,5},{5,4},{6,7},{7,6},{8,9},{9,8},{10,11... | collective-permute-start | bytes 196616 | tf_op jit(solution)/shard_map/ppermute | solution.py:272
  41.8 4.4 %collective-permute-start.2 = (f32[128,128]{1,0:T(8,128)S(1)}, f32[128,128]{1,0:T(8,128)S(1)}, u32[]{:S(2)}, u32[]{:S(2)}) collective-permute-start(f32[128,128]{1,0:T(8,128)S(1)} %get-tuple-element.19), channel_id=1, source_target_pairs={{0,32},{32,64},{64,96},{96,128},{128,160},{160,192},{192,224},{224... | collective-permute-start | bytes 196616 | tf_op jit(solution)/shard_map/ppermute | solution.py:256
  42.2 4.1 %collective-permute-start.1 = (f32[128,128]{1,0:T(8,128)S(1)}, f32[128,128]{1,0:T(8,128)S(1)}, u32[]{:S(2)}, u32[]{:S(2)}) collective-permute-start(f32[128,128]{1,0:T(8,128)S(1)} %get-tuple-element.19), channel_id=1, source_target_pairs={{0,224},{32,0},{64,32},{96,64},{128,96},{160,128},{192,160},{224,1... | collective-permute-start | bytes 196616 | tf_op jit(solution)/shard_map/ppermute | solution.py:256
  46.3 6.2 %collective-permute-start.4 = (f32[128,128]{1,0:T(8,128)S(1)}, f32[128,128]{1,0:T(8,128)S(1)}, u32[]{:S(2)}, u32[]{:S(2)}) collective-permute-start(f32[128,128]{1,0:T(8,128)S(1)} %get-tuple-element.18), channel_id=1, source_target_pairs={{0,96},{32,128},{64,160},{96,192},{128,224},{160,0},{192,32},{224,... | collective-permute-start | bytes 196616 | tf_op jit(solution)/shard_map/ppermute | solution.py:256
  47.1 7.2 %collective-permute-start.3 = (f32[128,128]{1,0:T(8,128)S(1)}, f32[128,128]{1,0:T(8,128)S(1)}, u32[]{:S(2)}, u32[]{:S(2)}) collective-permute-start(f32[128,128]{1,0:T(8,128)S(1)} %get-tuple-element.17), channel_id=1, source_target_pairs={{0,160},{32,192},{64,224},{96,0},{128,32},{160,64},{192,96},{224,1... | collective-permute-start | bytes 196616 | tf_op jit(solution)/shard_map/ppermute | solution.py:256
  54.4 4.7 %collective-permute-start.7 = (f32[128,128]{1,0:T(8,128)S(1)}, f32[128,128]{1,0:T(8,128)S(1)}, u32[]{:S(2)}, u32[]{:S(2)}) collective-permute-start(f32[128,128]{1,0:T(8,128)S(1)} %pad_maximum_fusion), channel_id=1, source_target_pairs={{0,4},{2,6},{4,0},{6,2},{8,12},{10,14},{12,8},{14,10},{16,20},{18,... | collective-permute-start | bytes 196616 | tf_op jit(solution)/shard_map/ppermute | solution.py:256
  55.3 3.8 %collective-permute-start.6 = (f32[128,128]{1,0:T(8,128)S(1)}, f32[128,128]{1,0:T(8,128)S(1)}, u32[]{:S(2)}, u32[]{:S(2)}) collective-permute-start(f32[128,128]{1,0:T(8,128)S(1)} %pad_maximum_fusion), channel_id=1, source_target_pairs={{0,6},{2,0},{4,2},{6,4},{8,14},{10,8},{12,10},{14,12},{16,22},{18,... | collective-permute-start | bytes 196616 | tf_op jit(solution)/shard_map/ppermute | solution.py:256
  57.3 4.8 %collective-permute-start.5 = (f32[128,128]{1,0:T(8,128)S(1)}, f32[128,128]{1,0:T(8,128)S(1)}, u32[]{:S(2)}, u32[]{:S(2)}) collective-permute-start(f32[128,128]{1,0:T(8,128)S(1)} %pad_maximum_fusion), channel_id=1, source_target_pairs={{0,2},{2,4},{4,6},{6,0},{8,10},{10,12},{12,14},{14,8},{16,18},{18,... | collective-permute-start | bytes 196616 | tf_op jit(solution)/shard_map/ppermute | solution.py:256
  62.0 4.7 %collective-permute-start.10 = (f32[128,128]{1,0:T(8,128)S(1)}, f32[128,128]{1,0:T(8,128)S(1)}, u32[]{:S(2)}, u32[]{:S(2)}) collective-permute-start(f32[128,128]{1,0:T(8,128)S(1)} %add_add_fusion.1), channel_id=1, source_target_pairs={{0,16},{2,18},{4,20},{6,22},{8,24},{10,26},{12,28},{14,30},{16,0},... | collective-permute-start | bytes 196616 | tf_op jit(solution)/shard_map/ppermute | solution.py:256
  63.1 3.6 %collective-permute-start.9 = (f32[128,128]{1,0:T(8,128)S(1)}, f32[128,128]{1,0:T(8,128)S(1)}, u32[]{:S(2)}, u32[]{:S(2)}) collective-permute-start(f32[128,128]{1,0:T(8,128)S(1)} %add_add_fusion.1), channel_id=1, source_target_pairs={{0,24},{2,26},{4,28},{6,30},{8,0},{10,2},{12,4},{14,6},{16,8},{18,... | collective-permute-start | bytes 196616 | tf_op jit(solution)/shard_map/ppermute | solution.py:256
  64.8 4.3 %collective-permute-start.8 = (f32[128,128]{1,0:T(8,128)S(1)}, f32[128,128]{1,0:T(8,128)S(1)}, u32[]{:S(2)}, u32[]{:S(2)}) collective-permute-start(f32[128,128]{1,0:T(8,128)S(1)} %add_add_fusion.1), channel_id=1, source_target_pairs={{0,8},{2,10},{4,12},{6,14},{8,16},{10,18},{12,20},{14,22},{16,24},... | collective-permute-start | bytes 196616 | tf_op jit(solution)/shard_map/ppermute | solution.py:256
  72.9 15.9 %all-to-all-start.2 = ((f32[32,8,128]{2,1,0:T(8,128)}), f32[32,8,128]{2,1,0:T(8,128)S(1)}, u32[]{:S(2)}, u32[]{:S(2)}) async-start(f32[32,8,128]{2,1,0:T(8,128)} %get-tuple-element.15), calls=%async_computation.2 | async-start | bytes 262144 | tf_op jit(solution)/shard_map/all_to_all | solution.py:310

commit v6 on v5

v6 whole, which is shorter than its diff:
```python
import functools

import jax
import jax.numpy as jnp
from jax import lax
from jax.experimental import pallas as pl
from jax.experimental.pallas import tpu as pltpu
from jax.sharding import PartitionSpec as P

STEPS = 2
STEP_SIZE = 0.1
F32 = jnp.float32
BF16 = jnp.bfloat16
HIGHEST = lax.Precision.HIGHEST
VMEM = pl.BlockSpec(memory_space=pltpu.VMEM)
HBM = pl.BlockSpec(memory_space=pltpu.HBM)
CHUNK = 512


def split(x):
    high = x.astype(BF16)
    return high, (x - high.astype(F32)).astype(BF16)


def lower_half(shape):
    return lax.broadcasted_iota(jnp.int32, shape, len(shape) - 1) < shape[-1] // 2


def turn(x):
    return pltpu.roll(x, x.shape[1] // 2, 1)


def from_lower(x):
    return jnp.where(lower_half(x.shape), x, turn(x))


def from_upper(x):
    return jnp.where(lower_half(x.shape), turn(x), x)


def gram(x):
    return lax.dot_general(
        x, x, (((0,), (0,)), ((), ())), precision=HIGHEST, preferred_element_type=F32
    )


def unpack_first(ac_ref, own_ref, other_ref, a2_ref, b2_ref, c2_ref):
    slots, each, width = ac_ref.shape
    core = lax.axis_index("gz")
    a2_ref[...] = from_lower(ac_ref[...].reshape(slots * each, width))
    for g in range(each):
        c2_ref[g * slots : (g + 1) * slots, :] = ac_ref[:, g, :]
    c2_ref[...] = from_upper(c2_ref[...])
    slots, each, width = own_ref.shape
    for n in range(slots):
        own, other = own_ref[n], other_ref[n]
        at = 2 * each * n
        b2_ref[at : at + each, :] = jnp.where(core == 0, own, other)
        b2_ref[at + each : at + 2 * each, :] = jnp.where(core == 0, other, own)
    b2_ref[...] = from_lower(b2_ref[...])


def unpack_second(ca_ref, b_ref, a2_ref, b2_ref, c2_ref):
    a2_ref[...] = from_upper(ca_ref[...])
    b2_ref[...] = from_upper(b_ref[...])
    c2_ref[...] = from_lower(ca_ref[...])


def pack_first(a, b, c_ref, a_ref, cb_ref):
    count_b = b.shape[0]
    c = c_ref[...]
    a_ref[...] = a
    cb_ref[:count_b, :] = jnp.where(lower_half(b.shape), c[:count_b], b)
    cb_ref[count_b:, :] = jnp.where(lower_half(c[count_b:].shape), c[count_b:], 0.0)


def pack_second(a, b, c_ref, ac_ref, b_ref):
    slots, each, width = ac_ref.shape
    lower = lower_half((each, width))
    for n in range(slots):
        block = c_ref[pl.ds(n, each, stride=slots), :]
        ac_ref[n, :, :] = jnp.where(lower, a[n * each : (n + 1) * each], block)
    b_ref[...] = b


def round_kernel(first, keep, scale, *refs):
    n_small = 3 if first else 2
    small, t_ref, outs, refs = refs[:n_small], refs[n_small], refs[n_small + 1 :][:2], refs[n_small + 3 :]
    if first:
        t_hbm, t_ref, sems, refs = t_ref, refs[0], refs[-1], refs[1:-1]
    a2_ref, b2_ref, c2_ref, wc_ref, ma_ref = refs
    count_i, count_j, count_k = a2_ref.shape[0], b2_ref.shape[0], c2_ref.shape[0]
    width = a2_ref.shape[1]
    rank = width // 2
    chunks = t_ref.shape[0] // CHUNK
    per = CHUNK // count_j

    def fetch(c):
        at = pl.ds(c * CHUNK, CHUNK)
        return pltpu.make_async_copy(t_hbm.at[at, :], t_ref.at[at, :], sems.at[c])

    for c in range(chunks if first else 0):
        fetch(c).start()

    (unpack_first if first else unpack_second)(*small, a2_ref, b2_ref, c2_ref)
    a2, b2, c2 = a2_ref[...], b2_ref[...], c2_ref[...]
    high = c2.astype(BF16).astype(F32)
    both = jnp.where(lower_half(c2.shape), high, c2 - high).astype(BF16)
    wc_ref[:count_k, :] = both
    wc_ref[count_k:, :] = both
    turned_a = a2.T[:rank]
    turned_b = b2.T[:rank]
    turned_b = jnp.concatenate([turned_b] * (128 // count_j), axis=1)
    gram_a, gram_b, gram_c = gram(a2), gram(b2), gram(c2)

    def model(factor, one, two):
        return 0.5 * jnp.dot(factor, one * two, precision=HIGHEST, preferred_element_type=F32)

    model_a = model(a2, gram_b, gram_c)
    model_b = model(b2, gram_a, gram_c)
    model_c = model(c2, gram_a, gram_b)
    group = 128 // count_j
    lane = lax.broadcasted_iota(jnp.int32, (rank, 128), 1) // count_j

    moment_b = jnp.zeros((count_j, width), F32)
    moment_c = jnp.zeros((width, 2 * count_k), F32)
    for c in range(chunks):
        if first and c % (chunks // 2) == 0:
            for n in range(c, c + chunks // 2):
                fetch(n).wait()
        high, low = split(t_ref[c * CHUNK : (c + 1) * CHUNK, :])
        terms = jnp.concatenate([high, low], axis=1)
        y = jnp.dot(terms, wc_ref[...], preferred_element_type=F32)
        y = y.reshape(per, count_j, width)
        at_i = c * per
        ma_ref[at_i : at_i + per, :] = jnp.sum(y * b2_ref[...][None], axis=1)
        for m in range(per):
            moment_b = moment_b + y[m] * a2_ref[at_i + m : at_i + m + 1, :]
        pieces = []
        for m in range(at_i, at_i + per, group):
            columns = jnp.broadcast_to(turned_a[:, m : m + 1], (rank, 128))
            for g in range(1, group):
                other = jnp.broadcast_to(turned_a[:, m + g : m + g + 1], (rank, 128))
                columns = jnp.where(lane == g, other, columns)
            pieces.append(columns * turned_b)
        rows_high, rows_low = split(jnp.concatenate(pieces, axis=1))
        rows = jnp.concatenate([rows_high, rows_low], axis=0)
        moment_c = moment_c + jnp.dot(rows, terms, preferred_element_type=F32)
    moment_c = moment_c[:, :count_k] + moment_c[:, count_k:]
    moment_c = moment_c[:rank] + moment_c[rank:]
    moment_c = jnp.concatenate([moment_c, moment_c], axis=0).T
    moment_a = ma_ref[...]

    def result(factor, whole, moment, weight, factor_scale):
        out = (whole - moment) * factor_scale
        return out + factor * weight if weight else out

    a = result(a2_ref[...], model_a, moment_a + turn(moment_a), keep[0], scale[0])
    b = result(b2_ref[...], model_b, moment_b + turn(moment_b), keep[1], scale[1])
    c2_ref[...] = result(c2_ref[...], model_c, moment_c, keep[2], scale[2])
    (pack_first if first else pack_second)(a, b, c2_ref, *outs)


def partials(first, keep, scale, small, tensor, sizes, out_shapes):
    count_i, count_j, count_k = sizes
    width = small[0].shape[-1]
    tall = count_i * count_j
    if first:
        tensor = pltpu.with_memory_space_constraint(tensor, pltpu.HBM)
        out_shapes += ((tall, count_k),)
    return pl.pallas_call(
        functools.partial(round_kernel, first, keep, scale),
        out_shape=tuple(jax.ShapeDtypeStruct(s, F32) for s in out_shapes),
        in_specs=[VMEM] * len(small) + [HBM if first else VMEM],
        out_specs=(VMEM,) * len(out_shapes),
        scratch_shapes=[
            pltpu.VMEM((count_i, width), F32),
            pltpu.VMEM((count_j, width), F32),
            pltpu.VMEM((count_k, width), F32),
            pltpu.VMEM((2 * count_k, width), BF16),
            pltpu.VMEM((count_i, width), F32),
        ]
        + [pltpu.SemaphoreType.DMA((tall // CHUNK,))] * first,
        compiler_params=pltpu.CompilerParams(vmem_limit_bytes=24 << 20),
        cost_estimate=pl.CostEstimate(flops=1 << 30, bytes_accessed=4 << 20, transcendentals=0),
        name="partials",
    )(*small, tensor)


def first_kernel(a_hbm, b_hbm, c_hbm, slots_ref, a_out_ref, a_ref, b_ref, c_ref, sems):
    own, rank = a_ref.shape
    pairs = ((a_hbm, a_ref), (b_hbm, b_ref), (c_hbm, c_ref))
    copies = [pltpu.make_async_copy(x, y, sems.at[n]) for n, (x, y) in enumerate(pairs)]
    for copy in copies:
        copy.start()
    for copy in copies:
        copy.wait()
    a = a_ref[...]
    a_out_ref[...] = jnp.concatenate([a, a], axis=1)
    slot = jnp.concatenate([b_ref[...], jnp.broadcast_to(c_ref[...], (own, rank))], axis=1)
    for n in range(slots_ref.shape[0]):
        slots_ref[n, :, :] = slot


def first_slots(a, b, c, count):
    own, rank = a.shape
    factors = [pltpu.with_memory_space_constraint(x, pltpu.HBM) for x in (a, b, c)]
    return pl.pallas_call(
        first_kernel,
        out_shape=(
            jax.ShapeDtypeStruct((count, own, 2 * rank), F32),
            jax.ShapeDtypeStruct((own, 2 * rank), F32),
        ),
        in_specs=[HBM] * 3,
        out_specs=(VMEM, VMEM),
        scratch_shapes=[pltpu.VMEM(x.shape, F32) for x in (a, b, c)]
        + [pltpu.SemaphoreType.DMA((3,))],
        compiler_params=pltpu.CompilerParams(vmem_limit_bytes=4 << 20),
        name="first_slots",
    )(*factors)


def last_kernel(ac_ref, other_ref, bc_ref, a_ref, b_ref, c_ref, sum_a_ref, sum_b_ref):
    own, rank = a_ref.shape
    sum_a_ref[...] = ac_ref[...] + other_ref[...]
    sum_b_ref[...] = jnp.sum(bc_ref[...], axis=0)
    mine = pl.ds(lax.axis_index("gz") * own, own)
    a_ref[...] = sum_a_ref[mine, :][:, :rank]
    b_ref[...] = sum_b_ref[mine, :][:, :rank]
    c_ref[...] = sum_b_ref[:1, :][:, rank:]


def last_sums(ac, other, bc, own, rank):
    return pl.pallas_call(
        last_kernel,
        out_shape=tuple(jax.ShapeDtypeStruct((n, rank), F32) for n in (own, own, 1)),
        scratch_shapes=[pltpu.VMEM(ac.shape, F32)] * 2,
        compiler_params=pltpu.CompilerParams(vmem_limit_bytes=4 << 20),
        name="last_sums",
    )(ac, other, bc)


def shift(x, axis, stride, count, by):
    pairs = []
    for n in range(lax.axis_size(axis)):
        place = n // stride % count
        pairs.append((n, n + ((place + by) % count - place) * stride))
    return lax.ppermute(x, axis, pairs)


def ring8(x):
    below, above = shift(x, "gx", 1, 8, 1), shift(x, "gx", 1, 8, -1)
    two = x + above
    three = two + below
    return three + (shift(three, "gx", 1, 8, -3) + shift(two, "gx", 1, 8, 3))


def ring4(x, stride):
    ones = shift(x, "gy", stride, 4, 1) + shift(x, "gy", stride, 4, -1)
    return (x + ones) + shift(x, "gy", stride, 4, 2)


def swap(x):
    return lax.ppermute(x, "gz", [(0, 1), (1, 0)])


def shards(tensor, factor_a, factor_b, factor_c):
    count_x, count_y, count_z = (lax.axis_size(n) for n in ("gx", "gy", "gz"))
    core = lax.axis_index("gz")
    count_i, count_j, count_k = tensor.shape
    whole = (
        float(count_j * count_y * count_k * count_z),
        float(count_i * count_x * count_k * count_z),
        float(count_i * count_x * count_j * count_y),
    )
    copies = (count_y * count_z, count_x * count_z, count_x * count_y)
    own, rank = factor_a.shape
    wide = 2 * rank

    slots, mine = first_slots(factor_a, factor_b, factor_c, count_x)
    other = swap(mine)
    along_x = lax.all_to_all(slots, "gx", 0, 0, tiled=True)
    rows_a = jnp.concatenate(
        [jnp.where(core == 0, mine, other), jnp.where(core == 0, other, mine)], axis=0
    )
    slot = jnp.where(lower_half(rows_a.shape), rows_a, along_x[:, 0])
    other_x = swap(along_x)
    along_y = lax.all_to_all(jnp.broadcast_to(slot[None], (count_y, *slot.shape)), "gy", 0, 0, tiled=True)

    keep = tuple(1.0 / n for n in copies)
    scale = tuple(-STEP_SIZE / n for n in whole)
    sizes = tensor.shape
    tensor = tensor.reshape(count_i * count_j, count_k)
    shapes = ((count_i, wide), (count_k, wide))
    a, cb, tensor = partials(True, keep, scale, (along_y, along_x, other_x), tensor, sizes, shapes)
    a = a + swap(a)
    cb = ring8(cb)
    ca = ring4(ring4(jnp.where(lower_half(cb.shape), cb, a), 1), 4)
    b = cb[:count_j]
    b = b + swap(b)

    scale = tuple(1.0 / n for n in whole)
    shapes = ((count_y, 2 * own, wide), (count_j, wide))
    slots_ac, b = partials(False, (0.0,) * 3, scale, (ca, b), tensor, sizes, shapes)
    b = b + swap(b)
    ac = jnp.sum(lax.all_to_all(slots_ac, "gy", 0, 0, tiled=True), axis=0)
    other = swap(ac)
    slots_b = b.reshape(count_x, 2 * own, wide)
    slots_bc = jnp.where(lower_half(slots_b.shape), slots_b, ac[:, None])
    bc = lax.all_to_all(slots_bc, "gx", 0, 0, tiled=True)
    return last_sums(ac, other, bc, own, rank)


def solution(mesh):
    factors = (
        P(("gx", "gy", "gz"), None),
        P(("gy", "gx", "gz"), None),
        P(("gz", "gx", "gy"), None),
    )
    return jax.shard_map(
        shards,
        mesh=mesh,
        in_specs=(P("gx", "gy", "gz"), *factors),
        out_specs=factors,
        check_vma=False,
    )
```

time: 105 us -> 99.2 us (0.945)
  the two profiles are of different devices: /device:TPU:1 before, /device:TPU:2 now
where the time goes in v6:
time: 99.2 us; the launch traced here: 98.9 us
  starting transfers between devices  45.4 us (46%)
  waiting for transfers between devices  42.2 us (43%)
  Pallas kernels  9.24 us (9%)
    ppermute x10, starting transfers between devices, shift(): return lax.ppermute(x, axis, pairs)  15.7 us
    ppermute x10, waiting for transfers between devices, shift(): return lax.ppermute(x, axis, pairs)  13.7 us
    all_to_all x1, starting transfers between devices, shards(): along_x = lax.all_to_all(slots, 'gx', 0, 0, tiled=True)  8.48 us
    all_to_all x1, starting transfers between devices, shards(): bc = lax.all_to_all(slots_bc, 'gx', 0, 0, tiled=True)  7.51 us
    all_to_all x1, starting transfers between devices, shards(): lax.all_to_all(jnp.broadcast_to(slot[None], (count_y, *slot.shape)), 'gy'...  7.48 us
    pallas_call x2, Pallas kernels, partials(): pl.pallas_call(functools.partial(round_kernel, first, keep, scale), out_s...  7.25 us
    all_to_all x1, waiting for transfers between devices, shards(): bc = lax.all_to_all(slots_bc, 'gx', 0, 0, tiled=True)  6.86 us
    all_to_all x1, waiting for transfers between devices, shards(): along_x = lax.all_to_all(slots, 'gx', 0, 0, tiled=True)  6.61 us
  transfers between devices with their start and end apart: 20, of which 16 were waited for; matrix products, arithmetic and copies ran while one was open for 0% of the time, Pallas kernels for 0%

profile of v6, /device:TPU:2, one launch (start us, length us, event | category | flops | bytes accessed | tf_op | source)
XLA Modules:
  0.0 98.9 jit_solution(1696840200630514381)
XLA Ops:
  0.6 1.4 %first_slots.1 = (f32[8,4,128]{2,1,0:T(4,128)}, f32[4,128]{1,0:T(4,128)S(1)}) custom-call(f32[4,64]{1,0:T(4,128)} %a_hbm.1, f32[4,64]{1,0:T(4,128)} %b_hbm.1, f32[1,64]{1,0:T(1,128)} %c_hbm.1), custom_call_target="tpu_custom_call" | custom-call | tf_op jit(solution)/shard_map/first_slots/pallas_call | solution.py:208
  2.0 8.5 %all-to-all-start = ((f32[8,4,128]{2,1,0:T(4,128)}), f32[8,4,128]{2,1,0:T(4,128)S(1)}, u32[]{:S(2)}, u32[]{:S(2)}) async-start(f32[8,4,128]{2,1,0:T(4,128)} %get-tuple-element.11), calls=%async_computation | async-start | bytes 32768 | tf_op jit(solution)/shard_map/all_to_all | solution.py:282
  11.7 6.6 %all-to-all-done.refs_1_ = f32[8,4,128]{2,1,0:T(4,128)S(1)} async-done(((f32[8,4,128]{2,1,0:T(4,128)}), f32[8,4,128]{2,1,0:T(4,128)S(1)}, u32[]{:S(2)}, u32[]{:S(2)}) %all-to-all-start) | async-done | bytes 16416 | tf_op jit(solution)/shard_map/all_to_all | solution.py:282
  18.9 7.5 %all-to-all-start.1 = ((f32[16,8,128]{2,1,0:T(8,128)}), f32[16,8,128]{2,1,0:T(8,128)S(1)}, u32[]{:S(2)}, u32[]{:S(2)}) async-start(f32[16,8,128]{2,1,0:T(8,128)} %broadcast_in_dim.7), calls=%async_computation.1 | async-start | bytes 131072 | tf_op jit(solution)/shard_map/all_to_all | solution.py:288
  26.4 1.2 %collective-permute-done.1.refs_2_ = f32[8,4,128]{2,1,0:T(4,128)S(1)} collective-permute-done((f32[8,4,128]{2,1,0:T(4,128)S(1)}, f32[8,4,128]{2,1,0:T(4,128)S(1)}, u32[]{:S(2)}, u32[]{:S(2)}) %collective-permute-start.1) | collective-permute-done | bytes 16416 | tf_op jit(solution)/shard_map/ppermute | solution.py:264
  27.6 5.1 %all-to-all-done.1.refs_0_ = f32[16,8,128]{2,1,0:T(8,128)S(1)} async-done(((f32[16,8,128]{2,1,0:T(8,128)}), f32[16,8,128]{2,1,0:T(8,128)S(1)}, u32[]{:S(2)}, u32[]{:S(2)}) %all-to-all-start.1) | async-done | bytes 65568 | tf_op jit(solution)/shard_map/all_to_all | solution.py:288
  32.7 3.9 %partials.2 = (f32[128,128]{1,0:T(8,128)S(1)}, f32[128,128]{1,0:T(8,128)S(1)}, f32[8192,128]{1,0:T(8,128)S(1)}) custom-call(f32[16,8,128]{2,1,0:T(8,128)S(1)} %all-to-all-done.1.refs_0_, f32[8,4,128]{2,1,0:T(4,128)S(1)} %all-to-all-done.refs_1_, f32[8,4,128]{2,1,0:T(4,128)S(1)} %collective-permute-done.1.refs_2_, f32[8192,128]{1,0:T(8,128)} %bitcast.4), custom_call_target="tpu_custom_call" | custom-call | flops 1073741824 | bytes 4194304 | tf_op jit(solution)/shard_map/partials/pallas_call | solution.py:171
  37.3 2.6 %collective-permute-start.2 = (f32[128,128]{1,0:T(8,128)S(1)}, f32[128,128]{1,0:T(8,128)S(1)}, u32[]{:S(2)}, u32[]{:S(2)}) collective-permute-start(f32[128,128]{1,0:T(8,128)S(1)} %get-tuple-element.12), channel_id=1, source_target_pairs={{0,224},{32,0},{64,32},{96,64},{128,96},{160,128},{192,160},{224,1... | collective-permute-start | bytes 196616 | tf_op jit(solution)/shard_map/ppermute | solution.py:248
  39.9 2.2 %collective-permute-done.3 = f32[128,128]{1,0:T(8,128)S(1)} collective-permute-done((f32[128,128]{1,0:T(8,128)S(1)}, f32[128,128]{1,0:T(8,128)S(1)}, u32[]{:S(2)}, u32[]{:S(2)}) %collective-permute-start.3) | collective-permute-done | bytes 65568 | tf_op jit(solution)/shard_map/ppermute | solution.py:248
  42.2 1.3 %collective-permute-start.5 = (f32[128,128]{1,0:T(8,128)S(1)}, f32[128,128]{1,0:T(8,128)S(1)}, u32[]{:S(2)}, u32[]{:S(2)}) collective-permute-start(f32[128,128]{1,0:T(8,128)S(1)} %get-tuple-element.20), channel_id=1, source_target_pairs={{0,96},{32,128},{64,160},{96,192},{128,224},{160,0},{192,32},{224,... | collective-permute-start | bytes 196616 | tf_op jit(solution)/shard_map/ppermute | solution.py:248
  43.5 3.9 %collective-permute-start.4 = (f32[128,128]{1,0:T(8,128)S(1)}, f32[128,128]{1,0:T(8,128)S(1)}, u32[]{:S(2)}, u32[]{:S(2)}) collective-permute-start(f32[128,128]{1,0:T(8,128)S(1)} %get-tuple-element.19), channel_id=1, source_target_pairs={{0,160},{32,192},{64,224},{96,0},{128,32},{160,64},{192,96},{224,1... | collective-permute-start | bytes 196616 | tf_op jit(solution)/shard_map/ppermute | solution.py:248
  47.3 2.2 %collective-permute-done.5 = f32[128,128]{1,0:T(8,128)S(1)} collective-permute-done((f32[128,128]{1,0:T(8,128)S(1)}, f32[128,128]{1,0:T(8,128)S(1)}, u32[]{:S(2)}, u32[]{:S(2)}) %collective-permute-start.5) | collective-permute-done | bytes 65568 | tf_op jit(solution)/shard_map/ppermute | solution.py:248
  50.0 1.5 %collective-permute-start.9 = (f32[128,128]{1,0:T(8,128)S(1)}, f32[128,128]{1,0:T(8,128)S(1)}, u32[]{:S(2)}, u32[]{:S(2)}) collective-permute-start(f32[128,128]{1,0:T(8,128)S(1)} %get-tuple-element.17), channel_id=1, source_target_pairs={{0,4},{2,6},{4,0},{6,2},{8,12},{10,14},{12,8},{14,10},{16,20},{18,... | collective-permute-start | bytes 196616 | tf_op jit(solution)/shard_map/ppermute | solution.py:248
  51.6 1.3 %collective-permute-start.8 = (f32[128,128]{1,0:T(8,128)S(1)}, f32[128,128]{1,0:T(8,128)S(1)}, u32[]{:S(2)}, u32[]{:S(2)}) collective-permute-start(f32[128,128]{1,0:T(8,128)S(1)} %get-tuple-element.17), channel_id=1, source_target_pairs={{0,6},{2,0},{4,2},{6,4},{8,14},{10,8},{12,10},{14,12},{16,22},{18,... | collective-permute-start | bytes 196616 | tf_op jit(solution)/shard_map/ppermute | solution.py:248
  53.6 2.4 %collective-permute-done.9 = f32[128,128]{1,0:T(8,128)S(1)} collective-permute-done((f32[128,128]{1,0:T(8,128)S(1)}, f32[128,128]{1,0:T(8,128)S(1)}, u32[]{:S(2)}, u32[]{:S(2)}) %collective-permute-start.9) | collective-permute-done | bytes 65568 | tf_op jit(solution)/shard_map/ppermute | solution.py:248
  57.2 1.7 %collective-permute-start.12 = (f32[128,128]{1,0:T(8,128)S(1)}, f32[128,128]{1,0:T(8,128)S(1)}, u32[]{:S(2)}, u32[]{:S(2)}) collective-permute-start(f32[128,128]{1,0:T(8,128)S(1)} %add_add_fusion.1), channel_id=1, source_target_pairs={{0,16},{2,18},{4,20},{6,22},{8,24},{10,26},{12,28},{14,30},{16,0},... | collective-permute-start | bytes 196616 | tf_op jit(solution)/shard_map/ppermute | solution.py:248
  58.9 1.8 %collective-permute-start.11 = (f32[128,128]{1,0:T(8,128)S(1)}, f32[128,128]{1,0:T(8,128)S(1)}, u32[]{:S(2)}, u32[]{:S(2)}) collective-permute-start(f32[128,128]{1,0:T(8,128)S(1)} %add_add_fusion.1), channel_id=1, source_target_pairs={{0,24},{2,26},{4,28},{6,30},{8,0},{10,2},{12,4},{14,6},{16,8},{18,... | collective-permute-start | bytes 196616 | tf_op jit(solution)/shard_map/ppermute | solution.py:248
  60.9 2.1 %collective-permute-done.12 = f32[128,128]{1,0:T(8,128)S(1)} collective-permute-done((f32[128,128]{1,0:T(8,128)S(1)}, f32[128,128]{1,0:T(8,128)S(1)}, u32[]{:S(2)}, u32[]{:S(2)}) %collective-permute-start.12) | collective-permute-done | bytes 65568 | tf_op jit(solution)/shard_map/ppermute | solution.py:248
  63.1 3.0 %collective-permute-done.10 = f32[128,128]{1,0:T(8,128)S(1)} collective-permute-done((f32[128,128]{1,0:T(8,128)S(1)}, f32[128,128]{1,0:T(8,128)S(1)}, u32[]{:S(2)}, u32[]{:S(2)}) %collective-permute-start.10) | collective-permute-done | bytes 65568 | tf_op jit(solution)/shard_map/ppermute | solution.py:248
  66.2 3.3 %partials.3 = (f32[16,8,128]{2,1,0:T(8,128)}, f32[64,128]{1,0:T(8,128)S(1)}) custom-call(f32[128,128]{1,0:T(8,128)S(1)} %add_add_fusion.refs_0_, f32[64,128]{1,0:T(8,128)S(1)} %slice_add_fusion.refs_1_, f32[8192,128]{1,0:T(8,128)S(1)} %get-tuple-element.14.refs_2_), custom_call_target="tpu_custom_call" | custom-call | flops 1073741824 | bytes 4194304 | tf_op jit(solution)/shard_map/partials/pallas_call | solution.py:171
  69.5 6.2 %all-to-all-start.2 = ((f32[16,8,128]{2,1,0:T(8,128)}), f32[16,8,128]{2,1,0:T(8,128)S(1)}, u32[]{:S(2)}, u32[]{:S(2)}) async-start(f32[16,8,128]{2,1,0:T(8,128)} %get-tuple-element.15), calls=%async_computation.2 | async-start | bytes 131072 | tf_op jit(solution)/shard_map/all_to_all | solution.py:306
  75.7 6.4 %all-to-all-done.2 = f32[16,8,128]{2,1,0:T(8,128)S(1)} async-done(((f32[16,8,128]{2,1,0:T(8,128)}), f32[16,8,128]{2,1,0:T(8,128)S(1)}, u32[]{:S(2)}, u32[]{:S(2)}) %all-to-all-start.2) | async-done | bytes 65568 | tf_op jit(solution)/shard_map/all_to_all | solution.py:306
  82.7 7.5 %all-to-all-start.3 = ((f32[8,8,128]{2,1,0:T(8,128)}), f32[8,8,128]{2,1,0:T(8,128)S(1)}, u32[]{:S(2)}, u32[]{:S(2)}) async-start(f32[8,8,128]{2,1,0:T(8,128)} %bitcast_select_fusion), calls=%async_computation.3 | async-start | bytes 65536 | tf_op jit(solution)/shard_map/all_to_all | solution.py:310
  91.4 6.9 %all-to-all-done.3.bc_ref = f32[8,8,128]{2,1,0:T(8,128)S(1)} async-done(((f32[8,8,128]{2,1,0:T(8,128)}), f32[8,8,128]{2,1,0:T(8,128)S(1)}, u32[]{:S(2)}, u32[]{:S(2)}) %all-to-all-start.3) | async-done | bytes 32800 | tf_op jit(solution)/shard_map/all_to_all | solution.py:310
  (33 shorter events, 7.6 us)
Async XLA Ops:
  2.0 16.3 %all-to-all-start = ((f32[8,4,128]{2,1,0:T(4,128)}), f32[8,4,128]{2,1,0:T(4,128)S(1)}, u32[]{:S(2)}, u32[]{:S(2)}) async-start(f32[8,4,128]{2,1,0:T(4,128)} %get-tuple-element.11), calls=%async_computation | async-start | bytes 32768 | tf_op jit(solution)/shard_map/all_to_all | solution.py:282
  10.5 1.2 %collective-permute-start = (f32[4,128]{1,0:T(4,128)S(1)}, f32[4,128]{1,0:T(4,128)S(1)}, u32[]{:S(2)}, u32[]{:S(2)}) collective-permute-start(f32[4,128]{1,0:T(4,128)S(1)} %get-tuple-element.10), channel_id=1, source_target_pairs={{0,1},{1,0},{2,3},{3,2},{4,5},{5,4},{6,7},{7,6},{8,9},{9,8},{10,11... | collective-permute-start | bytes 6152 | tf_op jit(solution)/shard_map/ppermute | solution.py:264
  18.9 13.8 %all-to-all-start.1 = ((f32[16,8,128]{2,1,0:T(8,128)}), f32[16,8,128]{2,1,0:T(8,128)S(1)}, u32[]{:S(2)}, u32[]{:S(2)}) async-start(f32[16,8,128]{2,1,0:T(8,128)} %broadcast_in_dim.7), calls=%async_computation.1 | async-start | bytes 131072 | tf_op jit(solution)/shard_map/all_to_all | solution.py:288
  26.4 1.2 %collective-permute-start.1 = (f32[8,4,128]{2,1,0:T(4,128)S(1)}, f32[8,4,128]{2,1,0:T(4,128)S(1)}, u32[]{:S(2)}, u32[]{:S(2)}) collective-permute-start(f32[8,4,128]{2,1,0:T(4,128)S(1)} %all-to-all-done.refs_1_), channel_id=1, source_target_pairs={{0,1},{1,0},{2,3},{3,2},{4,5},{5,4},{6,7},{7,6},{8,9},{9,8},{10,11... | collective-permute-start | bytes 49160 | tf_op jit(solution)/shard_map/ppermute | solution.py:264
  36.6 5.6 %collective-permute-start.3 = (f32[128,128]{1,0:T(8,128)S(1)}, f32[128,128]{1,0:T(8,128)S(1)}, u32[]{:S(2)}, u32[]{:S(2)}) collective-permute-start(f32[128,128]{1,0:T(8,128)S(1)} %get-tuple-element.12), channel_id=1, source_target_pairs={{0,32},{32,64},{64,96},{96,128},{128,160},{160,192},{192,224},{224... | collective-permute-start | bytes 196616 | tf_op jit(solution)/shard_map/ppermute | solution.py:248
  37.3 4.9 %collective-permute-start.2 = (f32[128,128]{1,0:T(8,128)S(1)}, f32[128,128]{1,0:T(8,128)S(1)}, u32[]{:S(2)}, u32[]{:S(2)}) collective-permute-start(f32[128,128]{1,0:T(8,128)S(1)} %get-tuple-element.12), channel_id=1, source_target_pairs={{0,224},{32,0},{64,32},{96,64},{128,96},{160,128},{192,160},{224,1... | collective-permute-start | bytes 196616 | tf_op jit(solution)/shard_map/ppermute | solution.py:248
  39.9 7.4 %collective-permute-start.6 = (f32[128,128]{1,0:T(8,128)S(1)}, f32[128,128]{1,0:T(8,128)S(1)}, u32[]{:S(2)}, u32[]{:S(2)}) collective-permute-start(f32[128,128]{1,0:T(8,128)S(1)} %get-tuple-element.13), channel_id=1, source_target_pairs={{0,1},{1,0},{2,3},{3,2},{4,5},{5,4},{6,7},{7,6},{8,9},{9,8},{10,11... | collective-permute-start | bytes 196616 | tf_op jit(solution)/shard_map/ppermute | solution.py:264
  42.2 7.4 %collective-permute-start.5 = (f32[128,128]{1,0:T(8,128)S(1)}, f32[128,128]{1,0:T(8,128)S(1)}, u32[]{:S(2)}, u32[]{:S(2)}) collective-permute-start(f32[128,128]{1,0:T(8,128)S(1)} %get-tuple-element.20), channel_id=1, source_target_pairs={{0,96},{32,128},{64,160},{96,192},{128,224},{160,0},{192,32},{224,... | collective-permute-start | bytes 196616 | tf_op jit(solution)/shard_map/ppermute | solution.py:248
  43.5 6.6 %collective-permute-start.4 = (f32[128,128]{1,0:T(8,128)S(1)}, f32[128,128]{1,0:T(8,128)S(1)}, u32[]{:S(2)}, u32[]{:S(2)}) collective-permute-start(f32[128,128]{1,0:T(8,128)S(1)} %get-tuple-element.19), channel_id=1, source_target_pairs={{0,160},{32,192},{64,224},{96,0},{128,32},{160,64},{192,96},{224,1... | collective-permute-start | bytes 196616 | tf_op jit(solution)/shard_map/ppermute | solution.py:248
  50.0 6.0 %collective-permute-start.9 = (f32[128,128]{1,0:T(8,128)S(1)}, f32[128,128]{1,0:T(8,128)S(1)}, u32[]{:S(2)}, u32[]{:S(2)}) collective-permute-start(f32[128,128]{1,0:T(8,128)S(1)} %get-tuple-element.17), channel_id=1, source_target_pairs={{0,4},{2,6},{4,0},{6,2},{8,12},{10,14},{12,8},{14,10},{16,20},{18,... | collective-permute-start | bytes 196616 | tf_op jit(solution)/shard_map/ppermute | solution.py:248
  51.6 5.0 %collective-permute-start.8 = (f32[128,128]{1,0:T(8,128)S(1)}, f32[128,128]{1,0:T(8,128)S(1)}, u32[]{:S(2)}, u32[]{:S(2)}) collective-permute-start(f32[128,128]{1,0:T(8,128)S(1)} %get-tuple-element.17), channel_id=1, source_target_pairs={{0,6},{2,0},{4,2},{6,4},{8,14},{10,8},{12,10},{14,12},{16,22},{18,... | collective-permute-start | bytes 196616 | tf_op jit(solution)/shard_map/ppermute | solution.py:248
  52.9 4.3 %collective-permute-start.7 = (f32[128,128]{1,0:T(8,128)S(1)}, f32[128,128]{1,0:T(8,128)S(1)}, u32[]{:S(2)}, u32[]{:S(2)}) collective-permute-start(f32[128,128]{1,0:T(8,128)S(1)} %get-tuple-element.17), channel_id=1, source_target_pairs={{0,2},{2,4},{4,6},{6,0},{8,10},{10,12},{12,14},{14,8},{16,18},{18,... | collective-permute-start | bytes 196616 | tf_op jit(solution)/shard_map/ppermute | solution.py:248
  53.6 7.3 %collective-permute-start.13 = (f32[64,128]{1,0:T(8,128)S(1)}, f32[64,128]{1,0:T(8,128)S(1)}, u32[]{:S(2)}, u32[]{:S(2)}) collective-permute-start(f32[64,128]{1,0:T(8,128)S(1)} %slice.9), channel_id=1, source_target_pairs={{0,1},{1,0},{2,3},{3,2},{4,5},{5,4},{6,7},{7,6},{8,9},{9,8},{10,11... | collective-permute-start | bytes 98312 | tf_op jit(solution)/shard_map/ppermute | solution.py:264
  57.2 5.9 %collective-permute-start.12 = (f32[128,128]{1,0:T(8,128)S(1)}, f32[128,128]{1,0:T(8,128)S(1)}, u32[]{:S(2)}, u32[]{:S(2)}) collective-permute-start(f32[128,128]{1,0:T(8,128)S(1)} %add_add_fusion.1), channel_id=1, source_target_pairs={{0,16},{2,18},{4,20},{6,22},{8,24},{10,26},{12,28},{14,30},{16,0},... | collective-permute-start | bytes 196616 | tf_op jit(solution)/shard_map/ppermute | solution.py:248
  58.9 4.3 %collective-permute-start.11 = (f32[128,128]{1,0:T(8,128)S(1)}, f32[128,128]{1,0:T(8,128)S(1)}, u32[]{:S(2)}, u32[]{:S(2)}) collective-permute-start(f32[128,128]{1,0:T(8,128)S(1)} %add_add_fusion.1), channel_id=1, source_target_pairs={{0,24},{2,26},{4,28},{6,30},{8,0},{10,2},{12,4},{14,6},{16,8},{18,... | collective-permute-start | bytes 196616 | tf_op jit(solution)/shard_map/ppermute | solution.py:248
  60.7 5.5 %collective-permute-start.10 = (f32[128,128]{1,0:T(8,128)S(1)}, f32[128,128]{1,0:T(8,128)S(1)}, u32[]{:S(2)}, u32[]{:S(2)}) collective-permute-start(f32[128,128]{1,0:T(8,128)S(1)} %add_add_fusion.1), channel_id=1, source_target_pairs={{0,8},{2,10},{4,12},{6,14},{8,16},{10,18},{12,20},{14,22},{16,24},... | collective-permute-start | bytes 196616 | tf_op jit(solution)/shard_map/ppermute | solution.py:248
  69.5 12.6 %all-to-all-start.2 = ((f32[16,8,128]{2,1,0:T(8,128)}), f32[16,8,128]{2,1,0:T(8,128)S(1)}, u32[]{:S(2)}, u32[]{:S(2)}) async-start(f32[16,8,128]{2,1,0:T(8,128)} %get-tuple-element.15), calls=%async_computation.2 | async-start | bytes 131072 | tf_op jit(solution)/shard_map/all_to_all | solution.py:306
  75.7 6.4 %collective-permute-start.15 = (f32[64,128]{1,0:T(8,128)S(1)}, f32[64,128]{1,0:T(8,128)S(1)}, u32[]{:S(2)}, u32[]{:S(2)}) collective-permute-start(f32[64,128]{1,0:T(8,128)S(1)} %get-tuple-element.16), channel_id=1, source_target_pairs={{0,1},{1,0},{2,3},{3,2},{4,5},{5,4},{6,7},{7,6},{8,9},{9,8},{10,11... | collective-permute-start | bytes 98312 | tf_op jit(solution)/shard_map/ppermute | solution.py:264
  82.7 15.5 %all-to-all-start.3 = ((f32[8,8,128]{2,1,0:T(8,128)}), f32[8,8,128]{2,1,0:T(8,128)S(1)}, u32[]{:S(2)}, u32[]{:S(2)}) async-start(f32[8,8,128]{2,1,0:T(8,128)} %bitcast_select_fusion), calls=%async_computation.3 | async-start | bytes 65536 | tf_op jit(solution)/shard_map/all_to_all | solution.py:310
  90.2 1.2 %collective-permute-start.14 = (f32[8,128]{1,0:T(8,128)S(1)}, f32[8,128]{1,0:T(8,128)S(1)}, u32[]{:S(2)}, u32[]{:S(2)}) collective-permute-start(f32[8,128]{1,0:T(8,128)S(1)} %reduce_sum.9.ac_ref), channel_id=1, source_target_pairs={{0,1},{1,0},{2,3},{3,2},{4,5},{5,4},{6,7},{7,6},{8,9},{9,8},{10,11... | collective-permute-start | bytes 12296 | tf_op jit(solution)/shard_map/ppermute | solution.py:264

commit v7 on v6

--- a/solution.py
+++ b/solution.py
@@ -222,7 +222,7 @@
 
 def last_kernel(ac_ref, other_ref, bc_ref, a_ref, b_ref, c_ref, sum_a_ref, sum_b_ref):
     own, rank = a_ref.shape
-    sum_a_ref[...] = ac_ref[...] + other_ref[...]
+    sum_a_ref[...] = ac_ref[...] + other_ref[other_ref.shape[0] - ac_ref.shape[0] :, :]
     sum_b_ref[...] = jnp.sum(bc_ref[...], axis=0)
     mine = pl.ds(lax.axis_index("gz") * own, own)
     a_ref[...] = sum_a_ref[mine, :][:, :rank]
@@ -278,13 +278,13 @@
     wide = 2 * rank
 
     slots, mine = first_slots(factor_a, factor_b, factor_c, count_x)
-    other = swap(mine)
     along_x = lax.all_to_all(slots, "gx", 0, 0, tiled=True)
+    others = swap(jnp.concatenate([along_x, mine[None]], axis=0))
+    other = others[-1]
     rows_a = jnp.concatenate(
         [jnp.where(core == 0, mine, other), jnp.where(core == 0, other, mine)], axis=0
     )
     slot = jnp.where(lower_half(rows_a.shape), rows_a, along_x[:, 0])
-    other_x = swap(along_x)
     along_y = lax.all_to_all(jnp.broadcast_to(slot[None], (count_y, *slot.shape)), "gy", 0, 0, tiled=True)
 
     keep = tuple(1.0 / n for n in copies)
@@ -292,7 +292,7 @@
     sizes = tensor.shape
     tensor = tensor.reshape(count_i * count_j, count_k)
     shapes = ((count_i, wide), (count_k, wide))
-    a, cb, tensor = partials(True, keep, scale, (along_y, along_x, other_x), tensor, sizes, shapes)
+    a, cb, tensor = partials(True, keep, scale, (along_y, along_x, others), tensor, sizes, shapes)
     a = a + swap(a)
     cb = ring8(cb)
     ca = ring4(ring4(jnp.where(lower_half(cb.shape), cb, a), 1), 4)
@@ -302,13 +302,13 @@
     scale = tuple(1.0 / n for n in whole)
     shapes = ((count_y, 2 * own, wide), (count_j, wide))
     slots_ac, b = partials(False, (0.0,) * 3, scale, (ca, b), tensor, sizes, shapes)
-    b = b + swap(b)
     ac = jnp.sum(lax.all_to_all(slots_ac, "gy", 0, 0, tiled=True), axis=0)
-    other = swap(ac)
+    others = swap(jnp.concatenate([b, ac], axis=0))
+    b = b + others[:count_j]
     slots_b = b.reshape(count_x, 2 * own, wide)
     slots_bc = jnp.where(lower_half(slots_b.shape), slots_b, ac[:, None])
     bc = lax.all_to_all(slots_bc, "gx", 0, 0, tiled=True)
-    return last_sums(ac, other, bc, own, rank)
+    return last_sums(ac, others, bc, own, rank)
 
 
 def solution(mesh):

time: 99.2 us -> 98 us (0.988)
  the two profiles are of different devices: /device:TPU:2 before, /device:TPU:1 now
where the time goes in v7:
time: 98 us; the launch traced here: 97.7 us
  blocking collectives  52 us (53%)
  starting transfers between devices  26.7 us (27%)
  waiting for transfers between devices  10.1 us (10%)
  Pallas kernels  8.02 us (8%)
    all_to_all x1, blocking collectives, shards(): along_x = lax.all_to_all(slots, 'gx', 0, 0, tiled=True)  15.4 us
    ppermute x4, starting transfers between devices, swap(): return lax.ppermute(x, 'gz', [(0, 1), (1, 0)])  13.9 us
    all_to_all x1, blocking collectives, shards(): bc = lax.all_to_all(slots_bc, 'gx', 0, 0, tiled=True)  13.2 us
    all_to_all x1, blocking collectives, shards(): lax.all_to_all(jnp.broadcast_to(slot[None], (count_y, *slot.shape)), 'gy'...  13.1 us
    ppermute x10, starting transfers between devices, shift(): return lax.ppermute(x, axis, pairs)  12.8 us
    all_to_all x1, blocking collectives, shards(): ac = jnp.sum(lax.all_to_all(slots_ac, 'gy', 0, 0, tiled=True), axis=0)  10.3 us
    ppermute x10, waiting for transfers between devices, shift(): return lax.ppermute(x, axis, pairs)  8.44 us
    pallas_call x2, Pallas kernels, partials(): pl.pallas_call(functools.partial(round_kernel, first, keep, scale), out_s...  6.63 us
  transfers between devices with their start and end apart: 14, of which 6 were waited for; matrix products, arithmetic and copies ran while one was open for 0% of the time, Pallas kernels for 0%

profile of v7, /device:TPU:1, one launch (start us, length us, event | category | flops | bytes accessed | tf_op | source)
XLA Modules:
  0.0 97.7 jit_solution(17608862299237753898)
XLA Ops:
  0.6 0.8 first_slots.1
  1.4 15.4 %all_to_all.20.refs_1_ = f32[8,4,128]{2,1,0:T(4,128)S(1)} all-to-all(f32[8,4,128]{2,1,0:T(4,128)S(1)} %get-tuple-element.11), channel_id=1, replica_groups=mesh['gx'=8,'gy'=16,'gz'=2] {'gx'}, dimensions={0} | all-to-all | bytes 32768 | tf_op jit(solution)/shard_map/all_to_all | solution.py:281
  16.9 2.1 %collective-permute-start = (f32[9,4,128]{2,1,0:T(4,128)S(1)}, f32[9,4,128]{2,1,0:T(4,128)S(1)}, u32[]{:S(2)}, u32[]{:S(2)}) collective-permute-start(f32[9,4,128]{2,1,0:T(4,128)S(1)} %pad_maximum_fusion.1), channel_id=1, source_target_pairs={{0,1},{1,0},{2,3},{3,2},{4,5},{5,4},{6,7},{7,6},{8,9},{9,8},{10,11... | collective-permute-start | bytes 55304 | tf_op jit(solution)/shard_map/ppermute | solution.py:264
  19.0 0.8 collective-permute-done.refs_2_
  19.9 13.1 %all_to_all.21.refs_0_ = f32[16,8,128]{2,1,0:T(8,128)S(1)} all-to-all(f32[16,8,128]{2,1,0:T(8,128)S(1)} %broadcast_in_dim.19), channel_id=1, replica_groups=mesh['gx'=8,'gy'=16,'gz'=2] {'gy'}, dimensions={0} | all-to-all | bytes 131072 | tf_op jit(solution)/shard_map/all_to_all | solution.py:288
  32.9 3.9 %partials.2 = (f32[128,128]{1,0:T(8,128)S(1)}, f32[128,128]{1,0:T(8,128)S(1)}, f32[8192,128]{1,0:T(8,128)S(1)}) custom-call(f32[16,8,128]{2,1,0:T(8,128)S(1)} %all_to_all.21.refs_0_, f32[8,4,128]{2,1,0:T(4,128)S(1)} %all_to_all.20.refs_1_, f32[9,4,128]{2,1,0:T(4,128)S(1)} %collective-permute-done.refs_2_, f32[8192,128]{1,0:T(8,128)} %bitcast.16), custom_call_target="tpu_custom_call" | custom-call | flops 1073741824 | bytes 4194304 | tf_op jit(solution)/shard_map/partials/pallas_call | solution.py:171
  36.9 0.4 collective-permute-start.2
  37.3 2.3 %collective-permute-start.1 = (f32[128,128]{1,0:T(8,128)S(1)}, f32[128,128]{1,0:T(8,128)S(1)}, u32[]{:S(2)}, u32[]{:S(2)}) collective-permute-start(f32[128,128]{1,0:T(8,128)S(1)} %get-tuple-element.12), channel_id=1, source_target_pairs={{0,224},{32,0},{64,32},{96,64},{128,96},{160,128},{192,160},{224,1... | collective-permute-start | bytes 196616 | tf_op jit(solution)/shard_map/ppermute | solution.py:248
  39.6 2.3 %collective-permute-start.5 = (f32[128,128]{1,0:T(8,128)S(1)}, f32[128,128]{1,0:T(8,128)S(1)}, u32[]{:S(2)}, u32[]{:S(2)}) collective-permute-start(f32[128,128]{1,0:T(8,128)S(1)} %get-tuple-element.13), channel_id=1, source_target_pairs={{0,1},{1,0},{2,3},{3,2},{4,5},{5,4},{6,7},{7,6},{8,9},{9,8},{10,11... | collective-permute-start | bytes 196616 | tf_op jit(solution)/shard_map/ppermute | solution.py:264
  42.1 4.5 %collective-permute-start.3 = (f32[128,128]{1,0:T(8,128)S(1)}, f32[128,128]{1,0:T(8,128)S(1)}, u32[]{:S(2)}, u32[]{:S(2)}) collective-permute-start(f32[128,128]{1,0:T(8,128)S(1)} %get-tuple-element.19), channel_id=1, source_target_pairs={{0,160},{32,192},{64,224},{96,0},{128,32},{160,64},{192,96},{224,1... | collective-permute-start | bytes 196616 | tf_op jit(solution)/shard_map/ppermute | solution.py:248
  46.5 3.2 %collective-permute-done.4 = f32[128,128]{1,0:T(8,128)S(1)} collective-permute-done((f32[128,128]{1,0:T(8,128)S(1)}, f32[128,128]{1,0:T(8,128)S(1)}, u32[]{:S(2)}, u32[]{:S(2)}) %collective-permute-start.4) | collective-permute-done | bytes 65568 | tf_op jit(solution)/shard_map/ppermute | solution.py:248
  49.8 2.7 %collective-permute-start.7 = (f32[128,128]{1,0:T(8,128)S(1)}, f32[128,128]{1,0:T(8,128)S(1)}, u32[]{:S(2)}, u32[]{:S(2)}) collective-permute-start(f32[128,128]{1,0:T(8,128)S(1)} %get-tuple-element.17), channel_id=1, source_target_pairs={{0,6},{2,0},{4,2},{6,4},{8,14},{10,8},{12,10},{14,12},{16,22},{18,... | collective-permute-start | bytes 196616 | tf_op jit(solution)/shard_map/ppermute | solution.py:248
  52.5 3.4 %collective-permute-start.12 = (f32[64,128]{1,0:T(8,128)S(1)}, f32[64,128]{1,0:T(8,128)S(1)}, u32[]{:S(2)}, u32[]{:S(2)}) collective-permute-start(f32[64,128]{1,0:T(8,128)S(1)} %slice.18), channel_id=1, source_target_pairs={{0,1},{1,0},{2,3},{3,2},{4,5},{5,4},{6,7},{7,6},{8,9},{9,8},{10,11... | collective-permute-start | bytes 98312 | tf_op jit(solution)/shard_map/ppermute | solution.py:264
  55.9 1.0 collective-permute-done.6
  56.8 0.1 collective-permute-start.11
  56.9 2.6 %collective-permute-start.10 = (f32[128,128]{1,0:T(8,128)S(1)}, f32[128,128]{1,0:T(8,128)S(1)}, u32[]{:S(2)}, u32[]{:S(2)}) collective-permute-start(f32[128,128]{1,0:T(8,128)S(1)} %add_add_fusion.1), channel_id=1, source_target_pairs={{0,24},{2,26},{4,28},{6,30},{8,0},{10,2},{12,4},{14,6},{16,8},{18,... | collective-permute-start | bytes 196616 | tf_op jit(solution)/shard_map/ppermute | solution.py:248
  59.6 2.0 %collective-permute-done.11 = f32[128,128]{1,0:T(8,128)S(1)} collective-permute-done((f32[128,128]{1,0:T(8,128)S(1)}, f32[128,128]{1,0:T(8,128)S(1)}, u32[]{:S(2)}, u32[]{:S(2)}) %collective-permute-start.11) | collective-permute-done | bytes 65568 | tf_op jit(solution)/shard_map/ppermute | solution.py:248
  61.5 2.3 %collective-permute-done.9 = f32[128,128]{1,0:T(8,128)S(1)} collective-permute-done((f32[128,128]{1,0:T(8,128)S(1)}, f32[128,128]{1,0:T(8,128)S(1)}, u32[]{:S(2)}, u32[]{:S(2)}) %collective-permute-start.9) | collective-permute-done | bytes 65568 | tf_op jit(solution)/shard_map/ppermute | solution.py:248
  63.9 2.7 %partials.3 = (f32[16,8,128]{2,1,0:T(8,128)S(1)}, f32[64,128]{1,0:T(8,128)S(1)}) custom-call(f32[128,128]{1,0:T(8,128)S(1)} %add_add_fusion.refs_0_, f32[64,128]{1,0:T(8,128)S(1)} %slice_add_fusion.1.refs_1_, f32[8192,128]{1,0:T(8,128)S(1)} %get-tuple-element.14.refs_2_), custom_call_target="tpu_custom_call" | custom-call | flops 1073741824 | bytes 4194304 | tf_op jit(solution)/shard_map/partials/pallas_call | solution.py:171
  66.6 10.3 %all_to_all.22 = f32[16,8,128]{2,1,0:T(8,128)S(1)} all-to-all(f32[16,8,128]{2,1,0:T(8,128)S(1)} %get-tuple-element.15), channel_id=1, replica_groups=mesh['gx'=8,'gy'=16,'gz'=2] {'gy'}, dimensions={0} | all-to-all | bytes 131072 | tf_op jit(solution)/shard_map/all_to_all | solution.py:305
  77.0 6.1 %collective-permute-start.13 = (f32[72,128]{1,0:T(8,128)S(1)}, f32[72,128]{1,0:T(8,128)S(1)}, u32[]{:S(2)}, u32[]{:S(2)}) collective-permute-start(f32[72,128]{1,0:T(8,128)S(1)} %pad_maximum_fusion), channel_id=1, source_target_pairs={{0,1},{1,0},{2,3},{3,2},{4,5},{5,4},{6,7},{7,6},{8,9},{9,8},{10,11... | collective-permute-start | bytes 110600 | tf_op jit(solution)/shard_map/ppermute | solution.py:264
  83.1 0.9 collective-permute-done.13.other_ref
  84.0 13.2 %all_to_all.23.bc_ref = f32[8,8,128]{2,1,0:T(8,128)S(1)} all-to-all(f32[8,8,128]{2,1,0:T(8,128)S(1)} %fusion.1), channel_id=1, replica_groups=mesh['gx'=8,'gy'=16,'gz'=2] {'gx'}, dimensions={0} | all-to-all | bytes 65536 | tf_op jit(solution)/shard_map/all_to_all | solution.py:310
  97.1 0.6 last_sums.1
  (27 shorter events, 0.3 us)
Async XLA Ops:
  16.9 2.9 %collective-permute-start = (f32[9,4,128]{2,1,0:T(4,128)S(1)}, f32[9,4,128]{2,1,0:T(4,128)S(1)}, u32[]{:S(2)}, u32[]{:S(2)}) collective-permute-start(f32[9,4,128]{2,1,0:T(4,128)S(1)} %pad_maximum_fusion.1), channel_id=1, source_target_pairs={{0,1},{1,0},{2,3},{3,2},{4,5},{5,4},{6,7},{7,6},{8,9},{9,8},{10,11... | collective-permute-start | bytes 55304 | tf_op jit(solution)/shard_map/ppermute | solution.py:264
  36.9 5.1 %collective-permute-start.2 = (f32[128,128]{1,0:T(8,128)S(1)}, f32[128,128]{1,0:T(8,128)S(1)}, u32[]{:S(2)}, u32[]{:S(2)}) collective-permute-start(f32[128,128]{1,0:T(8,128)S(1)} %get-tuple-element.12), channel_id=1, source_target_pairs={{0,32},{32,64},{64,96},{96,128},{128,160},{160,192},{192,224},{224... | collective-permute-start | bytes 196616 | tf_op jit(solution)/shard_map/ppermute | solution.py:248
  37.3 4.7 %collective-permute-start.1 = (f32[128,128]{1,0:T(8,128)S(1)}, f32[128,128]{1,0:T(8,128)S(1)}, u32[]{:S(2)}, u32[]{:S(2)}) collective-permute-start(f32[128,128]{1,0:T(8,128)S(1)} %get-tuple-element.12), channel_id=1, source_target_pairs={{0,224},{32,0},{64,32},{96,64},{128,96},{160,128},{192,160},{224,1... | collective-permute-start | bytes 196616 | tf_op jit(solution)/shard_map/ppermute | solution.py:248
  39.6 6.9 %collective-permute-start.5 = (f32[128,128]{1,0:T(8,128)S(1)}, f32[128,128]{1,0:T(8,128)S(1)}, u32[]{:S(2)}, u32[]{:S(2)}) collective-permute-start(f32[128,128]{1,0:T(8,128)S(1)} %get-tuple-element.13), channel_id=1, source_target_pairs={{0,1},{1,0},{2,3},{3,2},{4,5},{5,4},{6,7},{7,6},{8,9},{9,8},{10,11... | collective-permute-start | bytes 196616 | tf_op jit(solution)/shard_map/ppermute | solution.py:264
  42.0 7.7 %collective-permute-start.4 = (f32[128,128]{1,0:T(8,128)S(1)}, f32[128,128]{1,0:T(8,128)S(1)}, u32[]{:S(2)}, u32[]{:S(2)}) collective-permute-start(f32[128,128]{1,0:T(8,128)S(1)} %get-tuple-element.20), channel_id=1, source_target_pairs={{0,96},{32,128},{64,160},{96,192},{128,224},{160,0},{192,32},{224,... | collective-permute-start | bytes 196616 | tf_op jit(solution)/shard_map/ppermute | solution.py:248
  42.1 7.6 %collective-permute-start.3 = (f32[128,128]{1,0:T(8,128)S(1)}, f32[128,128]{1,0:T(8,128)S(1)}, u32[]{:S(2)}, u32[]{:S(2)}) collective-permute-start(f32[128,128]{1,0:T(8,128)S(1)} %get-tuple-element.19), channel_id=1, source_target_pairs={{0,160},{32,192},{64,224},{96,0},{128,32},{160,64},{192,96},{224,1... | collective-permute-start | bytes 196616 | tf_op jit(solution)/shard_map/ppermute | solution.py:248
  49.7 6.1 %collective-permute-start.8 = (f32[128,128]{1,0:T(8,128)S(1)}, f32[128,128]{1,0:T(8,128)S(1)}, u32[]{:S(2)}, u32[]{:S(2)}) collective-permute-start(f32[128,128]{1,0:T(8,128)S(1)} %get-tuple-element.17), channel_id=1, source_target_pairs={{0,4},{2,6},{4,0},{6,2},{8,12},{10,14},{12,8},{14,10},{16,20},{18,... | collective-permute-start | bytes 196616 | tf_op jit(solution)/shard_map/ppermute | solution.py:248
  49.8 6.0 %collective-permute-start.7 = (f32[128,128]{1,0:T(8,128)S(1)}, f32[128,128]{1,0:T(8,128)S(1)}, u32[]{:S(2)}, u32[]{:S(2)}) collective-permute-start(f32[128,128]{1,0:T(8,128)S(1)} %get-tuple-element.17), channel_id=1, source_target_pairs={{0,6},{2,0},{4,2},{6,4},{8,14},{10,8},{12,10},{14,12},{16,22},{18,... | collective-permute-start | bytes 196616 | tf_op jit(solution)/shard_map/ppermute | solution.py:248
  52.5 4.3 %collective-permute-start.6 = (f32[128,128]{1,0:T(8,128)S(1)}, f32[128,128]{1,0:T(8,128)S(1)}, u32[]{:S(2)}, u32[]{:S(2)}) collective-permute-start(f32[128,128]{1,0:T(8,128)S(1)} %get-tuple-element.17), channel_id=1, source_target_pairs={{0,2},{2,4},{4,6},{6,0},{8,10},{10,12},{12,14},{14,8},{16,18},{18,... | collective-permute-start | bytes 196616 | tf_op jit(solution)/shard_map/ppermute | solution.py:248
  52.5 7.1 %collective-permute-start.12 = (f32[64,128]{1,0:T(8,128)S(1)}, f32[64,128]{1,0:T(8,128)S(1)}, u32[]{:S(2)}, u32[]{:S(2)}) collective-permute-start(f32[64,128]{1,0:T(8,128)S(1)} %slice.18), channel_id=1, source_target_pairs={{0,1},{1,0},{2,3},{3,2},{4,5},{5,4},{6,7},{7,6},{8,9},{9,8},{10,11... | collective-permute-start | bytes 98312 | tf_op jit(solution)/shard_map/ppermute | solution.py:264
  56.8 4.7 %collective-permute-start.11 = (f32[128,128]{1,0:T(8,128)S(1)}, f32[128,128]{1,0:T(8,128)S(1)}, u32[]{:S(2)}, u32[]{:S(2)}) collective-permute-start(f32[128,128]{1,0:T(8,128)S(1)} %add_add_fusion.1), channel_id=1, source_target_pairs={{0,16},{2,18},{4,20},{6,22},{8,24},{10,26},{12,28},{14,30},{16,0},... | collective-permute-start | bytes 196616 | tf_op jit(solution)/shard_map/ppermute | solution.py:248
  56.9 4.6 %collective-permute-start.10 = (f32[128,128]{1,0:T(8,128)S(1)}, f32[128,128]{1,0:T(8,128)S(1)}, u32[]{:S(2)}, u32[]{:S(2)}) collective-permute-start(f32[128,128]{1,0:T(8,128)S(1)} %add_add_fusion.1), channel_id=1, source_target_pairs={{0,24},{2,26},{4,28},{6,30},{8,0},{10,2},{12,4},{14,6},{16,8},{18,... | collective-permute-start | bytes 196616 | tf_op jit(solution)/shard_map/ppermute | solution.py:248
  59.5 4.3 %collective-permute-start.9 = (f32[128,128]{1,0:T(8,128)S(1)}, f32[128,128]{1,0:T(8,128)S(1)}, u32[]{:S(2)}, u32[]{:S(2)}) collective-permute-start(f32[128,128]{1,0:T(8,128)S(1)} %add_add_fusion.1), channel_id=1, source_target_pairs={{0,8},{2,10},{4,12},{6,14},{8,16},{10,18},{12,20},{14,22},{16,24},... | collective-permute-start | bytes 196616 | tf_op jit(solution)/shard_map/ppermute | solution.py:248
  77.0 7.0 %collective-permute-start.13 = (f32[72,128]{1,0:T(8,128)S(1)}, f32[72,128]{1,0:T(8,128)S(1)}, u32[]{:S(2)}, u32[]{:S(2)}) collective-permute-start(f32[72,128]{1,0:T(8,128)S(1)} %pad_maximum_fusion), channel_id=1, source_target_pairs={{0,1},{1,0},{2,3},{3,2},{4,5},{5,4},{6,7},{7,6},{8,9},{9,8},{10,11... | collective-permute-start | bytes 110600 | tf_op jit(solution)/shard_map/ppermute | solution.py:264

commit v8 on v7

--- a/solution.py
+++ b/solution.py
@@ -15,6 +15,7 @@
 VMEM = pl.BlockSpec(memory_space=pltpu.VMEM)
 HBM = pl.BlockSpec(memory_space=pltpu.HBM)
 CHUNK = 512
+OWN = 4
 
 
 def split(x):
@@ -44,20 +45,18 @@
     )
 
 
-def unpack_first(ac_ref, own_ref, other_ref, a2_ref, b2_ref, c2_ref):
-    slots, each, width = ac_ref.shape
+def unpack_first(all_ref, own_ref, other_ref, a2_ref, b2_ref, c2_ref):
     core = lax.axis_index("gz")
-    a2_ref[...] = from_lower(ac_ref[...].reshape(slots * each, width))
-    for g in range(each):
-        c2_ref[g * slots : (g + 1) * slots, :] = ac_ref[:, g, :]
-    c2_ref[...] = from_upper(c2_ref[...])
-    slots, each, width = own_ref.shape
-    for n in range(slots):
-        own, other = own_ref[n], other_ref[n]
-        at = 2 * each * n
-        b2_ref[at : at + each, :] = jnp.where(core == 0, own, other)
-        b2_ref[at + each : at + 2 * each, :] = jnp.where(core == 0, other, own)
-    b2_ref[...] = from_lower(b2_ref[...])
+    slots, tall, width = all_ref.shape
+    each = tall // 2
+    for ref in (a2_ref, b2_ref):
+        for n in range(ref.shape[0] // tall):
+            own, other = (x[n * each : (n + 1) * each, :] for x in (own_ref, other_ref))
+            ref[n * tall : n * tall + each, :] = jnp.where(core == 0, own, other)
+            ref[n * tall + each : (n + 1) * tall, :] = jnp.where(core == 0, other, own)
+    a2_ref[...] = from_lower(a2_ref[...])
+    b2_ref[...] = from_upper(b2_ref[...])
+    c2_ref[...] = all_ref.reshape(slots * tall, width)[pl.ds(each, slots, stride=tall), :]
 
 
 def unpack_second(ca_ref, b_ref, a2_ref, b2_ref, c2_ref):
@@ -74,18 +73,24 @@
     cb_ref[count_b:, :] = jnp.where(lower_half(c[count_b:].shape), c[count_b:], 0.0)
 
 
-def pack_second(a, b, c_ref, ac_ref, b_ref):
-    slots, each, width = ac_ref.shape
-    lower = lower_half((each, width))
-    for n in range(slots):
-        block = c_ref[pl.ds(n, each, stride=slots), :]
-        ac_ref[n, :, :] = jnp.where(lower, a[n * each : (n + 1) * each], block)
-    b_ref[...] = b
+def pack_second(a, b, c_ref, keep_ref, give_ref, out_c_ref):
+    core = lax.axis_index("gz")
+    out_c_ref[...] = c_ref[...]
+    each = OWN
+    for n in range(a.shape[0] // (2 * each)):
+        rows = slice(2 * each * n, 2 * each * (n + 1))
+        both = a[rows]
+        if n < b.shape[0] // (2 * each):
+            both = jnp.where(lower_half(both.shape), both, b[rows])
+        low, high = both[:each], both[each:]
+        keep_ref[n * each : (n + 1) * each, :] = jnp.where(core == 0, low, high)
+        give_ref[n * each : (n + 1) * each, :] = jnp.where(core == 0, high, low)
 
 
 def round_kernel(first, keep, scale, *refs):
-    n_small = 3 if first else 2
-    small, t_ref, outs, refs = refs[:n_small], refs[n_small], refs[n_small + 1 :][:2], refs[n_small + 3 :]
+    n_small, n_out = (3, 2) if first else (2, 3)
+    small, t_ref, refs = refs[:n_small], refs[n_small], refs[n_small + 1 :]
+    outs, refs = refs[:n_out], refs[n_out:]
     if first:
         t_hbm, t_ref, sems, refs = t_ref, refs[0], refs[-1], refs[1:-1]
     a2_ref, b2_ref, c2_ref, wc_ref, ma_ref = refs
@@ -187,7 +192,7 @@
     )(*small, tensor)
 
 
-def first_kernel(a_hbm, b_hbm, c_hbm, slots_ref, a_out_ref, a_ref, b_ref, c_ref, sems):
+def first_kernel(a_hbm, b_hbm, c_hbm, slots_ref, a_ref, b_ref, c_ref, sems):
     own, rank = a_ref.shape
     pairs = ((a_hbm, a_ref), (b_hbm, b_ref), (c_hbm, c_ref))
     copies = [pltpu.make_async_copy(x, y, sems.at[n]) for n, (x, y) in enumerate(pairs)]
@@ -195,9 +200,9 @@
         copy.start()
     for copy in copies:
         copy.wait()
-    a = a_ref[...]
-    a_out_ref[...] = jnp.concatenate([a, a], axis=1)
-    slot = jnp.concatenate([b_ref[...], jnp.broadcast_to(c_ref[...], (own, rank))], axis=1)
+    rows = jnp.concatenate([a_ref[...], b_ref[...]], axis=1)
+    c = jnp.broadcast_to(c_ref[...], (own, rank))
+    slot = jnp.concatenate([rows, jnp.concatenate([c, c], axis=1)], axis=0)
     for n in range(slots_ref.shape[0]):
         slots_ref[n, :, :] = slot
 
@@ -207,12 +212,9 @@
     factors = [pltpu.with_memory_space_constraint(x, pltpu.HBM) for x in (a, b, c)]
     return pl.pallas_call(
         first_kernel,
-        out_shape=(
-            jax.ShapeDtypeStruct((count, own, 2 * rank), F32),
-            jax.ShapeDtypeStruct((own, 2 * rank), F32),
-        ),
+        out_shape=jax.ShapeDtypeStruct((count, 2 * own, 2 * rank), F32),
         in_specs=[HBM] * 3,
-        out_specs=(VMEM, VMEM),
+        out_specs=VMEM,
         scratch_shapes=[pltpu.VMEM(x.shape, F32) for x in (a, b, c)]
         + [pltpu.SemaphoreType.DMA((3,))],
         compiler_params=pltpu.CompilerParams(vmem_limit_bytes=4 << 20),
@@ -220,24 +222,71 @@
     )(*factors)
 
 
-def last_kernel(ac_ref, other_ref, bc_ref, a_ref, b_ref, c_ref, sum_a_ref, sum_b_ref):
+def pick_kernel(count_x, count_y, all_ref, out_ref):
+    me_x, me_y = lax.axis_index("gx"), lax.axis_index("gy")
+    own = out_ref.shape[0] // count_y
+    for n in range(count_y):
+        rows = all_ref[me_x * count_y + n, :own, :]
+        if n < count_x:
+            rows = jnp.where(lower_half(rows.shape), rows, all_ref[n * count_y + me_y, :own, :])
+        out_ref[n * own : (n + 1) * own, :] = rows
+
+
+def pick(received, count_x, count_y):
+    _, tall, width = received.shape
+    return pl.pallas_call(
+        functools.partial(pick_kernel, count_x, count_y),
+        out_shape=jax.ShapeDtypeStruct((count_y * tall // 2, width), F32),
+        in_specs=[VMEM],
+        out_specs=VMEM,
+        compiler_params=pltpu.CompilerParams(vmem_limit_bytes=4 << 20),
+        name="pick",
+    )(received)
+
+
+def build_kernel(count_x, count_y, keep_ref, other_ref, c_ref, slots_ref):
+    own = keep_ref.shape[0] // count_y
+    rows = keep_ref[...] + other_ref[...]
+    rows = [rows[n * own : (n + 1) * own] for n in range(count_y)]
+    lower = lower_half(rows[0].shape)
+    for x in range(count_x):
+        for y in range(count_y):
+            n = x * count_y + y
+            slots_ref[n, :own, :] = jnp.where(lower, rows[y], rows[x])
+            slots_ref[n, own:, :] = jnp.broadcast_to(c_ref[n : n + 1, :], rows[0].shape)
+
+
+def build(keep, other, c, count_x, count_y):
+    own = keep.shape[0] // count_y
+    return pl.pallas_call(
+        functools.partial(build_kernel, count_x, count_y),
+        out_shape=jax.ShapeDtypeStruct((count_x * count_y, 2 * own, keep.shape[1]), F32),
+        in_specs=[VMEM] * 3,
+        out_specs=VMEM,
+        compiler_params=pltpu.CompilerParams(vmem_limit_bytes=4 << 20),
+        name="build",
+    )(keep, other, c)
+
+
+def last_kernel(count_x, count_y, all_ref, a_ref, b_ref, c_ref):
+    me_x, me_y = lax.axis_index("gx"), lax.axis_index("gy")
     own, rank = a_ref.shape
-    sum_a_ref[...] = ac_ref[...] + other_ref[other_ref.shape[0] - ac_ref.shape[0] :, :]
-    sum_b_ref[...] = jnp.sum(bc_ref[...], axis=0)
-    mine = pl.ds(lax.axis_index("gz") * own, own)
-    a_ref[...] = sum_a_ref[mine, :][:, :rank]
-    b_ref[...] = sum_b_ref[mine, :][:, :rank]
-    c_ref[...] = sum_b_ref[:1, :][:, rank:]
-
-
-def last_sums(ac, other, bc, own, rank):
-    return pl.pallas_call(
-        last_kernel,
+    slots, tall, width = all_ref.shape
+    a = sum(all_ref[me_x * count_y + n, :own, :] for n in range(count_y))
+    b = sum(all_ref[n * count_y + me_y, :own, :] for n in range(count_x))
+    c = all_ref.reshape(slots * tall, width)[pl.ds(own, slots, stride=tall), :]
+    a_ref[...] = a[:, :rank]
+    b_ref[...] = b[:, rank:]
+    c_ref[...] = jnp.sum(c, axis=0, keepdims=True)[:, :rank]
+
+
+def last_sums(received, count_x, count_y, own, rank):
+    return pl.pallas_call(
+        functools.partial(last_kernel, count_x, count_y),
         out_shape=tuple(jax.ShapeDtypeStruct((n, rank), F32) for n in (own, own, 1)),
-        scratch_shapes=[pltpu.VMEM(ac.shape, F32)] * 2,
         compiler_params=pltpu.CompilerParams(vmem_limit_bytes=4 << 20),
         name="last_sums",
-    )(ac, other, bc)
+    )(received)
 
 
 def shift(x, axis, stride, count, by):
@@ -266,7 +315,6 @@
 
 def shards(tensor, factor_a, factor_b, factor_c):
     count_x, count_y, count_z = (lax.axis_size(n) for n in ("gx", "gy", "gz"))
-    core = lax.axis_index("gz")
     count_i, count_j, count_k = tensor.shape
     whole = (
         float(count_j * count_y * count_k * count_z),
@@ -277,22 +325,17 @@
     own, rank = factor_a.shape
     wide = 2 * rank
 
-    slots, mine = first_slots(factor_a, factor_b, factor_c, count_x)
-    along_x = lax.all_to_all(slots, "gx", 0, 0, tiled=True)
-    others = swap(jnp.concatenate([along_x, mine[None]], axis=0))
-    other = others[-1]
-    rows_a = jnp.concatenate(
-        [jnp.where(core == 0, mine, other), jnp.where(core == 0, other, mine)], axis=0
-    )
-    slot = jnp.where(lower_half(rows_a.shape), rows_a, along_x[:, 0])
-    along_y = lax.all_to_all(jnp.broadcast_to(slot[None], (count_y, *slot.shape)), "gy", 0, 0, tiled=True)
+    slots = first_slots(factor_a, factor_b, factor_c, count_x * count_y)
+    received = lax.all_to_all(slots, ("gx", "gy"), 0, 0, tiled=True)
+    rows = pick(received, count_x, count_y)
+    small = (received, rows, swap(rows))
 
     keep = tuple(1.0 / n for n in copies)
     scale = tuple(-STEP_SIZE / n for n in whole)
     sizes = tensor.shape
     tensor = tensor.reshape(count_i * count_j, count_k)
     shapes = ((count_i, wide), (count_k, wide))
-    a, cb, tensor = partials(True, keep, scale, (along_y, along_x, others), tensor, sizes, shapes)
+    a, cb, tensor = partials(True, keep, scale, small, tensor, sizes, shapes)
     a = a + swap(a)
     cb = ring8(cb)
     ca = ring4(ring4(jnp.where(lower_half(cb.shape), cb, a), 1), 4)
@@ -300,15 +343,11 @@
     b = b + swap(b)
 
     scale = tuple(1.0 / n for n in whole)
-    shapes = ((count_y, 2 * own, wide), (count_j, wide))
-    slots_ac, b = partials(False, (0.0,) * 3, scale, (ca, b), tensor, sizes, shapes)
-    ac = jnp.sum(lax.all_to_all(slots_ac, "gy", 0, 0, tiled=True), axis=0)
-    others = swap(jnp.concatenate([b, ac], axis=0))
-    b = b + others[:count_j]
-    slots_b = b.reshape(count_x, 2 * own, wide)
-    slots_bc = jnp.where(lower_half(slots_b.shape), slots_b, ac[:, None])
-    bc = lax.all_to_all(slots_bc, "gx", 0, 0, tiled=True)
-    return last_sums(ac, others, bc, own, rank)
+    shapes = ((count_y * own, wide), (count_y * own, wide), (count_k, wide))
+    rows, other, c = partials(False, (0.0,) * 3, scale, (ca, b), tensor, sizes, shapes)
+    slots = build(rows, swap(other), c, count_x, count_y)
+    received = lax.all_to_all(slots, ("gx", "gy"), 0, 0, tiled=True)
+    return last_sums(received, count_x, count_y, own, rank)
 
 
 def solution(mesh):

time: 98 us -> 108 us (1.10)
  blocking collectives: 52 us -> 61.5 us
    all_to_all x4 -> x2, blocking collectives: 52 us -> 61.5 us  [shards(): received = lax.all_to_all(slots, ('gx', 'gy'), 0, 0, tiled=True)]
    ppermute x10, starting transfers between devices: 12.8 us -> 11.5 us  [shift(): return lax.ppermute(x, axis, pairs)]
  transfers between devices with their start and end apart: 14 -> 14, of which waited for: 6 -> 10; matrix products, arithmetic and copies ran while one was open for 0% -> 0% of each run, Pallas kernels for 0% -> 0%
where the time goes in v8:
time: 108 us
  blocking collectives  61.5 us (57%)
  starting transfers between devices  26.2 us (24%)
  waiting for transfers between devices  11.1 us (10%)
  Pallas kernels  8.14 us (8%)
    all_to_all x2, blocking collectives, shards(): received = lax.all_to_all(slots, ('gx', 'gy'), 0, 0, tiled=True)  61.5 us
    ppermute x4, starting transfers between devices, swap(): return lax.ppermute(x, 'gz', [(0, 1), (1, 0)])  14.7 us
    ppermute x10, starting transfers between devices, shift(): return lax.ppermute(x, axis, pairs)  11.5 us
    ppermute x10, waiting for transfers between devices, shift(): return lax.ppermute(x, axis, pairs)  9.39 us
    pallas_call x2, Pallas kernels, partials(): pl.pallas_call(functools.partial(round_kernel, first, keep, scale), out_s...  6.57 us
  transfers between devices with their start and end apart: 14, of which 10 were waited for; matrix products, arithmetic and copies ran while one was open for 0% of the time, Pallas kernels for 0%

profile of v8, /device:TPU:1, one launch (start us, length us, event | category | flops | bytes accessed | tf_op | source)
XLA Modules:
  0.0 107.8 jit_solution(3223411812788354902)
XLA Ops:
  0.6 0.8 first_slots.1
  1.5 34.4 %all_to_all.10.all_ref.refs_0_ = f32[128,8,128]{2,1,0:T(8,128)S(1)} all-to-all(f32[128,8,128]{2,1,0:T(8,128)S(1)} %first_slots.1), channel_id=1, replica_groups=mesh['gx'=8,'gy'=16,'gz'=2] {'gx','gy'}, dimensions={0} | all-to-all | bytes 1048576 | tf_op jit(solution)/shard_map/all_to_all | solution.py:329
  35.9 3.4 %collective-permute-start = (f32[64,128]{1,0:T(8,128)S(1)}, f32[64,128]{1,0:T(8,128)S(1)}, u32[]{:S(2)}, u32[]{:S(2)}) collective-permute-start(f32[64,128]{1,0:T(8,128)S(1)} %pick.1.refs_1_), channel_id=1, source_target_pairs={{0,1},{1,0},{2,3},{3,2},{4,5},{5,4},{6,7},{7,6},{8,9},{9,8},{10,11... | collective-permute-start | bytes 98312 | tf_op jit(solution)/shard_map/ppermute | solution.py:313
  39.3 0.9 collective-permute-done.refs_2_
  40.2 3.9 %partials.2 = (f32[128,128]{1,0:T(8,128)S(1)}, f32[128,128]{1,0:T(8,128)S(1)}, f32[8192,128]{1,0:T(8,128)S(1)}) custom-call(f32[128,8,128]{2,1,0:T(8,128)S(1)} %all_to_all.10.all_ref.refs_0_, f32[64,128]{1,0:T(8,128)S(1)} %pick.1.refs_1_, f32[64,128]{1,0:T(8,128)S(1)} %collective-permute-done.refs_2_, f32[8192,128]{1,0:T(8,128)} %bitcast.1), custom_call_target="tpu_custom_call" | custom-call | flops 1073741824 | bytes 4194304 | tf_op jit(solution)/shard_map/partials/pallas_call | solution.py:176
  44.2 1.5 %collective-permute-start.2 = (f32[128,128]{1,0:T(8,128)S(1)}, f32[128,128]{1,0:T(8,128)S(1)}, u32[]{:S(2)}, u32[]{:S(2)}) collective-permute-start(f32[128,128]{1,0:T(8,128)S(1)} %get-tuple-element.9), channel_id=1, source_target_pairs={{0,32},{32,64},{64,96},{96,128},{128,160},{160,192},{192,224},{224... | collective-permute-start | bytes 196616 | tf_op jit(solution)/shard_map/ppermute | solution.py:297
  45.6 0.9 collective-permute-start.5
  46.5 0.7 collective-permute-done.1
  47.3 1.3 %collective-permute-done.2 = f32[128,128]{1,0:T(8,128)S(1)} collective-permute-done((f32[128,128]{1,0:T(8,128)S(1)}, f32[128,128]{1,0:T(8,128)S(1)}, u32[]{:S(2)}, u32[]{:S(2)}) %collective-permute-start.2) | collective-permute-done | bytes 65568 | tf_op jit(solution)/shard_map/ppermute | solution.py:297
  48.7 3.3 %collective-permute-start.4 = (f32[128,128]{1,0:T(8,128)S(1)}, f32[128,128]{1,0:T(8,128)S(1)}, u32[]{:S(2)}, u32[]{:S(2)}) collective-permute-start(f32[128,128]{1,0:T(8,128)S(1)} %get-tuple-element.18), channel_id=1, source_target_pairs={{0,96},{32,128},{64,160},{96,192},{128,224},{160,0},{192,32},{224,... | collective-permute-start | bytes 196616 | tf_op jit(solution)/shard_map/ppermute | solution.py:297
  51.9 1.8 %collective-permute-done.3 = f32[128,128]{1,0:T(8,128)S(1)} collective-permute-done((f32[128,128]{1,0:T(8,128)S(1)}, f32[128,128]{1,0:T(8,128)S(1)}, u32[]{:S(2)}, u32[]{:S(2)}) %collective-permute-start.3) | collective-permute-done | bytes 65568 | tf_op jit(solution)/shard_map/ppermute | solution.py:297
  53.7 1.2 %collective-permute-done.4 = f32[128,128]{1,0:T(8,128)S(1)} collective-permute-done((f32[128,128]{1,0:T(8,128)S(1)}, f32[128,128]{1,0:T(8,128)S(1)}, u32[]{:S(2)}, u32[]{:S(2)}) %collective-permute-start.4) | collective-permute-done | bytes 65568 | tf_op jit(solution)/shard_map/ppermute | solution.py:297
  55.3 2.4 %collective-permute-start.7 = (f32[128,128]{1,0:T(8,128)S(1)}, f32[128,128]{1,0:T(8,128)S(1)}, u32[]{:S(2)}, u32[]{:S(2)}) collective-permute-start(f32[128,128]{1,0:T(8,128)S(1)} %get-tuple-element.15), channel_id=1, source_target_pairs={{0,6},{2,0},{4,2},{6,4},{8,14},{10,8},{12,10},{14,12},{16,22},{18,... | collective-permute-start | bytes 196616 | tf_op jit(solution)/shard_map/ppermute | solution.py:297
  58.1 3.7 %collective-permute-start.12 = (f32[64,128]{1,0:T(8,128)S(1)}, f32[64,128]{1,0:T(8,128)S(1)}, u32[]{:S(2)}, u32[]{:S(2)}) collective-permute-start(f32[64,128]{1,0:T(8,128)S(1)} %slice.4), channel_id=1, source_target_pairs={{0,1},{1,0},{2,3},{3,2},{4,5},{5,4},{6,7},{7,6},{8,9},{9,8},{10,11... | collective-permute-start | bytes 98312 | tf_op jit(solution)/shard_map/ppermute | solution.py:313
  61.8 0.8 collective-permute-done.8
  62.7 1.5 %collective-permute-start.10 = (f32[128,128]{1,0:T(8,128)S(1)}, f32[128,128]{1,0:T(8,128)S(1)}, u32[]{:S(2)}, u32[]{:S(2)}) collective-permute-start(f32[128,128]{1,0:T(8,128)S(1)} %add_add_fusion.1), channel_id=1, source_target_pairs={{0,24},{2,26},{4,28},{6,30},{8,0},{10,2},{12,4},{14,6},{16,8},{18,... | collective-permute-start | bytes 196616 | tf_op jit(solution)/shard_map/ppermute | solution.py:297
  64.2 1.1 %collective-permute-start.11 = (f32[128,128]{1,0:T(8,128)S(1)}, f32[128,128]{1,0:T(8,128)S(1)}, u32[]{:S(2)}, u32[]{:S(2)}) collective-permute-start(f32[128,128]{1,0:T(8,128)S(1)} %add_add_fusion.1), channel_id=1, source_target_pairs={{0,16},{2,18},{4,20},{6,22},{8,24},{10,26},{12,28},{14,30},{16,0},... | collective-permute-start | bytes 196616 | tf_op jit(solution)/shard_map/ppermute | solution.py:297
  65.3 0.8 collective-permute-start.9
  66.3 2.5 %collective-permute-done.11 = f32[128,128]{1,0:T(8,128)S(1)} collective-permute-done((f32[128,128]{1,0:T(8,128)S(1)}, f32[128,128]{1,0:T(8,128)S(1)}, u32[]{:S(2)}, u32[]{:S(2)}) %collective-permute-start.11) | collective-permute-done | bytes 65568 | tf_op jit(solution)/shard_map/ppermute | solution.py:297
  68.8 0.8 collective-permute-done.9
  69.7 2.7 %partials.3 = (f32[64,128]{1,0:T(8,128)S(1)}, f32[64,128]{1,0:T(8,128)S(1)}, f32[128,128]{1,0:T(8,128)S(1)}) custom-call(f32[128,128]{1,0:T(8,128)S(1)} %add_add_fusion.refs_0_, f32[64,128]{1,0:T(8,128)S(1)} %slice_add_fusion.refs_1_, f32[8192,128]{1,0:T(8,128)S(1)} %get-tuple-element.11.refs_2_), custom_call_target="tpu_custom_call" | custom-call | flops 1073741824 | bytes 4194304 | tf_op jit(solution)/shard_map/partials/pallas_call | solution.py:176
  72.3 6.8 %collective-permute-start.13 = (f32[64,128]{1,0:T(8,128)S(1)}, f32[64,128]{1,0:T(8,128)S(1)}, u32[]{:S(2)}, u32[]{:S(2)}) collective-permute-start(f32[64,128]{1,0:T(8,128)S(1)} %get-tuple-element.13), channel_id=1, source_target_pairs={{0,1},{1,0},{2,3},{3,2},{4,5},{5,4},{6,7},{7,6},{8,9},{9,8},{10,11... | collective-permute-start | bytes 98312 | tf_op jit(solution)/shard_map/ppermute | solution.py:313
  79.1 0.9 collective-permute-done.13.other_ref
  80.0 27.1 %all_to_all.11.all_ref = f32[128,8,128]{2,1,0:T(8,128)S(1)} all-to-all(f32[128,8,128]{2,1,0:T(8,128)S(1)} %build.1), channel_id=1, replica_groups=mesh['gx'=8,'gy'=16,'gz'=2] {'gx','gy'}, dimensions={0} | all-to-all | bytes 1048576 | tf_op jit(solution)/shard_map/all_to_all | solution.py:349
  (19 shorter events, 2.0 us)
Async XLA Ops:
  35.9 4.3 %collective-permute-start = (f32[64,128]{1,0:T(8,128)S(1)}, f32[64,128]{1,0:T(8,128)S(1)}, u32[]{:S(2)}, u32[]{:S(2)}) collective-permute-start(f32[64,128]{1,0:T(8,128)S(1)} %pick.1.refs_1_), channel_id=1, source_target_pairs={{0,1},{1,0},{2,3},{3,2},{4,5},{5,4},{6,7},{7,6},{8,9},{9,8},{10,11... | collective-permute-start | bytes 98312 | tf_op jit(solution)/shard_map/ppermute | solution.py:313
  44.1 3.2 %collective-permute-start.1 = (f32[128,128]{1,0:T(8,128)S(1)}, f32[128,128]{1,0:T(8,128)S(1)}, u32[]{:S(2)}, u32[]{:S(2)}) collective-permute-start(f32[128,128]{1,0:T(8,128)S(1)} %get-tuple-element.9), channel_id=1, source_target_pairs={{0,224},{32,0},{64,32},{96,64},{128,96},{160,128},{192,160},{224,1... | collective-permute-start | bytes 196616 | tf_op jit(solution)/shard_map/ppermute | solution.py:297
  44.2 4.4 %collective-permute-start.2 = (f32[128,128]{1,0:T(8,128)S(1)}, f32[128,128]{1,0:T(8,128)S(1)}, u32[]{:S(2)}, u32[]{:S(2)}) collective-permute-start(f32[128,128]{1,0:T(8,128)S(1)} %get-tuple-element.9), channel_id=1, source_target_pairs={{0,32},{32,64},{64,96},{96,128},{128,160},{160,192},{192,224},{224... | collective-permute-start | bytes 196616 | tf_op jit(solution)/shard_map/ppermute | solution.py:297
  45.6 6.3 %collective-permute-start.5 = (f32[128,128]{1,0:T(8,128)S(1)}, f32[128,128]{1,0:T(8,128)S(1)}, u32[]{:S(2)}, u32[]{:S(2)}) collective-permute-start(f32[128,128]{1,0:T(8,128)S(1)} %get-tuple-element.10), channel_id=1, source_target_pairs={{0,1},{1,0},{2,3},{3,2},{4,5},{5,4},{6,7},{7,6},{8,9},{9,8},{10,11... | collective-permute-start | bytes 196616 | tf_op jit(solution)/shard_map/ppermute | solution.py:313
  48.6 5.1 %collective-permute-start.3 = (f32[128,128]{1,0:T(8,128)S(1)}, f32[128,128]{1,0:T(8,128)S(1)}, u32[]{:S(2)}, u32[]{:S(2)}) collective-permute-start(f32[128,128]{1,0:T(8,128)S(1)} %get-tuple-element.17), channel_id=1, source_target_pairs={{0,160},{32,192},{64,224},{96,0},{128,32},{160,64},{192,96},{224,1... | collective-permute-start | bytes 196616 | tf_op jit(solution)/shard_map/ppermute | solution.py:297
  48.7 6.2 %collective-permute-start.4 = (f32[128,128]{1,0:T(8,128)S(1)}, f32[128,128]{1,0:T(8,128)S(1)}, u32[]{:S(2)}, u32[]{:S(2)}) collective-permute-start(f32[128,128]{1,0:T(8,128)S(1)} %get-tuple-element.18), channel_id=1, source_target_pairs={{0,96},{32,128},{64,160},{96,192},{128,224},{160,0},{192,32},{224,... | collective-permute-start | bytes 196616 | tf_op jit(solution)/shard_map/ppermute | solution.py:297
  54.9 6.9 %collective-permute-start.6 = (f32[128,128]{1,0:T(8,128)S(1)}, f32[128,128]{1,0:T(8,128)S(1)}, u32[]{:S(2)}, u32[]{:S(2)}) collective-permute-start(f32[128,128]{1,0:T(8,128)S(1)} %get-tuple-element.15), channel_id=1, source_target_pairs={{0,2},{2,4},{4,6},{6,0},{8,10},{10,12},{12,14},{14,8},{16,18},{18,... | collective-permute-start | bytes 196616 | tf_op jit(solution)/shard_map/ppermute | solution.py:297
  55.3 6.5 %collective-permute-start.7 = (f32[128,128]{1,0:T(8,128)S(1)}, f32[128,128]{1,0:T(8,128)S(1)}, u32[]{:S(2)}, u32[]{:S(2)}) collective-permute-start(f32[128,128]{1,0:T(8,128)S(1)} %get-tuple-element.15), channel_id=1, source_target_pairs={{0,6},{2,0},{4,2},{6,4},{8,14},{10,8},{12,10},{14,12},{16,22},{18,... | collective-permute-start | bytes 196616 | tf_op jit(solution)/shard_map/ppermute | solution.py:297
  57.7 4.9 %collective-permute-start.8 = (f32[128,128]{1,0:T(8,128)S(1)}, f32[128,128]{1,0:T(8,128)S(1)}, u32[]{:S(2)}, u32[]{:S(2)}) collective-permute-start(f32[128,128]{1,0:T(8,128)S(1)} %get-tuple-element.15), channel_id=1, source_target_pairs={{0,4},{2,6},{4,0},{6,2},{8,12},{10,14},{12,8},{14,10},{16,20},{18,... | collective-permute-start | bytes 196616 | tf_op jit(solution)/shard_map/ppermute | solution.py:297
  58.1 7.9 %collective-permute-start.12 = (f32[64,128]{1,0:T(8,128)S(1)}, f32[64,128]{1,0:T(8,128)S(1)}, u32[]{:S(2)}, u32[]{:S(2)}) collective-permute-start(f32[64,128]{1,0:T(8,128)S(1)} %slice.4), channel_id=1, source_target_pairs={{0,1},{1,0},{2,3},{3,2},{4,5},{5,4},{6,7},{7,6},{8,9},{9,8},{10,11... | collective-permute-start | bytes 98312 | tf_op jit(solution)/shard_map/ppermute | solution.py:313
  62.7 3.7 %collective-permute-start.10 = (f32[128,128]{1,0:T(8,128)S(1)}, f32[128,128]{1,0:T(8,128)S(1)}, u32[]{:S(2)}, u32[]{:S(2)}) collective-permute-start(f32[128,128]{1,0:T(8,128)S(1)} %add_add_fusion.1), channel_id=1, source_target_pairs={{0,24},{2,26},{4,28},{6,30},{8,0},{10,2},{12,4},{14,6},{16,8},{18,... | collective-permute-start | bytes 196616 | tf_op jit(solution)/shard_map/ppermute | solution.py:297
  64.2 4.6 %collective-permute-start.11 = (f32[128,128]{1,0:T(8,128)S(1)}, f32[128,128]{1,0:T(8,128)S(1)}, u32[]{:S(2)}, u32[]{:S(2)}) collective-permute-start(f32[128,128]{1,0:T(8,128)S(1)} %add_add_fusion.1), channel_id=1, source_target_pairs={{0,16},{2,18},{4,20},{6,22},{8,24},{10,26},{12,28},{14,30},{16,0},... | collective-permute-start | bytes 196616 | tf_op jit(solution)/shard_map/ppermute | solution.py:297
  65.3 4.3 %collective-permute-start.9 = (f32[128,128]{1,0:T(8,128)S(1)}, f32[128,128]{1,0:T(8,128)S(1)}, u32[]{:S(2)}, u32[]{:S(2)}) collective-permute-start(f32[128,128]{1,0:T(8,128)S(1)} %add_add_fusion.1), channel_id=1, source_target_pairs={{0,8},{2,10},{4,12},{6,14},{8,16},{10,18},{12,20},{14,22},{16,24},... | collective-permute-start | bytes 196616 | tf_op jit(solution)/shard_map/ppermute | solution.py:297
  72.3 7.6 %collective-permute-start.13 = (f32[64,128]{1,0:T(8,128)S(1)}, f32[64,128]{1,0:T(8,128)S(1)}, u32[]{:S(2)}, u32[]{:S(2)}) collective-permute-start(f32[64,128]{1,0:T(8,128)S(1)} %get-tuple-element.13), channel_id=1, source_target_pairs={{0,1},{1,0},{2,3},{3,2},{4,5},{5,4},{6,7},{7,6},{8,9},{9,8},{10,11... | collective-permute-start | bytes 98312 | tf_op jit(solution)/shard_map/ppermute | solution.py:313

commit v9 on v7

--- a/solution.py
+++ b/solution.py
@@ -75,11 +75,15 @@
 
 
 def pack_second(a, b, c_ref, ac_ref, b_ref):
+    core = lax.axis_index("gz")
     slots, each, width = ac_ref.shape
-    lower = lower_half((each, width))
+    own, apart = a.shape[0] // slots, c_ref.shape[0] // each
+    lower = lower_half((own, width))
     for n in range(slots):
-        block = c_ref[pl.ds(n, each, stride=slots), :]
-        ac_ref[n, :, :] = jnp.where(lower, a[n * each : (n + 1) * each], block)
+        block = c_ref[pl.ds(n // 2, each, stride=apart), :]
+        block = jnp.where(core == n % 2, block, 0.0)
+        ac_ref[n, :own, :] = jnp.where(lower, a[n * own : (n + 1) * own], block[:own])
+        ac_ref[n, own:, :] = block[own:]
     b_ref[...] = b
 
 
@@ -220,24 +224,47 @@
     )(*factors)
 
 
-def last_kernel(ac_ref, other_ref, bc_ref, a_ref, b_ref, c_ref, sum_a_ref, sum_b_ref):
+def middle_kernel(received_ref, b_ref, ac_ref, slots_ref):
+    core = lax.axis_index("gz")
+    slots, own, width = slots_ref.shape
+    ac_ref[...] = jnp.sum(received_ref[...], axis=0)
+    lower = lower_half((own, width))
+    for n in range(slots):
+        c = jnp.broadcast_to(ac_ref[n // 2 : n // 2 + 1, :], (own, width))
+        c = jnp.where(core == n % 2, c, 0.0)
+        slots_ref[n, :, :] = jnp.where(lower, b_ref[n * own : (n + 1) * own, :], c)
+
+
+def middle(received, b, own):
+    _, each, width = received.shape
+    return pl.pallas_call(
+        middle_kernel,
+        out_shape=(
+            jax.ShapeDtypeStruct((each, width), F32),
+            jax.ShapeDtypeStruct((b.shape[0] // own, own, width), F32),
+        ),
+        in_specs=[VMEM] * 2,
+        out_specs=(VMEM,) * 2,
+        compiler_params=pltpu.CompilerParams(vmem_limit_bytes=4 << 20),
+        name="middle",
+    )(received, b)
+
+
+def last_kernel(ac_ref, bc_ref, a_ref, b_ref, c_ref):
     own, rank = a_ref.shape
-    sum_a_ref[...] = ac_ref[...] + other_ref[other_ref.shape[0] - ac_ref.shape[0] :, :]
-    sum_b_ref[...] = jnp.sum(bc_ref[...], axis=0)
-    mine = pl.ds(lax.axis_index("gz") * own, own)
-    a_ref[...] = sum_a_ref[mine, :][:, :rank]
-    b_ref[...] = sum_b_ref[mine, :][:, :rank]
-    c_ref[...] = sum_b_ref[:1, :][:, rank:]
-
-
-def last_sums(ac, other, bc, own, rank):
+    bc = jnp.sum(bc_ref[...], axis=0)
+    a_ref[...] = ac_ref[:own, :][:, :rank]
+    b_ref[...] = bc[:, :rank]
+    c_ref[...] = bc[:1, rank:]
+
+
+def last_sums(ac, bc, own, rank):
     return pl.pallas_call(
         last_kernel,
         out_shape=tuple(jax.ShapeDtypeStruct((n, rank), F32) for n in (own, own, 1)),
-        scratch_shapes=[pltpu.VMEM(ac.shape, F32)] * 2,
         compiler_params=pltpu.CompilerParams(vmem_limit_bytes=4 << 20),
         name="last_sums",
-    )(ac, other, bc)
+    )(ac, bc)
 
 
 def shift(x, axis, stride, count, by):
@@ -300,15 +327,12 @@
     b = b + swap(b)
 
     scale = tuple(1.0 / n for n in whole)
-    shapes = ((count_y, 2 * own, wide), (count_j, wide))
-    slots_ac, b = partials(False, (0.0,) * 3, scale, (ca, b), tensor, sizes, shapes)
-    ac = jnp.sum(lax.all_to_all(slots_ac, "gy", 0, 0, tiled=True), axis=0)
-    others = swap(jnp.concatenate([b, ac], axis=0))
-    b = b + others[:count_j]
-    slots_b = b.reshape(count_x, 2 * own, wide)
-    slots_bc = jnp.where(lower_half(slots_b.shape), slots_b, ac[:, None])
-    bc = lax.all_to_all(slots_bc, "gx", 0, 0, tiled=True)
-    return last_sums(ac, others, bc, own, rank)
+    shapes = ((count_y * count_z, count_x, wide), (count_j, wide))
+    slots, b = partials(False, (0.0,) * 3, scale, (ca, b), tensor, sizes, shapes)
+    received = lax.all_to_all(slots, ("gy", "gz"), 0, 0, tiled=True)
+    ac, slots = middle(received, b, own)
+    bc = lax.all_to_all(slots, ("gx", "gz"), 0, 0, tiled=True)
+    return last_sums(ac, bc, own, rank)
 
 
 def solution(mesh):

time: 98 us -> 98.4 us (level)
  blocking collectives: 52 us -> 59.3 us
  starting transfers between devices: 26.7 us -> 20.6 us
    all_to_all x2, blocking collectives: 23.5 us -> 30.8 us  [the longest x1 16.5 us: shards(): received = lax.all_to_all(slots, ('gy', 'gz'), 0, 0, tiled=True)]
    ppermute x4 -> x3, starting transfers between devices: 13.9 us -> 7.79 us  [swap(): return lax.ppermute(x, 'gz', [(0, 1), (1, 0)])]
  transfers between devices with their start and end apart: 14 -> 13, of which waited for: 6 -> 5; matrix products, arithmetic and copies ran while one was open for 0% -> 0% of each run, Pallas kernels for 0% -> 0%
where the time goes in v9:
time: 98.4 us; the launch traced here: 98.1 us
  blocking collectives  59.3 us (60%)
  starting transfers between devices  20.6 us (21%)
  waiting for transfers between devices  9.27 us (9%)
  Pallas kernels  8.09 us (8%)
    all_to_all x1, blocking collectives, shards(): received = lax.all_to_all(slots, ('gy', 'gz'), 0, 0, tiled=True)  16.5 us
    all_to_all x1, blocking collectives, shards(): along_x = lax.all_to_all(slots, 'gx', 0, 0, tiled=True)  15.4 us
    all_to_all x1, blocking collectives, shards(): bc = lax.all_to_all(slots, ('gx', 'gz'), 0, 0, tiled=True)  14.3 us
    all_to_all x1, blocking collectives, shards(): lax.all_to_all(jnp.broadcast_to(slot[None], (count_y, *slot.shape)), 'gy'...  13.1 us
    ppermute x10, starting transfers between devices, shift(): return lax.ppermute(x, axis, pairs)  12.8 us
    ppermute x10, waiting for transfers between devices, shift(): return lax.ppermute(x, axis, pairs)  8.44 us
    ppermute x3, starting transfers between devices, swap(): return lax.ppermute(x, 'gz', [(0, 1), (1, 0)])  7.79 us
    pallas_call x2, Pallas kernels, partials(): pl.pallas_call(functools.partial(round_kernel, first, keep, scale), out_s...  6.65 us
  transfers between devices with their start and end apart: 13, of which 5 were waited for; matrix products, arithmetic and copies ran while one was open for 0% of the time, Pallas kernels for 0%

profile of v9, /device:TPU:1, one launch (start us, length us, event | category | flops | bytes accessed | tf_op | source)
XLA Modules:
  0.0 98.1 jit_solution(4968412605467537713)
XLA Ops:
  0.6 0.8 first_slots.1
  1.4 15.4 %all_to_all.20.refs_1_ = f32[8,4,128]{2,1,0:T(4,128)S(1)} all-to-all(f32[8,4,128]{2,1,0:T(4,128)S(1)} %get-tuple-element.13), channel_id=1, replica_groups=mesh['gx'=8,'gy'=16,'gz'=2] {'gx'}, dimensions={0} | all-to-all | bytes 32768 | tf_op jit(solution)/shard_map/all_to_all | solution.py:308
  16.9 2.1 %collective-permute-start = (f32[9,4,128]{2,1,0:T(4,128)S(1)}, f32[9,4,128]{2,1,0:T(4,128)S(1)}, u32[]{:S(2)}, u32[]{:S(2)}) collective-permute-start(f32[9,4,128]{2,1,0:T(4,128)S(1)} %pad_maximum_fusion), channel_id=1, source_target_pairs={{0,1},{1,0},{2,3},{3,2},{4,5},{5,4},{6,7},{7,6},{8,9},{9,8},{10,11... | collective-permute-start | bytes 55304 | tf_op jit(solution)/shard_map/ppermute | solution.py:291
  19.0 0.8 collective-permute-done.refs_2_
  19.9 13.1 %all_to_all.21.refs_0_ = f32[16,8,128]{2,1,0:T(8,128)S(1)} all-to-all(f32[16,8,128]{2,1,0:T(8,128)S(1)} %broadcast_in_dim.10), channel_id=1, replica_groups=mesh['gx'=8,'gy'=16,'gz'=2] {'gy'}, dimensions={0} | all-to-all | bytes 131072 | tf_op jit(solution)/shard_map/all_to_all | solution.py:315
  32.9 3.9 %partials.2 = (f32[128,128]{1,0:T(8,128)S(1)}, f32[128,128]{1,0:T(8,128)S(1)}, f32[8192,128]{1,0:T(8,128)S(1)}) custom-call(f32[16,8,128]{2,1,0:T(8,128)S(1)} %all_to_all.21.refs_0_, f32[8,4,128]{2,1,0:T(4,128)S(1)} %all_to_all.20.refs_1_, f32[9,4,128]{2,1,0:T(4,128)S(1)} %collective-permute-done.refs_2_, f32[8192,128]{1,0:T(8,128)} %bitcast.12), custom_call_target="tpu_custom_call" | custom-call | flops 1073741824 | bytes 4194304 | tf_op jit(solution)/shard_map/partials/pallas_call | solution.py:175
  36.9 0.4 collective-permute-start.2
  37.3 2.3 %collective-permute-start.1 = (f32[128,128]{1,0:T(8,128)S(1)}, f32[128,128]{1,0:T(8,128)S(1)}, u32[]{:S(2)}, u32[]{:S(2)}) collective-permute-start(f32[128,128]{1,0:T(8,128)S(1)} %get-tuple-element.14), channel_id=1, source_target_pairs={{0,224},{32,0},{64,32},{96,64},{128,96},{160,128},{192,160},{224,1... | collective-permute-start | bytes 196616 | tf_op jit(solution)/shard_map/ppermute | solution.py:275
  39.6 2.3 %collective-permute-start.5 = (f32[128,128]{1,0:T(8,128)S(1)}, f32[128,128]{1,0:T(8,128)S(1)}, u32[]{:S(2)}, u32[]{:S(2)}) collective-permute-start(f32[128,128]{1,0:T(8,128)S(1)} %get-tuple-element.15), channel_id=1, source_target_pairs={{0,1},{1,0},{2,3},{3,2},{4,5},{5,4},{6,7},{7,6},{8,9},{9,8},{10,11... | collective-permute-start | bytes 196616 | tf_op jit(solution)/shard_map/ppermute | solution.py:291
  42.0 0.1 collective-permute-start.4
  42.1 4.5 %collective-permute-start.3 = (f32[128,128]{1,0:T(8,128)S(1)}, f32[128,128]{1,0:T(8,128)S(1)}, u32[]{:S(2)}, u32[]{:S(2)}) collective-permute-start(f32[128,128]{1,0:T(8,128)S(1)} %get-tuple-element.23), channel_id=1, source_target_pairs={{0,160},{32,192},{64,224},{96,0},{128,32},{160,64},{192,96},{224,1... | collective-permute-start | bytes 196616 | tf_op jit(solution)/shard_map/ppermute | solution.py:275
  46.5 3.2 %collective-permute-done.4 = f32[128,128]{1,0:T(8,128)S(1)} collective-permute-done((f32[128,128]{1,0:T(8,128)S(1)}, f32[128,128]{1,0:T(8,128)S(1)}, u32[]{:S(2)}, u32[]{:S(2)}) %collective-permute-start.4) | collective-permute-done | bytes 65568 | tf_op jit(solution)/shard_map/ppermute | solution.py:275
  49.7 0.1 collective-permute-start.8
  49.8 2.7 %collective-permute-start.7 = (f32[128,128]{1,0:T(8,128)S(1)}, f32[128,128]{1,0:T(8,128)S(1)}, u32[]{:S(2)}, u32[]{:S(2)}) collective-permute-start(f32[128,128]{1,0:T(8,128)S(1)} %get-tuple-element.21), channel_id=1, source_target_pairs={{0,6},{2,0},{4,2},{6,4},{8,14},{10,8},{12,10},{14,12},{16,22},{18,... | collective-permute-start | bytes 196616 | tf_op jit(solution)/shard_map/ppermute | solution.py:275
  52.5 3.4 %collective-permute-start.12 = (f32[64,128]{1,0:T(8,128)S(1)}, f32[64,128]{1,0:T(8,128)S(1)}, u32[]{:S(2)}, u32[]{:S(2)}) collective-permute-start(f32[64,128]{1,0:T(8,128)S(1)} %slice.14), channel_id=1, source_target_pairs={{0,1},{1,0},{2,3},{3,2},{4,5},{5,4},{6,7},{7,6},{8,9},{9,8},{10,11... | collective-permute-start | bytes 98312 | tf_op jit(solution)/shard_map/ppermute | solution.py:291
  55.9 1.0 collective-permute-done.6
  56.8 0.1 collective-permute-start.11
  56.9 2.6 %collective-permute-start.10 = (f32[128,128]{1,0:T(8,128)S(1)}, f32[128,128]{1,0:T(8,128)S(1)}, u32[]{:S(2)}, u32[]{:S(2)}) collective-permute-start(f32[128,128]{1,0:T(8,128)S(1)} %add_add_fusion.1), channel_id=1, source_target_pairs={{0,24},{2,26},{4,28},{6,30},{8,0},{10,2},{12,4},{14,6},{16,8},{18,... | collective-permute-start | bytes 196616 | tf_op jit(solution)/shard_map/ppermute | solution.py:275
  59.6 2.0 %collective-permute-done.11 = f32[128,128]{1,0:T(8,128)S(1)} collective-permute-done((f32[128,128]{1,0:T(8,128)S(1)}, f32[128,128]{1,0:T(8,128)S(1)}, u32[]{:S(2)}, u32[]{:S(2)}) %collective-permute-start.11) | collective-permute-done | bytes 65568 | tf_op jit(solution)/shard_map/ppermute | solution.py:275
  61.5 2.3 %collective-permute-done.9 = f32[128,128]{1,0:T(8,128)S(1)} collective-permute-done((f32[128,128]{1,0:T(8,128)S(1)}, f32[128,128]{1,0:T(8,128)S(1)}, u32[]{:S(2)}, u32[]{:S(2)}) %collective-permute-start.9) | collective-permute-done | bytes 65568 | tf_op jit(solution)/shard_map/ppermute | solution.py:275
  63.9 2.7 %partials.3 = (f32[32,8,128]{2,1,0:T(8,128)S(1)}, f32[64,128]{1,0:T(8,128)S(1)}) custom-call(f32[128,128]{1,0:T(8,128)S(1)} %add_add_fusion.refs_0_, f32[64,128]{1,0:T(8,128)S(1)} %slice_add_fusion.refs_1_, f32[8192,128]{1,0:T(8,128)S(1)} %get-tuple-element.16.refs_2_), custom_call_target="tpu_custom_call" | custom-call | flops 1073741824 | bytes 4194304 | tf_op jit(solution)/shard_map/partials/pallas_call | solution.py:175
  66.6 16.5 %all_to_all.22.received_ref = f32[32,8,128]{2,1,0:T(8,128)S(1)} all-to-all(f32[32,8,128]{2,1,0:T(8,128)S(1)} %get-tuple-element.17), channel_id=1, replica_groups=mesh['gx'=8,'gy'=16,'gz'=2] {'gy','gz'}, dimensions={0} | all-to-all | bytes 262144 | tf_op jit(solution)/shard_map/all_to_all | solution.py:332
  83.2 14.3 %all_to_all.23.bc_ref = f32[16,4,128]{2,1,0:T(4,128)S(1)} all-to-all(f32[16,4,128]{2,1,0:T(4,128)S(1)} %get-tuple-element.20), channel_id=1, replica_groups=mesh['gx'=8,'gy'=16,'gz'=2] {'gx','gz'}, dimensions={0} | all-to-all | bytes 65536 | tf_op jit(solution)/shard_map/all_to_all | solution.py:334
  97.5 0.6 last_sums.1
  (23 shorter events, 0.2 us)
Async XLA Ops:
  16.9 2.9 %collective-permute-start = (f32[9,4,128]{2,1,0:T(4,128)S(1)}, f32[9,4,128]{2,1,0:T(4,128)S(1)}, u32[]{:S(2)}, u32[]{:S(2)}) collective-permute-start(f32[9,4,128]{2,1,0:T(4,128)S(1)} %pad_maximum_fusion), channel_id=1, source_target_pairs={{0,1},{1,0},{2,3},{3,2},{4,5},{5,4},{6,7},{7,6},{8,9},{9,8},{10,11... | collective-permute-start | bytes 55304 | tf_op jit(solution)/shard_map/ppermute | solution.py:291
  36.9 5.1 %collective-permute-start.2 = (f32[128,128]{1,0:T(8,128)S(1)}, f32[128,128]{1,0:T(8,128)S(1)}, u32[]{:S(2)}, u32[]{:S(2)}) collective-permute-start(f32[128,128]{1,0:T(8,128)S(1)} %get-tuple-element.14), channel_id=1, source_target_pairs={{0,32},{32,64},{64,96},{96,128},{128,160},{160,192},{192,224},{224... | collective-permute-start | bytes 196616 | tf_op jit(solution)/shard_map/ppermute | solution.py:275
  37.3 4.7 %collective-permute-start.1 = (f32[128,128]{1,0:T(8,128)S(1)}, f32[128,128]{1,0:T(8,128)S(1)}, u32[]{:S(2)}, u32[]{:S(2)}) collective-permute-start(f32[128,128]{1,0:T(8,128)S(1)} %get-tuple-element.14), channel_id=1, source_target_pairs={{0,224},{32,0},{64,32},{96,64},{128,96},{160,128},{192,160},{224,1... | collective-permute-start | bytes 196616 | tf_op jit(solution)/shard_map/ppermute | solution.py:275
  39.6 6.9 %collective-permute-start.5 = (f32[128,128]{1,0:T(8,128)S(1)}, f32[128,128]{1,0:T(8,128)S(1)}, u32[]{:S(2)}, u32[]{:S(2)}) collective-permute-start(f32[128,128]{1,0:T(8,128)S(1)} %get-tuple-element.15), channel_id=1, source_target_pairs={{0,1},{1,0},{2,3},{3,2},{4,5},{5,4},{6,7},{7,6},{8,9},{9,8},{10,11... | collective-permute-start | bytes 196616 | tf_op jit(solution)/shard_map/ppermute | solution.py:291
  42.0 7.7 %collective-permute-start.4 = (f32[128,128]{1,0:T(8,128)S(1)}, f32[128,128]{1,0:T(8,128)S(1)}, u32[]{:S(2)}, u32[]{:S(2)}) collective-permute-start(f32[128,128]{1,0:T(8,128)S(1)} %get-tuple-element.24), channel_id=1, source_target_pairs={{0,96},{32,128},{64,160},{96,192},{128,224},{160,0},{192,32},{224,... | collective-permute-start | bytes 196616 | tf_op jit(solution)/shard_map/ppermute | solution.py:275
  42.1 7.6 %collective-permute-start.3 = (f32[128,128]{1,0:T(8,128)S(1)}, f32[128,128]{1,0:T(8,128)S(1)}, u32[]{:S(2)}, u32[]{:S(2)}) collective-permute-start(f32[128,128]{1,0:T(8,128)S(1)} %get-tuple-element.23), channel_id=1, source_target_pairs={{0,160},{32,192},{64,224},{96,0},{128,32},{160,64},{192,96},{224,1... | collective-permute-start | bytes 196616 | tf_op jit(solution)/shard_map/ppermute | solution.py:275
  49.7 6.1 %collective-permute-start.8 = (f32[128,128]{1,0:T(8,128)S(1)}, f32[128,128]{1,0:T(8,128)S(1)}, u32[]{:S(2)}, u32[]{:S(2)}) collective-permute-start(f32[128,128]{1,0:T(8,128)S(1)} %get-tuple-element.21), channel_id=1, source_target_pairs={{0,4},{2,6},{4,0},{6,2},{8,12},{10,14},{12,8},{14,10},{16,20},{18,... | collective-permute-start | bytes 196616 | tf_op jit(solution)/shard_map/ppermute | solution.py:275
  49.8 6.0 %collective-permute-start.7 = (f32[128,128]{1,0:T(8,128)S(1)}, f32[128,128]{1,0:T(8,128)S(1)}, u32[]{:S(2)}, u32[]{:S(2)}) collective-permute-start(f32[128,128]{1,0:T(8,128)S(1)} %get-tuple-element.21), channel_id=1, source_target_pairs={{0,6},{2,0},{4,2},{6,4},{8,14},{10,8},{12,10},{14,12},{16,22},{18,... | collective-permute-start | bytes 196616 | tf_op jit(solution)/shard_map/ppermute | solution.py:275
  52.5 4.3 %collective-permute-start.6 = (f32[128,128]{1,0:T(8,128)S(1)}, f32[128,128]{1,0:T(8,128)S(1)}, u32[]{:S(2)}, u32[]{:S(2)}) collective-permute-start(f32[128,128]{1,0:T(8,128)S(1)} %get-tuple-element.21), channel_id=1, source_target_pairs={{0,2},{2,4},{4,6},{6,0},{8,10},{10,12},{12,14},{14,8},{16,18},{18,... | collective-permute-start | bytes 196616 | tf_op jit(solution)/shard_map/ppermute | solution.py:275
  52.5 7.1 %collective-permute-start.12 = (f32[64,128]{1,0:T(8,128)S(1)}, f32[64,128]{1,0:T(8,128)S(1)}, u32[]{:S(2)}, u32[]{:S(2)}) collective-permute-start(f32[64,128]{1,0:T(8,128)S(1)} %slice.14), channel_id=1, source_target_pairs={{0,1},{1,0},{2,3},{3,2},{4,5},{5,4},{6,7},{7,6},{8,9},{9,8},{10,11... | collective-permute-start | bytes 98312 | tf_op jit(solution)/shard_map/ppermute | solution.py:291
  56.8 4.7 %collective-permute-start.11 = (f32[128,128]{1,0:T(8,128)S(1)}, f32[128,128]{1,0:T(8,128)S(1)}, u32[]{:S(2)}, u32[]{:S(2)}) collective-permute-start(f32[128,128]{1,0:T(8,128)S(1)} %add_add_fusion.1), channel_id=1, source_target_pairs={{0,16},{2,18},{4,20},{6,22},{8,24},{10,26},{12,28},{14,30},{16,0},... | collective-permute-start | bytes 196616 | tf_op jit(solution)/shard_map/ppermute | solution.py:275
  56.9 4.6 %collective-permute-start.10 = (f32[128,128]{1,0:T(8,128)S(1)}, f32[128,128]{1,0:T(8,128)S(1)}, u32[]{:S(2)}, u32[]{:S(2)}) collective-permute-start(f32[128,128]{1,0:T(8,128)S(1)} %add_add_fusion.1), channel_id=1, source_target_pairs={{0,24},{2,26},{4,28},{6,30},{8,0},{10,2},{12,4},{14,6},{16,8},{18,... | collective-permute-start | bytes 196616 | tf_op jit(solution)/shard_map/ppermute | solution.py:275
  59.5 4.3 %collective-permute-start.9 = (f32[128,128]{1,0:T(8,128)S(1)}, f32[128,128]{1,0:T(8,128)S(1)}, u32[]{:S(2)}, u32[]{:S(2)}) collective-permute-start(f32[128,128]{1,0:T(8,128)S(1)} %add_add_fusion.1), channel_id=1, source_target_pairs={{0,8},{2,10},{4,12},{6,14},{8,16},{10,18},{12,20},{14,22},{16,24},... | collective-permute-start | bytes 196616 | tf_op jit(solution)/shard_map/ppermute | solution.py:275

commit v10 on v7

--- a/solution.py
+++ b/solution.py
@@ -44,19 +44,16 @@
     )
 
 
-def unpack_first(ac_ref, own_ref, other_ref, a2_ref, b2_ref, c2_ref):
+def unpack_first(ac_ref, b_ref, a2_ref, b2_ref, c2_ref):
     slots, each, width = ac_ref.shape
-    core = lax.axis_index("gz")
     a2_ref[...] = from_lower(ac_ref[...].reshape(slots * each, width))
     for g in range(each):
         c2_ref[g * slots : (g + 1) * slots, :] = ac_ref[:, g, :]
     c2_ref[...] = from_upper(c2_ref[...])
-    slots, each, width = own_ref.shape
+    slots = b_ref.shape[0]
+    own = b2_ref.shape[0] // slots
     for n in range(slots):
-        own, other = own_ref[n], other_ref[n]
-        at = 2 * each * n
-        b2_ref[at : at + each, :] = jnp.where(core == 0, own, other)
-        b2_ref[at + each : at + 2 * each, :] = jnp.where(core == 0, other, own)
+        b2_ref[n * own : (n + 1) * own, :] = b_ref[n, :own, :]
     b2_ref[...] = from_lower(b2_ref[...])
 
 
@@ -84,8 +81,7 @@
 
 
 def round_kernel(first, keep, scale, *refs):
-    n_small = 3 if first else 2
-    small, t_ref, outs, refs = refs[:n_small], refs[n_small], refs[n_small + 1 :][:2], refs[n_small + 3 :]
+    small, t_ref, outs, refs = refs[:2], refs[2], refs[3:5], refs[5:]
     if first:
         t_hbm, t_ref, sems, refs = t_ref, refs[0], refs[-1], refs[1:-1]
     a2_ref, b2_ref, c2_ref, wc_ref, ma_ref = refs
@@ -187,7 +183,7 @@
     )(*small, tensor)
 
 
-def first_kernel(a_hbm, b_hbm, c_hbm, slots_ref, a_out_ref, a_ref, b_ref, c_ref, sems):
+def first_kernel(a_hbm, b_hbm, c_hbm, slots_ref, a_ref, b_ref, c_ref, sems):
     own, rank = a_ref.shape
     pairs = ((a_hbm, a_ref), (b_hbm, b_ref), (c_hbm, c_ref))
     copies = [pltpu.make_async_copy(x, y, sems.at[n]) for n, (x, y) in enumerate(pairs)]
@@ -196,8 +192,8 @@
     for copy in copies:
         copy.wait()
     a = a_ref[...]
-    a_out_ref[...] = jnp.concatenate([a, a], axis=1)
-    slot = jnp.concatenate([b_ref[...], jnp.broadcast_to(c_ref[...], (own, rank))], axis=1)
+    rows = jnp.concatenate([b_ref[...], jnp.broadcast_to(c_ref[...], (own, rank))], axis=1)
+    slot = jnp.concatenate([rows, jnp.concatenate([a, a], axis=1)], axis=0)
     for n in range(slots_ref.shape[0]):
         slots_ref[n, :, :] = slot
 
@@ -207,17 +203,39 @@
     factors = [pltpu.with_memory_space_constraint(x, pltpu.HBM) for x in (a, b, c)]
     return pl.pallas_call(
         first_kernel,
-        out_shape=(
-            jax.ShapeDtypeStruct((count, own, 2 * rank), F32),
-            jax.ShapeDtypeStruct((own, 2 * rank), F32),
-        ),
+        out_shape=jax.ShapeDtypeStruct((count, 2 * own, 2 * rank), F32),
         in_specs=[HBM] * 3,
-        out_specs=(VMEM, VMEM),
+        out_specs=VMEM,
         scratch_shapes=[pltpu.VMEM(x.shape, F32) for x in (a, b, c)]
         + [pltpu.SemaphoreType.DMA((3,))],
         compiler_params=pltpu.CompilerParams(vmem_limit_bytes=4 << 20),
         name="first_slots",
     )(*factors)
+
+
+def second_kernel(all_ref, slots_ref):
+    core = lax.axis_index("gz")
+    chip = lax.axis_index("gx") * 2
+    slots, tall, width = all_ref.shape
+    own = tall // 2
+    a = jnp.concatenate([all_ref[chip, own:, :], all_ref[chip + 1, own:, :]], axis=0)
+    flat = all_ref.reshape(slots * tall, width)
+    c = flat[pl.ds(core * tall, slots // 2, stride=2 * tall), :]
+    slot = jnp.where(lower_half(a.shape), a, c)
+    for n in range(slots_ref.shape[0]):
+        slots_ref[n, :, :] = slot
+
+
+def second_slots(received, count):
+    _, tall, width = received.shape
+    return pl.pallas_call(
+        second_kernel,
+        out_shape=jax.ShapeDtypeStruct((count, tall, width), F32),
+        in_specs=[VMEM],
+        out_specs=VMEM,
+        compiler_params=pltpu.CompilerParams(vmem_limit_bytes=4 << 20),
+        name="second_slots",
+    )(received)
 
 
 def last_kernel(ac_ref, other_ref, bc_ref, a_ref, b_ref, c_ref, sum_a_ref, sum_b_ref):
@@ -249,10 +267,8 @@
 
 
 def ring8(x):
-    below, above = shift(x, "gx", 1, 8, 1), shift(x, "gx", 1, 8, -1)
-    two = x + above
-    three = two + below
-    return three + (shift(three, "gx", 1, 8, -3) + shift(two, "gx", 1, 8, 3))
+    three = x + shift(x, "gx", 1, 8, 1) + shift(x, "gx", 1, 8, -1)
+    return three + shift(three, "gx", 1, 8, 4) + shift(x, "gx", 1, 8, 2) + shift(x, "gx", 1, 8, -2)
 
 
 def ring4(x, stride):
@@ -266,7 +282,6 @@
 
 def shards(tensor, factor_a, factor_b, factor_c):
     count_x, count_y, count_z = (lax.axis_size(n) for n in ("gx", "gy", "gz"))
-    core = lax.axis_index("gz")
     count_i, count_j, count_k = tensor.shape
     whole = (
         float(count_j * count_y * count_k * count_z),
@@ -277,22 +292,16 @@
     own, rank = factor_a.shape
     wide = 2 * rank
 
-    slots, mine = first_slots(factor_a, factor_b, factor_c, count_x)
-    along_x = lax.all_to_all(slots, "gx", 0, 0, tiled=True)
-    others = swap(jnp.concatenate([along_x, mine[None]], axis=0))
-    other = others[-1]
-    rows_a = jnp.concatenate(
-        [jnp.where(core == 0, mine, other), jnp.where(core == 0, other, mine)], axis=0
-    )
-    slot = jnp.where(lower_half(rows_a.shape), rows_a, along_x[:, 0])
-    along_y = lax.all_to_all(jnp.broadcast_to(slot[None], (count_y, *slot.shape)), "gy", 0, 0, tiled=True)
+    slots = first_slots(factor_a, factor_b, factor_c, count_x * count_z)
+    along_x = lax.all_to_all(slots, ("gx", "gz"), 0, 0, tiled=True)
+    along_y = lax.all_to_all(second_slots(along_x, count_y), "gy", 0, 0, tiled=True)
 
     keep = tuple(1.0 / n for n in copies)
     scale = tuple(-STEP_SIZE / n for n in whole)
     sizes = tensor.shape
     tensor = tensor.reshape(count_i * count_j, count_k)
     shapes = ((count_i, wide), (count_k, wide))
-    a, cb, tensor = partials(True, keep, scale, (along_y, along_x, others), tensor, sizes, shapes)
+    a, cb, tensor = partials(True, keep, scale, (along_y, along_x), tensor, sizes, shapes)
     a = a + swap(a)
     cb = ring8(cb)
     ca = ring4(ring4(jnp.where(lower_half(cb.shape), cb, a), 1), 4)

time: 98 us -> 95.9 us (0.979)
  waiting for transfers between devices: 10.1 us -> 16.7 us
  starting transfers between devices: 26.7 us -> 21 us
  blocking collectives: 52 us -> 49.1 us
    ppermute x10 -> x11, waiting for transfers between devices: 8.44 us -> 15.9 us  [shift(): return lax.ppermute(x, axis, pairs)]
    ppermute x4 -> x3, starting transfers between devices: 13.9 us -> 8.89 us  [swap(): return lax.ppermute(x, 'gz', [(0, 1), (1, 0)])]
    all_to_all x1, blocking collectives: 13.2 us -> 9.37 us  [shards(): bc = lax.all_to_all(slots_bc, 'gx', 0, 0, tiled=True)]
    all_to_all x2, blocking collectives: 28.5 us -> 30.7 us  [the longest x1 17.6 us: shards(): along_x = lax.all_to_all(slots, ('gx', 'gz'), 0, 0, tiled=True)]
    all_to_all x1, blocking collectives: 10.3 us -> 9.07 us  [shards(): ac = jnp.sum(lax.all_to_all(slots_ac, 'gy', 0, 0, tiled=True), axis=0)]
    ppermute x10 -> x11, starting transfers between devices: 12.8 us -> 12.1 us  [shift(): return lax.ppermute(x, axis, pairs)]
  transfers between devices with their start and end apart: 14 -> 14, of which waited for: 6 -> 7; matrix products, arithmetic and copies ran while one was open for 0% -> 0% of each run, Pallas kernels for 0% -> 0%
where the time goes in v10:
time: 95.9 us; the launch traced here: 95.7 us
  blocking collectives  49.1 us (51%)
  starting transfers between devices  21 us (22%)
  waiting for transfers between devices  16.7 us (17%)
  Pallas kernels  8.07 us (8%)
    all_to_all x1, blocking collectives, shards(): along_x = lax.all_to_all(slots, ('gx', 'gz'), 0, 0, tiled=True)  17.6 us
    ppermute x11, waiting for transfers between devices, shift(): return lax.ppermute(x, axis, pairs)  15.9 us
    all_to_all x1, blocking collectives, shards(): lax.all_to_all(second_slots(along_x, count_y), 'gy', 0, 0, tiled=True)  13.1 us
    ppermute x11, starting transfers between devices, shift(): return lax.ppermute(x, axis, pairs)  12.1 us
    all_to_all x1, blocking collectives, shards(): bc = lax.all_to_all(slots_bc, 'gx', 0, 0, tiled=True)  9.37 us
    all_to_all x1, blocking collectives, shards(): ac = jnp.sum(lax.all_to_all(slots_ac, 'gy', 0, 0, tiled=True), axis=0)  9.07 us
    ppermute x3, starting transfers between devices, swap(): return lax.ppermute(x, 'gz', [(0, 1), (1, 0)])  8.89 us
    pallas_call x2, Pallas kernels, partials(): pl.pallas_call(functools.partial(round_kernel, first, keep, scale), out_s...  6.66 us
  transfers between devices with their start and end apart: 14, of which 7 were waited for; matrix products, arithmetic and copies ran while one was open for 0% of the time, Pallas kernels for 0%

profile of v10, /device:TPU:1, one launch (start us, length us, event | category | flops | bytes accessed | tf_op | source)
XLA Modules:
  0.0 95.7 jit_solution(8848611694805808290)
XLA Ops:
  0.6 0.8 first_slots.1
  1.4 17.6 %all_to_all.20.all_ref.refs_1_ = f32[16,8,128]{2,1,0:T(8,128)S(1)} all-to-all(f32[16,8,128]{2,1,0:T(8,128)S(1)} %first_slots.1), channel_id=1, replica_groups=mesh['gx'=8,'gy'=16,'gz'=2] {'gx','gz'}, dimensions={0} | all-to-all | bytes 131072 | tf_op jit(solution)/shard_map/all_to_all | solution.py:296
  19.0 13.1 %all_to_all.21.refs_0_ = f32[16,8,128]{2,1,0:T(8,128)S(1)} all-to-all(f32[16,8,128]{2,1,0:T(8,128)S(1)} %second_slots.1), channel_id=1, replica_groups=mesh['gx'=8,'gy'=16,'gz'=2] {'gy'}, dimensions={0} | all-to-all | bytes 131072 | tf_op jit(solution)/shard_map/all_to_all | solution.py:297
  32.1 3.9 %partials.2 = (f32[128,128]{1,0:T(8,128)S(1)}, f32[128,128]{1,0:T(8,128)S(1)}, f32[8192,128]{1,0:T(8,128)S(1)}) custom-call(f32[16,8,128]{2,1,0:T(8,128)S(1)} %all_to_all.21.refs_0_, f32[16,8,128]{2,1,0:T(8,128)S(1)} %all_to_all.20.all_ref.refs_1_, f32[8192,128]{1,0:T(8,128)} %bitcast.5), custom_call_target="tpu_custom_call" | custom-call | flops 1073741824 | bytes 4194304 | tf_op jit(solution)/shard_map/partials/pallas_call | solution.py:167
  36.3 2.5 %collective-permute-start.1 = (f32[128,128]{1,0:T(8,128)S(1)}, f32[128,128]{1,0:T(8,128)S(1)}, u32[]{:S(2)}, u32[]{:S(2)}) collective-permute-start(f32[128,128]{1,0:T(8,128)S(1)} %get-tuple-element.8), channel_id=1, source_target_pairs={{0,224},{32,0},{64,32},{96,64},{128,96},{160,128},{192,160},{224,1... | collective-permute-start | bytes 196616 | tf_op jit(solution)/shard_map/ppermute | solution.py:266
  38.8 3.6 %collective-permute-start.4 = (f32[128,128]{1,0:T(8,128)S(1)}, f32[128,128]{1,0:T(8,128)S(1)}, u32[]{:S(2)}, u32[]{:S(2)}) collective-permute-start(f32[128,128]{1,0:T(8,128)S(1)} %get-tuple-element.8), channel_id=1, source_target_pairs={{0,192},{32,224},{64,0},{96,32},{128,64},{160,96},{192,128},{224,1... | collective-permute-start | bytes 196616 | tf_op jit(solution)/shard_map/ppermute | solution.py:266
  42.4 2.7 %collective-permute-start.5 = (f32[128,128]{1,0:T(8,128)S(1)}, f32[128,128]{1,0:T(8,128)S(1)}, u32[]{:S(2)}, u32[]{:S(2)}) collective-permute-start(f32[128,128]{1,0:T(8,128)S(1)} %get-tuple-element.9), channel_id=1, source_target_pairs={{0,1},{1,0},{2,3},{3,2},{4,5},{5,4},{6,7},{7,6},{8,9},{9,8},{10,11... | collective-permute-start | bytes 196616 | tf_op jit(solution)/shard_map/ppermute | solution.py:280
  45.1 0.9 collective-permute-start.2
  46.1 8.0 %collective-permute-done.2 = f32[128,128]{1,0:T(8,128)S(1)} collective-permute-done((f32[128,128]{1,0:T(8,128)S(1)}, f32[128,128]{1,0:T(8,128)S(1)}, u32[]{:S(2)}, u32[]{:S(2)}) %collective-permute-start.2) | collective-permute-done | bytes 65568 | tf_op jit(solution)/shard_map/ppermute | solution.py:266
  54.4 2.4 %collective-permute-start.7 = (f32[128,128]{1,0:T(8,128)S(1)}, f32[128,128]{1,0:T(8,128)S(1)}, u32[]{:S(2)}, u32[]{:S(2)}) collective-permute-start(f32[128,128]{1,0:T(8,128)S(1)} %get-tuple-element.13), channel_id=1, source_target_pairs={{0,6},{2,0},{4,2},{6,4},{8,14},{10,8},{12,10},{14,12},{16,22},{18,... | collective-permute-start | bytes 196616 | tf_op jit(solution)/shard_map/ppermute | solution.py:266
  56.8 1.1 %collective-permute-start.12 = (f32[64,128]{1,0:T(8,128)S(1)}, f32[64,128]{1,0:T(8,128)S(1)}, u32[]{:S(2)}, u32[]{:S(2)}) collective-permute-start(f32[64,128]{1,0:T(8,128)S(1)} %slice.8), channel_id=1, source_target_pairs={{0,1},{1,0},{2,3},{3,2},{4,5},{5,4},{6,7},{7,6},{8,9},{9,8},{10,11... | collective-permute-start | bytes 98312 | tf_op jit(solution)/shard_map/ppermute | solution.py:280
  57.9 0.6 collective-permute-done.6
  58.5 3.0 %collective-permute-done.8 = f32[128,128]{1,0:T(8,128)S(1)} collective-permute-done((f32[128,128]{1,0:T(8,128)S(1)}, f32[128,128]{1,0:T(8,128)S(1)}, u32[]{:S(2)}, u32[]{:S(2)}) %collective-permute-start.8) | collective-permute-done | bytes 65568 | tf_op jit(solution)/shard_map/ppermute | solution.py:266
  61.5 0.9 collective-permute-start.10
  62.4 1.2 %collective-permute-start.11 = (f32[128,128]{1,0:T(8,128)S(1)}, f32[128,128]{1,0:T(8,128)S(1)}, u32[]{:S(2)}, u32[]{:S(2)}) collective-permute-start(f32[128,128]{1,0:T(8,128)S(1)} %add_add_fusion.1), channel_id=1, source_target_pairs={{0,16},{2,18},{4,20},{6,22},{8,24},{10,26},{12,28},{14,30},{16,0},... | collective-permute-start | bytes 196616 | tf_op jit(solution)/shard_map/ppermute | solution.py:266
  63.6 1.1 %collective-permute-done.10 = f32[128,128]{1,0:T(8,128)S(1)} collective-permute-done((f32[128,128]{1,0:T(8,128)S(1)}, f32[128,128]{1,0:T(8,128)S(1)}, u32[]{:S(2)}, u32[]{:S(2)}) %collective-permute-start.10) | collective-permute-done | bytes 65568 | tf_op jit(solution)/shard_map/ppermute | solution.py:266
  64.7 2.3 %collective-permute-done.11 = f32[128,128]{1,0:T(8,128)S(1)} collective-permute-done((f32[128,128]{1,0:T(8,128)S(1)}, f32[128,128]{1,0:T(8,128)S(1)}, u32[]{:S(2)}, u32[]{:S(2)}) %collective-permute-start.11) | collective-permute-done | bytes 65568 | tf_op jit(solution)/shard_map/ppermute | solution.py:266
  67.0 0.9 collective-permute-done.9
  67.9 2.7 %partials.3 = (f32[16,8,128]{2,1,0:T(8,128)S(1)}, f32[64,128]{1,0:T(8,128)S(1)}) custom-call(f32[128,128]{1,0:T(8,128)S(1)} %add_add_fusion.refs_0_, f32[64,128]{1,0:T(8,128)S(1)} %slice_add_fusion.1.refs_1_, f32[8192,128]{1,0:T(8,128)S(1)} %get-tuple-element.10.refs_2_), custom_call_target="tpu_custom_call" | custom-call | flops 1073741824 | bytes 4194304 | tf_op jit(solution)/shard_map/partials/pallas_call | solution.py:167
  70.6 9.1 %all_to_all.22 = f32[16,8,128]{2,1,0:T(8,128)S(1)} all-to-all(f32[16,8,128]{2,1,0:T(8,128)S(1)} %get-tuple-element.11), channel_id=1, replica_groups=mesh['gx'=8,'gy'=16,'gz'=2] {'gy'}, dimensions={0} | all-to-all | bytes 131072 | tf_op jit(solution)/shard_map/all_to_all | solution.py:314
  79.7 5.1 %collective-permute-start.13 = (f32[72,128]{1,0:T(8,128)S(1)}, f32[72,128]{1,0:T(8,128)S(1)}, u32[]{:S(2)}, u32[]{:S(2)}) collective-permute-start(f32[72,128]{1,0:T(8,128)S(1)} %pad_maximum_fusion), channel_id=1, source_target_pairs={{0,1},{1,0},{2,3},{3,2},{4,5},{5,4},{6,7},{7,6},{8,9},{9,8},{10,11... | collective-permute-start | bytes 110600 | tf_op jit(solution)/shard_map/ppermute | solution.py:280
  84.8 0.9 collective-permute-done.13.other_ref
  85.7 9.4 %all_to_all.23.bc_ref = f32[8,8,128]{2,1,0:T(8,128)S(1)} all-to-all(f32[8,8,128]{2,1,0:T(8,128)S(1)} %fusion.1), channel_id=1, replica_groups=mesh['gx'=8,'gy'=16,'gz'=2] {'gx'}, dimensions={0} | all-to-all | bytes 65536 | tf_op jit(solution)/shard_map/all_to_all | solution.py:319
  95.1 0.6 last_sums.1
  (23 shorter events, 0.8 us)
Async XLA Ops:
  36.1 9.1 %collective-permute-start = (f32[128,128]{1,0:T(8,128)S(1)}, f32[128,128]{1,0:T(8,128)S(1)}, u32[]{:S(2)}, u32[]{:S(2)}) collective-permute-start(f32[128,128]{1,0:T(8,128)S(1)} %get-tuple-element.8), channel_id=1, source_target_pairs={{0,32},{32,64},{64,96},{96,128},{128,160},{160,192},{192,224},{224... | collective-permute-start | bytes 196616 | tf_op jit(solution)/shard_map/ppermute | solution.py:266
  36.3 8.8 %collective-permute-start.1 = (f32[128,128]{1,0:T(8,128)S(1)}, f32[128,128]{1,0:T(8,128)S(1)}, u32[]{:S(2)}, u32[]{:S(2)}) collective-permute-start(f32[128,128]{1,0:T(8,128)S(1)} %get-tuple-element.8), channel_id=1, source_target_pairs={{0,224},{32,0},{64,32},{96,64},{128,96},{160,128},{192,160},{224,1... | collective-permute-start | bytes 196616 | tf_op jit(solution)/shard_map/ppermute | solution.py:266
  38.8 7.2 %collective-permute-start.3 = (f32[128,128]{1,0:T(8,128)S(1)}, f32[128,128]{1,0:T(8,128)S(1)}, u32[]{:S(2)}, u32[]{:S(2)}) collective-permute-start(f32[128,128]{1,0:T(8,128)S(1)} %get-tuple-element.8), channel_id=1, source_target_pairs={{0,64},{32,96},{64,128},{96,160},{128,192},{160,224},{192,0},{224,... | collective-permute-start | bytes 196616 | tf_op jit(solution)/shard_map/ppermute | solution.py:266
  38.8 7.2 %collective-permute-start.4 = (f32[128,128]{1,0:T(8,128)S(1)}, f32[128,128]{1,0:T(8,128)S(1)}, u32[]{:S(2)}, u32[]{:S(2)}) collective-permute-start(f32[128,128]{1,0:T(8,128)S(1)} %get-tuple-element.8), channel_id=1, source_target_pairs={{0,192},{32,224},{64,0},{96,32},{128,64},{160,96},{192,128},{224,1... | collective-permute-start | bytes 196616 | tf_op jit(solution)/shard_map/ppermute | solution.py:266
  42.4 3.6 %collective-permute-start.5 = (f32[128,128]{1,0:T(8,128)S(1)}, f32[128,128]{1,0:T(8,128)S(1)}, u32[]{:S(2)}, u32[]{:S(2)}) collective-permute-start(f32[128,128]{1,0:T(8,128)S(1)} %get-tuple-element.9), channel_id=1, source_target_pairs={{0,1},{1,0},{2,3},{3,2},{4,5},{5,4},{6,7},{7,6},{8,9},{9,8},{10,11... | collective-permute-start | bytes 196616 | tf_op jit(solution)/shard_map/ppermute | solution.py:280
  45.1 8.9 %collective-permute-start.2 = (f32[128,128]{1,0:T(8,128)S(1)}, f32[128,128]{1,0:T(8,128)S(1)}, u32[]{:S(2)}, u32[]{:S(2)}) collective-permute-start(f32[128,128]{1,0:T(8,128)S(1)} %add_add_fusion.3), channel_id=1, source_target_pairs={{0,128},{32,160},{64,192},{96,224},{128,0},{160,32},{192,64},{224,... | collective-permute-start | bytes 196616 | tf_op jit(solution)/shard_map/ppermute | solution.py:266
  54.1 4.4 %collective-permute-start.6 = (f32[128,128]{1,0:T(8,128)S(1)}, f32[128,128]{1,0:T(8,128)S(1)}, u32[]{:S(2)}, u32[]{:S(2)}) collective-permute-start(f32[128,128]{1,0:T(8,128)S(1)} %get-tuple-element.13), channel_id=1, source_target_pairs={{0,2},{2,4},{4,6},{6,0},{8,10},{10,12},{12,14},{14,8},{16,18},{18,... | collective-permute-start | bytes 196616 | tf_op jit(solution)/shard_map/ppermute | solution.py:266
  54.4 4.0 %collective-permute-start.7 = (f32[128,128]{1,0:T(8,128)S(1)}, f32[128,128]{1,0:T(8,128)S(1)}, u32[]{:S(2)}, u32[]{:S(2)}) collective-permute-start(f32[128,128]{1,0:T(8,128)S(1)} %get-tuple-element.13), channel_id=1, source_target_pairs={{0,6},{2,0},{4,2},{6,4},{8,14},{10,8},{12,10},{14,12},{16,22},{18,... | collective-permute-start | bytes 196616 | tf_op jit(solution)/shard_map/ppermute | solution.py:266
  56.8 4.6 %collective-permute-start.8 = (f32[128,128]{1,0:T(8,128)S(1)}, f32[128,128]{1,0:T(8,128)S(1)}, u32[]{:S(2)}, u32[]{:S(2)}) collective-permute-start(f32[128,128]{1,0:T(8,128)S(1)} %get-tuple-element.13), channel_id=1, source_target_pairs={{0,4},{2,6},{4,0},{6,2},{8,12},{10,14},{12,8},{14,10},{16,20},{18,... | collective-permute-start | bytes 196616 | tf_op jit(solution)/shard_map/ppermute | solution.py:266
  56.8 6.7 %collective-permute-start.12 = (f32[64,128]{1,0:T(8,128)S(1)}, f32[64,128]{1,0:T(8,128)S(1)}, u32[]{:S(2)}, u32[]{:S(2)}) collective-permute-start(f32[64,128]{1,0:T(8,128)S(1)} %slice.8), channel_id=1, source_target_pairs={{0,1},{1,0},{2,3},{3,2},{4,5},{5,4},{6,7},{7,6},{8,9},{9,8},{10,11... | collective-permute-start | bytes 98312 | tf_op jit(solution)/shard_map/ppermute | solution.py:280
  61.5 3.2 %collective-permute-start.10 = (f32[128,128]{1,0:T(8,128)S(1)}, f32[128,128]{1,0:T(8,128)S(1)}, u32[]{:S(2)}, u32[]{:S(2)}) collective-permute-start(f32[128,128]{1,0:T(8,128)S(1)} %add_add_fusion.1), channel_id=1, source_target_pairs={{0,24},{2,26},{4,28},{6,30},{8,0},{10,2},{12,4},{14,6},{16,8},{18,... | collective-permute-start | bytes 196616 | tf_op jit(solution)/shard_map/ppermute | solution.py:266
  62.4 4.6 %collective-permute-start.11 = (f32[128,128]{1,0:T(8,128)S(1)}, f32[128,128]{1,0:T(8,128)S(1)}, u32[]{:S(2)}, u32[]{:S(2)}) collective-permute-start(f32[128,128]{1,0:T(8,128)S(1)} %add_add_fusion.1), channel_id=1, source_target_pairs={{0,16},{2,18},{4,20},{6,22},{8,24},{10,26},{12,28},{14,30},{16,0},... | collective-permute-start | bytes 196616 | tf_op jit(solution)/shard_map/ppermute | solution.py:266
  63.6 4.3 %collective-permute-start.9 = (f32[128,128]{1,0:T(8,128)S(1)}, f32[128,128]{1,0:T(8,128)S(1)}, u32[]{:S(2)}, u32[]{:S(2)}) collective-permute-start(f32[128,128]{1,0:T(8,128)S(1)} %add_add_fusion.1), channel_id=1, source_target_pairs={{0,8},{2,10},{4,12},{6,14},{8,16},{10,18},{12,20},{14,22},{16,24},... | collective-permute-start | bytes 196616 | tf_op jit(solution)/shard_map/ppermute | solution.py:266
  79.7 6.0 %collective-permute-start.13 = (f32[72,128]{1,0:T(8,128)S(1)}, f32[72,128]{1,0:T(8,128)S(1)}, u32[]{:S(2)}, u32[]{:S(2)}) collective-permute-start(f32[72,128]{1,0:T(8,128)S(1)} %pad_maximum_fusion), channel_id=1, source_target_pairs={{0,1},{1,0},{2,3},{3,2},{4,5},{5,4},{6,7},{7,6},{8,9},{9,8},{10,11... | collective-permute-start | bytes 110600 | tf_op jit(solution)/shard_map/ppermute | solution.py:280

commit v11 on v10

--- a/solution.py
+++ b/solution.py
@@ -118,11 +118,13 @@
     group = 128 // count_j
     lane = lax.broadcasted_iota(jnp.int32, (rank, 128), 1) // count_j
 
+    half, quarter = chunks // 2, chunks // 4
+    waits = {0: half, half: half + quarter, half + quarter: chunks}
     moment_b = jnp.zeros((count_j, width), F32)
     moment_c = jnp.zeros((width, 2 * count_k), F32)
     for c in range(chunks):
-        if first and c % (chunks // 2) == 0:
-            for n in range(c, c + chunks // 2):
+        if first and c in waits:
+            for n in range(c, waits[c]):
                 fetch(n).wait()
         high, low = split(t_ref[c * CHUNK : (c + 1) * CHUNK, :])
         terms = jnp.concatenate([high, low], axis=1)
@@ -238,24 +240,48 @@
     )(received)
 
 
-def last_kernel(ac_ref, other_ref, bc_ref, a_ref, b_ref, c_ref, sum_a_ref, sum_b_ref):
+def middle_kernel(received_ref, b_ref, slots_ref, ac_ref):
+    core, me_x = lax.axis_index("gz"), lax.axis_index("gx")
+    slots, tall, width = slots_ref.shape
+    own = tall // 2
+    ac_ref[...] = jnp.sum(received_ref[...], axis=0)
+    lower = lower_half((own, width))
+    for n in range(slots):
+        x, z = n // 2, n % 2
+        c = jnp.broadcast_to(ac_ref[x : x + 1, :], (own, width))
+        c = jnp.where(core == z, c, 0.0)
+        slots_ref[n, :own, :] = jnp.where(lower, b_ref[n * own : (n + 1) * own, :], c)
+        slots_ref[n, own:, :] = jnp.where(me_x == x, ac_ref[z * own : (z + 1) * own, :], 0.0)
+
+
+def middle_slots(received, b, count):
+    _, tall, width = received.shape
+    return pl.pallas_call(
+        middle_kernel,
+        out_shape=jax.ShapeDtypeStruct((count, tall, width), F32),
+        in_specs=[VMEM] * 2,
+        out_specs=VMEM,
+        scratch_shapes=[pltpu.VMEM((tall, width), F32)],
+        compiler_params=pltpu.CompilerParams(vmem_limit_bytes=4 << 20),
+        name="middle_slots",
+    )(received, b)
+
+
+def last_kernel(all_ref, a_ref, b_ref, c_ref):
     own, rank = a_ref.shape
-    sum_a_ref[...] = ac_ref[...] + other_ref[other_ref.shape[0] - ac_ref.shape[0] :, :]
-    sum_b_ref[...] = jnp.sum(bc_ref[...], axis=0)
-    mine = pl.ds(lax.axis_index("gz") * own, own)
-    a_ref[...] = sum_a_ref[mine, :][:, :rank]
-    b_ref[...] = sum_b_ref[mine, :][:, :rank]
-    c_ref[...] = sum_b_ref[:1, :][:, rank:]
-
-
-def last_sums(ac, other, bc, own, rank):
+    sums = jnp.sum(all_ref[...], axis=0)
+    a_ref[...] = sums[own:, :rank]
+    b_ref[...] = sums[:own, :rank]
+    c_ref[...] = sums[:1, rank:]
+
+
+def last_sums(received, own, rank):
     return pl.pallas_call(
         last_kernel,
         out_shape=tuple(jax.ShapeDtypeStruct((n, rank), F32) for n in (own, own, 1)),
-        scratch_shapes=[pltpu.VMEM(ac.shape, F32)] * 2,
         compiler_params=pltpu.CompilerParams(vmem_limit_bytes=4 << 20),
         name="last_sums",
-    )(ac, other, bc)
+    )(received)
 
 
 def shift(x, axis, stride, count, by):
@@ -311,13 +337,9 @@
     scale = tuple(1.0 / n for n in whole)
     shapes = ((count_y, 2 * own, wide), (count_j, wide))
     slots_ac, b = partials(False, (0.0,) * 3, scale, (ca, b), tensor, sizes, shapes)
-    ac = jnp.sum(lax.all_to_all(slots_ac, "gy", 0, 0, tiled=True), axis=0)
-    others = swap(jnp.concatenate([b, ac], axis=0))
-    b = b + others[:count_j]
-    slots_b = b.reshape(count_x, 2 * own, wide)
-    slots_bc = jnp.where(lower_half(slots_b.shape), slots_b, ac[:, None])
-    bc = lax.all_to_all(slots_bc, "gx", 0, 0, tiled=True)
-    return last_sums(ac, others, bc, own, rank)
+    received = lax.all_to_all(slots_ac, "gy", 0, 0, tiled=True)
+    slots = middle_slots(received, b, count_x * count_z)
+    return last_sums(lax.all_to_all(slots, ("gx", "gz"), 0, 0, tiled=True), own, rank)
 
 
 def solution(mesh):

time: 95.9 us -> 96.3 us (level)
  blocking collectives: 49.1 us -> 55.3 us
  starting transfers between devices: 21 us -> 15.9 us
    all_to_all x2, blocking collectives: 18.4 us -> 24.6 us  [the longest x1 15.5 us: shards(): lax.all_to_all(slots, ('gx', 'gz'), 0, 0, tiled=True)]
    ppermute x3 -> x2, starting transfers between devices: 8.89 us -> 3.8 us  [swap(): return lax.ppermute(x, 'gz', [(0, 1), (1, 0)])]
  transfers between devices with their start and end apart: 14 -> 13, of which waited for: 7 -> 6; matrix products, arithmetic and copies ran while one was open for 0% -> 0% of each run, Pallas kernels for 0% -> 0%
where the time goes in v11:
time: 96.3 us; the launch traced here: 96.1 us
  blocking collectives  55.3 us (57%)
  starting transfers between devices  15.9 us (17%)
  waiting for transfers between devices  15.9 us (17%)
  Pallas kernels  8.29 us (9%)
    all_to_all x1, blocking collectives, shards(): along_x = lax.all_to_all(slots, ('gx', 'gz'), 0, 0, tiled=True)  17.6 us
    ppermute x11, waiting for transfers between devices, shift(): return lax.ppermute(x, axis, pairs)  15.9 us
    all_to_all x1, blocking collectives, shards(): lax.all_to_all(slots, ('gx', 'gz'), 0, 0, tiled=True)  15.5 us
    all_to_all x1, blocking collectives, shards(): lax.all_to_all(second_slots(along_x, count_y), 'gy', 0, 0, tiled=True)  13.1 us
    ppermute x11, starting transfers between devices, shift(): return lax.ppermute(x, axis, pairs)  12.1 us
    all_to_all x1, blocking collectives, shards(): received = lax.all_to_all(slots_ac, 'gy', 0, 0, tiled=True)  9.07 us
    pallas_call x2, Pallas kernels, partials(): pl.pallas_call(functools.partial(round_kernel, first, keep, scale), out_s...  6.84 us
    ppermute x2, starting transfers between devices, swap(): return lax.ppermute(x, 'gz', [(0, 1), (1, 0)])  3.8 us
  transfers between devices with their start and end apart: 13, of which 6 were waited for; matrix products, arithmetic and copies ran while one was open for 0% of the time, Pallas kernels for 0%

profile of v11, /device:TPU:1, one launch (start us, length us, event | category | flops | bytes accessed | tf_op | source)
XLA Modules:
  0.0 96.1 jit_solution(1977056539037467877)
XLA Ops:
  0.6 0.8 first_slots.1
  1.4 17.6 %all_to_all.20.all_ref.refs_1_ = f32[16,8,128]{2,1,0:T(8,128)S(1)} all-to-all(f32[16,8,128]{2,1,0:T(8,128)S(1)} %first_slots.1), channel_id=1, replica_groups=mesh['gx'=8,'gy'=16,'gz'=2] {'gx','gz'}, dimensions={0} | all-to-all | bytes 131072 | tf_op jit(solution)/shard_map/all_to_all | solution.py:322
  19.0 13.1 %all_to_all.21.refs_0_ = f32[16,8,128]{2,1,0:T(8,128)S(1)} all-to-all(f32[16,8,128]{2,1,0:T(8,128)S(1)} %second_slots.1), channel_id=1, replica_groups=mesh['gx'=8,'gy'=16,'gz'=2] {'gy'}, dimensions={0} | all-to-all | bytes 131072 | tf_op jit(solution)/shard_map/all_to_all | solution.py:323
  32.1 4.1 %partials.2 = (f32[128,128]{1,0:T(8,128)S(1)}, f32[128,128]{1,0:T(8,128)S(1)}, f32[8192,128]{1,0:T(8,128)S(1)}) custom-call(f32[16,8,128]{2,1,0:T(8,128)S(1)} %all_to_all.21.refs_0_, f32[16,8,128]{2,1,0:T(8,128)S(1)} %all_to_all.20.all_ref.refs_1_, f32[8192,128]{1,0:T(8,128)} %bitcast.1), custom_call_target="tpu_custom_call" | custom-call | flops 1073741824 | bytes 4194304 | tf_op jit(solution)/shard_map/partials/pallas_call | solution.py:169
  36.2 0.3 collective-permute-start
  36.5 2.5 %collective-permute-start.1 = (f32[128,128]{1,0:T(8,128)S(1)}, f32[128,128]{1,0:T(8,128)S(1)}, u32[]{:S(2)}, u32[]{:S(2)}) collective-permute-start(f32[128,128]{1,0:T(8,128)S(1)} %get-tuple-element.8), channel_id=1, source_target_pairs={{0,224},{32,0},{64,32},{96,64},{128,96},{160,128},{192,160},{224,1... | collective-permute-start | bytes 196616 | tf_op jit(solution)/shard_map/ppermute | solution.py:292
  39.0 3.6 %collective-permute-start.4 = (f32[128,128]{1,0:T(8,128)S(1)}, f32[128,128]{1,0:T(8,128)S(1)}, u32[]{:S(2)}, u32[]{:S(2)}) collective-permute-start(f32[128,128]{1,0:T(8,128)S(1)} %get-tuple-element.8), channel_id=1, source_target_pairs={{0,192},{32,224},{64,0},{96,32},{128,64},{160,96},{192,128},{224,1... | collective-permute-start | bytes 196616 | tf_op jit(solution)/shard_map/ppermute | solution.py:292
  42.6 2.7 %collective-permute-start.5 = (f32[128,128]{1,0:T(8,128)S(1)}, f32[128,128]{1,0:T(8,128)S(1)}, u32[]{:S(2)}, u32[]{:S(2)}) collective-permute-start(f32[128,128]{1,0:T(8,128)S(1)} %get-tuple-element.9), channel_id=1, source_target_pairs={{0,1},{1,0},{2,3},{3,2},{4,5},{5,4},{6,7},{7,6},{8,9},{9,8},{10,11... | collective-permute-start | bytes 196616 | tf_op jit(solution)/shard_map/ppermute | solution.py:306
  45.3 0.9 collective-permute-start.2
  46.2 8.0 %collective-permute-done.2 = f32[128,128]{1,0:T(8,128)S(1)} collective-permute-done((f32[128,128]{1,0:T(8,128)S(1)}, f32[128,128]{1,0:T(8,128)S(1)}, u32[]{:S(2)}, u32[]{:S(2)}) %collective-permute-start.2) | collective-permute-done | bytes 65568 | tf_op jit(solution)/shard_map/ppermute | solution.py:292
  54.3 0.4 collective-permute-start.6
  54.6 2.4 %collective-permute-start.7 = (f32[128,128]{1,0:T(8,128)S(1)}, f32[128,128]{1,0:T(8,128)S(1)}, u32[]{:S(2)}, u32[]{:S(2)}) collective-permute-start(f32[128,128]{1,0:T(8,128)S(1)} %get-tuple-element.13), channel_id=1, source_target_pairs={{0,6},{2,0},{4,2},{6,4},{8,14},{10,8},{12,10},{14,12},{16,22},{18,... | collective-permute-start | bytes 196616 | tf_op jit(solution)/shard_map/ppermute | solution.py:292
  57.0 1.1 %collective-permute-start.12 = (f32[64,128]{1,0:T(8,128)S(1)}, f32[64,128]{1,0:T(8,128)S(1)}, u32[]{:S(2)}, u32[]{:S(2)}) collective-permute-start(f32[64,128]{1,0:T(8,128)S(1)} %slice.4), channel_id=1, source_target_pairs={{0,1},{1,0},{2,3},{3,2},{4,5},{5,4},{6,7},{7,6},{8,9},{9,8},{10,11... | collective-permute-start | bytes 98312 | tf_op jit(solution)/shard_map/ppermute | solution.py:306
  58.1 0.6 collective-permute-done.6
  58.7 3.0 %collective-permute-done.8 = f32[128,128]{1,0:T(8,128)S(1)} collective-permute-done((f32[128,128]{1,0:T(8,128)S(1)}, f32[128,128]{1,0:T(8,128)S(1)}, u32[]{:S(2)}, u32[]{:S(2)}) %collective-permute-start.8) | collective-permute-done | bytes 65568 | tf_op jit(solution)/shard_map/ppermute | solution.py:292
  61.7 0.9 collective-permute-start.10
  62.6 1.2 %collective-permute-start.11 = (f32[128,128]{1,0:T(8,128)S(1)}, f32[128,128]{1,0:T(8,128)S(1)}, u32[]{:S(2)}, u32[]{:S(2)}) collective-permute-start(f32[128,128]{1,0:T(8,128)S(1)} %add_add_fusion.1), channel_id=1, source_target_pairs={{0,16},{2,18},{4,20},{6,22},{8,24},{10,26},{12,28},{14,30},{16,0},... | collective-permute-start | bytes 196616 | tf_op jit(solution)/shard_map/ppermute | solution.py:292
  63.8 1.1 %collective-permute-done.10 = f32[128,128]{1,0:T(8,128)S(1)} collective-permute-done((f32[128,128]{1,0:T(8,128)S(1)}, f32[128,128]{1,0:T(8,128)S(1)}, u32[]{:S(2)}, u32[]{:S(2)}) %collective-permute-start.10) | collective-permute-done | bytes 65568 | tf_op jit(solution)/shard_map/ppermute | solution.py:292
  64.8 2.3 %collective-permute-done.11 = f32[128,128]{1,0:T(8,128)S(1)} collective-permute-done((f32[128,128]{1,0:T(8,128)S(1)}, f32[128,128]{1,0:T(8,128)S(1)}, u32[]{:S(2)}, u32[]{:S(2)}) %collective-permute-start.11) | collective-permute-done | bytes 65568 | tf_op jit(solution)/shard_map/ppermute | solution.py:292
  67.2 0.9 collective-permute-done.9
  68.1 2.7 %partials.3 = (f32[16,8,128]{2,1,0:T(8,128)S(1)}, f32[64,128]{1,0:T(8,128)S(1)}) custom-call(f32[128,128]{1,0:T(8,128)S(1)} %add_add_fusion.refs_0_, f32[64,128]{1,0:T(8,128)S(1)} %slice_add_fusion.refs_1_, f32[8192,128]{1,0:T(8,128)S(1)} %get-tuple-element.10.refs_2_), custom_call_target="tpu_custom_call" | custom-call | flops 1073741824 | bytes 4194304 | tf_op jit(solution)/shard_map/partials/pallas_call | solution.py:169
  70.8 9.1 %all_to_all.22.received_ref = f32[16,8,128]{2,1,0:T(8,128)S(1)} all-to-all(f32[16,8,128]{2,1,0:T(8,128)S(1)} %get-tuple-element.11), channel_id=1, replica_groups=mesh['gx'=8,'gy'=16,'gz'=2] {'gy'}, dimensions={0} | all-to-all | bytes 131072 | tf_op jit(solution)/shard_map/all_to_all | solution.py:340
  79.9 15.5 %all_to_all.23.all_ref = f32[16,8,128]{2,1,0:T(8,128)S(1)} all-to-all(f32[16,8,128]{2,1,0:T(8,128)S(1)} %middle_slots.1), channel_id=1, replica_groups=mesh['gx'=8,'gy'=16,'gz'=2] {'gx','gz'}, dimensions={0} | all-to-all | bytes 131072 | tf_op jit(solution)/shard_map/all_to_all | solution.py:342
  95.5 0.6 last_sums.1
  (19 shorter events, 0.2 us)
Async XLA Ops:
  36.2 9.1 %collective-permute-start = (f32[128,128]{1,0:T(8,128)S(1)}, f32[128,128]{1,0:T(8,128)S(1)}, u32[]{:S(2)}, u32[]{:S(2)}) collective-permute-start(f32[128,128]{1,0:T(8,128)S(1)} %get-tuple-element.8), channel_id=1, source_target_pairs={{0,32},{32,64},{64,96},{96,128},{128,160},{160,192},{192,224},{224... | collective-permute-start | bytes 196616 | tf_op jit(solution)/shard_map/ppermute | solution.py:292
  36.5 8.8 %collective-permute-start.1 = (f32[128,128]{1,0:T(8,128)S(1)}, f32[128,128]{1,0:T(8,128)S(1)}, u32[]{:S(2)}, u32[]{:S(2)}) collective-permute-start(f32[128,128]{1,0:T(8,128)S(1)} %get-tuple-element.8), channel_id=1, source_target_pairs={{0,224},{32,0},{64,32},{96,64},{128,96},{160,128},{192,160},{224,1... | collective-permute-start | bytes 196616 | tf_op jit(solution)/shard_map/ppermute | solution.py:292
  39.0 7.2 %collective-permute-start.3 = (f32[128,128]{1,0:T(8,128)S(1)}, f32[128,128]{1,0:T(8,128)S(1)}, u32[]{:S(2)}, u32[]{:S(2)}) collective-permute-start(f32[128,128]{1,0:T(8,128)S(1)} %get-tuple-element.8), channel_id=1, source_target_pairs={{0,64},{32,96},{64,128},{96,160},{128,192},{160,224},{192,0},{224,... | collective-permute-start | bytes 196616 | tf_op jit(solution)/shard_map/ppermute | solution.py:292
  39.0 7.2 %collective-permute-start.4 = (f32[128,128]{1,0:T(8,128)S(1)}, f32[128,128]{1,0:T(8,128)S(1)}, u32[]{:S(2)}, u32[]{:S(2)}) collective-permute-start(f32[128,128]{1,0:T(8,128)S(1)} %get-tuple-element.8), channel_id=1, source_target_pairs={{0,192},{32,224},{64,0},{96,32},{128,64},{160,96},{192,128},{224,1... | collective-permute-start | bytes 196616 | tf_op jit(solution)/shard_map/ppermute | solution.py:292
  42.6 3.6 %collective-permute-start.5 = (f32[128,128]{1,0:T(8,128)S(1)}, f32[128,128]{1,0:T(8,128)S(1)}, u32[]{:S(2)}, u32[]{:S(2)}) collective-permute-start(f32[128,128]{1,0:T(8,128)S(1)} %get-tuple-element.9), channel_id=1, source_target_pairs={{0,1},{1,0},{2,3},{3,2},{4,5},{5,4},{6,7},{7,6},{8,9},{9,8},{10,11... | collective-permute-start | bytes 196616 | tf_op jit(solution)/shard_map/ppermute | solution.py:306
  45.3 8.9 %collective-permute-start.2 = (f32[128,128]{1,0:T(8,128)S(1)}, f32[128,128]{1,0:T(8,128)S(1)}, u32[]{:S(2)}, u32[]{:S(2)}) collective-permute-start(f32[128,128]{1,0:T(8,128)S(1)} %add_add_fusion.3), channel_id=1, source_target_pairs={{0,128},{32,160},{64,192},{96,224},{128,0},{160,32},{192,64},{224,... | collective-permute-start | bytes 196616 | tf_op jit(solution)/shard_map/ppermute | solution.py:292
  54.3 4.4 %collective-permute-start.6 = (f32[128,128]{1,0:T(8,128)S(1)}, f32[128,128]{1,0:T(8,128)S(1)}, u32[]{:S(2)}, u32[]{:S(2)}) collective-permute-start(f32[128,128]{1,0:T(8,128)S(1)} %get-tuple-element.13), channel_id=1, source_target_pairs={{0,2},{2,4},{4,6},{6,0},{8,10},{10,12},{12,14},{14,8},{16,18},{18,... | collective-permute-start | bytes 196616 | tf_op jit(solution)/shard_map/ppermute | solution.py:292
  54.6 4.0 %collective-permute-start.7 = (f32[128,128]{1,0:T(8,128)S(1)}, f32[128,128]{1,0:T(8,128)S(1)}, u32[]{:S(2)}, u32[]{:S(2)}) collective-permute-start(f32[128,128]{1,0:T(8,128)S(1)} %get-tuple-element.13), channel_id=1, source_target_pairs={{0,6},{2,0},{4,2},{6,4},{8,14},{10,8},{12,10},{14,12},{16,22},{18,... | collective-permute-start | bytes 196616 | tf_op jit(solution)/shard_map/ppermute | solution.py:292
  57.0 4.6 %collective-permute-start.8 = (f32[128,128]{1,0:T(8,128)S(1)}, f32[128,128]{1,0:T(8,128)S(1)}, u32[]{:S(2)}, u32[]{:S(2)}) collective-permute-start(f32[128,128]{1,0:T(8,128)S(1)} %get-tuple-element.13), channel_id=1, source_target_pairs={{0,4},{2,6},{4,0},{6,2},{8,12},{10,14},{12,8},{14,10},{16,20},{18,... | collective-permute-start | bytes 196616 | tf_op jit(solution)/shard_map/ppermute | solution.py:292
  57.0 6.7 %collective-permute-start.12 = (f32[64,128]{1,0:T(8,128)S(1)}, f32[64,128]{1,0:T(8,128)S(1)}, u32[]{:S(2)}, u32[]{:S(2)}) collective-permute-start(f32[64,128]{1,0:T(8,128)S(1)} %slice.4), channel_id=1, source_target_pairs={{0,1},{1,0},{2,3},{3,2},{4,5},{5,4},{6,7},{7,6},{8,9},{9,8},{10,11... | collective-permute-start | bytes 98312 | tf_op jit(solution)/shard_map/ppermute | solution.py:306
  61.7 3.2 %collective-permute-start.10 = (f32[128,128]{1,0:T(8,128)S(1)}, f32[128,128]{1,0:T(8,128)S(1)}, u32[]{:S(2)}, u32[]{:S(2)}) collective-permute-start(f32[128,128]{1,0:T(8,128)S(1)} %add_add_fusion.1), channel_id=1, source_target_pairs={{0,24},{2,26},{4,28},{6,30},{8,0},{10,2},{12,4},{14,6},{16,8},{18,... | collective-permute-start | bytes 196616 | tf_op jit(solution)/shard_map/ppermute | solution.py:292
  62.6 4.6 %collective-permute-start.11 = (f32[128,128]{1,0:T(8,128)S(1)}, f32[128,128]{1,0:T(8,128)S(1)}, u32[]{:S(2)}, u32[]{:S(2)}) collective-permute-start(f32[128,128]{1,0:T(8,128)S(1)} %add_add_fusion.1), channel_id=1, source_target_pairs={{0,16},{2,18},{4,20},{6,22},{8,24},{10,26},{12,28},{14,30},{16,0},... | collective-permute-start | bytes 196616 | tf_op jit(solution)/shard_map/ppermute | solution.py:292
  63.7 4.3 %collective-permute-start.9 = (f32[128,128]{1,0:T(8,128)S(1)}, f32[128,128]{1,0:T(8,128)S(1)}, u32[]{:S(2)}, u32[]{:S(2)}) collective-permute-start(f32[128,128]{1,0:T(8,128)S(1)} %add_add_fusion.1), channel_id=1, source_target_pairs={{0,8},{2,10},{4,12},{6,14},{8,16},{10,18},{12,20},{14,22},{16,24},... | collective-permute-start | bytes 196616 | tf_op jit(solution)/shard_map/ppermute | solution.py:292

commit v12 on v11

--- a/solution.py
+++ b/solution.py
@@ -118,8 +118,7 @@
     group = 128 // count_j
     lane = lax.broadcasted_iota(jnp.int32, (rank, 128), 1) // count_j
 
-    half, quarter = chunks // 2, chunks // 4
-    waits = {0: half, half: half + quarter, half + quarter: chunks}
+    waits = {0: chunks // 2, chunks // 2: chunks}
     moment_b = jnp.zeros((count_j, width), F32)
     moment_c = jnp.zeros((width, 2 * count_k), F32)
     for c in range(chunks):
@@ -297,9 +296,18 @@
     return three + shift(three, "gx", 1, 8, 4) + shift(x, "gx", 1, 8, 2) + shift(x, "gx", 1, 8, -2)
 
 
+def cross(x, stride, by):
+    pairs = []
+    for n in range(lax.axis_size("gy")):
+        place = n // stride % 4
+        to = n + ((place + by) % 4 - place) * stride
+        pairs += [(2 * n, 2 * to + 1), (2 * n + 1, 2 * to)]
+    return lax.ppermute(x, ("gy", "gz"), pairs)
+
+
 def ring4(x, stride):
-    ones = shift(x, "gy", stride, 4, 1) + shift(x, "gy", stride, 4, -1)
-    return (x + ones) + shift(x, "gy", stride, 4, 2)
+    ones = cross(x, stride, 1) + cross(x, stride, -1)
+    return (swap(x) + ones) + cross(x, stride, 2)
 
 
 def swap(x):

time: 96.3 us -> 97.3 us (1.010)
  waiting for transfers between devices: 15.9 us -> 18.7 us
  blocking collectives: 55.3 us -> 52.6 us
    ppermute x0 -> x6, waiting for transfers between devices: none -> 10.7 us  [cross(): return lax.ppermute(x, ('gy', 'gz'), pairs)]
    ppermute x11 -> x5, waiting for transfers between devices: 15.9 us -> 8.01 us  [shift(): return lax.ppermute(x, axis, pairs)]
    ppermute x0 -> x6, starting transfers between devices: none -> 5.93 us  [cross(): return lax.ppermute(x, ('gy', 'gz'), pairs)]
    ppermute x11 -> x5, starting transfers between devices: 12.1 us -> 7.22 us  [shift(): return lax.ppermute(x, axis, pairs)]
    all_to_all x1, blocking collectives: 15.5 us -> 12.3 us  [shards(): lax.all_to_all(slots, ('gx', 'gz'), 0, 0, tiled=True)]
    ppermute x2 -> x4, starting transfers between devices: 3.8 us -> 3.65 us  [swap(): return lax.ppermute(x, 'gz', [(0, 1), (1, 0)])]
  transfers between devices with their start and end apart: 13 -> 15, of which waited for: 6 -> 7; matrix products, arithmetic and copies ran while one was open for 0% -> 0% of each run, Pallas kernels for 0% -> 0%
where the time goes in v12:
time: 97.3 us; the launch traced here: 97.1 us
  blocking collectives  52.6 us (54%)
  waiting for transfers between devices  18.7 us (19%)
  starting transfers between devices  16.8 us (17%)
  Pallas kernels  8.11 us (8%)
    all_to_all x1, blocking collectives, shards(): along_x = lax.all_to_all(slots, ('gx', 'gz'), 0, 0, tiled=True)  17.6 us
    all_to_all x1, blocking collectives, shards(): lax.all_to_all(second_slots(along_x, count_y), 'gy', 0, 0, tiled=True)  13.1 us
    all_to_all x1, blocking collectives, shards(): lax.all_to_all(slots, ('gx', 'gz'), 0, 0, tiled=True)  12.3 us
    ppermute x6, waiting for transfers between devices, cross(): return lax.ppermute(x, ('gy', 'gz'), pairs)  10.7 us
    all_to_all x1, blocking collectives, shards(): received = lax.all_to_all(slots_ac, 'gy', 0, 0, tiled=True)  9.65 us
    ppermute x5, waiting for transfers between devices, shift(): return lax.ppermute(x, axis, pairs)  8.01 us
    ppermute x5, starting transfers between devices, shift(): return lax.ppermute(x, axis, pairs)  7.22 us
    pallas_call x2, Pallas kernels, partials(): pl.pallas_call(functools.partial(round_kernel, first, keep, scale), out_s...  6.66 us
  transfers between devices with their start and end apart: 15, of which 7 were waited for; matrix products, arithmetic and copies ran while one was open for 0% of the time, Pallas kernels for 0%

profile of v12, /device:TPU:1, one launch (start us, length us, event | category | flops | bytes accessed | tf_op | source)
XLA Modules:
  0.0 97.1 jit_solution(13290052238471343897)
XLA Ops:
  0.6 0.8 first_slots.1
  1.4 17.6 %all_to_all.20.all_ref.refs_1_ = f32[16,8,128]{2,1,0:T(8,128)S(1)} all-to-all(f32[16,8,128]{2,1,0:T(8,128)S(1)} %first_slots.1), channel_id=1, replica_groups=mesh['gx'=8,'gy'=16,'gz'=2] {'gx','gz'}, dimensions={0} | all-to-all | bytes 131072 | tf_op jit(solution)/shard_map/all_to_all | solution.py:330
  19.0 13.1 %all_to_all.21.refs_0_ = f32[16,8,128]{2,1,0:T(8,128)S(1)} all-to-all(f32[16,8,128]{2,1,0:T(8,128)S(1)} %second_slots.1), channel_id=1, replica_groups=mesh['gx'=8,'gy'=16,'gz'=2] {'gy'}, dimensions={0} | all-to-all | bytes 131072 | tf_op jit(solution)/shard_map/all_to_all | solution.py:331
  32.1 3.9 %partials.2 = (f32[128,128]{1,0:T(8,128)S(1)}, f32[128,128]{1,0:T(8,128)S(1)}, f32[8192,128]{1,0:T(8,128)S(1)}) custom-call(f32[16,8,128]{2,1,0:T(8,128)S(1)} %all_to_all.21.refs_0_, f32[16,8,128]{2,1,0:T(8,128)S(1)} %all_to_all.20.all_ref.refs_1_, f32[8192,128]{1,0:T(8,128)} %bitcast.1), custom_call_target="tpu_custom_call" | custom-call | flops 1073741824 | bytes 4194304 | tf_op jit(solution)/shard_map/partials/pallas_call | solution.py:168
  36.1 0.3 collective-permute-start
  36.3 2.5 %collective-permute-start.1 = (f32[128,128]{1,0:T(8,128)S(1)}, f32[128,128]{1,0:T(8,128)S(1)}, u32[]{:S(2)}, u32[]{:S(2)}) collective-permute-start(f32[128,128]{1,0:T(8,128)S(1)} %get-tuple-element.8), channel_id=1, source_target_pairs={{0,224},{32,0},{64,32},{96,64},{128,96},{160,128},{192,160},{224,1... | collective-permute-start | bytes 196616 | tf_op jit(solution)/shard_map/ppermute | solution.py:291
  38.8 3.6 %collective-permute-start.4 = (f32[128,128]{1,0:T(8,128)S(1)}, f32[128,128]{1,0:T(8,128)S(1)}, u32[]{:S(2)}, u32[]{:S(2)}) collective-permute-start(f32[128,128]{1,0:T(8,128)S(1)} %get-tuple-element.8), channel_id=1, source_target_pairs={{0,192},{32,224},{64,0},{96,32},{128,64},{160,96},{192,128},{224,1... | collective-permute-start | bytes 196616 | tf_op jit(solution)/shard_map/ppermute | solution.py:291
  42.4 2.7 %collective-permute-start.5 = (f32[128,128]{1,0:T(8,128)S(1)}, f32[128,128]{1,0:T(8,128)S(1)}, u32[]{:S(2)}, u32[]{:S(2)}) collective-permute-start(f32[128,128]{1,0:T(8,128)S(1)} %get-tuple-element.9), channel_id=1, source_target_pairs={{0,1},{1,0},{2,3},{3,2},{4,5},{5,4},{6,7},{7,6},{8,9},{9,8},{10,11... | collective-permute-start | bytes 196616 | tf_op jit(solution)/shard_map/ppermute | solution.py:314
  45.1 0.9 collective-permute-start.2
  46.1 8.0 %collective-permute-done.2 = f32[128,128]{1,0:T(8,128)S(1)} collective-permute-done((f32[128,128]{1,0:T(8,128)S(1)}, f32[128,128]{1,0:T(8,128)S(1)}, u32[]{:S(2)}, u32[]{:S(2)}) %collective-permute-start.2) | collective-permute-done | bytes 65568 | tf_op jit(solution)/shard_map/ppermute | solution.py:291
  54.1 0.5 collective-permute-start.6
  54.9 2.7 %collective-permute-start.8 = (f32[128,128]{1,0:T(8,128)S(1)}, f32[128,128]{1,0:T(8,128)S(1)}, u32[]{:S(2)}, u32[]{:S(2)}) collective-permute-start(f32[128,128]{1,0:T(8,128)S(1)} %get-tuple-element.13), channel_id=1, source_target_pairs={{0,7},{1,6},{2,1},{3,0},{4,3},{5,2},{6,5},{7,4},{8,15},{9,14},{10,... | collective-permute-start | bytes 196616 | tf_op jit(solution)/shard_map/ppermute | solution.py:305
  57.8 1.8 %collective-permute-done.7 = f32[128,128]{1,0:T(8,128)S(1)} collective-permute-done((f32[128,128]{1,0:T(8,128)S(1)}, f32[128,128]{1,0:T(8,128)S(1)}, u32[]{:S(2)}, u32[]{:S(2)}) %collective-permute-start.7) | collective-permute-done | bytes 65568 | tf_op jit(solution)/shard_map/ppermute | solution.py:305
  59.6 0.9 collective-permute-done.8
  60.5 2.4 %collective-permute-done.9 = f32[128,128]{1,0:T(8,128)S(1)} collective-permute-done((f32[128,128]{1,0:T(8,128)S(1)}, f32[128,128]{1,0:T(8,128)S(1)}, u32[]{:S(2)}, u32[]{:S(2)}) %collective-permute-start.9) | collective-permute-done | bytes 65568 | tf_op jit(solution)/shard_map/ppermute | solution.py:305
  63.1 0.5 collective-permute-start.11
  63.6 2.4 %collective-permute-start.12 = (f32[128,128]{1,0:T(8,128)S(1)}, f32[128,128]{1,0:T(8,128)S(1)}, u32[]{:S(2)}, u32[]{:S(2)}) collective-permute-start(f32[128,128]{1,0:T(8,128)S(1)} %add_add_fusion.1), channel_id=1, source_target_pairs={{0,25},{1,24},{2,27},{3,26},{4,29},{5,28},{6,31},{7,30},{8,1},{9,0... | collective-permute-start | bytes 196616 | tf_op jit(solution)/shard_map/ppermute | solution.py:305
  66.1 2.3 %collective-permute-done.11 = f32[128,128]{1,0:T(8,128)S(1)} collective-permute-done((f32[128,128]{1,0:T(8,128)S(1)}, f32[128,128]{1,0:T(8,128)S(1)}, u32[]{:S(2)}, u32[]{:S(2)}) %collective-permute-start.11) | collective-permute-done | bytes 65568 | tf_op jit(solution)/shard_map/ppermute | solution.py:305
  68.4 0.5 collective-permute-done.12
  68.9 2.8 %collective-permute-done.13 = f32[128,128]{1,0:T(8,128)S(1)} collective-permute-done((f32[128,128]{1,0:T(8,128)S(1)}, f32[128,128]{1,0:T(8,128)S(1)}, u32[]{:S(2)}, u32[]{:S(2)}) %collective-permute-start.13) | collective-permute-done | bytes 65568 | tf_op jit(solution)/shard_map/ppermute | solution.py:305
  71.7 2.7 %partials.3 = (f32[16,8,128]{2,1,0:T(8,128)S(1)}, f32[64,128]{1,0:T(8,128)S(1)}) custom-call(f32[128,128]{1,0:T(8,128)S(1)} %add_add_fusion.refs_0_, f32[64,128]{1,0:T(8,128)S(1)} %slice_add_fusion.refs_1_, f32[8192,128]{1,0:T(8,128)S(1)} %get-tuple-element.10.refs_2_), custom_call_target="tpu_custom_call" | custom-call | flops 1073741824 | bytes 4194304 | tf_op jit(solution)/shard_map/partials/pallas_call | solution.py:168
  74.4 9.7 %all_to_all.22.received_ref = f32[16,8,128]{2,1,0:T(8,128)S(1)} all-to-all(f32[16,8,128]{2,1,0:T(8,128)S(1)} %get-tuple-element.11), channel_id=1, replica_groups=mesh['gx'=8,'gy'=16,'gz'=2] {'gy'}, dimensions={0} | all-to-all | bytes 131072 | tf_op jit(solution)/shard_map/all_to_all | solution.py:348
  84.1 12.3 %all_to_all.23.all_ref = f32[16,8,128]{2,1,0:T(8,128)S(1)} all-to-all(f32[16,8,128]{2,1,0:T(8,128)S(1)} %middle_slots.1), channel_id=1, replica_groups=mesh['gx'=8,'gy'=16,'gz'=2] {'gx','gz'}, dimensions={0} | all-to-all | bytes 131072 | tf_op jit(solution)/shard_map/all_to_all | solution.py:350
  96.5 0.6 last_sums.1
  (23 shorter events, 0.8 us)
Async XLA Ops:
  36.1 9.1 %collective-permute-start = (f32[128,128]{1,0:T(8,128)S(1)}, f32[128,128]{1,0:T(8,128)S(1)}, u32[]{:S(2)}, u32[]{:S(2)}) collective-permute-start(f32[128,128]{1,0:T(8,128)S(1)} %get-tuple-element.8), channel_id=1, source_target_pairs={{0,32},{32,64},{64,96},{96,128},{128,160},{160,192},{192,224},{224... | collective-permute-start | bytes 196616 | tf_op jit(solution)/shard_map/ppermute | solution.py:291
  36.3 8.8 %collective-permute-start.1 = (f32[128,128]{1,0:T(8,128)S(1)}, f32[128,128]{1,0:T(8,128)S(1)}, u32[]{:S(2)}, u32[]{:S(2)}) collective-permute-start(f32[128,128]{1,0:T(8,128)S(1)} %get-tuple-element.8), channel_id=1, source_target_pairs={{0,224},{32,0},{64,32},{96,64},{128,96},{160,128},{192,160},{224,1... | collective-permute-start | bytes 196616 | tf_op jit(solution)/shard_map/ppermute | solution.py:291
  38.8 7.2 %collective-permute-start.3 = (f32[128,128]{1,0:T(8,128)S(1)}, f32[128,128]{1,0:T(8,128)S(1)}, u32[]{:S(2)}, u32[]{:S(2)}) collective-permute-start(f32[128,128]{1,0:T(8,128)S(1)} %get-tuple-element.8), channel_id=1, source_target_pairs={{0,64},{32,96},{64,128},{96,160},{128,192},{160,224},{192,0},{224,... | collective-permute-start | bytes 196616 | tf_op jit(solution)/shard_map/ppermute | solution.py:291
  38.8 7.2 %collective-permute-start.4 = (f32[128,128]{1,0:T(8,128)S(1)}, f32[128,128]{1,0:T(8,128)S(1)}, u32[]{:S(2)}, u32[]{:S(2)}) collective-permute-start(f32[128,128]{1,0:T(8,128)S(1)} %get-tuple-element.8), channel_id=1, source_target_pairs={{0,192},{32,224},{64,0},{96,32},{128,64},{160,96},{192,128},{224,1... | collective-permute-start | bytes 196616 | tf_op jit(solution)/shard_map/ppermute | solution.py:291
  42.4 3.6 %collective-permute-start.5 = (f32[128,128]{1,0:T(8,128)S(1)}, f32[128,128]{1,0:T(8,128)S(1)}, u32[]{:S(2)}, u32[]{:S(2)}) collective-permute-start(f32[128,128]{1,0:T(8,128)S(1)} %get-tuple-element.9), channel_id=1, source_target_pairs={{0,1},{1,0},{2,3},{3,2},{4,5},{5,4},{6,7},{7,6},{8,9},{9,8},{10,11... | collective-permute-start | bytes 196616 | tf_op jit(solution)/shard_map/ppermute | solution.py:314
  45.1 8.9 %collective-permute-start.2 = (f32[128,128]{1,0:T(8,128)S(1)}, f32[128,128]{1,0:T(8,128)S(1)}, u32[]{:S(2)}, u32[]{:S(2)}) collective-permute-start(f32[128,128]{1,0:T(8,128)S(1)} %add_add_fusion.3), channel_id=1, source_target_pairs={{0,128},{32,160},{64,192},{96,224},{128,0},{160,32},{192,64},{224,... | collective-permute-start | bytes 196616 | tf_op jit(solution)/shard_map/ppermute | solution.py:291
  54.1 3.7 %collective-permute-start.6 = (f32[128,128]{1,0:T(8,128)S(1)}, f32[128,128]{1,0:T(8,128)S(1)}, u32[]{:S(2)}, u32[]{:S(2)}) collective-permute-start(f32[128,128]{1,0:T(8,128)S(1)} %get-tuple-element.13), channel_id=1, source_target_pairs={{0,1},{1,0},{2,3},{3,2},{4,5},{5,4},{6,7},{7,6},{8,9},{9,8},{10,11... | collective-permute-start | bytes 196616 | tf_op jit(solution)/shard_map/ppermute | solution.py:314
  54.6 5.0 %collective-permute-start.7 = (f32[128,128]{1,0:T(8,128)S(1)}, f32[128,128]{1,0:T(8,128)S(1)}, u32[]{:S(2)}, u32[]{:S(2)}) collective-permute-start(f32[128,128]{1,0:T(8,128)S(1)} %get-tuple-element.13), channel_id=1, source_target_pairs={{0,3},{1,2},{2,5},{3,4},{4,7},{5,6},{6,1},{7,0},{8,11},{9,10},{10,... | collective-permute-start | bytes 196616 | tf_op jit(solution)/shard_map/ppermute | solution.py:305
  54.9 5.6 %collective-permute-start.8 = (f32[128,128]{1,0:T(8,128)S(1)}, f32[128,128]{1,0:T(8,128)S(1)}, u32[]{:S(2)}, u32[]{:S(2)}) collective-permute-start(f32[128,128]{1,0:T(8,128)S(1)} %get-tuple-element.13), channel_id=1, source_target_pairs={{0,7},{1,6},{2,1},{3,0},{4,3},{5,2},{6,5},{7,4},{8,15},{9,14},{10,... | collective-permute-start | bytes 196616 | tf_op jit(solution)/shard_map/ppermute | solution.py:305
  57.6 5.3 %collective-permute-start.9 = (f32[128,128]{1,0:T(8,128)S(1)}, f32[128,128]{1,0:T(8,128)S(1)}, u32[]{:S(2)}, u32[]{:S(2)}) collective-permute-start(f32[128,128]{1,0:T(8,128)S(1)} %get-tuple-element.13), channel_id=1, source_target_pairs={{0,5},{1,4},{2,7},{3,6},{4,1},{5,0},{6,3},{7,2},{8,13},{9,12},{10,... | collective-permute-start | bytes 196616 | tf_op jit(solution)/shard_map/ppermute | solution.py:305
  57.6 8.5 %collective-permute-start.14 = (f32[64,128]{1,0:T(8,128)S(1)}, f32[64,128]{1,0:T(8,128)S(1)}, u32[]{:S(2)}, u32[]{:S(2)}) collective-permute-start(f32[64,128]{1,0:T(8,128)S(1)} %slice.4), channel_id=1, source_target_pairs={{0,1},{1,0},{2,3},{3,2},{4,5},{5,4},{6,7},{7,6},{8,9},{9,8},{10,11... | collective-permute-start | bytes 98312 | tf_op jit(solution)/shard_map/ppermute | solution.py:314
  62.9 3.2 %collective-permute-start.10 = (f32[128,128]{1,0:T(8,128)S(1)}, f32[128,128]{1,0:T(8,128)S(1)}, u32[]{:S(2)}, u32[]{:S(2)}) collective-permute-start(f32[128,128]{1,0:T(8,128)S(1)} %add_add_fusion.1), channel_id=1, source_target_pairs={{0,1},{1,0},{2,3},{3,2},{4,5},{5,4},{6,7},{7,6},{8,9},{9,8},{10,11... | collective-permute-start | bytes 196616 | tf_op jit(solution)/shard_map/ppermute | solution.py:314
  63.1 5.3 %collective-permute-start.11 = (f32[128,128]{1,0:T(8,128)S(1)}, f32[128,128]{1,0:T(8,128)S(1)}, u32[]{:S(2)}, u32[]{:S(2)}) collective-permute-start(f32[128,128]{1,0:T(8,128)S(1)} %add_add_fusion.1), channel_id=1, source_target_pairs={{0,9},{1,8},{2,11},{3,10},{4,13},{5,12},{6,15},{7,14},{8,17},{9,16... | collective-permute-start | bytes 196616 | tf_op jit(solution)/shard_map/ppermute | solution.py:305
  63.6 5.3 %collective-permute-start.12 = (f32[128,128]{1,0:T(8,128)S(1)}, f32[128,128]{1,0:T(8,128)S(1)}, u32[]{:S(2)}, u32[]{:S(2)}) collective-permute-start(f32[128,128]{1,0:T(8,128)S(1)} %add_add_fusion.1), channel_id=1, source_target_pairs={{0,25},{1,24},{2,27},{3,26},{4,29},{5,28},{6,31},{7,30},{8,1},{9,0... | collective-permute-start | bytes 196616 | tf_op jit(solution)/shard_map/ppermute | solution.py:305
  66.0 5.7 %collective-permute-start.13 = (f32[128,128]{1,0:T(8,128)S(1)}, f32[128,128]{1,0:T(8,128)S(1)}, u32[]{:S(2)}, u32[]{:S(2)}) collective-permute-start(f32[128,128]{1,0:T(8,128)S(1)} %add_add_fusion.1), channel_id=1, source_target_pairs={{0,17},{1,16},{2,19},{3,18},{4,21},{5,20},{6,23},{7,22},{8,25},{9,... | collective-permute-start | bytes 196616 | tf_op jit(solution)/shard_map/ppermute | solution.py:305

commit v13 on v11

--- a/solution.py
+++ b/solution.py
@@ -118,8 +118,7 @@
     group = 128 // count_j
     lane = lax.broadcasted_iota(jnp.int32, (rank, 128), 1) // count_j
 
-    half, quarter = chunks // 2, chunks // 4
-    waits = {0: half, half: half + quarter, half + quarter: chunks}
+    waits = {0: chunks // 2, chunks // 2: chunks}
     moment_b = jnp.zeros((count_j, width), F32)
     moment_c = jnp.zeros((width, 2 * count_k), F32)
     for c in range(chunks):
@@ -293,8 +292,10 @@
 
 
 def ring8(x):
-    three = x + shift(x, "gx", 1, 8, 1) + shift(x, "gx", 1, 8, -1)
-    return three + shift(three, "gx", 1, 8, 4) + shift(x, "gx", 1, 8, 2) + shift(x, "gx", 1, 8, -2)
+    below, above = shift(x, "gx", 1, 8, 1), shift(x, "gx", 1, 8, -1)
+    two = x + above
+    three = two + below
+    return three + (shift(three, "gx", 1, 8, -3) + shift(two, "gx", 1, 8, 3))
 
 
 def ring4(x, stride):

time: 96.3 us -> 97.6 us (1.013)
  waiting for transfers between devices: 15.9 us -> 6.61 us
  blocking collectives: 55.3 us -> 62.8 us
  starting transfers between devices: 15.9 us -> 19.1 us
    ppermute x11 -> x10, waiting for transfers between devices: 15.9 us -> 6.6 us  [shift(): return lax.ppermute(x, axis, pairs)]
    all_to_all x1, blocking collectives: 15.5 us -> 21 us  [shards(): lax.all_to_all(slots, ('gx', 'gz'), 0, 0, tiled=True)]
    ppermute x2, starting transfers between devices: 3.8 us -> 6.3 us  [swap(): return lax.ppermute(x, 'gz', [(0, 1), (1, 0)])]
    all_to_all x1, blocking collectives: 9.07 us -> 11.1 us  [shards(): received = lax.all_to_all(slots_ac, 'gy', 0, 0, tiled=True)]
    ppermute x11 -> x10, starting transfers between devices: 12.1 us -> 12.8 us  [shift(): return lax.ppermute(x, axis, pairs)]
  transfers between devices with their start and end apart: 13 -> 12, of which waited for: 6 -> 5; matrix products, arithmetic and copies ran while one was open for 0% -> 0% of each run, Pallas kernels for 0% -> 0%
where the time goes in v13:
time: 97.6 us; the launch traced here: 97.4 us
  blocking collectives  62.8 us (64%)
  starting transfers between devices  19.1 us (20%)
  Pallas kernels  8.11 us (8%)
  waiting for transfers between devices  6.61 us (7%)
    all_to_all x1, blocking collectives, shards(): lax.all_to_all(slots, ('gx', 'gz'), 0, 0, tiled=True)  21 us
    all_to_all x1, blocking collectives, shards(): along_x = lax.all_to_all(slots, ('gx', 'gz'), 0, 0, tiled=True)  17.6 us
    all_to_all x1, blocking collectives, shards(): lax.all_to_all(second_slots(along_x, count_y), 'gy', 0, 0, tiled=True)  13.1 us
    ppermute x10, starting transfers between devices, shift(): return lax.ppermute(x, axis, pairs)  12.8 us
    all_to_all x1, blocking collectives, shards(): received = lax.all_to_all(slots_ac, 'gy', 0, 0, tiled=True)  11.1 us
    pallas_call x2, Pallas kernels, partials(): pl.pallas_call(functools.partial(round_kernel, first, keep, scale), out_s...  6.66 us
    ppermute x10, waiting for transfers between devices, shift(): return lax.ppermute(x, axis, pairs)  6.6 us
    ppermute x2, starting transfers between devices, swap(): return lax.ppermute(x, 'gz', [(0, 1), (1, 0)])  6.3 us
  transfers between devices with their start and end apart: 12, of which 5 were waited for; matrix products, arithmetic and copies ran while one was open for 0% of the time, Pallas kernels for 0%

profile of v13, /device:TPU:1, one launch (start us, length us, event | category | flops | bytes accessed | tf_op | source)
XLA Modules:
  0.0 97.4 jit_solution(6557663990397690513)
XLA Ops:
  0.6 0.8 first_slots.1
  1.4 17.6 %all_to_all.20.all_ref.refs_1_ = f32[16,8,128]{2,1,0:T(8,128)S(1)} all-to-all(f32[16,8,128]{2,1,0:T(8,128)S(1)} %first_slots.1), channel_id=1, replica_groups=mesh['gx'=8,'gy'=16,'gz'=2] {'gx','gz'}, dimensions={0} | all-to-all | bytes 131072 | tf_op jit(solution)/shard_map/all_to_all | solution.py:323
  19.0 13.1 %all_to_all.21.refs_0_ = f32[16,8,128]{2,1,0:T(8,128)S(1)} all-to-all(f32[16,8,128]{2,1,0:T(8,128)S(1)} %second_slots.1), channel_id=1, replica_groups=mesh['gx'=8,'gy'=16,'gz'=2] {'gy'}, dimensions={0} | all-to-all | bytes 131072 | tf_op jit(solution)/shard_map/all_to_all | solution.py:324
  32.1 3.9 %partials.2 = (f32[128,128]{1,0:T(8,128)S(1)}, f32[128,128]{1,0:T(8,128)S(1)}, f32[8192,128]{1,0:T(8,128)S(1)}) custom-call(f32[16,8,128]{2,1,0:T(8,128)S(1)} %all_to_all.21.refs_0_, f32[16,8,128]{2,1,0:T(8,128)S(1)} %all_to_all.20.all_ref.refs_1_, f32[8192,128]{1,0:T(8,128)} %bitcast.1), custom_call_target="tpu_custom_call" | custom-call | flops 1073741824 | bytes 4194304 | tf_op jit(solution)/shard_map/partials/pallas_call | solution.py:168
  36.1 0.3 collective-permute-start.1
  36.3 2.5 %collective-permute-start = (f32[128,128]{1,0:T(8,128)S(1)}, f32[128,128]{1,0:T(8,128)S(1)}, u32[]{:S(2)}, u32[]{:S(2)}) collective-permute-start(f32[128,128]{1,0:T(8,128)S(1)} %get-tuple-element.8), channel_id=1, source_target_pairs={{0,224},{32,0},{64,32},{96,64},{128,96},{160,128},{192,160},{224,1... | collective-permute-start | bytes 196616 | tf_op jit(solution)/shard_map/ppermute | solution.py:291
  38.8 2.2 %collective-permute-start.4 = (f32[128,128]{1,0:T(8,128)S(1)}, f32[128,128]{1,0:T(8,128)S(1)}, u32[]{:S(2)}, u32[]{:S(2)}) collective-permute-start(f32[128,128]{1,0:T(8,128)S(1)} %get-tuple-element.9), channel_id=1, source_target_pairs={{0,1},{1,0},{2,3},{3,2},{4,5},{5,4},{6,7},{7,6},{8,9},{9,8},{10,11... | collective-permute-start | bytes 196616 | tf_op jit(solution)/shard_map/ppermute | solution.py:307
  41.0 0.4 collective-permute-start.3
  41.4 4.1 %collective-permute-start.2 = (f32[128,128]{1,0:T(8,128)S(1)}, f32[128,128]{1,0:T(8,128)S(1)}, u32[]{:S(2)}, u32[]{:S(2)}) collective-permute-start(f32[128,128]{1,0:T(8,128)S(1)} %get-tuple-element.15), channel_id=1, source_target_pairs={{0,160},{32,192},{64,224},{96,0},{128,32},{160,64},{192,96},{224,1... | collective-permute-start | bytes 196616 | tf_op jit(solution)/shard_map/ppermute | solution.py:291
  45.6 1.7 %collective-permute-done.3 = f32[128,128]{1,0:T(8,128)S(1)} collective-permute-done((f32[128,128]{1,0:T(8,128)S(1)}, f32[128,128]{1,0:T(8,128)S(1)}, u32[]{:S(2)}, u32[]{:S(2)}) %collective-permute-start.3) | collective-permute-done | bytes 65568 | tf_op jit(solution)/shard_map/ppermute | solution.py:291
  47.2 0.5 collective-permute-done.2
  47.7 1.1 %collective-permute-start.7 = (f32[128,128]{1,0:T(8,128)S(1)}, f32[128,128]{1,0:T(8,128)S(1)}, u32[]{:S(2)}, u32[]{:S(2)}) collective-permute-start(f32[128,128]{1,0:T(8,128)S(1)} %get-tuple-element.13), channel_id=1, source_target_pairs={{0,4},{2,6},{4,0},{6,2},{8,12},{10,14},{12,8},{14,10},{16,20},{18,... | collective-permute-start | bytes 196616 | tf_op jit(solution)/shard_map/ppermute | solution.py:291
  48.8 1.6 %collective-permute-start.6 = (f32[128,128]{1,0:T(8,128)S(1)}, f32[128,128]{1,0:T(8,128)S(1)}, u32[]{:S(2)}, u32[]{:S(2)}) collective-permute-start(f32[128,128]{1,0:T(8,128)S(1)} %get-tuple-element.13), channel_id=1, source_target_pairs={{0,6},{2,0},{4,2},{6,4},{8,14},{10,8},{12,10},{14,12},{16,22},{18,... | collective-permute-start | bytes 196616 | tf_op jit(solution)/shard_map/ppermute | solution.py:291
  50.5 4.1 %collective-permute-start.11 = (f32[64,128]{1,0:T(8,128)S(1)}, f32[64,128]{1,0:T(8,128)S(1)}, u32[]{:S(2)}, u32[]{:S(2)}) collective-permute-start(f32[64,128]{1,0:T(8,128)S(1)} %slice.4), channel_id=1, source_target_pairs={{0,1},{1,0},{2,3},{3,2},{4,5},{5,4},{6,7},{7,6},{8,9},{9,8},{10,11... | collective-permute-start | bytes 98312 | tf_op jit(solution)/shard_map/ppermute | solution.py:307
  54.6 0.2 collective-permute-done.5
  54.8 1.0 %collective-permute-start.10 = (f32[128,128]{1,0:T(8,128)S(1)}, f32[128,128]{1,0:T(8,128)S(1)}, u32[]{:S(2)}, u32[]{:S(2)}) collective-permute-start(f32[128,128]{1,0:T(8,128)S(1)} %add_add_fusion.1), channel_id=1, source_target_pairs={{0,16},{2,18},{4,20},{6,22},{8,24},{10,26},{12,28},{14,30},{16,0},... | collective-permute-start | bytes 196616 | tf_op jit(solution)/shard_map/ppermute | solution.py:291
  55.8 1.7 %collective-permute-start.9 = (f32[128,128]{1,0:T(8,128)S(1)}, f32[128,128]{1,0:T(8,128)S(1)}, u32[]{:S(2)}, u32[]{:S(2)}) collective-permute-start(f32[128,128]{1,0:T(8,128)S(1)} %add_add_fusion.1), channel_id=1, source_target_pairs={{0,24},{2,26},{4,28},{6,30},{8,0},{10,2},{12,4},{14,6},{16,8},{18,... | collective-permute-start | bytes 196616 | tf_op jit(solution)/shard_map/ppermute | solution.py:291
  57.5 0.0 collective-permute-start.8
  57.6 2.0 %collective-permute-done.10 = f32[128,128]{1,0:T(8,128)S(1)} collective-permute-done((f32[128,128]{1,0:T(8,128)S(1)}, f32[128,128]{1,0:T(8,128)S(1)}, u32[]{:S(2)}, u32[]{:S(2)}) %collective-permute-start.10) | collective-permute-done | bytes 65568 | tf_op jit(solution)/shard_map/ppermute | solution.py:291
  59.5 2.3 %collective-permute-done.8 = f32[128,128]{1,0:T(8,128)S(1)} collective-permute-done((f32[128,128]{1,0:T(8,128)S(1)}, f32[128,128]{1,0:T(8,128)S(1)}, u32[]{:S(2)}, u32[]{:S(2)}) %collective-permute-start.8) | collective-permute-done | bytes 65568 | tf_op jit(solution)/shard_map/ppermute | solution.py:291
  61.9 2.7 %partials.3 = (f32[16,8,128]{2,1,0:T(8,128)S(1)}, f32[64,128]{1,0:T(8,128)S(1)}) custom-call(f32[128,128]{1,0:T(8,128)S(1)} %add_add_fusion.refs_0_, f32[64,128]{1,0:T(8,128)S(1)} %slice_add_fusion.refs_1_, f32[8192,128]{1,0:T(8,128)S(1)} %get-tuple-element.10.refs_2_), custom_call_target="tpu_custom_call" | custom-call | flops 1073741824 | bytes 4194304 | tf_op jit(solution)/shard_map/partials/pallas_call | solution.py:168
  64.6 11.1 %all_to_all.22.received_ref = f32[16,8,128]{2,1,0:T(8,128)S(1)} all-to-all(f32[16,8,128]{2,1,0:T(8,128)S(1)} %get-tuple-element.11), channel_id=1, replica_groups=mesh['gx'=8,'gy'=16,'gz'=2] {'gy'}, dimensions={0} | all-to-all | bytes 131072 | tf_op jit(solution)/shard_map/all_to_all | solution.py:341
  75.7 21.0 %all_to_all.23.all_ref = f32[16,8,128]{2,1,0:T(8,128)S(1)} all-to-all(f32[16,8,128]{2,1,0:T(8,128)S(1)} %middle_slots.1), channel_id=1, replica_groups=mesh['gx'=8,'gy'=16,'gz'=2] {'gx','gz'}, dimensions={0} | all-to-all | bytes 131072 | tf_op jit(solution)/shard_map/all_to_all | solution.py:343
  96.8 0.6 last_sums.1
  (17 shorter events, 0.1 us)
Async XLA Ops:
  36.1 4.9 %collective-permute-start.1 = (f32[128,128]{1,0:T(8,128)S(1)}, f32[128,128]{1,0:T(8,128)S(1)}, u32[]{:S(2)}, u32[]{:S(2)}) collective-permute-start(f32[128,128]{1,0:T(8,128)S(1)} %get-tuple-element.8), channel_id=1, source_target_pairs={{0,32},{32,64},{64,96},{96,128},{128,160},{160,192},{192,224},{224... | collective-permute-start | bytes 196616 | tf_op jit(solution)/shard_map/ppermute | solution.py:291
  36.3 4.6 %collective-permute-start = (f32[128,128]{1,0:T(8,128)S(1)}, f32[128,128]{1,0:T(8,128)S(1)}, u32[]{:S(2)}, u32[]{:S(2)}) collective-permute-start(f32[128,128]{1,0:T(8,128)S(1)} %get-tuple-element.8), channel_id=1, source_target_pairs={{0,224},{32,0},{64,32},{96,64},{128,96},{160,128},{192,160},{224,1... | collective-permute-start | bytes 196616 | tf_op jit(solution)/shard_map/ppermute | solution.py:291
  38.8 6.7 %collective-permute-start.4 = (f32[128,128]{1,0:T(8,128)S(1)}, f32[128,128]{1,0:T(8,128)S(1)}, u32[]{:S(2)}, u32[]{:S(2)}) collective-permute-start(f32[128,128]{1,0:T(8,128)S(1)} %get-tuple-element.9), channel_id=1, source_target_pairs={{0,1},{1,0},{2,3},{3,2},{4,5},{5,4},{6,7},{7,6},{8,9},{9,8},{10,11... | collective-permute-start | bytes 196616 | tf_op jit(solution)/shard_map/ppermute | solution.py:307
  41.0 6.2 %collective-permute-start.3 = (f32[128,128]{1,0:T(8,128)S(1)}, f32[128,128]{1,0:T(8,128)S(1)}, u32[]{:S(2)}, u32[]{:S(2)}) collective-permute-start(f32[128,128]{1,0:T(8,128)S(1)} %get-tuple-element.16), channel_id=1, source_target_pairs={{0,96},{32,128},{64,160},{96,192},{128,224},{160,0},{192,32},{224,... | collective-permute-start | bytes 196616 | tf_op jit(solution)/shard_map/ppermute | solution.py:291
  41.4 6.2 %collective-permute-start.2 = (f32[128,128]{1,0:T(8,128)S(1)}, f32[128,128]{1,0:T(8,128)S(1)}, u32[]{:S(2)}, u32[]{:S(2)}) collective-permute-start(f32[128,128]{1,0:T(8,128)S(1)} %get-tuple-element.15), channel_id=1, source_target_pairs={{0,160},{32,192},{64,224},{96,0},{128,32},{160,64},{192,96},{224,1... | collective-permute-start | bytes 196616 | tf_op jit(solution)/shard_map/ppermute | solution.py:291
  47.7 6.9 %collective-permute-start.7 = (f32[128,128]{1,0:T(8,128)S(1)}, f32[128,128]{1,0:T(8,128)S(1)}, u32[]{:S(2)}, u32[]{:S(2)}) collective-permute-start(f32[128,128]{1,0:T(8,128)S(1)} %get-tuple-element.13), channel_id=1, source_target_pairs={{0,4},{2,6},{4,0},{6,2},{8,12},{10,14},{12,8},{14,10},{16,20},{18,... | collective-permute-start | bytes 196616 | tf_op jit(solution)/shard_map/ppermute | solution.py:291
  48.8 5.8 %collective-permute-start.6 = (f32[128,128]{1,0:T(8,128)S(1)}, f32[128,128]{1,0:T(8,128)S(1)}, u32[]{:S(2)}, u32[]{:S(2)}) collective-permute-start(f32[128,128]{1,0:T(8,128)S(1)} %get-tuple-element.13), channel_id=1, source_target_pairs={{0,6},{2,0},{4,2},{6,4},{8,14},{10,8},{12,10},{14,12},{16,22},{18,... | collective-permute-start | bytes 196616 | tf_op jit(solution)/shard_map/ppermute | solution.py:291
  50.5 4.3 %collective-permute-start.5 = (f32[128,128]{1,0:T(8,128)S(1)}, f32[128,128]{1,0:T(8,128)S(1)}, u32[]{:S(2)}, u32[]{:S(2)}) collective-permute-start(f32[128,128]{1,0:T(8,128)S(1)} %get-tuple-element.13), channel_id=1, source_target_pairs={{0,2},{2,4},{4,6},{6,0},{8,10},{10,12},{12,14},{14,8},{16,18},{18,... | collective-permute-start | bytes 196616 | tf_op jit(solution)/shard_map/ppermute | solution.py:291
  50.5 7.1 %collective-permute-start.11 = (f32[64,128]{1,0:T(8,128)S(1)}, f32[64,128]{1,0:T(8,128)S(1)}, u32[]{:S(2)}, u32[]{:S(2)}) collective-permute-start(f32[64,128]{1,0:T(8,128)S(1)} %slice.4), channel_id=1, source_target_pairs={{0,1},{1,0},{2,3},{3,2},{4,5},{5,4},{6,7},{7,6},{8,9},{9,8},{10,11... | collective-permute-start | bytes 98312 | tf_op jit(solution)/shard_map/ppermute | solution.py:307
  54.8 4.7 %collective-permute-start.10 = (f32[128,128]{1,0:T(8,128)S(1)}, f32[128,128]{1,0:T(8,128)S(1)}, u32[]{:S(2)}, u32[]{:S(2)}) collective-permute-start(f32[128,128]{1,0:T(8,128)S(1)} %add_add_fusion.1), channel_id=1, source_target_pairs={{0,16},{2,18},{4,20},{6,22},{8,24},{10,26},{12,28},{14,30},{16,0},... | collective-permute-start | bytes 196616 | tf_op jit(solution)/shard_map/ppermute | solution.py:291
  55.8 3.7 %collective-permute-start.9 = (f32[128,128]{1,0:T(8,128)S(1)}, f32[128,128]{1,0:T(8,128)S(1)}, u32[]{:S(2)}, u32[]{:S(2)}) collective-permute-start(f32[128,128]{1,0:T(8,128)S(1)} %add_add_fusion.1), channel_id=1, source_target_pairs={{0,24},{2,26},{4,28},{6,30},{8,0},{10,2},{12,4},{14,6},{16,8},{18,... | collective-permute-start | bytes 196616 | tf_op jit(solution)/shard_map/ppermute | solution.py:291
  57.5 4.3 %collective-permute-start.8 = (f32[128,128]{1,0:T(8,128)S(1)}, f32[128,128]{1,0:T(8,128)S(1)}, u32[]{:S(2)}, u32[]{:S(2)}) collective-permute-start(f32[128,128]{1,0:T(8,128)S(1)} %add_add_fusion.1), channel_id=1, source_target_pairs={{0,8},{2,10},{4,12},{6,14},{8,16},{10,18},{12,20},{14,22},{16,24},... | collective-permute-start | bytes 196616 | tf_op jit(solution)/shard_map/ppermute | solution.py:291

commit v14 on v11

--- a/solution.py
+++ b/solution.py
@@ -118,8 +118,7 @@
     group = 128 // count_j
     lane = lax.broadcasted_iota(jnp.int32, (rank, 128), 1) // count_j
 
-    half, quarter = chunks // 2, chunks // 4
-    waits = {0: half, half: half + quarter, half + quarter: chunks}
+    waits = {0: chunks // 2, chunks // 2: chunks}
     moment_b = jnp.zeros((count_j, width), F32)
     moment_c = jnp.zeros((width, 2 * count_k), F32)
     for c in range(chunks):

time: 96.3 us -> 96.1 us (level)
  no operation moved by 1% of the time
where the time goes in v14:
time: 96.1 us; the launch traced here: 95.9 us
  blocking collectives  55.3 us (58%)
  starting transfers between devices  15.9 us (17%)
  waiting for transfers between devices  15.9 us (17%)
  Pallas kernels  8.11 us (8%)
    all_to_all x1, blocking collectives, shards(): along_x = lax.all_to_all(slots, ('gx', 'gz'), 0, 0, tiled=True)  17.6 us
    ppermute x11, waiting for transfers between devices, shift(): return lax.ppermute(x, axis, pairs)  15.8 us
    all_to_all x1, blocking collectives, shards(): lax.all_to_all(slots, ('gx', 'gz'), 0, 0, tiled=True)  15.5 us
    all_to_all x1, blocking collectives, shards(): lax.all_to_all(second_slots(along_x, count_y), 'gy', 0, 0, tiled=True)  13.1 us
    ppermute x11, starting transfers between devices, shift(): return lax.ppermute(x, axis, pairs)  12.1 us
    all_to_all x1, blocking collectives, shards(): received = lax.all_to_all(slots_ac, 'gy', 0, 0, tiled=True)  9.07 us
    pallas_call x2, Pallas kernels, partials(): pl.pallas_call(functools.partial(round_kernel, first, keep, scale), out_s...  6.66 us
    ppermute x2, starting transfers between devices, swap(): return lax.ppermute(x, 'gz', [(0, 1), (1, 0)])  3.8 us
  transfers between devices with their start and end apart: 13, of which 6 were waited for; matrix products, arithmetic and copies ran while one was open for 0% of the time, Pallas kernels for 0%

profile of v14, /device:TPU:1, one launch (start us, length us, event | category | flops | bytes accessed | tf_op | source)
XLA Modules:
  0.0 95.9 jit_solution(13690867545750845486)
XLA Ops:
  0.6 0.8 first_slots.1
  1.4 17.6 %all_to_all.20.all_ref.refs_1_ = f32[16,8,128]{2,1,0:T(8,128)S(1)} all-to-all(f32[16,8,128]{2,1,0:T(8,128)S(1)} %first_slots.1), channel_id=1, replica_groups=mesh['gx'=8,'gy'=16,'gz'=2] {'gx','gz'}, dimensions={0} | all-to-all | bytes 131072 | tf_op jit(solution)/shard_map/all_to_all | solution.py:321
  19.0 13.1 %all_to_all.21.refs_0_ = f32[16,8,128]{2,1,0:T(8,128)S(1)} all-to-all(f32[16,8,128]{2,1,0:T(8,128)S(1)} %second_slots.1), channel_id=1, replica_groups=mesh['gx'=8,'gy'=16,'gz'=2] {'gy'}, dimensions={0} | all-to-all | bytes 131072 | tf_op jit(solution)/shard_map/all_to_all | solution.py:322
  32.1 3.9 %partials.2 = (f32[128,128]{1,0:T(8,128)S(1)}, f32[128,128]{1,0:T(8,128)S(1)}, f32[8192,128]{1,0:T(8,128)S(1)}) custom-call(f32[16,8,128]{2,1,0:T(8,128)S(1)} %all_to_all.21.refs_0_, f32[16,8,128]{2,1,0:T(8,128)S(1)} %all_to_all.20.all_ref.refs_1_, f32[8192,128]{1,0:T(8,128)} %bitcast.1), custom_call_target="tpu_custom_call" | custom-call | flops 1073741824 | bytes 4194304 | tf_op jit(solution)/shard_map/partials/pallas_call | solution.py:168
  36.1 0.3 collective-permute-start
  36.3 2.5 %collective-permute-start.1 = (f32[128,128]{1,0:T(8,128)S(1)}, f32[128,128]{1,0:T(8,128)S(1)}, u32[]{:S(2)}, u32[]{:S(2)}) collective-permute-start(f32[128,128]{1,0:T(8,128)S(1)} %get-tuple-element.8), channel_id=1, source_target_pairs={{0,224},{32,0},{64,32},{96,64},{128,96},{160,128},{192,160},{224,1... | collective-permute-start | bytes 196616 | tf_op jit(solution)/shard_map/ppermute | solution.py:291
  38.8 3.6 %collective-permute-start.4 = (f32[128,128]{1,0:T(8,128)S(1)}, f32[128,128]{1,0:T(8,128)S(1)}, u32[]{:S(2)}, u32[]{:S(2)}) collective-permute-start(f32[128,128]{1,0:T(8,128)S(1)} %get-tuple-element.8), channel_id=1, source_target_pairs={{0,192},{32,224},{64,0},{96,32},{128,64},{160,96},{192,128},{224,1... | collective-permute-start | bytes 196616 | tf_op jit(solution)/shard_map/ppermute | solution.py:291
  42.4 2.7 %collective-permute-start.5 = (f32[128,128]{1,0:T(8,128)S(1)}, f32[128,128]{1,0:T(8,128)S(1)}, u32[]{:S(2)}, u32[]{:S(2)}) collective-permute-start(f32[128,128]{1,0:T(8,128)S(1)} %get-tuple-element.9), channel_id=1, source_target_pairs={{0,1},{1,0},{2,3},{3,2},{4,5},{5,4},{6,7},{7,6},{8,9},{9,8},{10,11... | collective-permute-start | bytes 196616 | tf_op jit(solution)/shard_map/ppermute | solution.py:305
  45.1 0.9 collective-permute-start.2
  46.1 8.0 %collective-permute-done.2 = f32[128,128]{1,0:T(8,128)S(1)} collective-permute-done((f32[128,128]{1,0:T(8,128)S(1)}, f32[128,128]{1,0:T(8,128)S(1)}, u32[]{:S(2)}, u32[]{:S(2)}) %collective-permute-start.2) | collective-permute-done | bytes 65568 | tf_op jit(solution)/shard_map/ppermute | solution.py:291
  54.1 0.4 collective-permute-start.6
  54.4 2.4 %collective-permute-start.7 = (f32[128,128]{1,0:T(8,128)S(1)}, f32[128,128]{1,0:T(8,128)S(1)}, u32[]{:S(2)}, u32[]{:S(2)}) collective-permute-start(f32[128,128]{1,0:T(8,128)S(1)} %get-tuple-element.13), channel_id=1, source_target_pairs={{0,6},{2,0},{4,2},{6,4},{8,14},{10,8},{12,10},{14,12},{16,22},{18,... | collective-permute-start | bytes 196616 | tf_op jit(solution)/shard_map/ppermute | solution.py:291
  56.8 1.1 %collective-permute-start.12 = (f32[64,128]{1,0:T(8,128)S(1)}, f32[64,128]{1,0:T(8,128)S(1)}, u32[]{:S(2)}, u32[]{:S(2)}) collective-permute-start(f32[64,128]{1,0:T(8,128)S(1)} %slice.4), channel_id=1, source_target_pairs={{0,1},{1,0},{2,3},{3,2},{4,5},{5,4},{6,7},{7,6},{8,9},{9,8},{10,11... | collective-permute-start | bytes 98312 | tf_op jit(solution)/shard_map/ppermute | solution.py:305
  57.9 0.6 collective-permute-done.6
  58.5 3.0 %collective-permute-done.8 = f32[128,128]{1,0:T(8,128)S(1)} collective-permute-done((f32[128,128]{1,0:T(8,128)S(1)}, f32[128,128]{1,0:T(8,128)S(1)}, u32[]{:S(2)}, u32[]{:S(2)}) %collective-permute-start.8) | collective-permute-done | bytes 65568 | tf_op jit(solution)/shard_map/ppermute | solution.py:291
  61.5 0.9 collective-permute-start.10
  62.4 1.2 %collective-permute-start.11 = (f32[128,128]{1,0:T(8,128)S(1)}, f32[128,128]{1,0:T(8,128)S(1)}, u32[]{:S(2)}, u32[]{:S(2)}) collective-permute-start(f32[128,128]{1,0:T(8,128)S(1)} %add_add_fusion.1), channel_id=1, source_target_pairs={{0,16},{2,18},{4,20},{6,22},{8,24},{10,26},{12,28},{14,30},{16,0},... | collective-permute-start | bytes 196616 | tf_op jit(solution)/shard_map/ppermute | solution.py:291
  63.6 1.1 %collective-permute-done.10 = f32[128,128]{1,0:T(8,128)S(1)} collective-permute-done((f32[128,128]{1,0:T(8,128)S(1)}, f32[128,128]{1,0:T(8,128)S(1)}, u32[]{:S(2)}, u32[]{:S(2)}) %collective-permute-start.10) | collective-permute-done | bytes 65568 | tf_op jit(solution)/shard_map/ppermute | solution.py:291
  64.7 2.3 %collective-permute-done.11 = f32[128,128]{1,0:T(8,128)S(1)} collective-permute-done((f32[128,128]{1,0:T(8,128)S(1)}, f32[128,128]{1,0:T(8,128)S(1)}, u32[]{:S(2)}, u32[]{:S(2)}) %collective-permute-start.11) | collective-permute-done | bytes 65568 | tf_op jit(solution)/shard_map/ppermute | solution.py:291
  67.0 0.9 collective-permute-done.9
  67.9 2.7 %partials.3 = (f32[16,8,128]{2,1,0:T(8,128)S(1)}, f32[64,128]{1,0:T(8,128)S(1)}) custom-call(f32[128,128]{1,0:T(8,128)S(1)} %add_add_fusion.refs_0_, f32[64,128]{1,0:T(8,128)S(1)} %slice_add_fusion.refs_1_, f32[8192,128]{1,0:T(8,128)S(1)} %get-tuple-element.10.refs_2_), custom_call_target="tpu_custom_call" | custom-call | flops 1073741824 | bytes 4194304 | tf_op jit(solution)/shard_map/partials/pallas_call | solution.py:168
  70.6 9.1 %all_to_all.22.received_ref = f32[16,8,128]{2,1,0:T(8,128)S(1)} all-to-all(f32[16,8,128]{2,1,0:T(8,128)S(1)} %get-tuple-element.11), channel_id=1, replica_groups=mesh['gx'=8,'gy'=16,'gz'=2] {'gy'}, dimensions={0} | all-to-all | bytes 131072 | tf_op jit(solution)/shard_map/all_to_all | solution.py:339
  79.7 15.5 %all_to_all.23.all_ref = f32[16,8,128]{2,1,0:T(8,128)S(1)} all-to-all(f32[16,8,128]{2,1,0:T(8,128)S(1)} %middle_slots.1), channel_id=1, replica_groups=mesh['gx'=8,'gy'=16,'gz'=2] {'gx','gz'}, dimensions={0} | all-to-all | bytes 131072 | tf_op jit(solution)/shard_map/all_to_all | solution.py:341
  95.3 0.6 last_sums.1
  (19 shorter events, 0.2 us)
Async XLA Ops:
  36.1 9.1 %collective-permute-start = (f32[128,128]{1,0:T(8,128)S(1)}, f32[128,128]{1,0:T(8,128)S(1)}, u32[]{:S(2)}, u32[]{:S(2)}) collective-permute-start(f32[128,128]{1,0:T(8,128)S(1)} %get-tuple-element.8), channel_id=1, source_target_pairs={{0,32},{32,64},{64,96},{96,128},{128,160},{160,192},{192,224},{224... | collective-permute-start | bytes 196616 | tf_op jit(solution)/shard_map/ppermute | solution.py:291
  36.3 8.8 %collective-permute-start.1 = (f32[128,128]{1,0:T(8,128)S(1)}, f32[128,128]{1,0:T(8,128)S(1)}, u32[]{:S(2)}, u32[]{:S(2)}) collective-permute-start(f32[128,128]{1,0:T(8,128)S(1)} %get-tuple-element.8), channel_id=1, source_target_pairs={{0,224},{32,0},{64,32},{96,64},{128,96},{160,128},{192,160},{224,1... | collective-permute-start | bytes 196616 | tf_op jit(solution)/shard_map/ppermute | solution.py:291
  38.8 7.2 %collective-permute-start.3 = (f32[128,128]{1,0:T(8,128)S(1)}, f32[128,128]{1,0:T(8,128)S(1)}, u32[]{:S(2)}, u32[]{:S(2)}) collective-permute-start(f32[128,128]{1,0:T(8,128)S(1)} %get-tuple-element.8), channel_id=1, source_target_pairs={{0,64},{32,96},{64,128},{96,160},{128,192},{160,224},{192,0},{224,... | collective-permute-start | bytes 196616 | tf_op jit(solution)/shard_map/ppermute | solution.py:291
  38.8 7.2 %collective-permute-start.4 = (f32[128,128]{1,0:T(8,128)S(1)}, f32[128,128]{1,0:T(8,128)S(1)}, u32[]{:S(2)}, u32[]{:S(2)}) collective-permute-start(f32[128,128]{1,0:T(8,128)S(1)} %get-tuple-element.8), channel_id=1, source_target_pairs={{0,192},{32,224},{64,0},{96,32},{128,64},{160,96},{192,128},{224,1... | collective-permute-start | bytes 196616 | tf_op jit(solution)/shard_map/ppermute | solution.py:291
  42.4 3.6 %collective-permute-start.5 = (f32[128,128]{1,0:T(8,128)S(1)}, f32[128,128]{1,0:T(8,128)S(1)}, u32[]{:S(2)}, u32[]{:S(2)}) collective-permute-start(f32[128,128]{1,0:T(8,128)S(1)} %get-tuple-element.9), channel_id=1, source_target_pairs={{0,1},{1,0},{2,3},{3,2},{4,5},{5,4},{6,7},{7,6},{8,9},{9,8},{10,11... | collective-permute-start | bytes 196616 | tf_op jit(solution)/shard_map/ppermute | solution.py:305
  45.1 8.9 %collective-permute-start.2 = (f32[128,128]{1,0:T(8,128)S(1)}, f32[128,128]{1,0:T(8,128)S(1)}, u32[]{:S(2)}, u32[]{:S(2)}) collective-permute-start(f32[128,128]{1,0:T(8,128)S(1)} %add_add_fusion.3), channel_id=1, source_target_pairs={{0,128},{32,160},{64,192},{96,224},{128,0},{160,32},{192,64},{224,... | collective-permute-start | bytes 196616 | tf_op jit(solution)/shard_map/ppermute | solution.py:291
  54.1 4.4 %collective-permute-start.6 = (f32[128,128]{1,0:T(8,128)S(1)}, f32[128,128]{1,0:T(8,128)S(1)}, u32[]{:S(2)}, u32[]{:S(2)}) collective-permute-start(f32[128,128]{1,0:T(8,128)S(1)} %get-tuple-element.13), channel_id=1, source_target_pairs={{0,2},{2,4},{4,6},{6,0},{8,10},{10,12},{12,14},{14,8},{16,18},{18,... | collective-permute-start | bytes 196616 | tf_op jit(solution)/shard_map/ppermute | solution.py:291
  54.4 4.0 %collective-permute-start.7 = (f32[128,128]{1,0:T(8,128)S(1)}, f32[128,128]{1,0:T(8,128)S(1)}, u32[]{:S(2)}, u32[]{:S(2)}) collective-permute-start(f32[128,128]{1,0:T(8,128)S(1)} %get-tuple-element.13), channel_id=1, source_target_pairs={{0,6},{2,0},{4,2},{6,4},{8,14},{10,8},{12,10},{14,12},{16,22},{18,... | collective-permute-start | bytes 196616 | tf_op jit(solution)/shard_map/ppermute | solution.py:291
  56.8 4.6 %collective-permute-start.8 = (f32[128,128]{1,0:T(8,128)S(1)}, f32[128,128]{1,0:T(8,128)S(1)}, u32[]{:S(2)}, u32[]{:S(2)}) collective-permute-start(f32[128,128]{1,0:T(8,128)S(1)} %get-tuple-element.13), channel_id=1, source_target_pairs={{0,4},{2,6},{4,0},{6,2},{8,12},{10,14},{12,8},{14,10},{16,20},{18,... | collective-permute-start | bytes 196616 | tf_op jit(solution)/shard_map/ppermute | solution.py:291
  56.8 6.7 %collective-permute-start.12 = (f32[64,128]{1,0:T(8,128)S(1)}, f32[64,128]{1,0:T(8,128)S(1)}, u32[]{:S(2)}, u32[]{:S(2)}) collective-permute-start(f32[64,128]{1,0:T(8,128)S(1)} %slice.4), channel_id=1, source_target_pairs={{0,1},{1,0},{2,3},{3,2},{4,5},{5,4},{6,7},{7,6},{8,9},{9,8},{10,11... | collective-permute-start | bytes 98312 | tf_op jit(solution)/shard_map/ppermute | solution.py:305
  61.5 3.2 %collective-permute-start.10 = (f32[128,128]{1,0:T(8,128)S(1)}, f32[128,128]{1,0:T(8,128)S(1)}, u32[]{:S(2)}, u32[]{:S(2)}) collective-permute-start(f32[128,128]{1,0:T(8,128)S(1)} %add_add_fusion.1), channel_id=1, source_target_pairs={{0,24},{2,26},{4,28},{6,30},{8,0},{10,2},{12,4},{14,6},{16,8},{18,... | collective-permute-start | bytes 196616 | tf_op jit(solution)/shard_map/ppermute | solution.py:291
  62.4 4.6 %collective-permute-start.11 = (f32[128,128]{1,0:T(8,128)S(1)}, f32[128,128]{1,0:T(8,128)S(1)}, u32[]{:S(2)}, u32[]{:S(2)}) collective-permute-start(f32[128,128]{1,0:T(8,128)S(1)} %add_add_fusion.1), channel_id=1, source_target_pairs={{0,16},{2,18},{4,20},{6,22},{8,24},{10,26},{12,28},{14,30},{16,0},... | collective-permute-start | bytes 196616 | tf_op jit(solution)/shard_map/ppermute | solution.py:291
  63.6 4.3 %collective-permute-start.9 = (f32[128,128]{1,0:T(8,128)S(1)}, f32[128,128]{1,0:T(8,128)S(1)}, u32[]{:S(2)}, u32[]{:S(2)}) collective-permute-start(f32[128,128]{1,0:T(8,128)S(1)} %add_add_fusion.1), channel_id=1, source_target_pairs={{0,8},{2,10},{4,12},{6,14},{8,16},{10,18},{12,20},{14,22},{16,24},... | collective-permute-start | bytes 196616 | tf_op jit(solution)/shard_map/ppermute | solution.py:291

commit v15 on v10

--- a/solution.py
+++ b/solution.py
@@ -92,10 +92,10 @@
     per = CHUNK // count_j
 
     def fetch(c):
-        at = pl.ds(c * CHUNK, CHUNK)
+        at = pl.ds(c * (chunks // 4) * CHUNK, chunks // 4 * CHUNK)
         return pltpu.make_async_copy(t_hbm.at[at, :], t_ref.at[at, :], sems.at[c])
 
-    for c in range(chunks if first else 0):
+    for c in range(4 if first else 0):
         fetch(c).start()
 
     (unpack_first if first else unpack_second)(*small, a2_ref, b2_ref, c2_ref)
@@ -122,8 +122,8 @@
     moment_c = jnp.zeros((width, 2 * count_k), F32)
     for c in range(chunks):
         if first and c % (chunks // 2) == 0:
-            for n in range(c, c + chunks // 2):
-                fetch(n).wait()
+            for n in range(2):
+                fetch(4 * c // chunks + n).wait()
         high, low = split(t_ref[c * CHUNK : (c + 1) * CHUNK, :])
         terms = jnp.concatenate([high, low], axis=1)
         y = jnp.dot(terms, wc_ref[...], preferred_element_type=F32)
@@ -176,7 +176,7 @@
             pltpu.VMEM((2 * count_k, width), BF16),
             pltpu.VMEM((count_i, width), F32),
         ]
-        + [pltpu.SemaphoreType.DMA((tall // CHUNK,))] * first,
+        + [pltpu.SemaphoreType.DMA((4,))] * first,
         compiler_params=pltpu.CompilerParams(vmem_limit_bytes=24 << 20),
         cost_estimate=pl.CostEstimate(flops=1 << 30, bytes_accessed=4 << 20, transcendentals=0),
         name="partials",

time: 95.9 us -> 95.8 us (level)
  no operation moved by 1% of the time
where the time goes in v15:
time: 95.8 us; the launch traced here: 95.5 us
  blocking collectives  49.1 us (51%)
  starting transfers between devices  21 us (22%)
  waiting for transfers between devices  16.7 us (17%)
  Pallas kernels  7.95 us (8%)
    all_to_all x1, blocking collectives, shards(): along_x = lax.all_to_all(slots, ('gx', 'gz'), 0, 0, tiled=True)  17.6 us
    ppermute x11, waiting for transfers between devices, shift(): return lax.ppermute(x, axis, pairs)  15.8 us
    all_to_all x1, blocking collectives, shards(): lax.all_to_all(second_slots(along_x, count_y), 'gy', 0, 0, tiled=True)  13.1 us
    ppermute x11, starting transfers between devices, shift(): return lax.ppermute(x, axis, pairs)  12.1 us
    all_to_all x1, blocking collectives, shards(): bc = lax.all_to_all(slots_bc, 'gx', 0, 0, tiled=True)  9.37 us
    all_to_all x1, blocking collectives, shards(): ac = jnp.sum(lax.all_to_all(slots_ac, 'gy', 0, 0, tiled=True), axis=0)  9.07 us
    ppermute x3, starting transfers between devices, swap(): return lax.ppermute(x, 'gz', [(0, 1), (1, 0)])  8.89 us
    pallas_call x2, Pallas kernels, partials(): pl.pallas_call(functools.partial(round_kernel, first, keep, scale), out_s...  6.54 us
  transfers between devices with their start and end apart: 14, of which 7 were waited for; matrix products, arithmetic and copies ran while one was open for 0% of the time, Pallas kernels for 0%

profile of v15, /device:TPU:1, one launch (start us, length us, event | category | flops | bytes accessed | tf_op | source)
XLA Modules:
  0.0 95.5 jit_solution(2068596567122572996)
XLA Ops:
  0.6 0.8 first_slots.1
  1.4 17.6 %all_to_all.20.all_ref.refs_1_ = f32[16,8,128]{2,1,0:T(8,128)S(1)} all-to-all(f32[16,8,128]{2,1,0:T(8,128)S(1)} %first_slots.1), channel_id=1, replica_groups=mesh['gx'=8,'gy'=16,'gz'=2] {'gx','gz'}, dimensions={0} | all-to-all | bytes 131072 | tf_op jit(solution)/shard_map/all_to_all | solution.py:296
  19.0 13.1 %all_to_all.21.refs_0_ = f32[16,8,128]{2,1,0:T(8,128)S(1)} all-to-all(f32[16,8,128]{2,1,0:T(8,128)S(1)} %second_slots.1), channel_id=1, replica_groups=mesh['gx'=8,'gy'=16,'gz'=2] {'gy'}, dimensions={0} | all-to-all | bytes 131072 | tf_op jit(solution)/shard_map/all_to_all | solution.py:297
  32.1 3.8 %partials.2 = (f32[128,128]{1,0:T(8,128)S(1)}, f32[128,128]{1,0:T(8,128)S(1)}, f32[8192,128]{1,0:T(8,128)S(1)}) custom-call(f32[16,8,128]{2,1,0:T(8,128)S(1)} %all_to_all.21.refs_0_, f32[16,8,128]{2,1,0:T(8,128)S(1)} %all_to_all.20.all_ref.refs_1_, f32[8192,128]{1,0:T(8,128)} %bitcast.5), custom_call_target="tpu_custom_call" | custom-call | flops 1073741824 | bytes 4194304 | tf_op jit(solution)/shard_map/partials/pallas_call | solution.py:167
  36.2 2.5 %collective-permute-start.1 = (f32[128,128]{1,0:T(8,128)S(1)}, f32[128,128]{1,0:T(8,128)S(1)}, u32[]{:S(2)}, u32[]{:S(2)}) collective-permute-start(f32[128,128]{1,0:T(8,128)S(1)} %get-tuple-element.8), channel_id=1, source_target_pairs={{0,224},{32,0},{64,32},{96,64},{128,96},{160,128},{192,160},{224,1... | collective-permute-start | bytes 196616 | tf_op jit(solution)/shard_map/ppermute | solution.py:266
  38.7 3.6 %collective-permute-start.4 = (f32[128,128]{1,0:T(8,128)S(1)}, f32[128,128]{1,0:T(8,128)S(1)}, u32[]{:S(2)}, u32[]{:S(2)}) collective-permute-start(f32[128,128]{1,0:T(8,128)S(1)} %get-tuple-element.8), channel_id=1, source_target_pairs={{0,192},{32,224},{64,0},{96,32},{128,64},{160,96},{192,128},{224,1... | collective-permute-start | bytes 196616 | tf_op jit(solution)/shard_map/ppermute | solution.py:266
  42.3 2.7 %collective-permute-start.5 = (f32[128,128]{1,0:T(8,128)S(1)}, f32[128,128]{1,0:T(8,128)S(1)}, u32[]{:S(2)}, u32[]{:S(2)}) collective-permute-start(f32[128,128]{1,0:T(8,128)S(1)} %get-tuple-element.9), channel_id=1, source_target_pairs={{0,1},{1,0},{2,3},{3,2},{4,5},{5,4},{6,7},{7,6},{8,9},{9,8},{10,11... | collective-permute-start | bytes 196616 | tf_op jit(solution)/shard_map/ppermute | solution.py:280
  45.0 0.9 collective-permute-start.2
  45.9 8.0 %collective-permute-done.2 = f32[128,128]{1,0:T(8,128)S(1)} collective-permute-done((f32[128,128]{1,0:T(8,128)S(1)}, f32[128,128]{1,0:T(8,128)S(1)}, u32[]{:S(2)}, u32[]{:S(2)}) %collective-permute-start.2) | collective-permute-done | bytes 65568 | tf_op jit(solution)/shard_map/ppermute | solution.py:266
  54.3 2.4 %collective-permute-start.7 = (f32[128,128]{1,0:T(8,128)S(1)}, f32[128,128]{1,0:T(8,128)S(1)}, u32[]{:S(2)}, u32[]{:S(2)}) collective-permute-start(f32[128,128]{1,0:T(8,128)S(1)} %get-tuple-element.13), channel_id=1, source_target_pairs={{0,6},{2,0},{4,2},{6,4},{8,14},{10,8},{12,10},{14,12},{16,22},{18,... | collective-permute-start | bytes 196616 | tf_op jit(solution)/shard_map/ppermute | solution.py:266
  56.7 1.1 %collective-permute-start.12 = (f32[64,128]{1,0:T(8,128)S(1)}, f32[64,128]{1,0:T(8,128)S(1)}, u32[]{:S(2)}, u32[]{:S(2)}) collective-permute-start(f32[64,128]{1,0:T(8,128)S(1)} %slice.8), channel_id=1, source_target_pairs={{0,1},{1,0},{2,3},{3,2},{4,5},{5,4},{6,7},{7,6},{8,9},{9,8},{10,11... | collective-permute-start | bytes 98312 | tf_op jit(solution)/shard_map/ppermute | solution.py:280
  57.8 0.6 collective-permute-done.6
  58.4 3.0 %collective-permute-done.8 = f32[128,128]{1,0:T(8,128)S(1)} collective-permute-done((f32[128,128]{1,0:T(8,128)S(1)}, f32[128,128]{1,0:T(8,128)S(1)}, u32[]{:S(2)}, u32[]{:S(2)}) %collective-permute-start.8) | collective-permute-done | bytes 65568 | tf_op jit(solution)/shard_map/ppermute | solution.py:266
  61.3 0.9 collective-permute-start.10
  62.3 1.2 %collective-permute-start.11 = (f32[128,128]{1,0:T(8,128)S(1)}, f32[128,128]{1,0:T(8,128)S(1)}, u32[]{:S(2)}, u32[]{:S(2)}) collective-permute-start(f32[128,128]{1,0:T(8,128)S(1)} %add_add_fusion.1), channel_id=1, source_target_pairs={{0,16},{2,18},{4,20},{6,22},{8,24},{10,26},{12,28},{14,30},{16,0},... | collective-permute-start | bytes 196616 | tf_op jit(solution)/shard_map/ppermute | solution.py:266
  63.5 1.1 %collective-permute-done.10 = f32[128,128]{1,0:T(8,128)S(1)} collective-permute-done((f32[128,128]{1,0:T(8,128)S(1)}, f32[128,128]{1,0:T(8,128)S(1)}, u32[]{:S(2)}, u32[]{:S(2)}) %collective-permute-start.10) | collective-permute-done | bytes 65568 | tf_op jit(solution)/shard_map/ppermute | solution.py:266
  64.5 2.4 %collective-permute-done.11 = f32[128,128]{1,0:T(8,128)S(1)} collective-permute-done((f32[128,128]{1,0:T(8,128)S(1)}, f32[128,128]{1,0:T(8,128)S(1)}, u32[]{:S(2)}, u32[]{:S(2)}) %collective-permute-start.11) | collective-permute-done | bytes 65568 | tf_op jit(solution)/shard_map/ppermute | solution.py:266
  66.9 0.9 collective-permute-done.9
  67.8 2.7 %partials.3 = (f32[16,8,128]{2,1,0:T(8,128)S(1)}, f32[64,128]{1,0:T(8,128)S(1)}) custom-call(f32[128,128]{1,0:T(8,128)S(1)} %add_add_fusion.refs_0_, f32[64,128]{1,0:T(8,128)S(1)} %slice_add_fusion.1.refs_1_, f32[8192,128]{1,0:T(8,128)S(1)} %get-tuple-element.10.refs_2_), custom_call_target="tpu_custom_call" | custom-call | flops 1073741824 | bytes 4194304 | tf_op jit(solution)/shard_map/partials/pallas_call | solution.py:167
  70.5 9.1 %all_to_all.22 = f32[16,8,128]{2,1,0:T(8,128)S(1)} all-to-all(f32[16,8,128]{2,1,0:T(8,128)S(1)} %get-tuple-element.11), channel_id=1, replica_groups=mesh['gx'=8,'gy'=16,'gz'=2] {'gy'}, dimensions={0} | all-to-all | bytes 131072 | tf_op jit(solution)/shard_map/all_to_all | solution.py:314
  79.6 5.1 %collective-permute-start.13 = (f32[72,128]{1,0:T(8,128)S(1)}, f32[72,128]{1,0:T(8,128)S(1)}, u32[]{:S(2)}, u32[]{:S(2)}) collective-permute-start(f32[72,128]{1,0:T(8,128)S(1)} %pad_maximum_fusion), channel_id=1, source_target_pairs={{0,1},{1,0},{2,3},{3,2},{4,5},{5,4},{6,7},{7,6},{8,9},{9,8},{10,11... | collective-permute-start | bytes 110600 | tf_op jit(solution)/shard_map/ppermute | solution.py:280
  84.7 0.9 collective-permute-done.13.other_ref
  85.6 9.4 %all_to_all.23.bc_ref = f32[8,8,128]{2,1,0:T(8,128)S(1)} all-to-all(f32[8,8,128]{2,1,0:T(8,128)S(1)} %fusion.1), channel_id=1, replica_groups=mesh['gx'=8,'gy'=16,'gz'=2] {'gx'}, dimensions={0} | all-to-all | bytes 65536 | tf_op jit(solution)/shard_map/all_to_all | solution.py:319
  95.0 0.6 last_sums.1
  (23 shorter events, 0.8 us)
Async XLA Ops:
  35.9 9.1 %collective-permute-start = (f32[128,128]{1,0:T(8,128)S(1)}, f32[128,128]{1,0:T(8,128)S(1)}, u32[]{:S(2)}, u32[]{:S(2)}) collective-permute-start(f32[128,128]{1,0:T(8,128)S(1)} %get-tuple-element.8), channel_id=1, source_target_pairs={{0,32},{32,64},{64,96},{96,128},{128,160},{160,192},{192,224},{224... | collective-permute-start | bytes 196616 | tf_op jit(solution)/shard_map/ppermute | solution.py:266
  36.2 8.8 %collective-permute-start.1 = (f32[128,128]{1,0:T(8,128)S(1)}, f32[128,128]{1,0:T(8,128)S(1)}, u32[]{:S(2)}, u32[]{:S(2)}) collective-permute-start(f32[128,128]{1,0:T(8,128)S(1)} %get-tuple-element.8), channel_id=1, source_target_pairs={{0,224},{32,0},{64,32},{96,64},{128,96},{160,128},{192,160},{224,1... | collective-permute-start | bytes 196616 | tf_op jit(solution)/shard_map/ppermute | solution.py:266
  38.7 7.2 %collective-permute-start.3 = (f32[128,128]{1,0:T(8,128)S(1)}, f32[128,128]{1,0:T(8,128)S(1)}, u32[]{:S(2)}, u32[]{:S(2)}) collective-permute-start(f32[128,128]{1,0:T(8,128)S(1)} %get-tuple-element.8), channel_id=1, source_target_pairs={{0,64},{32,96},{64,128},{96,160},{128,192},{160,224},{192,0},{224,... | collective-permute-start | bytes 196616 | tf_op jit(solution)/shard_map/ppermute | solution.py:266
  38.7 7.2 %collective-permute-start.4 = (f32[128,128]{1,0:T(8,128)S(1)}, f32[128,128]{1,0:T(8,128)S(1)}, u32[]{:S(2)}, u32[]{:S(2)}) collective-permute-start(f32[128,128]{1,0:T(8,128)S(1)} %get-tuple-element.8), channel_id=1, source_target_pairs={{0,192},{32,224},{64,0},{96,32},{128,64},{160,96},{192,128},{224,1... | collective-permute-start | bytes 196616 | tf_op jit(solution)/shard_map/ppermute | solution.py:266
  42.3 3.6 %collective-permute-start.5 = (f32[128,128]{1,0:T(8,128)S(1)}, f32[128,128]{1,0:T(8,128)S(1)}, u32[]{:S(2)}, u32[]{:S(2)}) collective-permute-start(f32[128,128]{1,0:T(8,128)S(1)} %get-tuple-element.9), channel_id=1, source_target_pairs={{0,1},{1,0},{2,3},{3,2},{4,5},{5,4},{6,7},{7,6},{8,9},{9,8},{10,11... | collective-permute-start | bytes 196616 | tf_op jit(solution)/shard_map/ppermute | solution.py:280
  45.0 8.9 %collective-permute-start.2 = (f32[128,128]{1,0:T(8,128)S(1)}, f32[128,128]{1,0:T(8,128)S(1)}, u32[]{:S(2)}, u32[]{:S(2)}) collective-permute-start(f32[128,128]{1,0:T(8,128)S(1)} %add_add_fusion.3), channel_id=1, source_target_pairs={{0,128},{32,160},{64,192},{96,224},{128,0},{160,32},{192,64},{224,... | collective-permute-start | bytes 196616 | tf_op jit(solution)/shard_map/ppermute | solution.py:266
  54.0 4.4 %collective-permute-start.6 = (f32[128,128]{1,0:T(8,128)S(1)}, f32[128,128]{1,0:T(8,128)S(1)}, u32[]{:S(2)}, u32[]{:S(2)}) collective-permute-start(f32[128,128]{1,0:T(8,128)S(1)} %get-tuple-element.13), channel_id=1, source_target_pairs={{0,2},{2,4},{4,6},{6,0},{8,10},{10,12},{12,14},{14,8},{16,18},{18,... | collective-permute-start | bytes 196616 | tf_op jit(solution)/shard_map/ppermute | solution.py:266
  54.3 4.0 %collective-permute-start.7 = (f32[128,128]{1,0:T(8,128)S(1)}, f32[128,128]{1,0:T(8,128)S(1)}, u32[]{:S(2)}, u32[]{:S(2)}) collective-permute-start(f32[128,128]{1,0:T(8,128)S(1)} %get-tuple-element.13), channel_id=1, source_target_pairs={{0,6},{2,0},{4,2},{6,4},{8,14},{10,8},{12,10},{14,12},{16,22},{18,... | collective-permute-start | bytes 196616 | tf_op jit(solution)/shard_map/ppermute | solution.py:266
  56.7 4.6 %collective-permute-start.8 = (f32[128,128]{1,0:T(8,128)S(1)}, f32[128,128]{1,0:T(8,128)S(1)}, u32[]{:S(2)}, u32[]{:S(2)}) collective-permute-start(f32[128,128]{1,0:T(8,128)S(1)} %get-tuple-element.13), channel_id=1, source_target_pairs={{0,4},{2,6},{4,0},{6,2},{8,12},{10,14},{12,8},{14,10},{16,20},{18,... | collective-permute-start | bytes 196616 | tf_op jit(solution)/shard_map/ppermute | solution.py:266
  56.7 6.7 %collective-permute-start.12 = (f32[64,128]{1,0:T(8,128)S(1)}, f32[64,128]{1,0:T(8,128)S(1)}, u32[]{:S(2)}, u32[]{:S(2)}) collective-permute-start(f32[64,128]{1,0:T(8,128)S(1)} %slice.8), channel_id=1, source_target_pairs={{0,1},{1,0},{2,3},{3,2},{4,5},{5,4},{6,7},{7,6},{8,9},{9,8},{10,11... | collective-permute-start | bytes 98312 | tf_op jit(solution)/shard_map/ppermute | solution.py:280
  61.3 3.2 %collective-permute-start.10 = (f32[128,128]{1,0:T(8,128)S(1)}, f32[128,128]{1,0:T(8,128)S(1)}, u32[]{:S(2)}, u32[]{:S(2)}) collective-permute-start(f32[128,128]{1,0:T(8,128)S(1)} %add_add_fusion.1), channel_id=1, source_target_pairs={{0,24},{2,26},{4,28},{6,30},{8,0},{10,2},{12,4},{14,6},{16,8},{18,... | collective-permute-start | bytes 196616 | tf_op jit(solution)/shard_map/ppermute | solution.py:266
  62.3 4.6 %collective-permute-start.11 = (f32[128,128]{1,0:T(8,128)S(1)}, f32[128,128]{1,0:T(8,128)S(1)}, u32[]{:S(2)}, u32[]{:S(2)}) collective-permute-start(f32[128,128]{1,0:T(8,128)S(1)} %add_add_fusion.1), channel_id=1, source_target_pairs={{0,16},{2,18},{4,20},{6,22},{8,24},{10,26},{12,28},{14,30},{16,0},... | collective-permute-start | bytes 196616 | tf_op jit(solution)/shard_map/ppermute | solution.py:266
  63.5 4.3 %collective-permute-start.9 = (f32[128,128]{1,0:T(8,128)S(1)}, f32[128,128]{1,0:T(8,128)S(1)}, u32[]{:S(2)}, u32[]{:S(2)}) collective-permute-start(f32[128,128]{1,0:T(8,128)S(1)} %add_add_fusion.1), channel_id=1, source_target_pairs={{0,8},{2,10},{4,12},{6,14},{8,16},{10,18},{12,20},{14,22},{16,24},... | collective-permute-start | bytes 196616 | tf_op jit(solution)/shard_map/ppermute | solution.py:266
  79.6 6.0 %collective-permute-start.13 = (f32[72,128]{1,0:T(8,128)S(1)}, f32[72,128]{1,0:T(8,128)S(1)}, u32[]{:S(2)}, u32[]{:S(2)}) collective-permute-start(f32[72,128]{1,0:T(8,128)S(1)} %pad_maximum_fusion), channel_id=1, source_target_pairs={{0,1},{1,0},{2,3},{3,2},{4,5},{5,4},{6,7},{7,6},{8,9},{9,8},{10,11... | collective-permute-start | bytes 110600 | tf_op jit(solution)/shard_map/ppermute | solution.py:280
